TPU v7x, 32 devices: a whole 2x2x4 slice. The times are simulated.
32 devices in a mesh: dom: 8 (over z, x), feat: 4 (over y, core).
Axes of the slice: x: 2, y: 2, z: 4, core: 2. Of those that a mesh axis runs over, the one named last changes fastest.
Arguments:
- node_feats: bfloat16 [16384, 512], P('dom', 'feat'), may hold values from -6 to 6
- edge_tiles: bfloat16 [848, 128, 128], P('dom'), may hold values from -0.14941406 to 0.14941406
- tile_dst: int32 [848], P('dom'), may hold values from 0 to 15, as said below
- tile_src: int32 [848], P('dom'), may hold values from 0 to 25, as said below
- hub_ids: int32 [256], P('dom'), may hold values from 0 to 2047, as said below
- send_rows: int32 [8, 8, 128], P('dom'), may hold values from 0 to 2047
- send_count: int32 [8, 8], P('dom'), may hold values from 32 to 128, as said below
- w_self: bfloat16 [512, 512], P(None, 'feat'), may hold values from -0.25 to 0.25
- w_neigh: bfloat16 [512, 512], P(None, 'feat'), may hold values from -0.25 to 0.25
- out_bias: float32 [512], P('feat'), may hold values from -3 to 3
- grad_out: bfloat16 [16384, 512], P('dom', 'feat'), may hold values from -6 to 6
Outputs:
- output: bfloat16 [16384, 512], P('dom', 'feat')
- grad_feats: float32 [16384, 512], P('dom', 'feat')
- grad_self: float32 [512, 512], P(None, 'feat')
- grad_neigh: float32 [512, 512], P(None, 'feat')
- grad_bias: float32 [512], P('feat')
Inputs may be any that keep to these rules, and one draw needn't show every extreme that they name: `tile_dst`: every one of the 16 blocks of a partition receives at least 5 of its tiles. `tile_src`: source blocks of a partition: its own rows, then all hub rows, then received rows in order of sender; every block is read by at least one tile of every partition. `hub_ids`: distinct within each partition. `send_count`: every partition sends exactly 128 rows to at least one partition, and some partition receives exactly 128 rows from every partition.
All inputs are finite; a program needn't handle non-finite values.
Results may differ from a plain program's by a relative error of at most 0.0055.
Values may be sent and summed in bfloat16 or wider, within the bound.
No kernel may reach another device: no remote copies, remote signals or barrier semaphores. Data moves between devices by JAX's collectives and lax.ppermute only.
A program may use at most 128 MiB of HBM per device.

v0:
```python
import jax
import jax.numpy as jnp
from jax import lax
from jax.sharding import PartitionSpec as P


def body(
    node_feats,
    edge_tiles,
    tile_dst,
    tile_src,
    hub_ids,
    send_rows,
    send_count,
    w_self,
    w_neigh,
    out_bias,
    grad_out,
):
    own_count, width = node_feats.shape
    tile_size = edge_tiles.shape[1]
    peer_count, capacity = (send_rows.shape[1], send_rows.shape[2])
    hub_local = node_feats[hub_ids]
    hub_table = lax.all_gather(hub_local, "dom", axis=0, tiled=True)
    listed = send_rows[0]
    filled = jnp.arange(capacity, dtype=jnp.int32)[None, :] < send_count[0][:, None]
    outgoing = jnp.where(filled[:, :, None], node_feats[listed], jnp.zeros((), node_feats.dtype))
    incoming = lax.all_to_all(outgoing, "dom", split_axis=0, concat_axis=0, tiled=True)
    source = jnp.concatenate(
        [node_feats, hub_table, incoming.reshape(peer_count * capacity, width)], axis=0
    )
    source_blocks = source.shape[0] // tile_size
    row_blocks = own_count // tile_size
    blocks = source.reshape(source_blocks, tile_size, width)
    products = jnp.einsum(
        "tij,tjf->tif", edge_tiles, blocks[tile_src], preferred_element_type=jnp.float32
    )
    summed = jax.ops.segment_sum(products, tile_dst, row_blocks)
    aggregated = summed.reshape(own_count, width).astype(jnp.bfloat16)
    whole_feats, whole_agg = (
        lax.all_gather(node_feats, "feat", axis=1, tiled=True),
        lax.all_gather(aggregated, "feat", axis=1, tiled=True),
    )
    pre_act = (
        jnp.dot(whole_feats, w_self, preferred_element_type=jnp.float32)
        + jnp.dot(whole_agg, w_neigh, preferred_element_type=jnp.float32)
        + out_bias
    )
    gate_sig = jax.nn.sigmoid(pre_act)
    output = (pre_act * gate_sig).astype(jnp.bfloat16)
    grad_pre = (
        grad_out.astype(jnp.float32) * gate_sig * (1.0 + pre_act * (1.0 - gate_sig))
    ).astype(jnp.bfloat16)
    contract_rows = (((0,), (0,)), ((), ()))
    grad_self = lax.dot_general(
        whole_feats, grad_pre, contract_rows, preferred_element_type=jnp.float32
    )
    grad_neigh = lax.dot_general(
        whole_agg, grad_pre, contract_rows, preferred_element_type=jnp.float32
    )
    grad_bias = jnp.sum(grad_pre.astype(jnp.float32), axis=0)
    grad_self, grad_neigh, grad_bias = lax.psum((grad_self, grad_neigh, grad_bias), "dom")
    contract_last = (((1,), (1,)), ((), ()))
    first = lax.dot_general(w_self, grad_pre, contract_last, preferred_element_type=jnp.float32)
    second = lax.dot_general(w_neigh, grad_pre, contract_last, preferred_element_type=jnp.float32)
    shares = lax.psum_scatter(
        jnp.concatenate([first, second], axis=1), "feat", scatter_dimension=0, tiled=True
    )
    direct = shares[:, :own_count].T
    back_agg = shares[:, own_count:].T.astype(jnp.bfloat16)
    back_blocks = back_agg.reshape(row_blocks, tile_size, width)[tile_dst]
    spread = jnp.einsum("tji,tjf->tif", edge_tiles, back_blocks, preferred_element_type=jnp.float32)
    back_source = jax.ops.segment_sum(spread, tile_src, source_blocks).reshape(-1, width)
    hub_total = hub_table.shape[0]
    hub_part = back_source[own_count : own_count + hub_total]
    recv_part = back_source[own_count + hub_total :].reshape(peer_count, capacity, width)
    hub_back = lax.psum_scatter(hub_part, "dom", scatter_dimension=0, tiled=True)
    sent_back = lax.all_to_all(
        recv_part.astype(jnp.bfloat16), "dom", split_axis=0, concat_axis=0, tiled=True
    ).astype(recv_part.dtype)
    returned = jnp.where(filled[:, :, None], sent_back, jnp.zeros((), jnp.float32))
    grad_feats = direct + back_source[:own_count]
    grad_feats = grad_feats.at[hub_ids].add(hub_back)
    grad_feats = grad_feats.at[listed.reshape(-1)].add(
        returned.reshape(peer_count * capacity, width)
    )
    return (output, grad_feats, grad_self, grad_neigh, grad_bias)


def solution(mesh):
    in_specs = (
        P("dom", "feat"),
        P("dom", None, None),
        P("dom"),
        P("dom"),
        P("dom"),
        P("dom", None, None),
        P("dom", None),
        P(None, "feat"),
        P(None, "feat"),
        P("feat"),
        P("dom", "feat"),
    )
    out_specs = (P("dom", "feat"), P("dom", "feat"), P(None, "feat"), P(None, "feat"), P("feat"))
    return jax.shard_map(body, mesh=mesh, in_specs=in_specs, out_specs=out_specs, check_vma=False)
```

profile of v0, /device:TPU:0, one launch (start us, length us, event | category | flops | bytes accessed | tf_op | source)
XLA Modules:
  0.0 419.4 jit_solution(15320924251841132812)
XLA Ops:
  8.8 5.2 %gather_fusion.1 = bf16[1024,128]{1,0:T(8,128)(2,1)} fusion(bf16[2048,128]{1,0:T(8,128)(2,1)} %param.11, s32[1024]{0:T(1024)S(1)} %fusion.3), kind=kCustom, calls=%fused_computation.1 | custom fusion | bytes 528384 | tf_op jit(solution)/shard_map/gather | solution.py:27
  14.7 1.9 broadcast_select_fusion
  16.5 7.3 %all-to-all-start = ((bf16[8,128,128]{2,1,0:T(8,128)(2,1)}), bf16[8,128,128]{2,1,0:T(8,128)(2,1)}, u32[]{:S(2)}, u32[]{:S(2)}) async-start(bf16[8,128,128]{2,1,0:T(8,128)(2,1)} %broadcast_select_fusion), calls=%async_computation | async-start | bytes 524288 | tf_op jit(solution)/shard_map/all_to_all | solution.py:28
  25.6 31.1 %all-gather = bf16[256,128]{1,0:T(8,128)(2,1)S(1)} all-gather(bf16[32,128]{1,0:T(8,128)(2,1)S(1)} %gather_fusion), channel_id=2, replica_groups=mesh['dom'=8,'feat'=4] {'dom'}, dimensions={0}, use_global_device_ids=true | all-gather | bytes 73728 | tf_op jit(solution)/shard_map/all_gather | solution.py:24
  57.4 2.1 pad_maximum_fusion.1
  59.5 4.0 gather_fusion.2
  63.5 7.4 %convolution_bitcast_fusion.3 = f32[106,128,128]{1,2,0:T(8,128)} fusion(bf16[106,128,128]{2,1,0:T(8,128)(2,1)} %gather_fusion.2, bf16[106,128,128]{2,1,0:T(8,128)(2,1)S(1)} %copy-done), kind=kOutput, calls=%fused_computation.12 | convolution fusion | flops 444596224 | bytes 13893632 | tf_op jit(solution)/shard_map/tij,tjf->tif/dot_general | solution.py:35
  70.9 8.3 %copy.20 = f32[106,128,128]{2,1,0:T(8,128)} copy(f32[106,128,128]{1,2,0:T(8,128)} %convolution_bitcast_fusion.3) | data formatting | bytes 13893632 | tf_op jit(solution)/shard_map/tij,tjf->tif/dot_general | solution.py:35
  80.3 22.4 %scatter_fusion = f32[16,128,128]{2,1,0:T(8,128)} fusion(f32[16,128,128]{2,1,0:T(8,128)} %broadcast_in_dim.50, s32[106]{0:T(128)S(1)} %copy-done.6, f32[106,128,128]{2,1,0:T(8,128)} %copy.20), kind=kCustom, calls=%fused_computation.4 | custom fusion | flops 1736704 | bytes 20840872 | tf_op jit(solution)/shard_map/scatter-add | solution.py:38
  102.8 2.1 convert_element_type.26
  105.0 3.3 fusion.4
  108.3 20.4 %all-gather.6.cloned.1.call-done = bf16[2048,512]{1,0:T(8,128)(2,1)} async-done(((bf16[2048,128]{1,0:T(8,128)(2,1)}), bf16[2048,512]{1,0:T(8,128)(2,1)}) %all-gather.6.cloned.1.call-update) | async-done | bytes 2097168 | tf_op jit(solution)/shard_map/all_gather | solution.py:42
  128.6 3.7 convert_reduce_fusion
  132.3 2.7 convolution_bitcast_fusion
  135.0 2.8 convolution_bitcast_fusion.1
  140.4 7.7 %pad_maximum_fusion = f32[512,4096]{0,1:T(8,128)} fusion(f32[512,2048]{0,1:T(8,128)} %convolution_bitcast_fusion, f32[512,2048]{0,1:T(8,128)} %convolution_bitcast_fusion.1), kind=kLoop, calls=%fused_computation.8 | loop fusion | flops 2097152 | bytes 16777216 | tf_op jit(solution)/shard_map/concatenate | solution.py:67
  148.8 22.0 %psum.23 = f32[128]{0:T(128)} all-reduce(f32[128]{0:T(128)S(1)} %get-tuple-element.17), channel_id=1, replica_groups=mesh['dom'=8,'feat'=4] {'dom'}, use_global_device_ids=true, to_apply=%region_9.10 | all-reduce | flops 128 | bytes 1024 | tf_op jit(solution)/shard_map/psum | solution.py:62
  170.8 42.4 %all-reduce.3.cloned.1.call-done = (f32[512,128]{0,1:T(8,128)}, f32[512,128]{1,0:T(8,128)}) async-done(((f32[512,128]{0,1:T(8,128)}, f32[512,128]{1,0:T(8,128)}), (f32[512,128]{0,1:T(8,128)}, f32[512,128]{1,0:T(8,128)})) %all-reduce.3.cloned.1.call-update) | async-done | bytes 524304 | tf_op jit(solution)/shard_map/psum | solution.py:62
  215.0 71.8 %reduce-scatter.3.cloned.1.call-done = f32[128,4096]{0,1:T(8,128)} async-done(((f32[512,4096]{0,1:T(8,128)}), f32[128,4096]{0,1:T(8,128)}) %reduce-scatter.3.cloned.1.call-update) | async-done | bytes 2097168 | tf_op jit(solution)/shard_map/reduce_scatter | solution.py:66
  286.8 2.1 slice.49
  288.9 3.8 gather_fusion.3
  292.7 6.2 %convolution_bitcast_fusion.2 = f32[106,128,128]{1,2,0:T(8,128)} fusion(bf16[106,128,128]{2,1,0:T(8,128)(2,1)} %gather_fusion.3, bf16[106,128,128]{2,1,0:T(8,128)(2,1)S(1)} %copy-done), kind=kOutput, calls=%fused_computation.11 | convolution fusion | flops 444596224 | bytes 13893632 | tf_op jit(solution)/shard_map/tji,tjf->tif/dot_general | solution.py:72
  298.9 8.3 %copy.22 = f32[106,128,128]{2,1,0:T(8,128)} copy(f32[106,128,128]{1,2,0:T(8,128)} %convolution_bitcast_fusion.2) | data formatting | bytes 13893632 | tf_op jit(solution)/shard_map/tji,tjf->tif/dot_general | solution.py:72
  308.7 22.8 %scatter_fusion.1 = f32[26,128,128]{2,1,0:T(8,128)} fusion(f32[26,128,128]{2,1,0:T(8,128)} %broadcast_in_dim.56, s32[106]{0:T(128)S(1)} %copy-done.7, f32[106,128,128]{2,1,0:T(8,128)} %copy.22), kind=kCustom, calls=%fused_computation.5 | custom fusion | flops 1736704 | bytes 20840872 | tf_op jit(solution)/shard_map/scatter-add | solution.py:73
  333.0 1.8 slice.50
  334.8 2.4 slice.41
  337.2 5.4 %all-to-all-start.1 = ((bf16[8,128,128]{2,1,0:T(8,128)(2,1)}), bf16[8,128,128]{2,1,0:T(8,128)(2,1)}, u32[]{:S(2)}, u32[]{:S(2)}) async-start(bf16[8,128,128]{2,1,0:T(8,128)(2,1)} %slice.50), calls=%async_computation.3 | async-start | bytes 524288 | tf_op jit(solution)/shard_map/all_to_all | solution.py:78
  342.6 2.6 fusion.1
  345.3 53.0 %reduce-scatter.5.cloned.1.call-done = f32[32,128]{1,0:T(8,128)} async-done(((f32[256,128]{1,0:T(8,128)}), f32[32,128]{1,0:T(8,128)}) %reduce-scatter.5.cloned.1.call-update) | async-done | bytes 16400 | tf_op jit(solution)/shard_map/reduce_scatter | solution.py:77
  398.2 3.1 scatter_fusion.2
  401.3 1.9 convert_select_fusion
  403.2 8.0 %scatter_fusion.3 = f32[2048,128]{1,0:T(8,128)} fusion(f32[2048,128]{1,0:T(8,128)} %scatter_fusion.2, s32[1024]{0:T(1024)S(1)} %bitcast.56, f32[1024,128]{1,0:T(8,128)} %bitcast.53), kind=kCustom, calls=%fused_computation.7 | custom fusion | flops 131072 | bytes 1576960 | tf_op jit(solution)/shard_map/scatter-add | solution.py:84
  (50 shorter events, 15.7 us)
Async XLA Ops:
  7.2 56.3 %copy-start = (bf16[106,128,128]{2,1,0:T(8,128)(2,1)S(1)}, bf16[106,128,128]{2,1,0:T(8,128)(2,1)}, u32[]{:S(2)}) copy-start(bf16[106,128,128]{2,1,0:T(8,128)(2,1)} %param.12) | copy-start | bytes 10420228
  7.2 16.7 %copy-start.8 = (s32[32]{0:T(128)S(1)}, s32[32]{0:T(128)}, u32[]{:S(2)}) copy-start(s32[32]{0:T(128)} %param.15) | copy-start | bytes 388
  7.2 97.8 %all-gather.4.cloned.1.call-start = ((), (), s32[]{:S(2)}) async-start(), calls=%async_computation.4 | async-start | bytes 2621440 | tf_op jit(solution)/shard_map/all_gather | solution.py:41
  16.5 40.8 %all-to-all-start = ((bf16[8,128,128]{2,1,0:T(8,128)(2,1)}), bf16[8,128,128]{2,1,0:T(8,128)(2,1)}, u32[]{:S(2)}, u32[]{:S(2)}) async-start(bf16[8,128,128]{2,1,0:T(8,128)(2,1)} %broadcast_select_fusion), calls=%async_computation | async-start | bytes 524288 | tf_op jit(solution)/shard_map/all_to_all | solution.py:28
  23.8 104.8 %all-gather.6.cloned.1.call-start = ((), (), s32[]{:S(2)}) async-start(), calls=%async_computation.5 | async-start | bytes 2621440 | tf_op jit(solution)/shard_map/all_gather | solution.py:42
  70.9 9.4 %copy-start.6 = (s32[106]{0:T(128)S(1)}, s32[106]{0:T(128)}, u32[]{:S(2)}) copy-start(s32[106]{0:T(128)} %param.13) | copy-start | bytes 1276
  102.8 25.9 %copy-start.9 = (f32[128]{0:T(128)S(1)}, f32[128]{0:T(128)}, u32[]{:S(2)}) copy-start(f32[128]{0:T(128)} %param.20) | copy-start | bytes 1540
  104.9 108.3 %all-reduce.3.cloned.1.call-start = ((), (), s32[]{:S(2)}) async-start(), calls=%async_computation.8 | async-start | bytes 1048576 | tf_op jit(solution)/shard_map/psum | solution.py:62
  128.6 3.7 copy-start.4
  132.3 2.7 copy-start.3
  135.0 2.8 copy-start.2
  135.0 4.2 %copy-start.1 = (bf16[2048,512]{1,0:T(8,128)(2,1)S(1)}, bf16[2048,512]{1,0:T(8,128)(2,1)}, u32[]{:S(2)}) copy-start(bf16[2048,512]{1,0:T(8,128)(2,1)} %all-gather.4.cloned.1.call-done) | copy-start | bytes 6291460
  140.4 146.4 %reduce-scatter.3.cloned.1.call-start = ((), (), s32[]{:S(2)}) async-start(), calls=%async_computation.6 | async-start | bytes 10485760 | tf_op jit(solution)/shard_map/reduce_scatter | solution.py:66
  148.1 0.7 copy-start.5
  148.1 250.1 %reduce-scatter.5.cloned.1.call-start = ((), (), s32[]{:S(2)}) async-start(), calls=%async_computation.7 | async-start | bytes 147456 | tf_op jit(solution)/shard_map/reduce_scatter | solution.py:77
  298.9 9.7 %copy-start.7 = (s32[106]{0:T(128)S(1)}, s32[106]{0:T(128)}, u32[]{:S(2)}) copy-start(s32[106]{0:T(128)} %param.14) | copy-start | bytes 1276
  337.2 64.1 %all-to-all-start.1 = ((bf16[8,128,128]{2,1,0:T(8,128)(2,1)}), bf16[8,128,128]{2,1,0:T(8,128)(2,1)}, u32[]{:S(2)}, u32[]{:S(2)}) async-start(bf16[8,128,128]{2,1,0:T(8,128)(2,1)} %slice.50), calls=%async_computation.3 | async-start | bytes 524288 | tf_op jit(solution)/shard_map/all_to_all | solution.py:78
Sparse Core Ops, SparseCore 0:
  9.6 25.5 all-gather.3
  105.0 23.5 all-gather.5
  140.5 72.6 all-reduce.2
  215.8 70.9 reduce-scatter.2
  337.3 60.8 reduce-scatter.4
where the time goes:
time: 421 us; the launch traced here: 419 us
  waiting for transfers between devices  188 us (45%)
  other arithmetic  76.8 us (18%)
  blocking collectives  53.2 us (13%)
  local copies, waits for them, and re-layouts  45.8 us (11%)
  matrix products  28.6 us (7%)
  between operations  13.9 us (3%)
  starting transfers between devices  12.9 us (3%)
    reduce_scatter x1, waiting for transfers between devices, body(): lax.psum_scatter(jnp.concatenate([first, second], axis=1), 'feat', scatte...  71.8 us
    reduce_scatter x1, waiting for transfers between devices, body(): lax.psum_scatter(hub_part, 'dom', scatter_dimension=0, tiled=True)  53 us
    psum x1, waiting for transfers between devices, body(): lax.psum((grad_self, grad_neigh, grad_bias), 'dom')  42.4 us
    all_gather x1, blocking collectives, body(): hub_table = lax.all_gather(hub_local, 'dom', axis=0, tiled=True)  31.1 us
    scatter-add x1, other arithmetic, body(): jax.ops.segment_sum(spread, tile_src, source_blocks).reshape(-1, width)  22.8 us
    scatter-add x1, other arithmetic, body(): summed = jax.ops.segment_sum(products, tile_dst, row_blocks)  22.4 us
    psum x1, blocking collectives, body(): lax.psum((grad_self, grad_neigh, grad_bias), 'dom')  22 us
    all_gather x1, waiting for transfers between devices, body(): lax.all_gather(aggregated, 'feat', axis=1, tiled=True)  20.4 us
  transfers between devices with their start and end apart: 7, of which 4 were waited for; matrix products, arithmetic and copies ran while one was open for 18% of the time, Pallas kernels for 0%

commit v1 on v0

v1 whole, which is shorter than its diff:
```python
import jax
import jax.numpy as jnp
from jax import lax
from jax.sharding import PartitionSpec as P

F32 = jnp.float32
BF16 = jnp.bfloat16


def body(
    node_feats,
    edge_tiles,
    tile_dst,
    tile_src,
    hub_ids,
    send_rows,
    send_count,
    w_self,
    w_neigh,
    out_bias,
    grad_out,
    *,
    n_feat,
):
    own_count, width = node_feats.shape
    tile_size = edge_tiles.shape[1]
    n_dom, capacity = send_rows.shape[1], send_rows.shape[2]
    hub_dev = hub_ids.shape[0]
    me = lax.axis_index("feat")
    order = me ^ jnp.arange(n_feat, dtype=jnp.int32)

    def swap(x, k):
        return lax.ppermute(x, "feat", [(j, j ^ k) for j in range(n_feat)])

    def gather_feat(x):
        shards = {0: x}
        bit = n_feat // 2
        while bit:
            for k in list(shards):
                shards[k ^ bit] = swap(shards[k], bit)
            bit //= 2
        return [shards[k] for k in range(n_feat)]

    whole_feats = jnp.concatenate(gather_feat(node_feats), axis=1)

    listed = send_rows[0]
    slots = jnp.arange(capacity, dtype=jnp.int32)
    filled = slots[None, :] < send_count[0][:, None]
    index = jnp.concatenate(
        [listed, jnp.broadcast_to(hub_ids[None, :], (n_dom, hub_dev))], axis=1
    )
    keep = jnp.concatenate([filled, jnp.ones((n_dom, hub_dev), bool)], axis=1)
    outgoing = jnp.where(keep[:, :, None], node_feats[index], jnp.zeros((), BF16))
    incoming = lax.all_to_all(outgoing, "dom", 0, 0, tiled=True)
    source = jnp.concatenate(
        [
            node_feats,
            incoming[:, capacity:].reshape(-1, width),
            incoming[:, :capacity].reshape(-1, width),
        ],
        axis=0,
    )
    source_blocks = source.shape[0] // tile_size
    row_blocks = own_count // tile_size
    blocks = source.reshape(source_blocks, tile_size, width)
    products = jnp.einsum("tij,tjf->tif", edge_tiles, blocks[tile_src], preferred_element_type=F32)
    summed = jax.ops.segment_sum(products, tile_dst, row_blocks)
    aggregated = summed.reshape(own_count, width).astype(BF16)

    whole_agg = jnp.concatenate(gather_feat(aggregated), axis=1)
    ws = w_self.reshape(n_feat, width, -1)[order].reshape(-1, w_self.shape[1])
    wn = w_neigh.reshape(n_feat, width, -1)[order].reshape(-1, w_self.shape[1])
    pre_act = (
        jnp.dot(whole_feats, ws, preferred_element_type=F32)
        + jnp.dot(whole_agg, wn, preferred_element_type=F32)
        + out_bias
    )
    gate_sig = jax.nn.sigmoid(pre_act)
    output = (pre_act * gate_sig).astype(BF16)
    grad_pre = (grad_out.astype(F32) * gate_sig * (1.0 + pre_act * (1.0 - gate_sig))).astype(BF16)

    whole_grad = jnp.concatenate(gather_feat(grad_pre), axis=1)

    contract_rows = (((0,), (0,)), ((), ()))
    part_self = lax.dot_general(whole_feats, grad_pre, contract_rows, preferred_element_type=F32)
    part_neigh = lax.dot_general(whole_agg, grad_pre, contract_rows, preferred_element_type=F32)
    part_bias = jnp.sum(grad_pre.astype(F32), axis=0, keepdims=True)
    parts = jnp.stack([part_self, part_neigh]).reshape(n_dom, -1, width)
    chunk = parts.shape[1]
    parts = jnp.concatenate([parts, jnp.broadcast_to(part_bias[None], (n_dom, 8, width))], axis=1)
    summed_w = jnp.sum(lax.all_to_all(parts, "dom", 0, 0, tiled=True), axis=0)
    grad_bias = summed_w[chunk]
    weights_out = summed_w[:chunk].astype(BF16)

    both = jnp.stack([w_self, w_neigh]).reshape(2, n_feat, width, -1)[:, order]
    rows = lax.concatenate(
        [both[:, 0:1]] + [swap(both[:, k : k + 1], k) for k in range(1, n_feat)], 1
    )
    contract_last = (((1,), (2,)), ((), ()))

    def back(w):
        return lax.dot_general(
            whole_grad,
            w.transpose(1, 0, 2).reshape(width, -1),
            (((1,), (1,)), ((), ())),
            preferred_element_type=F32,
        )

    direct = back(rows[0])
    back_agg = back(rows[1]).astype(BF16)
    back_blocks = back_agg.reshape(row_blocks, tile_size, width)[tile_dst]
    spread = jnp.einsum("tji,tjf->tif", edge_tiles, back_blocks, preferred_element_type=F32)
    back_source = jax.ops.segment_sum(spread, tile_src, source_blocks).reshape(-1, width)
    hub_total = n_dom * hub_dev
    hub_part = back_source[own_count : own_count + hub_total].reshape(n_dom, hub_dev, width)
    recv_part = back_source[own_count + hub_total :].reshape(n_dom, capacity, width)
    back_out = jnp.concatenate(
        [
            recv_part.astype(BF16),
            hub_part.astype(BF16),
            jnp.broadcast_to(weights_out[None], (n_dom, chunk, width)),
        ],
        axis=1,
    )
    back_in = lax.all_to_all(back_out, "dom", 0, 0, tiled=True)
    weights_in = back_in[:, capacity + hub_dev :].reshape(2, n_feat, width, -1)[:, order]
    grads = weights_in.astype(F32).reshape(2, n_feat * width, -1)
    rows_in = back_in[:, : capacity + hub_dev].astype(F32)
    rows_in = jnp.where(keep[:, :, None], rows_in, 0.0)
    grad_feats = direct + back_source[:own_count]
    grad_feats = grad_feats.at[index.reshape(-1)].add(rows_in.reshape(-1, width))
    return (output, grad_feats, grads[0], grads[1], grad_bias)


def solution(mesh):
    in_specs = (
        P("dom", "feat"),
        P("dom", None, None),
        P("dom"),
        P("dom"),
        P("dom"),
        P("dom", None, None),
        P("dom", None),
        P(None, "feat"),
        P(None, "feat"),
        P("feat"),
        P("dom", "feat"),
    )
    out_specs = (P("dom", "feat"), P("dom", "feat"), P(None, "feat"), P(None, "feat"), P("feat"))
    n_feat = mesh.shape["feat"]

    def run(*args):
        return body(*args, n_feat=n_feat)

    return jax.shard_map(run, mesh=mesh, in_specs=in_specs, out_specs=out_specs, check_vma=False)
```

time: 421 us -> 217 us (0.52)
  waiting for transfers between devices: 188 us -> 24.7 us
  blocking collectives: 53.2 us -> 0 us
  local copies, waits for them, and re-layouts: 45.8 us -> 62.4 us
  between operations: 13.9 us -> 0.86 us
  starting transfers between devices: 12.9 us -> 24.8 us
    reduce_scatter x2 -> x0, waiting for transfers between devices: 125 us -> none  [the longest x1 71.8 us: body(): lax.psum_scatter(jnp.concatenate([first, second], axis=1), 'feat', scatte...]
    psum x1 -> x0, waiting for transfers between devices: 42.4 us -> none  [body(): lax.psum((grad_self, grad_neigh, grad_bias), 'dom')]
    all_gather x1 -> x0, blocking collectives: 31.1 us -> none  [body(): hub_table = lax.all_gather(hub_local, 'dom', axis=0, tiled=True)]
    psum x1 -> x0, blocking collectives: 22 us -> none  [body(): lax.psum((grad_self, grad_neigh, grad_bias), 'dom')]
    all_gather x2 -> x0, waiting for transfers between devices: 20.4 us -> none  [the longest x1 20.4 us: body(): lax.all_gather(aggregated, 'feat', axis=1, tiled=True)]
    all_to_all x2 -> x3, waiting for transfers between devices: 0.01 us -> 19 us  [the longest x1 8.87 us: body(): incoming = lax.all_to_all(outgoing, 'dom', 0, 0, tiled=True)]
    ppermute x0 -> x12, starting transfers between devices: none -> 7.86 us  [swap(): return lax.ppermute(x, 'feat', [(j, j ^ k) for j in range(n_feat)])]
    gather x2 -> x5, local copies, waits for them, and re-layouts: 6.88 us -> 13.1 us  [the longest x1 4.27 us: body(): node_feats[index]]
  transfers between devices with their start and end apart: 7 -> 15, of which waited for: 4 -> 5; matrix products, arithmetic and copies ran while one was open for 18% -> 38% of each run, Pallas kernels for 0% -> 0%
where the time goes in v1:
time: 217 us; the launch traced here: 214 us
  other arithmetic  74 us (34%)
  local copies, waits for them, and re-layouts  62.4 us (29%)
  matrix products  27.6 us (13%)
  starting transfers between devices  24.8 us (11%)
  waiting for transfers between devices  24.7 us (11%)
    scatter-add x1, other arithmetic, body(): jax.ops.segment_sum(spread, tile_src, source_blocks).reshape(-1, width)  23 us
    scatter-add x1, other arithmetic, body(): summed = jax.ops.segment_sum(products, tile_dst, row_blocks)  22.4 us
    scatter-add x1, other arithmetic, body(): grad_feats.at[index.reshape(-1)].add(rows_in.reshape(-1, width))  10.5 us
    all_to_all x1, waiting for transfers between devices, body(): incoming = lax.all_to_all(outgoing, 'dom', 0, 0, tiled=True)  8.87 us
    dot_general x1, local copies, waits for them, and re-layouts, body(): jnp.einsum('tij,tjf->tif', edge_tiles, blocks[tile_src], preferred_elemen...  8.31 us
    dot_general x1, local copies, waits for them, and re-layouts, body(): jnp.einsum('tji,tjf->tif', edge_tiles, back_blocks, preferred_element_typ...  8.29 us
    ppermute x12, starting transfers between devices, swap(): return lax.ppermute(x, 'feat', [(j, j ^ k) for j in range(n_feat)])  7.86 us
    dot_general x1, matrix products, body(): jnp.einsum('tij,tjf->tif', edge_tiles, blocks[tile_src], preferred_elemen...  7.42 us
  transfers between devices with their start and end apart: 15, of which 5 were waited for; matrix products, arithmetic and copies ran while one was open for 38% of the time, Pallas kernels for 0%

profile of v1, /device:TPU:0, one launch (start us, length us, event | category | flops | bytes accessed | tf_op | source)
XLA Modules:
  0.0 214.3 jit_solution(10511885489220374692)
XLA Ops:
  3.5 4.3 %gather_fusion.1 = bf16[1280,128]{1,0:T(8,128)(2,1)} fusion(bf16[2048,128]{1,0:T(8,128)(2,1)} %param.11, s32[2048]{0:T(1024)S(1)} %pad_clamp_fusion), kind=kCustom, calls=%fused_computation.1 | custom fusion | bytes 660480 | tf_op jit(solution)/shard_map/gather | solution.py:53
  7.8 1.9 broadcast_select_fusion
  9.7 7.2 %all-to-all-start = ((bf16[8,160,128]{2,1,0:T(8,128)(2,1)}), bf16[8,160,128]{2,1,0:T(8,128)(2,1)}, u32[]{:S(2)}, u32[]{:S(2)}) async-start(bf16[8,160,128]{2,1,0:T(8,128)(2,1)} %broadcast_select_fusion), calls=%async_computation | async-start | bytes 655360 | tf_op jit(solution)/shard_map/all_to_all | solution.py:54
  18.5 8.9 %all-to-all-done = bf16[8,160,128]{2,1,0:T(8,128)(2,1)} async-done(((bf16[8,160,128]{2,1,0:T(8,128)(2,1)}), bf16[8,160,128]{2,1,0:T(8,128)(2,1)}, u32[]{:S(2)}, u32[]{:S(2)}) %all-to-all-start) | async-done | bytes 327712 | tf_op jit(solution)/shard_map/all_to_all | solution.py:54
  29.2 2.0 pad_maximum_fusion.2
  31.2 4.0 %gather_fusion.2 = bf16[106,128,128]{2,1,0:T(8,128)(2,1)} fusion(bf16[26,128,128]{2,1,0:T(8,128)(2,1)} %bitcast.62, s32[1024]{0:T(1024)S(1)} %get-tuple-element.16), kind=kCustom, calls=%fused_computation.2 | custom fusion | bytes 6947240 | tf_op jit(solution)/shard_map/gather | solution.py:66
  35.2 7.4 %convolution_bitcast_fusion.1 = f32[106,128,128]{1,2,0:T(8,128)} fusion(bf16[106,128,128]{2,1,0:T(8,128)(2,1)} %gather_fusion.2, bf16[106,128,128]{2,1,0:T(8,128)(2,1)S(1)} %copy-done), kind=kOutput, calls=%fused_computation.11 | convolution fusion | flops 444596224 | bytes 13893632 | tf_op jit(solution)/shard_map/tij,tjf->tif/dot_general | solution.py:66
  42.7 8.3 %copy.23 = f32[106,128,128]{2,1,0:T(8,128)} copy(f32[106,128,128]{1,2,0:T(8,128)} %convolution_bitcast_fusion.1) | data formatting | bytes 13893632 | tf_op jit(solution)/shard_map/tij,tjf->tif/dot_general | solution.py:66
  52.1 22.4 %scatter_fusion = f32[16,128,128]{2,1,0:T(8,128)} fusion(f32[16,128,128]{2,1,0:T(8,128)} %broadcast_in_dim.38, s32[106]{0:T(128)S(1)} %copy-done.5, f32[106,128,128]{2,1,0:T(8,128)} %copy.23), kind=kCustom, calls=%fused_computation.7 | custom fusion | flops 1736704 | bytes 20840872 | tf_op jit(solution)/shard_map/scatter-add | solution.py:67
  74.5 2.1 convert_element_type.33
  80.5 2.1 gather_fusion.3
  82.6 2.1 gather_fusion
  84.8 3.5 %collective-permute-done.4 = bf16[2048,128]{1,0:T(8,128)(2,1)} collective-permute-done((bf16[2048,128]{1,0:T(8,128)(2,1)}, bf16[2048,128]{1,0:T(8,128)(2,1)}, u32[]{:S(2)}, u32[]{:S(2)}) %collective-permute-start.4) | collective-permute-done | bytes 524320 | tf_op jit(solution)/shard_map/ppermute | solution.py:33
  88.2 1.9 constant_dynamic-update-slice_fusion.2
  92.0 1.9 constant_dynamic-update-slice_fusion
  94.0 2.1 fusion.1
  101.2 2.1 convolution_bitcast_fusion.2
  104.2 5.5 %all-to-all-start.1 = ((f32[8,136,128]{2,1,0:T(8,128)}), f32[8,136,128]{2,1,0:T(8,128)}, u32[]{:S(2)}, u32[]{:S(2)}) async-start(f32[8,136,128]{2,1,0:T(8,128)} %pad_maximum_fusion.4), calls=%async_computation.1 | async-start | bytes 1114112 | tf_op jit(solution)/shard_map/all_to_all | solution.py:91
  111.4 2.2 %gather_fusion.4 = bf16[4,2,128,128]{3,2,1,0:T(8,128)(2,1)} fusion(bf16[2,4,128,128]{3,2,1,0:T(8,128)(2,1)} %pad_maximum_fusion.10, s32[1024]{0:T(1024)S(1)} %get-tuple-element.17), kind=kCustom, calls=%fused_computation.4 | custom fusion | bytes 524304 | tf_op jit(solution)/shard_map/gather | solution.py:95
  117.3 2.2 %collective-permute-done.10 = bf16[2,1,128,128]{3,2,0,1:T(8,128)(2,1)S(1)} collective-permute-done((bf16[2,1,128,128]{3,2,0,1:T(8,128)(2,1)S(1)}, bf16[2,1,128,128]{3,2,0,1:T(8,128)(2,1)S(1)}, u32[]{:S(2)}, u32[]{:S(2)}) %collective-permute-start.10) | collective-permute-done | bytes 65568 | tf_op jit(solution)/shard_map/ppermute | solution.py:33
  122.0 3.4 %all-to-all-done.1 = f32[8,136,128]{2,1,0:T(8,128)} async-done(((f32[8,136,128]{2,1,0:T(8,128)}), f32[8,136,128]{2,1,0:T(8,128)}, u32[]{:S(2)}, u32[]{:S(2)}) %all-to-all-start.1) | async-done | bytes 557088 | tf_op jit(solution)/shard_map/all_to_all | solution.py:91
  127.1 3.0 %convolution_convert_fusion = bf16[2048,128]{1,0:T(8,128)(2,1)} fusion(bf16[128,512]{0,1:T(8,128)(2,1)} %bitcast.80, bf16[2048,128]{1,0:T(8,128)(2,1)} %collective-permute-done.8, bf16[2048,128]{1,0:T(8,128)(2,1)} %collective-permute-done.7, bf16[2048,128]{1,0:T(8,128)(2,1)} %collective-permute-done.6, bf16[2048,128]{1,0:T(8,128)(2,1)} %get-tuple-element.6), kind=kOutput, calls=%fused_computation.15 | convolution fusion | flops 277086208 | bytes 2752512 | tf_op jit(solution)/shard_map/dot_general | solution.py:102
  130.2 3.8 %gather_fusion.5 = bf16[106,128,128]{2,1,0:T(8,128)(2,1)} fusion(bf16[16,128,128]{2,1,0:T(8,128)(2,1)} %bitcast.61, s32[1024]{0:T(1024)S(1)} %pad_clamp_fusion.1), kind=kCustom, calls=%fused_computation.5 | custom fusion | bytes 6947240 | tf_op jit(solution)/shard_map/gather | solution.py:111
  134.0 6.2 %convolution_bitcast_fusion = f32[106,128,128]{1,2,0:T(8,128)} fusion(bf16[106,128,128]{2,1,0:T(8,128)(2,1)} %gather_fusion.5, bf16[106,128,128]{2,1,0:T(8,128)(2,1)S(1)} %copy-done), kind=kOutput, calls=%fused_computation.10 | convolution fusion | flops 444596224 | bytes 13893632 | tf_op jit(solution)/shard_map/tji,tjf->tif/dot_general | solution.py:112
  140.2 8.3 %copy.27 = f32[106,128,128]{2,1,0:T(8,128)} copy(f32[106,128,128]{1,2,0:T(8,128)} %convolution_bitcast_fusion) | data formatting | bytes 13893632 | tf_op jit(solution)/shard_map/tji,tjf->tif/dot_general | solution.py:112
  149.9 23.0 %scatter_fusion.1 = f32[26,128,128]{2,1,0:T(8,128)} fusion(f32[26,128,128]{2,1,0:T(8,128)} %broadcast_in_dim.76, s32[106]{0:T(128)S(1)} %copy-done.6, f32[106,128,128]{2,1,0:T(8,128)} %copy.27), kind=kCustom, calls=%fused_computation.8 | custom fusion | flops 1736704 | bytes 20840872 | tf_op jit(solution)/shard_map/scatter-add | solution.py:113
  176.2 4.2 %all-to-all-start.2 = ((bf16[8,288,128]{2,1,0:T(8,128)(2,1)}), bf16[8,288,128]{2,1,0:T(8,128)(2,1)}, u32[]{:S(2)}, u32[]{:S(2)}) async-start(bf16[8,288,128]{2,1,0:T(8,128)(2,1)} %pad_maximum_fusion.3), calls=%async_computation.2 | async-start | bytes 1179648 | tf_op jit(solution)/shard_map/all_to_all | solution.py:125
  186.0 3.2 %convolution_add_fusion = f32[2048,128]{1,0:T(8,128)} fusion(f32[2048,128]{1,0:T(8,128)S(1)} %bitcast.68, bf16[128,512]{0,1:T(8,128)(2,1)} %bitcast.81, bf16[2048,128]{1,0:T(8,128)(2,1)} %collective-permute-done.8, bf16[2048,128]{1,0:T(8,128)(2,1)} %collective-permute-done.7, bf16[2048,128]{1,0:T(8,128)(2,1)} %collective-permute-done.6, ...), kind=kOutput, calls=%fused_computation.12 | convolution fusion | flops 277086208 | bytes 4325376 | tf_op jit(solution)/shard_map/dot_general | solution.py:102
  189.2 6.8 %all-to-all-done.2 = bf16[8,288,128]{2,1,0:T(8,128)(2,1)} async-done(((bf16[8,288,128]{2,1,0:T(8,128)(2,1)}), bf16[8,288,128]{2,1,0:T(8,128)(2,1)}, u32[]{:S(2)}, u32[]{:S(2)}) %all-to-all-start.2) | async-done | bytes 589856 | tf_op jit(solution)/shard_map/all_to_all | solution.py:125
  197.6 2.4 %gather_fusion.6 = bf16[4,2,128,128]{3,2,1,0:T(8,128)(2,1)} fusion(bf16[2,4,128,128]{3,2,1,0:T(8,128)(2,1)} %bitcast.67, s32[1024]{0:T(1024)} %copy-done.3), kind=kCustom, calls=%fused_computation.6 | custom fusion | bytes 524304 | tf_op jit(solution)/shard_map/gather | solution.py:126
  201.8 2.1 convert_select_fusion
  203.8 10.5 %scatter_fusion.2 = f32[2048,128]{1,0:T(8,128)} fusion(f32[2048,128]{1,0:T(8,128)} %convolution_add_fusion, s32[1280]{0:T(1024)S(1)} %fusion.2, f32[1280,128]{1,0:T(8,128)} %bitcast.63), kind=kCustom, calls=%fused_computation.9 | custom fusion | flops 163840 | bytes 1971200 | tf_op jit(solution)/shard_map/scatter-add | solution.py:131
  (83 shorter events, 42.4 us)
Async XLA Ops:
  0.6 34.6 %copy-start = (bf16[106,128,128]{2,1,0:T(8,128)(2,1)S(1)}, bf16[106,128,128]{2,1,0:T(8,128)(2,1)}, u32[]{:S(2)}) copy-start(bf16[106,128,128]{2,1,0:T(8,128)(2,1)} %param.12) | copy-start | bytes 10420228
  0.6 17.8 %copy-start.6 = (s32[106]{0:T(128)S(1)}, s32[106]{0:T(128)}, u32[]{:S(2)}) copy-start(s32[106]{0:T(128)} %param.14) | copy-start | bytes 1276
  1.5 0.5 copy-start.4
  9.7 17.7 %all-to-all-start = ((bf16[8,160,128]{2,1,0:T(8,128)(2,1)}), bf16[8,160,128]{2,1,0:T(8,128)(2,1)}, u32[]{:S(2)}, u32[]{:S(2)}) async-start(bf16[8,160,128]{2,1,0:T(8,128)(2,1)} %broadcast_select_fusion), calls=%async_computation | async-start | bytes 655360 | tf_op jit(solution)/shard_map/all_to_all | solution.py:54
  17.0 61.2 %collective-permute-start.1 = (bf16[2048,128]{1,0:T(8,128)(2,1)}, bf16[2048,128]{1,0:T(8,128)(2,1)}, u32[]{:S(2)}, u32[]{:S(2)}) collective-permute-start(bf16[2048,128]{1,0:T(8,128)(2,1)} %param.11), channel_id=1, source_target_pairs={{0,2},{1,3},{2,0},{3,1},{4,6},{5,7},{6,4},{7,5},{8,10},{9,11},{10,... | collective-permute-start | bytes 1572872 | tf_op jit(solution)/shard_map/ppermute | solution.py:33
  18.5 92.9 %copy-start.3 = (s32[1024]{0:T(1024)}, s32[1024]{0:T(1024)S(1)}, u32[]{:S(2)}) copy-start(s32[1024]{0:T(1024)S(1)} %get-tuple-element.17) | copy-start | bytes 12292
  42.7 9.4 %copy-start.5 = (s32[106]{0:T(128)S(1)}, s32[106]{0:T(128)}, u32[]{:S(2)}) copy-start(s32[106]{0:T(128)} %param.13) | copy-start | bytes 1276
  76.6 11.6 %collective-permute-start.4 = (bf16[2048,128]{1,0:T(8,128)(2,1)}, bf16[2048,128]{1,0:T(8,128)(2,1)}, u32[]{:S(2)}, u32[]{:S(2)}) collective-permute-start(bf16[2048,128]{1,0:T(8,128)(2,1)} %bitcast.10), channel_id=1, source_target_pairs={{0,2},{1,3},{2,0},{3,1},{4,6},{5,7},{6,4},{7,5},{8,10},{9,11},{10,... | collective-permute-start | bytes 1572872 | tf_op jit(solution)/shard_map/ppermute | solution.py:33
  78.1 10.1 %collective-permute-start = (bf16[2048,128]{1,0:T(8,128)(2,1)}, bf16[2048,128]{1,0:T(8,128)(2,1)}, u32[]{:S(2)}, u32[]{:S(2)}) collective-permute-start(bf16[2048,128]{1,0:T(8,128)(2,1)} %param.11), channel_id=1, source_target_pairs={{0,1},{1,0},{2,3},{3,2},{4,5},{5,4},{6,7},{7,6},{8,9},{9,8},{10,11... | collective-permute-start | bytes 1572872 | tf_op jit(solution)/shard_map/ppermute | solution.py:33
  78.1 13.9 %collective-permute-start.2 = (bf16[2048,128]{1,0:T(8,128)(2,1)}, bf16[2048,128]{1,0:T(8,128)(2,1)}, u32[]{:S(2)}, u32[]{:S(2)}) collective-permute-start(bf16[2048,128]{1,0:T(8,128)(2,1)} %collective-permute-done.1), channel_id=1, source_target_pairs={{0,1},{1,0},{2,3},{3,2},{4,5},{5,4},{6,7},{7,6},{8,9},{9,8},{10,11... | collective-permute-start | bytes 1572872 | tf_op jit(solution)/shard_map/ppermute | solution.py:33
  84.8 9.2 %collective-permute-start.3 = (bf16[2048,128]{1,0:T(8,128)(2,1)}, bf16[2048,128]{1,0:T(8,128)(2,1)S(1)}, u32[]{:S(2)}, u32[]{:S(2)}) collective-permute-start(bf16[2048,128]{1,0:T(8,128)(2,1)} %bitcast.10), channel_id=1, source_target_pairs={{0,1},{1,0},{2,3},{3,2},{4,5},{5,4},{6,7},{7,6},{8,9},{9,8},{10,11... | collective-permute-start | bytes 1572872 | tf_op jit(solution)/shard_map/ppermute | solution.py:33
  88.2 5.7 %collective-permute-start.5 = (bf16[2048,128]{1,0:T(8,128)(2,1)}, bf16[2048,128]{1,0:T(8,128)(2,1)S(1)}, u32[]{:S(2)}, u32[]{:S(2)}) collective-permute-start(bf16[2048,128]{1,0:T(8,128)(2,1)} %collective-permute-done.4), channel_id=1, source_target_pairs={{0,1},{1,0},{2,3},{3,2},{4,5},{5,4},{6,7},{7,6},{8,9},{9,8},{10,11... | collective-permute-start | bytes 1572872 | tf_op jit(solution)/shard_map/ppermute | solution.py:33
  93.9 2.1 copy-start.1
  93.9 2.1 copy-start.2
  93.9 2.1 copy-start.7
  94.0 2.1 copy-start.8
  99.6 17.2 %collective-permute-start.7 = (bf16[2048,128]{1,0:T(8,128)(2,1)}, bf16[2048,128]{1,0:T(8,128)(2,1)}, u32[]{:S(2)}, u32[]{:S(2)}) collective-permute-start(bf16[2048,128]{1,0:T(8,128)(2,1)} %get-tuple-element.6), channel_id=1, source_target_pairs={{0,2},{1,3},{2,0},{3,1},{4,6},{5,7},{6,4},{7,5},{8,10},{9,11},{10,... | collective-permute-start | bytes 1572872 | tf_op jit(solution)/shard_map/ppermute | solution.py:33
  104.2 21.2 %all-to-all-start.1 = ((f32[8,136,128]{2,1,0:T(8,128)}), f32[8,136,128]{2,1,0:T(8,128)}, u32[]{:S(2)}, u32[]{:S(2)}) async-start(f32[8,136,128]{2,1,0:T(8,128)} %pad_maximum_fusion.4), calls=%async_computation.1 | async-start | bytes 1114112 | tf_op jit(solution)/shard_map/all_to_all | solution.py:91
  114.6 5.0 %collective-permute-start.10 = (bf16[2,1,128,128]{3,2,0,1:T(8,128)(2,1)S(1)}, bf16[2,1,128,128]{3,2,0,1:T(8,128)(2,1)S(1)}, u32[]{:S(2)}, u32[]{:S(2)}) collective-permute-start(bf16[2,1,128,128]{3,2,0,1:T(8,128)(2,1)S(1)} %get-tuple-element.13), channel_id=1, source_target_pairs={{0,2},{1,3},{2,0},{3,1},{4,6},{5,7},{6,4},{7,5},{8,10},{9,11},{10,... | collective-permute-start | bytes 196616 | tf_op jit(solution)/shard_map/ppermute | solution.py:33
  115.2 4.4 %collective-permute-start.11 = (bf16[2,1,128,128]{3,2,0,1:T(8,128)(2,1)S(1)}, bf16[2,1,128,128]{3,2,0,1:T(8,128)(2,1)S(1)}, u32[]{:S(2)}, u32[]{:S(2)}) collective-permute-start(bf16[2,1,128,128]{3,2,0,1:T(8,128)(2,1)S(1)} %get-tuple-element.15), channel_id=1, source_target_pairs={{0,3},{1,2},{2,1},{3,0},{4,7},{5,6},{6,5},{7,4},{8,11},{9,10},{10,... | collective-permute-start | bytes 196616 | tf_op jit(solution)/shard_map/ppermute | solution.py:33
  116.0 3.6 %collective-permute-start.9 = (bf16[2,1,128,128]{3,2,0,1:T(8,128)(2,1)S(1)}, bf16[2,1,128,128]{3,2,0,1:T(8,128)(2,1)S(1)}, u32[]{:S(2)}, u32[]{:S(2)}) collective-permute-start(bf16[2,1,128,128]{3,2,0,1:T(8,128)(2,1)S(1)} %get-tuple-element.14), channel_id=1, source_target_pairs={{0,1},{1,0},{2,3},{3,2},{4,5},{5,4},{6,7},{7,6},{8,9},{9,8},{10,11... | collective-permute-start | bytes 196616 | tf_op jit(solution)/shard_map/ppermute | solution.py:33
  116.8 10.3 %collective-permute-start.6 = (bf16[2048,128]{1,0:T(8,128)(2,1)}, bf16[2048,128]{1,0:T(8,128)(2,1)}, u32[]{:S(2)}, u32[]{:S(2)}) collective-permute-start(bf16[2048,128]{1,0:T(8,128)(2,1)} %get-tuple-element.6), channel_id=1, source_target_pairs={{0,1},{1,0},{2,3},{3,2},{4,5},{5,4},{6,7},{7,6},{8,9},{9,8},{10,11... | collective-permute-start | bytes 1572872 | tf_op jit(solution)/shard_map/ppermute | solution.py:33
  116.8 10.3 %collective-permute-start.8 = (bf16[2048,128]{1,0:T(8,128)(2,1)}, bf16[2048,128]{1,0:T(8,128)(2,1)}, u32[]{:S(2)}, u32[]{:S(2)}) collective-permute-start(bf16[2048,128]{1,0:T(8,128)(2,1)} %collective-permute-done.7), channel_id=1, source_target_pairs={{0,1},{1,0},{2,3},{3,2},{4,5},{5,4},{6,7},{7,6},{8,9},{9,8},{10,11... | collective-permute-start | bytes 1572872 | tf_op jit(solution)/shard_map/ppermute | solution.py:33
  176.2 19.7 %all-to-all-start.2 = ((bf16[8,288,128]{2,1,0:T(8,128)(2,1)}), bf16[8,288,128]{2,1,0:T(8,128)(2,1)}, u32[]{:S(2)}, u32[]{:S(2)}) async-start(bf16[8,288,128]{2,1,0:T(8,128)(2,1)} %pad_maximum_fusion.3), calls=%async_computation.2 | async-start | bytes 1179648 | tf_op jit(solution)/shard_map/all_to_all | solution.py:125

commit v2 on v1

v2 whole, which is shorter than its diff:
```python
import functools

import jax
import jax.numpy as jnp
from jax import lax
from jax.experimental import pallas as pl
from jax.experimental.pallas import tpu as pltpu
from jax.sharding import PartitionSpec as P

F32 = jnp.float32
BF16 = jnp.bfloat16
VMEM = pl.BlockSpec(memory_space=pltpu.VMEM)
SMEM = pl.BlockSpec(memory_space=pltpu.SMEM)
UNROLL = 8
T_BITS, S_BITS = 10, 10


def params(mib):
    return pltpu.CompilerParams(vmem_limit_bytes=mib << 20)


def cost(flops, nbytes):
    return pl.CostEstimate(flops=flops, bytes_accessed=nbytes, transcendentals=0)


def pick_kernel(rows_s, count_s, hub_s, x, out, x32, stage):
    n_dom, capacity = rows_s.shape
    hub_dev = hub_s.shape[0]
    step = 16
    x32[...] = x[...].astype(F32)
    for j in range(hub_dev):
        stage[capacity + j : capacity + j + 1, :] = x32[pl.ds(hub_s[j], 1), :]
    hub = stage[capacity:, :].astype(BF16)
    slot = lax.broadcasted_iota(jnp.int32, (capacity, x.shape[1]), 0)

    def peer(q, carry):
        def some(g, carry):
            for u in range(step):
                c = g * step + u
                stage[pl.ds(c, 1), :] = x32[pl.ds(rows_s[q, c], 1), :]
            return carry

        lax.fori_loop(0, capacity // step, some, 0)
        kept = jnp.where(slot < count_s[0, q], stage[:capacity, :], 0.0)
        out[q, :capacity, :] = kept.astype(BF16)
        out[q, capacity:, :] = hub
        return carry

    lax.fori_loop(0, n_dom, peer, 0)


def pick(send_rows, send_count, hub_ids, x):
    n_dom, capacity = send_rows.shape
    rows = capacity + hub_ids.shape[0]
    return pl.pallas_call(
        pick_kernel,
        out_shape=jax.ShapeDtypeStruct((n_dom, rows, x.shape[1]), BF16),
        in_specs=[SMEM, SMEM, SMEM, VMEM],
        out_specs=VMEM,
        scratch_shapes=[pltpu.VMEM(x.shape, F32), pltpu.VMEM((rows, x.shape[1]), F32)],
        compiler_params=params(16),
        cost_estimate=cost(0, 1 << 21),
        name="pick_rows",
    )(send_rows, send_count, hub_ids, x)


def unpack(entry):
    t = entry & ((1 << T_BITS) - 1)
    s = (entry >> T_BITS) & ((1 << S_BITS) - 1)
    return t, s, entry >> (T_BITS + S_BITS)


def make_lists(dst_s, src_s, lists, own_blocks, far_blocks):
    length = lists.shape[1] - 1

    def step(t, n):
        s = src_s[t]
        d = dst_s[t]
        far = (s >= own_blocks).astype(jnp.int32)
        lists[0, n[0]] = t + (s << T_BITS) + (d << (T_BITS + S_BITS))
        lists[1, n[1]] = t + ((s - own_blocks) << T_BITS) + (d << (T_BITS + S_BITS))
        return n[0] + 1 - far, n[1] + far

    n = lax.fori_loop(0, dst_s.shape[0], step, (jnp.int32(0), jnp.int32(0)))
    for which, blocks in ((0, own_blocks), (1, far_blocks)):
        spare = (blocks << T_BITS) + (own_blocks << (T_BITS + S_BITS))
        for u in range(UNROLL - 1):
            lists[which, n[which] + u] = jnp.int32(spare)
        lists[which, length] = n[which]


def add_tiles(lists, which, tiles, source, acc, spare):
    n = lists[which, lists.shape[1] - 1]

    def group(g, carry):
        done = []
        for u in range(UNROLL):
            t, s, d = unpack(lists[which, g * UNROLL + u])
            s = jnp.where(d == spare, 0, s)
            done.append((d, jnp.dot(tiles[t], source[s], preferred_element_type=F32)))
        for d, product in done:
            acc[d] += product
        return carry

    lax.fori_loop(0, (n + UNROLL - 1) // UNROLL, group, 0)


def add_tiles_t(lists, which, tiles, source, acc, spare):
    n = lists[which, lists.shape[1] - 1]

    def group(g, carry):
        done = []
        for u in range(UNROLL):
            t, s, d = unpack(lists[which, g * UNROLL + u])
            d = jnp.where(d == spare, 0, d)
            product = lax.dot_general(
                tiles[t], source[d], (((0,), (0,)), ((), ())), preferred_element_type=F32
            )
            done.append((s, product))
        for s, product in done:
            acc[s] += product
        return carry

    lax.fori_loop(0, (n + UNROLL - 1) // UNROLL, group, 0)


def own_kernel(dst_s, src_s, tiles, x, out, lists, acc, *, far_blocks):
    own_blocks = x.shape[0]
    make_lists(dst_s, src_s, lists, own_blocks, far_blocks)
    acc[...] = jnp.zeros_like(acc)
    add_tiles(lists, 0, tiles, x, acc, own_blocks)
    out[...] = acc[:own_blocks]


def own_tiles(tile_dst, tile_src, tiles, x, far_blocks):
    n = tiles.shape[0]
    return pl.pallas_call(
        functools.partial(own_kernel, far_blocks=far_blocks),
        out_shape=(
            jax.ShapeDtypeStruct(x.shape, F32),
            jax.ShapeDtypeStruct((2, n + UNROLL), jnp.int32),
        ),
        in_specs=[SMEM, SMEM, VMEM, VMEM],
        out_specs=(VMEM, SMEM),
        scratch_shapes=[pltpu.VMEM((x.shape[0] + 1,) + x.shape[1:], F32)],
        compiler_params=params(20),
        cost_estimate=cost(2 * n * 128**3, 1 << 23),
        name="own_tiles",
    )(tile_dst, tile_src, tiles, x)


def far_kernel(lists, tiles, incoming, base, out, source, acc):
    n_dom = incoming.shape[0]
    own_blocks, tile, _ = base.shape
    capacity = tile
    hub_dev = incoming.shape[1] - capacity
    hub_blocks = n_dom * hub_dev // tile
    for q in range(n_dom):
        source[hub_blocks + q] = incoming[q, :capacity, :]
        block, row = divmod(q * hub_dev, tile)
        source[block, row : row + hub_dev, :] = incoming[q, capacity:, :]
    acc[:own_blocks] = base[...]
    add_tiles(lists, 1, tiles, source, acc, own_blocks)
    out[...] = acc[:own_blocks].astype(BF16)


def far_tiles(lists, tiles, incoming, base, far_blocks):
    own_blocks, tile, width = base.shape
    return pl.pallas_call(
        far_kernel,
        out_shape=jax.ShapeDtypeStruct(base.shape, BF16),
        in_specs=[SMEM, VMEM, VMEM, VMEM],
        out_specs=VMEM,
        scratch_shapes=[
            pltpu.VMEM((far_blocks, tile, width), BF16),
            pltpu.VMEM((own_blocks + 1, tile, width), F32),
        ],
        compiler_params=params(20),
        cost_estimate=cost(tiles.shape[0] * 128**3, 1 << 22),
        name="far_tiles",
    )(lists, tiles, incoming, base)


def forward_kernel(me_s, *refs, n_feat):
    xs, aggs = refs[:n_feat], refs[n_feat : 2 * n_feat]
    w_self, w_neigh, bias, grad_out, output, grad_pre = refs[2 * n_feat :]
    me = me_s[0]
    width = xs[0].shape[1]

    def product(shards, w):
        rows = [w[pl.ds(pl.multiple_of((me ^ k) * width, width), width), :] for k in range(n_feat)]
        return jnp.dot(
            jnp.concatenate([s[...] for s in shards], axis=1),
            jnp.concatenate(rows, axis=0),
            preferred_element_type=F32,
        )

    pre_act = product(xs, w_self) + product(aggs, w_neigh) + bias[...]
    gate = jax.nn.sigmoid(pre_act)
    output[...] = (pre_act * gate).astype(BF16)
    grad = grad_out[...].astype(F32) * gate * (1.0 + pre_act * (1.0 - gate))
    grad_pre[...] = grad.astype(BF16)


def forward(me, xs, aggs, w_self, w_neigh, bias, grad_out, block=512):
    n_feat = len(xs)
    rows, width = grad_out.shape
    by_rows = pl.BlockSpec((block, width), lambda i, m: (i, 0))
    whole = lambda a: pl.BlockSpec(a.shape, lambda i, m: (0, 0))
    return pl.pallas_call(
        functools.partial(forward_kernel, n_feat=n_feat),
        out_shape=(jax.ShapeDtypeStruct((rows, width), BF16),) * 2,
        grid_spec=pltpu.PrefetchScalarGridSpec(
            num_scalar_prefetch=1,
            grid=(rows // block,),
            in_specs=[by_rows] * (2 * n_feat)
            + [whole(w_self), whole(w_neigh), whole(bias), by_rows],
            out_specs=[by_rows, by_rows],
        ),
        compiler_params=params(20),
        cost_estimate=cost(4 * rows * width * n_feat * width, 1 << 23),
        name="forward_dense",
    )(me, *xs, *aggs, w_self, w_neigh, bias, grad_out)


def weights_kernel(*refs, n_feat):
    shards, grad, out = refs[: 2 * n_feat], refs[2 * n_feat], refs[2 * n_feat + 1]
    n_dom, chunk = out.shape[0], out.shape[1] - 8
    width = grad.shape[1]
    flipped = grad[...].T
    bias = jnp.sum(grad[...].astype(F32), axis=0, keepdims=True)
    for i, shard in enumerate(shards):
        block = jnp.dot(flipped, shard[...], preferred_element_type=F32).T
        for row in range(0, width, min(chunk, width)):
            q, start = divmod(i * width + row, chunk)
            n = min(chunk, width)
            out[q, start : start + n, :] = block[row : row + n, :]
    for q in range(n_dom):
        out[q, chunk:, :] = jnp.broadcast_to(bias, (8, width))


def weight_parts(shards, grad, n_dom):
    n_feat = len(shards) // 2
    width = grad.shape[1]
    chunk = 2 * n_feat * width // n_dom
    return pl.pallas_call(
        functools.partial(weights_kernel, n_feat=n_feat),
        out_shape=jax.ShapeDtypeStruct((n_dom, chunk + 8, width), F32),
        in_specs=[VMEM] * (2 * n_feat + 1),
        out_specs=VMEM,
        compiler_params=params(20),
        cost_estimate=cost(4 * n_feat * width * width * grad.shape[0], 1 << 22),
        name="weight_parts",
    )(*shards, grad)


def back_kernel(*refs):
    grads, w, out = refs[:-2], refs[-2], refs[-1]
    whole = jnp.concatenate([g[...] for g in grads], axis=1)
    rows = jnp.concatenate([w[k] for k in range(w.shape[0])], axis=1)
    product = lax.dot_general(whole, rows, (((1,), (1,)), ((), ())), preferred_element_type=F32)
    out[...] = product.astype(out.dtype)


def back_dense(grads, w, dtype, name, block=512):
    rows, width = grads[0].shape
    by_rows = pl.BlockSpec((block, width), lambda i: (i, 0))
    return pl.pallas_call(
        back_kernel,
        out_shape=jax.ShapeDtypeStruct((rows, width), dtype),
        grid=(rows // block,),
        in_specs=[by_rows] * len(grads) + [pl.BlockSpec(w.shape, lambda i: (0, 0, 0))],
        out_specs=by_rows,
        compiler_params=params(20),
        cost_estimate=cost(2 * rows * width * width * len(grads), 1 << 22),
        name=name,
    )(*grads, w)


def back_far_kernel(lists, tiles, back, weights, out, acc):
    n_dom = out.shape[0]
    own_blocks, tile, _ = back.shape
    chunk = weights.shape[0]
    hub_dev = out.shape[1] - tile - chunk
    hub_blocks = n_dom * hub_dev // tile
    acc[...] = jnp.zeros_like(acc)
    add_tiles_t(lists, 1, tiles, back, acc, own_blocks)
    for q in range(n_dom):
        out[q, :tile, :] = acc[hub_blocks + q].astype(BF16)
        block, row = divmod(q * hub_dev, tile)
        out[q, tile : tile + hub_dev, :] = acc[block, row : row + hub_dev, :].astype(BF16)
        out[q, tile + hub_dev :, :] = weights[...]


def back_far(lists, tiles, back, weights, n_dom, hub_dev):
    _, tile, width = back.shape
    far_blocks = n_dom * hub_dev // tile + n_dom
    rows = tile + hub_dev + weights.shape[0]
    return pl.pallas_call(
        back_far_kernel,
        out_shape=jax.ShapeDtypeStruct((n_dom, rows, width), BF16),
        in_specs=[SMEM, VMEM, VMEM, VMEM],
        out_specs=VMEM,
        scratch_shapes=[pltpu.VMEM((far_blocks + 1, tile, width), F32)],
        compiler_params=params(24),
        cost_estimate=cost(tiles.shape[0] * 128**3, 1 << 22),
        name="back_far",
    )(lists, tiles, back, weights)


def back_own_kernel(lists, tiles, back, direct, out, acc):
    own_blocks = back.shape[0]
    acc[:own_blocks] = direct[...]
    add_tiles_t(lists, 0, tiles, back, acc, own_blocks)
    out[...] = acc[:own_blocks]


def back_own(lists, tiles, back, direct):
    return pl.pallas_call(
        back_own_kernel,
        out_shape=jax.ShapeDtypeStruct(direct.shape, F32),
        in_specs=[SMEM, VMEM, VMEM, VMEM],
        out_specs=VMEM,
        scratch_shapes=[pltpu.VMEM((direct.shape[0] + 1,) + direct.shape[1:], F32)],
        compiler_params=params(20),
        cost_estimate=cost(2 * tiles.shape[0] * 128**3, 1 << 23),
        name="back_own",
    )(lists, tiles, back, direct)


def finish_kernel(count_s, hub_s, me_s, rows, incoming, base, out, self_out, neigh_out, *, n_feat):
    n_dom, capacity = rows.shape
    hub_dev = hub_s.shape[0]
    own_count, width = base.shape
    chunk = incoming.shape[1] - capacity - hub_dev
    block, peers = 256, min(8, n_dom)
    lane = lax.broadcasted_iota(jnp.int32, (1, capacity), 1)

    def some(g, carry):
        start = pl.multiple_of(g * block, block)
        vertex = lax.broadcasted_iota(jnp.int32, (block, capacity), 0) + start
        total = base[pl.ds(start, block), :]
        for first in range(0, n_dom, peers):
            hot, sent = [], []
            for q in range(first, first + peers):
                wanted = jnp.where(lane < count_s[0, q], rows[q : q + 1, :], -1)
                hot.append((vertex == wanted).astype(F32).astype(BF16))
                sent.append(incoming[q, :capacity, :])
            total += jnp.dot(
                jnp.concatenate(hot, axis=1),
                jnp.concatenate(sent, axis=0),
                preferred_element_type=F32,
            )
        out[pl.ds(start, block), :] = total
        return carry

    lax.fori_loop(0, own_count // block, some, 0)
    hub = incoming[0, capacity : capacity + hub_dev, :].astype(F32)
    for q in range(1, n_dom):
        hub += incoming[q, capacity : capacity + hub_dev, :].astype(F32)
    for j in range(hub_dev):
        out[pl.ds(hub_s[j], 1), :] += hub[j : j + 1, :]
    me = me_s[0]
    n = min(chunk, width)
    for row in range(0, 2 * n_feat * width, n):
        q, start = divmod(row, chunk)
        which, k = divmod(row // width, n_feat)
        target = (self_out, neigh_out)[which]
        piece = incoming[q, capacity + hub_dev + start : capacity + hub_dev + start + n, :]
        at = pl.multiple_of((me ^ k) * width + row % width, n)
        target[pl.ds(at, n), :] = piece.astype(F32)


def finish(send_rows, send_count, hub_ids, me, incoming, base, n_feat):
    width = base.shape[1]
    w_shape = jax.ShapeDtypeStruct((n_feat * width, width), F32)
    return pl.pallas_call(
        functools.partial(finish_kernel, n_feat=n_feat),
        out_shape=(jax.ShapeDtypeStruct(base.shape, F32), w_shape, w_shape),
        in_specs=[SMEM, SMEM, SMEM, VMEM, VMEM, VMEM],
        out_specs=(VMEM, VMEM, VMEM),
        compiler_params=params(24),
        cost_estimate=cost(2 * base.size * send_rows.size, 1 << 22),
        name="finish",
    )(send_count, hub_ids, me, send_rows, incoming, base)


def body(
    node_feats,
    edge_tiles,
    tile_dst,
    tile_src,
    hub_ids,
    send_rows,
    send_count,
    w_self,
    w_neigh,
    out_bias,
    grad_out,
    *,
    n_feat,
):
    own_count, width = node_feats.shape
    tile_size = edge_tiles.shape[1]
    listed = send_rows[0]
    n_dom, capacity = listed.shape
    hub_dev = hub_ids.shape[0]
    me = lax.axis_index("feat").astype(jnp.int32)
    me_s = me.reshape(1)
    order = me ^ jnp.arange(n_feat, dtype=jnp.int32)
    far_blocks = n_dom * hub_dev // tile_size + n_dom

    def swap(x, k):
        return lax.ppermute(x, "feat", [(j, j ^ k) for j in range(n_feat)])

    def gather_feat(x):
        shards = {0: x}
        bit = n_feat // 2
        while bit:
            for k in list(shards):
                shards[k ^ bit] = swap(shards[k], bit)
            bit //= 2
        return [shards[k] for k in range(n_feat)]

    feats = gather_feat(node_feats)

    outgoing = pick(listed, send_count, hub_ids, node_feats)
    incoming = lax.all_to_all(outgoing, "dom", 0, 0, tiled=True)
    own_feats = node_feats.reshape(-1, tile_size, width)
    base, lists = own_tiles(tile_dst, tile_src, edge_tiles, own_feats, far_blocks)
    aggregated = far_tiles(lists, edge_tiles, incoming, base, far_blocks).reshape(own_count, width)

    aggs = gather_feat(aggregated)
    output, grad_pre = forward(
        me_s, feats, aggs, w_self, w_neigh, out_bias[None, :], grad_out
    )
    grads = gather_feat(grad_pre)

    parts = weight_parts(feats + aggs, grad_pre, n_dom)
    chunk = parts.shape[1] - 8
    summed_w = jnp.sum(lax.all_to_all(parts, "dom", 0, 0, tiled=True), axis=0)
    grad_bias = summed_w[chunk]
    weights_out = summed_w[:chunk].astype(BF16)

    both = jnp.stack([w_self, w_neigh]).reshape(2, n_feat, width, -1)[:, order]
    rows = lax.concatenate(
        [both[:, 0:1]] + [swap(both[:, k : k + 1], k) for k in range(1, n_feat)], 1
    )
    back_agg = back_dense(grads, rows[1], BF16, "back_agg").reshape(own_feats.shape)
    direct = back_dense(grads, rows[0], F32, "direct").reshape(own_feats.shape)
    back_out = back_far(lists, edge_tiles, back_agg, weights_out, n_dom, hub_dev)
    back_in = lax.all_to_all(back_out, "dom", 0, 0, tiled=True)
    own = back_own(lists, edge_tiles, back_agg, direct).reshape(own_count, width)
    grad_feats, grad_self, grad_neigh = finish(
        listed, send_count, hub_ids, me_s, back_in, own, n_feat
    )
    return (output, grad_feats, grad_self, grad_neigh, grad_bias)


def solution(mesh):
    in_specs = (
        P("dom", "feat"),
        P("dom", None, None),
        P("dom"),
        P("dom"),
        P("dom"),
        P("dom", None, None),
        P("dom", None),
        P(None, "feat"),
        P(None, "feat"),
        P("feat"),
        P("dom", "feat"),
    )
    out_specs = (P("dom", "feat"), P("dom", "feat"), P(None, "feat"), P(None, "feat"), P("feat"))
    n_feat = mesh.shape["feat"]

    def run(*args):
        return body(*args, n_feat=n_feat)

    return jax.shard_map(run, mesh=mesh, in_specs=in_specs, out_specs=out_specs, check_vma=False)
```

time: 217 us -> 115 us (0.53)
  other arithmetic: 74 us -> 2.84 us
  local copies, waits for them, and re-layouts: 62.4 us -> 21.2 us
  Pallas kernels: 0 us -> 37.3 us
  matrix products: 27.6 us -> 0 us
  waiting for transfers between devices: 24.7 us -> 28.1 us
    scatter-add x3 -> x0, other arithmetic: 55.9 us -> none  [the longest x1 23 us: body(): jax.ops.segment_sum(spread, tile_src, source_blocks).reshape(-1, width)]
    pallas_call x0 -> x10, Pallas kernels: none -> 37.3 us  [the longest x2 6.24 us: back_dense(): pl.pallas_call(back_kernel, out_shape=jax.ShapeDtypeStruct((rows, width),...]
    dot_general x8 -> x0, matrix products: 27.6 us -> none  [the longest x1 7.42 us: body(): jnp.einsum('tij,tjf->tif', edge_tiles, blocks[tile_src], preferred_elemen...]
    gather x6 -> x0, local copies, waits for them, and re-layouts: 18.7 us -> none  [the longest x1 4.27 us: body(): node_feats[index]]
    dot_general x2 -> x0, local copies, waits for them, and re-layouts: 16.6 us -> none  [the longest x1 8.31 us: body(): jnp.einsum('tij,tjf->tif', edge_tiles, blocks[tile_src], preferred_elemen...]
    ppermute x12, waiting for transfers between devices: 5.7 us -> 17.5 us  [swap(): return lax.ppermute(x, 'feat', [(j, j ^ k) for j in range(n_feat)])]
    unnamed x21 -> x48, local copies, waits for them, and re-layouts: 6.22 us -> 16.7 us
    all_to_all x1, waiting for transfers between devices: 8.87 us -> 0.01 us  [body(): incoming = lax.all_to_all(outgoing, 'dom', 0, 0, tiled=True)]
  transfers between devices with their start and end apart: 15 -> 15, of which waited for: 5 -> 6; matrix products, arithmetic and copies ran while one was open for 38% -> 6% of each run, Pallas kernels for 0% -> 16%
where the time goes in v2:
time: 115 us; the launch traced here: 114 us
  Pallas kernels  37.3 us (32%)
  waiting for transfers between devices  28.1 us (24%)
  starting transfers between devices  23.3 us (20%)
  local copies, waits for them, and re-layouts  21.2 us (18%)
  other arithmetic  2.84 us (2%)
    ppermute x12, waiting for transfers between devices, swap(): return lax.ppermute(x, 'feat', [(j, j ^ k) for j in range(n_feat)])  17.5 us
    unnamed x48, local copies, waits for them, and re-layouts  16.7 us
    all_to_all x1, starting transfers between devices, body(): incoming = lax.all_to_all(outgoing, 'dom', 0, 0, tiled=True)  7.25 us
    all_to_all x1, waiting for transfers between devices, body(): back_in = lax.all_to_all(back_out, 'dom', 0, 0, tiled=True)  6.92 us
    pallas_call x2, Pallas kernels, back_dense(): pl.pallas_call(back_kernel, out_shape=jax.ShapeDtypeStruct((rows, width),...  6.24 us
    ppermute x12, starting transfers between devices, swap(): return lax.ppermute(x, 'feat', [(j, j ^ k) for j in range(n_feat)])  6.16 us
    all_to_all x1, starting transfers between devices, body(): summed_w = jnp.sum(lax.all_to_all(parts, 'dom', 0, 0, tiled=True), axis=0)  5.71 us
    pallas_call x1, Pallas kernels, own_tiles(): pl.pallas_call(functools.partial(own_kernel, far_blocks=far_blocks), out_...  5.32 us
  transfers between devices with their start and end apart: 15, of which 6 were waited for; matrix products, arithmetic and copies ran while one was open for 6% of the time, Pallas kernels for 16%

profile of v2, /device:TPU:0, one launch (start us, length us, event | category | flops | bytes accessed | tf_op | source)
XLA Modules:
  0.0 113.7 jit_solution(7083884486853582111)
XLA Ops:
  2.6 4.4 %pick_rows.1 = bf16[8,160,128]{2,1,0:T(8,128)(2,1)} custom-call(s32[8,128]{1,0:T(8,128)S(1)} %bitcast.27, s32[1,8]{1,0:T(1,128)S(1)} %copy-done.19, s32[32]{0:T(128)S(1)} %copy-done.21, bf16[2048,128]{1,0:T(8,128)(2,1)} %refs_0_.3), custom_call_target="tpu_custom_call" | custom-call | bytes 2097152 | tf_op jit(solution)/shard_map/pick_rows/pallas_call | solution.py:55
  7.0 7.3 %all-to-all-start = ((bf16[8,160,128]{2,1,0:T(8,128)(2,1)}), bf16[8,160,128]{2,1,0:T(8,128)(2,1)}, u32[]{:S(2)}, u32[]{:S(2)}) async-start(bf16[8,160,128]{2,1,0:T(8,128)(2,1)} %pick_rows.1), calls=%async_computation | async-start | bytes 655360 | tf_op jit(solution)/shard_map/all_to_all | solution.py:428
  14.3 1.5 %collective-permute-start.1 = (bf16[2048,128]{1,0:T(8,128)(2,1)}, bf16[2048,128]{1,0:T(8,128)(2,1)}, u32[]{:S(2)}, u32[]{:S(2)}) collective-permute-start(bf16[2048,128]{1,0:T(8,128)(2,1)} %refs_0_.3), channel_id=1, source_target_pairs={{0,2},{1,3},{2,0},{3,1},{4,6},{5,7},{6,4},{7,5},{8,10},{9,11},{10,... | collective-permute-start | bytes 1572872 | tf_op jit(solution)/shard_map/ppermute | solution.py:414
  15.8 2.0 %copy-done = bf16[106,128,128]{2,1,0:T(8,128)(2,1)S(1)} copy-done((bf16[106,128,128]{2,1,0:T(8,128)(2,1)S(1)}, bf16[106,128,128]{2,1,0:T(8,128)(2,1)}, u32[]{:S(2)}) %copy-start) | copy-done | bytes 3473432
  19.1 5.3 %own_tiles.1 = (f32[16,128,128]{2,1,0:T(8,128)S(1)}, s32[2,114]{1,0:T(2,128)S(1)}) custom-call(s32[106]{0:T(128)S(1)} %copy-done.17, s32[106]{0:T(128)S(1)} %copy-done.18, bf16[106,128,128]{2,1,0:T(8,128)(2,1)S(1)} %copy-done, bf16[16,128,128]{2,1,0:T(8,128)(2,1)} %bitcast.1.x), custom_call_target="tpu_custom_call" | custom-call | flops 444596224 | bytes 8388608 | tf_op jit(solution)/shard_map/own_tiles/pallas_call | solution.py:137
  24.5 1.0 copy-done.8
  25.4 1.2 %copy-done.9 = f32[16,128,128]{2,1,0:T(8,128)S(1)} copy-done((f32[16,128,128]{2,1,0:T(8,128)S(1)}, f32[16,128,128]{2,1,0:T(8,128)}, u32[]{:S(2)}) %copy-start.9) | copy-done | bytes 1048600
  26.7 3.1 %far_tiles.1 = bf16[16,128,128]{2,1,0:T(8,128)(2,1)} custom-call(s32[2,114]{1,0:T(2,128)S(1)} %get-tuple-element.12.lists, bf16[106,128,128]{2,1,0:T(8,128)(2,1)S(1)} %copy-done.1, bf16[8,160,128]{2,1,0:T(8,128)(2,1)} %all-to-all-done.incoming, f32[16,128,128]{2,1,0:T(8,128)S(1)} %copy-done.9), custom_call_target="tpu_custom_call" | custom-call | flops 222298112 | bytes 4194304 | tf_op jit(solution)/shard_map/far_tiles/pallas_call | solution.py:169
  31.1 12.1 %collective-permute-done.4.refs_6_ = bf16[2048,128]{1,0:T(8,128)(2,1)} collective-permute-done((bf16[2048,128]{1,0:T(8,128)(2,1)}, bf16[2048,128]{1,0:T(8,128)(2,1)}, u32[]{:S(2)}, u32[]{:S(2)}) %collective-permute-start.4) | collective-permute-done | bytes 524320 | tf_op jit(solution)/shard_map/ppermute | solution.py:414
  43.2 2.2 %collective-permute-done.5.refs_7_ = bf16[2048,128]{1,0:T(8,128)(2,1)} collective-permute-done((bf16[2048,128]{1,0:T(8,128)(2,1)}, bf16[2048,128]{1,0:T(8,128)(2,1)}, u32[]{:S(2)}, u32[]{:S(2)}) %collective-permute-start.5) | collective-permute-done | bytes 524320 | tf_op jit(solution)/shard_map/ppermute | solution.py:414
  45.5 0.9 copy-done.10
  47.3 1.0 copy-done.13
  48.3 4.8 %forward_dense.1 = (bf16[2048,128]{1,0:T(8,128)(2,1)}, bf16[2048,128]{1,0:T(8,128)(2,1)}) custom-call(s32[1]{0:T(128)} %bitcast.me_s, bf16[2048,128]{1,0:T(8,128)(2,1)} %refs_0_.3, bf16[2048,128]{1,0:T(8,128)(2,1)} %collective-permute-done.refs_1_, bf16[2048,128]{1,0:T(8,128)(2,1)} %collective-permute-done.1.refs_2_, ...), custom_call_target="tpu_custom_call" | custom-call | flops 536870912 | bytes 8388608 | tf_op jit(solution)/shard_map/forward_dense/pallas_call | solution.py:210
  53.7 3.7 %weight_parts.1 = f32[8,136,128]{2,1,0:T(8,128)S(1)} custom-call(bf16[2048,128]{1,0:T(8,128)(2,1)} %refs_0_.3, bf16[2048,128]{1,0:T(8,128)(2,1)} %collective-permute-done.refs_1_, bf16[2048,128]{1,0:T(8,128)(2,1)} %collective-permute-done.1.refs_2_, bf16[2048,128]{1,0:T(8,128)(2,1)} %collective-permute-done.2.refs_3_, bf16[2048,128]{1,0:T(8,128)(2,1)} %bitcast.3.refs_4_, ...), custom_call_target="tpu_custom_call" | custom-call | flops 536870912 | bytes 4194304 | tf_op jit(solution)/shard_map/weight_parts/pallas_call | solution.py:246
  58.2 5.7 %all-to-all-start.1 = ((f32[8,136,128]{2,1,0:T(8,128)}), f32[8,136,128]{2,1,0:T(8,128)}, u32[]{:S(2)}, u32[]{:S(2)}) async-start(f32[8,136,128]{2,1,0:T(8,128)} %copy-done.5), calls=%async_computation.1 | async-start | bytes 1114112 | tf_op jit(solution)/shard_map/all_to_all | solution.py:441
  63.9 1.7 %pad_maximum_fusion = bf16[2,4,128,128]{3,2,1,0:T(8,128)(2,1)} fusion(bf16[1,4,128,128]{3,2,1,0:T(8,128)(2,1)} %bitcast.26, bf16[1,4,128,128]{3,2,1,0:T(8,128)(2,1)} %bitcast.25), kind=kLoop, calls=%fused_computation.1 | loop fusion | flops 131072 | bytes 524288 | tf_op jit(solution)/shard_map/stack | solution.py:445
  65.6 2.2 %gather_fusion = bf16[4,2,128,128]{3,2,1,0:T(8,128)(2,1)} fusion(bf16[2,4,128,128]{3,2,1,0:T(8,128)(2,1)} %pad_maximum_fusion, s32[1024]{0:T(1024)S(1)} %pad_clamp_fusion), kind=kCustom, calls=%fused_computation | custom fusion | bytes 524304 | tf_op jit(solution)/shard_map/gather | solution.py:445
  67.8 1.0 copy.18
  69.4 1.6 %collective-permute-start.10 = (bf16[2,1,128,128]{3,2,1,0:T(8,128)(2,1)S(1)}, bf16[2,1,128,128]{3,2,1,0:T(8,128)(2,1)S(1)}, u32[]{:S(2)}, u32[]{:S(2)}) collective-permute-start(bf16[2,1,128,128]{3,2,1,0:T(8,128)(2,1)S(1)} %get-tuple-element.22), channel_id=1, source_target_pairs={{0,2},{1,3},{2,0},{3,1},{4,6},{5,7},{6,4},{7,5},{8,10},{9,11},{10,... | collective-permute-start | bytes 196616 | tf_op jit(solution)/shard_map/ppermute | solution.py:414
  71.6 2.1 %collective-permute-done.10 = bf16[2,1,128,128]{3,2,1,0:T(8,128)(2,1)S(1)} collective-permute-done((bf16[2,1,128,128]{3,2,1,0:T(8,128)(2,1)S(1)}, bf16[2,1,128,128]{3,2,1,0:T(8,128)(2,1)S(1)}, u32[]{:S(2)}, u32[]{:S(2)}) %collective-permute-start.10) | collective-permute-done | bytes 65568 | tf_op jit(solution)/shard_map/ppermute | solution.py:414
  73.7 1.0 collective-permute-done.11
  75.5 3.7 %all-to-all-done.1 = f32[8,136,128]{2,1,0:T(8,128)} async-done(((f32[8,136,128]{2,1,0:T(8,128)}), f32[8,136,128]{2,1,0:T(8,128)}, u32[]{:S(2)}, u32[]{:S(2)}) %all-to-all-start.1) | async-done | bytes 557088 | tf_op jit(solution)/shard_map/all_to_all | solution.py:441
  79.2 1.1 reduce_sum.9
  81.2 3.1 %back_agg.1 = bf16[2048,128]{1,0:T(8,128)(2,1)S(1)} custom-call(bf16[2048,128]{1,0:T(8,128)(2,1)} %get-tuple-element.15.refs_0_.refs_8_, bf16[2048,128]{1,0:T(8,128)(2,1)} %collective-permute-done.6.refs_1_, bf16[2048,128]{1,0:T(8,128)(2,1)} %collective-permute-done.7.refs_2_, bf16[2048,128]{1,0:T(8,128)(2,1)} %collective-permute-done.8.refs_3_, ...), custom_call_target="tpu_custom_call" | custom-call | flops 268435456 | bytes 4194304 | tf_op jit(solution)/shard_map/back_agg/pallas_call | solution.py:268
  84.4 2.0 %back_far.1 = bf16[8,288,128]{2,1,0:T(8,128)(2,1)S(1)} custom-call(s32[2,114]{1,0:T(2,128)S(1)} %get-tuple-element.12.lists, bf16[106,128,128]{2,1,0:T(8,128)(2,1)S(1)} %copy-done.1, bf16[16,128,128]{2,1,0:T(8,128)(2,1)S(1)} %bitcast.21, bf16[128,128]{1,0:T(8,128)(2,1)S(1)} %slice.47.weights), custom_call_target="tpu_custom_call" | custom-call | flops 222298112 | bytes 4194304 | tf_op jit(solution)/shard_map/back_far/pallas_call | solution.py:299
  88.0 4.2 %all-to-all-start.2 = ((bf16[8,288,128]{2,1,0:T(8,128)(2,1)}), bf16[8,288,128]{2,1,0:T(8,128)(2,1)}, u32[]{:S(2)}, u32[]{:S(2)}) async-start(bf16[8,288,128]{2,1,0:T(8,128)(2,1)} %copy-done.4), calls=%async_computation.2 | async-start | bytes 1179648 | tf_op jit(solution)/shard_map/all_to_all | solution.py:452
  93.6 3.1 %direct.1 = f32[2048,128]{1,0:T(8,128)S(1)} custom-call(bf16[2048,128]{1,0:T(8,128)(2,1)} %get-tuple-element.15.refs_0_.refs_8_, bf16[2048,128]{1,0:T(8,128)(2,1)} %collective-permute-done.6.refs_1_, bf16[2048,128]{1,0:T(8,128)(2,1)} %collective-permute-done.7.refs_2_, bf16[2048,128]{1,0:T(8,128)(2,1)} %collective-permute-done.8.refs_3_, ...), custom_call_target="tpu_custom_call" | custom-call | flops 268435456 | bytes 4194304 | tf_op jit(solution)/shard_map/direct/pallas_call | solution.py:268
  96.8 3.1 %back_own.1 = f32[16,128,128]{2,1,0:T(8,128)S(1)} custom-call(s32[2,114]{1,0:T(2,128)S(1)} %get-tuple-element.12.lists, bf16[106,128,128]{2,1,0:T(8,128)(2,1)S(1)} %copy-done.1, bf16[16,128,128]{2,1,0:T(8,128)(2,1)S(1)} %bitcast.22, f32[16,128,128]{2,1,0:T(8,128)S(1)} %bitcast.23), custom_call_target="tpu_custom_call" | custom-call | flops 444596224 | bytes 8388608 | tf_op jit(solution)/shard_map/back_own/pallas_call | solution.py:319
  100.0 1.0 copy-done.6
  100.9 6.9 %all-to-all-done.2.incoming = bf16[8,288,128]{2,1,0:T(8,128)(2,1)} async-done(((bf16[8,288,128]{2,1,0:T(8,128)(2,1)}), bf16[8,288,128]{2,1,0:T(8,128)(2,1)}, u32[]{:S(2)}, u32[]{:S(2)}) %all-to-all-start.2) | async-done | bytes 589856 | tf_op jit(solution)/shard_map/all_to_all | solution.py:452
  107.9 1.2 %copy-done.7 = f32[16,128,128]{2,1,0:T(8,128)S(1)} copy-done((f32[16,128,128]{2,1,0:T(8,128)S(1)}, f32[16,128,128]{2,1,0:T(8,128)}, u32[]{:S(2)}) %copy-start.7) | copy-done | bytes 1048600
  109.1 4.6 %finish.1 = (f32[2048,128]{1,0:T(8,128)}, f32[512,128]{1,0:T(8,128)}, f32[512,128]{1,0:T(8,128)}) custom-call(s32[1,8]{1,0:T(1,128)S(1)} %copy-done.20, s32[32]{0:T(128)S(1)} %copy-done.22, s32[1]{0:T(128)} %bitcast.me_s, s32[8,128]{1,0:T(8,128)S(1)} %bitcast.28, bf16[8,288,128]{2,1,0:T(8,128)(2,1)} %all-to-all-done.2.incoming, f32[2048,128]{1,0:T(8,128)S(1)} %bitcast.24), custom_call_target="tpu_custom_call" | custom-call | flops 536870912 | bytes 4194304 | tf_op jit(solution)/shard_map/finish/pallas_call | solution.py:377
  (67 shorter events, 12.8 us)
Async XLA Ops:
  7.0 18.4 %all-to-all-start = ((bf16[8,160,128]{2,1,0:T(8,128)(2,1)}), bf16[8,160,128]{2,1,0:T(8,128)(2,1)}, u32[]{:S(2)}, u32[]{:S(2)}) async-start(bf16[8,160,128]{2,1,0:T(8,128)(2,1)} %pick_rows.1), calls=%async_computation | async-start | bytes 655360 | tf_op jit(solution)/shard_map/all_to_all | solution.py:428
  14.3 16.3 %collective-permute-start.1 = (bf16[2048,128]{1,0:T(8,128)(2,1)}, bf16[2048,128]{1,0:T(8,128)(2,1)}, u32[]{:S(2)}, u32[]{:S(2)}) collective-permute-start(bf16[2048,128]{1,0:T(8,128)(2,1)} %refs_0_.3), channel_id=1, source_target_pairs={{0,2},{1,3},{2,0},{3,1},{4,6},{5,7},{6,4},{7,5},{8,10},{9,11},{10,... | collective-permute-start | bytes 1572872 | tf_op jit(solution)/shard_map/ppermute | solution.py:414
  15.8 2.0 %copy-start = (bf16[106,128,128]{2,1,0:T(8,128)(2,1)S(1)}, bf16[106,128,128]{2,1,0:T(8,128)(2,1)}, u32[]{:S(2)}) copy-start(bf16[106,128,128]{2,1,0:T(8,128)(2,1)} %tiles.7) | copy-start | bytes 10420228
  19.1 6.3 %copy-start.1 = (bf16[106,128,128]{2,1,0:T(8,128)(2,1)S(1)}, bf16[106,128,128]{2,1,0:T(8,128)(2,1)}, u32[]{:S(2)}) copy-start(bf16[106,128,128]{2,1,0:T(8,128)(2,1)} %tiles.7) | copy-start | bytes 10420228
  24.4 1.0 copy-start.8
  25.4 20.0 %copy-start.23 = (f32[128]{0:T(128)S(1)}, f32[128]{0:T(128)}, u32[]{:S(2)}) copy-start(f32[128]{0:T(128)} %param.20) | copy-start | bytes 1540
  25.4 1.2 %copy-start.9 = (f32[16,128,128]{2,1,0:T(8,128)S(1)}, f32[16,128,128]{2,1,0:T(8,128)}, u32[]{:S(2)}) copy-start(f32[16,128,128]{2,1,0:T(8,128)} %copy-done.8) | copy-start | bytes 3145732
  29.8 13.4 %collective-permute-start.4 = (bf16[2048,128]{1,0:T(8,128)(2,1)}, bf16[2048,128]{1,0:T(8,128)(2,1)}, u32[]{:S(2)}, u32[]{:S(2)}) collective-permute-start(bf16[2048,128]{1,0:T(8,128)(2,1)} %bitcast.3.refs_4_), channel_id=1, source_target_pairs={{0,2},{1,3},{2,0},{3,1},{4,6},{5,7},{6,4},{7,5},{8,10},{9,11},{10,... | collective-permute-start | bytes 1572872 | tf_op jit(solution)/shard_map/ppermute | solution.py:414
  30.6 12.6 %collective-permute-start = (bf16[2048,128]{1,0:T(8,128)(2,1)}, bf16[2048,128]{1,0:T(8,128)(2,1)}, u32[]{:S(2)}, u32[]{:S(2)}) collective-permute-start(bf16[2048,128]{1,0:T(8,128)(2,1)} %refs_0_.3), channel_id=1, source_target_pairs={{0,1},{1,0},{2,3},{3,2},{4,5},{5,4},{6,7},{7,6},{8,9},{9,8},{10,11... | collective-permute-start | bytes 1572872 | tf_op jit(solution)/shard_map/ppermute | solution.py:414
  30.6 12.6 %collective-permute-start.2 = (bf16[2048,128]{1,0:T(8,128)(2,1)}, bf16[2048,128]{1,0:T(8,128)(2,1)}, u32[]{:S(2)}, u32[]{:S(2)}) collective-permute-start(bf16[2048,128]{1,0:T(8,128)(2,1)} %collective-permute-done.1.refs_2_), channel_id=1, source_target_pairs={{0,1},{1,0},{2,3},{3,2},{4,5},{5,4},{6,7},{7,6},{8,9},{9,8},{10,11... | collective-permute-start | bytes 1572872 | tf_op jit(solution)/shard_map/ppermute | solution.py:414
  31.1 12.1 %collective-permute-start.3 = (bf16[2048,128]{1,0:T(8,128)(2,1)}, bf16[2048,128]{1,0:T(8,128)(2,1)}, u32[]{:S(2)}, u32[]{:S(2)}) collective-permute-start(bf16[2048,128]{1,0:T(8,128)(2,1)} %bitcast.3.refs_4_), channel_id=1, source_target_pairs={{0,1},{1,0},{2,3},{3,2},{4,5},{5,4},{6,7},{7,6},{8,9},{9,8},{10,11... | collective-permute-start | bytes 1572872 | tf_op jit(solution)/shard_map/ppermute | solution.py:414
  43.2 2.3 %collective-permute-start.5 = (bf16[2048,128]{1,0:T(8,128)(2,1)}, bf16[2048,128]{1,0:T(8,128)(2,1)}, u32[]{:S(2)}, u32[]{:S(2)}) collective-permute-start(bf16[2048,128]{1,0:T(8,128)(2,1)} %collective-permute-done.4.refs_6_), channel_id=1, source_target_pairs={{0,1},{1,0},{2,3},{3,2},{4,5},{5,4},{6,7},{7,6},{8,9},{9,8},{10,11... | collective-permute-start | bytes 1572872 | tf_op jit(solution)/shard_map/ppermute | solution.py:414
  45.5 0.9 copy-start.10
  46.4 0.9 copy-start.11
  47.3 1.0 copy-start.13
  53.2 15.7 %collective-permute-start.7 = (bf16[2048,128]{1,0:T(8,128)(2,1)}, bf16[2048,128]{1,0:T(8,128)(2,1)}, u32[]{:S(2)}, u32[]{:S(2)}) collective-permute-start(bf16[2048,128]{1,0:T(8,128)(2,1)} %get-tuple-element.15.refs_0_.refs_8_), channel_id=1, source_target_pairs={{0,2},{1,3},{2,0},{3,1},{4,6},{5,7},{6,4},{7,5},{8,10},{9,11},{10,... | collective-permute-start | bytes 1572872 | tf_op jit(solution)/shard_map/ppermute | solution.py:414
  58.2 21.0 %all-to-all-start.1 = ((f32[8,136,128]{2,1,0:T(8,128)}), f32[8,136,128]{2,1,0:T(8,128)}, u32[]{:S(2)}, u32[]{:S(2)}) async-start(f32[8,136,128]{2,1,0:T(8,128)} %copy-done.5), calls=%async_computation.1 | async-start | bytes 1114112 | tf_op jit(solution)/shard_map/all_to_all | solution.py:441
  68.8 11.5 %collective-permute-start.6 = (bf16[2048,128]{1,0:T(8,128)(2,1)}, bf16[2048,128]{1,0:T(8,128)(2,1)}, u32[]{:S(2)}, u32[]{:S(2)}) collective-permute-start(bf16[2048,128]{1,0:T(8,128)(2,1)} %get-tuple-element.15.refs_0_.refs_8_), channel_id=1, source_target_pairs={{0,1},{1,0},{2,3},{3,2},{4,5},{5,4},{6,7},{7,6},{8,9},{9,8},{10,11... | collective-permute-start | bytes 1572872 | tf_op jit(solution)/shard_map/ppermute | solution.py:414
  68.9 11.4 %collective-permute-start.8 = (bf16[2048,128]{1,0:T(8,128)(2,1)}, bf16[2048,128]{1,0:T(8,128)(2,1)}, u32[]{:S(2)}, u32[]{:S(2)}) collective-permute-start(bf16[2048,128]{1,0:T(8,128)(2,1)} %collective-permute-done.7.refs_2_), channel_id=1, source_target_pairs={{0,1},{1,0},{2,3},{3,2},{4,5},{5,4},{6,7},{7,6},{8,9},{9,8},{10,11... | collective-permute-start | bytes 1572872 | tf_op jit(solution)/shard_map/ppermute | solution.py:414
  69.4 4.3 %collective-permute-start.10 = (bf16[2,1,128,128]{3,2,1,0:T(8,128)(2,1)S(1)}, bf16[2,1,128,128]{3,2,1,0:T(8,128)(2,1)S(1)}, u32[]{:S(2)}, u32[]{:S(2)}) collective-permute-start(bf16[2,1,128,128]{3,2,1,0:T(8,128)(2,1)S(1)} %get-tuple-element.22), channel_id=1, source_target_pairs={{0,2},{1,3},{2,0},{3,1},{4,6},{5,7},{6,4},{7,5},{8,10},{9,11},{10,... | collective-permute-start | bytes 196616 | tf_op jit(solution)/shard_map/ppermute | solution.py:414
  71.0 2.7 %collective-permute-start.9 = (bf16[2,1,128,128]{3,2,1,0:T(8,128)(2,1)S(1)}, bf16[2,1,128,128]{3,2,1,0:T(8,128)(2,1)S(1)}, u32[]{:S(2)}, u32[]{:S(2)}) collective-permute-start(bf16[2,1,128,128]{3,2,1,0:T(8,128)(2,1)S(1)} %get-tuple-element.23), channel_id=1, source_target_pairs={{0,1},{1,0},{2,3},{3,2},{4,5},{5,4},{6,7},{7,6},{8,9},{9,8},{10,11... | collective-permute-start | bytes 196616 | tf_op jit(solution)/shard_map/ppermute | solution.py:414
  71.0 3.7 %collective-permute-start.11 = (bf16[2,1,128,128]{3,2,1,0:T(8,128)(2,1)S(1)}, bf16[2,1,128,128]{3,2,1,0:T(8,128)(2,1)S(1)}, u32[]{:S(2)}, u32[]{:S(2)}) collective-permute-start(bf16[2,1,128,128]{3,2,1,0:T(8,128)(2,1)S(1)} %get-tuple-element.24), channel_id=1, source_target_pairs={{0,3},{1,2},{2,1},{3,0},{4,7},{5,6},{6,5},{7,4},{8,11},{9,10},{10,... | collective-permute-start | bytes 196616 | tf_op jit(solution)/shard_map/ppermute | solution.py:414
  80.3 0.9 copy-start.14
  87.2 0.8 copy-start.4
  88.0 19.8 %all-to-all-start.2 = ((bf16[8,288,128]{2,1,0:T(8,128)(2,1)}), bf16[8,288,128]{2,1,0:T(8,128)(2,1)}, u32[]{:S(2)}, u32[]{:S(2)}) async-start(bf16[8,288,128]{2,1,0:T(8,128)(2,1)} %copy-done.4), calls=%async_computation.2 | async-start | bytes 1179648 | tf_op jit(solution)/shard_map/all_to_all | solution.py:452
  92.2 4.6 %copy-start.3 = (bf16[2048,128]{1,0:T(8,128)(2,1)S(1)}, bf16[2048,128]{1,0:T(8,128)(2,1)}, u32[]{:S(2)}) copy-start(bf16[2048,128]{1,0:T(8,128)(2,1)} %copy-done.2) | copy-start | bytes 1572868
  92.7 0.9 copy-start.12
  96.8 11.1 %copy-start.16 = (s32[1,8,128]{2,1,0:T(8,128)S(1)}, s32[1,8,128]{2,1,0:T(8,128)}, u32[]{:S(2)}) copy-start(s32[1,8,128]{2,1,0:T(8,128)} %param.16) | copy-start | bytes 12292
  96.8 11.1 %copy-start.20 = (s32[1,8]{1,0:T(1,128)S(1)}, s32[1,8]{1,0:T(1,128)}, u32[]{:S(2)}) copy-start(s32[1,8]{1,0:T(1,128)} %count_s.3) | copy-start | bytes 100
  96.8 11.1 %copy-start.22 = (s32[32]{0:T(128)S(1)}, s32[32]{0:T(128)}, u32[]{:S(2)}) copy-start(s32[32]{0:T(128)} %hub_s.3) | copy-start | bytes 388
  100.0 1.0 copy-start.6
  107.9 1.2 %copy-start.7 = (f32[16,128,128]{2,1,0:T(8,128)S(1)}, f32[16,128,128]{2,1,0:T(8,128)}, u32[]{:S(2)}) copy-start(f32[16,128,128]{2,1,0:T(8,128)} %copy-done.6) | copy-start | bytes 3145732
  (7 other events, 4.9 us)

commit v3 on v2

v3 whole, which is shorter than its diff:
```python
import functools

import jax
import jax.numpy as jnp
from jax import lax
from jax.experimental import pallas as pl
from jax.experimental.pallas import tpu as pltpu
from jax.sharding import PartitionSpec as P

F32 = jnp.float32
BF16 = jnp.bfloat16
VMEM = pl.BlockSpec(memory_space=pltpu.VMEM)
SMEM = pl.BlockSpec(memory_space=pltpu.SMEM)
HBM = pl.BlockSpec(memory_space=pltpu.HBM)
UNROLL = 8
T_BITS, S_BITS = 10, 10


def params(mib=24):
    return pltpu.CompilerParams(vmem_limit_bytes=mib << 20)


def hbm(x):
    return pltpu.with_memory_space_constraint(x, pltpu.HBM)


def cost(flops, nbytes):
    return pl.CostEstimate(flops=flops, bytes_accessed=nbytes, transcendentals=0)


def start_copies(sems, *pairs):
    copies = [pltpu.make_async_copy(a, b, sems.at[i]) for i, (a, b) in enumerate(pairs)]
    for copy in copies:
        copy.start()
    return copies


def wait_copies(copies):
    for copy in copies:
        copy.wait()


def pick_kernel(rows_h, count_h, hub_h, x_h, out_h, rows_s, count_s, hub_s, x, x32, stage, out, sems):
    copies = start_copies(sems, (x_h, x), (rows_h, rows_s), (count_h, count_s), (hub_h, hub_s))
    n_dom, capacity = rows_s.shape
    hub_dev = hub_s.shape[0]
    step = 16
    wait_copies(copies)
    x32[...] = x[...].astype(F32)
    for j in range(hub_dev):
        stage[capacity + j : capacity + j + 1, :] = x32[pl.ds(hub_s[j], 1), :]
    hub = stage[capacity:, :].astype(BF16)
    slot = lax.broadcasted_iota(jnp.int32, (capacity, x.shape[1]), 0)

    def peer(q, carry):
        def some(g, carry):
            for u in range(step):
                c = g * step + u
                stage[pl.ds(c, 1), :] = x32[pl.ds(rows_s[q, c], 1), :]
            return carry

        lax.fori_loop(0, capacity // step, some, 0)
        kept = jnp.where(slot < count_s[0, q], stage[:capacity, :], 0.0)
        out[q, :capacity, :] = kept.astype(BF16)
        out[q, capacity:, :] = hub
        return carry

    lax.fori_loop(0, n_dom, peer, 0)
    wait_copies(start_copies(sems, (out, out_h)))


def pick(send_rows, send_count, hub_ids, x):
    n_dom, capacity = send_rows.shape
    rows = capacity + hub_ids.shape[0]
    shape = (n_dom, rows, x.shape[1])
    return pl.pallas_call(
        pick_kernel,
        out_shape=pltpu.HBM(shape, BF16),
        in_specs=[HBM] * 4,
        out_specs=HBM,
        scratch_shapes=[
            pltpu.SMEM(send_rows.shape, jnp.int32),
            pltpu.SMEM(send_count.shape, jnp.int32),
            pltpu.SMEM(hub_ids.shape, jnp.int32),
            pltpu.VMEM(x.shape, BF16),
            pltpu.VMEM(x.shape, F32),
            pltpu.VMEM((rows, x.shape[1]), F32),
            pltpu.VMEM(shape, BF16),
            pltpu.SemaphoreType.DMA((4,)),
        ],
        compiler_params=params(),
        cost_estimate=cost(0, 1 << 21),
        name="pick_rows",
    )(hbm(send_rows), hbm(send_count), hbm(hub_ids), hbm(x))


def unpack(entry):
    t = entry & ((1 << T_BITS) - 1)
    s = (entry >> T_BITS) & ((1 << S_BITS) - 1)
    return t, s, entry >> (T_BITS + S_BITS)


def make_lists(dst_s, src_s, lists, own_blocks, far_blocks):
    length = lists.shape[1] - 1

    def step(t, n):
        s = src_s[t]
        d = dst_s[t]
        far = (s >= own_blocks).astype(jnp.int32)
        lists[0, n[0]] = t + (s << T_BITS) + (d << (T_BITS + S_BITS))
        lists[1, n[1]] = t + ((s - own_blocks) << T_BITS) + (d << (T_BITS + S_BITS))
        return n[0] + 1 - far, n[1] + far

    n = lax.fori_loop(0, dst_s.shape[0], step, (jnp.int32(0), jnp.int32(0)))
    for which, blocks in ((0, own_blocks), (1, far_blocks)):
        spare = (blocks << T_BITS) + (own_blocks << (T_BITS + S_BITS))
        for u in range(UNROLL - 1):
            lists[which, n[which] + u] = jnp.int32(spare)
        lists[which, length] = n[which]


def add_tiles(lists, which, tiles, source, acc, spare):
    n = lists[which, lists.shape[1] - 1]

    def group(g, carry):
        done = []
        for u in range(UNROLL):
            t, s, d = unpack(lists[which, g * UNROLL + u])
            s = jnp.where(d == spare, 0, s)
            done.append((d, jnp.dot(tiles[t], source[s], preferred_element_type=F32)))
        for d, product in done:
            acc[d] += product
        return carry

    lax.fori_loop(0, (n + UNROLL - 1) // UNROLL, group, 0)


def add_tiles_t(lists, which, tiles, source, acc, spare):
    n = lists[which, lists.shape[1] - 1]

    def group(g, carry):
        done = []
        for u in range(UNROLL):
            t, s, d = unpack(lists[which, g * UNROLL + u])
            d = jnp.where(d == spare, 0, d)
            product = lax.dot_general(
                tiles[t], source[d], (((0,), (0,)), ((), ())), preferred_element_type=F32
            )
            done.append((s, product))
        for s, product in done:
            acc[s] += product
        return carry

    lax.fori_loop(0, (n + UNROLL - 1) // UNROLL, group, 0)


def own_kernel(dst_h, src_h, tiles, x_h, out_h, lists, dst_s, src_s, x, acc, sems, *, far_blocks):
    own_blocks = x.shape[0]
    copies = start_copies(sems, (x_h, x), (dst_h, dst_s), (src_h, src_s))
    acc[...] = jnp.zeros_like(acc)
    wait_copies(copies)
    make_lists(dst_s, src_s, lists, own_blocks, far_blocks)
    add_tiles(lists, 0, tiles, x, acc, own_blocks)
    wait_copies(start_copies(sems, (acc.at[pl.ds(0, own_blocks)], out_h)))


def own_tiles(tile_dst, tile_src, tiles, x, far_blocks):
    n = tiles.shape[0]
    return pl.pallas_call(
        functools.partial(own_kernel, far_blocks=far_blocks),
        out_shape=(
            pltpu.HBM(x.shape, F32),
            jax.ShapeDtypeStruct((2, n + UNROLL), jnp.int32),
        ),
        in_specs=[HBM, HBM, VMEM, HBM],
        out_specs=(HBM, SMEM),
        scratch_shapes=[
            pltpu.SMEM((n,), jnp.int32),
            pltpu.SMEM((n,), jnp.int32),
            pltpu.VMEM(x.shape, BF16),
            pltpu.VMEM((x.shape[0] + 1,) + x.shape[1:], F32),
            pltpu.SemaphoreType.DMA((3,)),
        ],
        compiler_params=params(),
        cost_estimate=cost(2 * n * 128**3, 1 << 23),
        name="own_tiles",
    )(hbm(tile_dst), hbm(tile_src), tiles, hbm(x))


def far_kernel(lists, tiles, incoming_h, base_h, out_h, source, acc, out, sems):
    n_dom, rows, _ = incoming_h.shape
    own_blocks, tile, _ = base_h.shape
    hub_dev = rows - tile
    hub_blocks = n_dom * hub_dev // tile
    pairs = [(incoming_h.at[:, pl.ds(0, tile), :], source.at[pl.ds(hub_blocks, n_dom)])]
    pairs.append((base_h, acc.at[pl.ds(0, own_blocks)]))
    for q in range(n_dom):
        block, row = divmod(q * hub_dev, tile)
        pairs.append(
            (incoming_h.at[q, pl.ds(tile, hub_dev), :], source.at[block, pl.ds(row, hub_dev), :])
        )
    wait_copies(start_copies(sems, *pairs))
    add_tiles(lists, 1, tiles, source, acc, own_blocks)
    out[...] = acc[:own_blocks].astype(BF16)
    wait_copies(start_copies(sems, (out, out_h)))


def far_tiles(lists, tiles, incoming, base, far_blocks):
    own_blocks, tile, width = base.shape
    return pl.pallas_call(
        far_kernel,
        out_shape=pltpu.HBM(base.shape, BF16),
        in_specs=[SMEM, VMEM, HBM, HBM],
        out_specs=HBM,
        scratch_shapes=[
            pltpu.VMEM((far_blocks, tile, width), BF16),
            pltpu.VMEM((own_blocks + 1, tile, width), F32),
            pltpu.VMEM(base.shape, BF16),
            pltpu.SemaphoreType.DMA((incoming.shape[0] + 2,)),
        ],
        compiler_params=params(),
        cost_estimate=cost(tiles.shape[0] * 128**3, 1 << 22),
        name="far_tiles",
    )(lists, tiles, hbm(incoming), hbm(base))


def by_shards(me, shards, w):
    width = shards[0].shape[1]
    rows = [
        w[pl.ds(pl.multiple_of((me ^ k) * width, width), width), :] for k in range(len(shards))
    ]
    return jnp.dot(
        jnp.concatenate([s[...] for s in shards], axis=1),
        jnp.concatenate(rows, axis=0),
        preferred_element_type=F32,
    )


def self_kernel(me_s, *refs):
    shards, w, bias, out = refs[:-3], refs[-3], refs[-2], refs[-1]
    out[...] = by_shards(me_s[0], shards, w) + bias[...]


def forward_kernel(me_s, *refs):
    shards = refs[:-5]
    w, own_part, grad_out, output, grad_pre = refs[-5:]
    pre_act = own_part[...] + by_shards(me_s[0], shards, w)
    gate = jax.nn.sigmoid(pre_act)
    output[...] = (pre_act * gate).astype(BF16)
    grad = grad_out[...].astype(F32) * gate * (1.0 + pre_act * (1.0 - gate))
    grad_pre[...] = grad.astype(BF16)


def row_blocks_call(kernel, me, by_row, operands, outs, flops, name, block=512):
    rows, width = by_row[0].shape
    row_spec = pl.BlockSpec((block, width), lambda i, m: (i, 0))
    return pl.pallas_call(
        kernel,
        out_shape=tuple(pltpu.HBM((rows, width), t) for t in outs),
        grid_spec=pltpu.PrefetchScalarGridSpec(
            num_scalar_prefetch=1,
            grid=(rows // block,),
            in_specs=[
                row_spec if a.shape == (rows, width) else pl.BlockSpec(a.shape, lambda i, m: (0, 0))
                for a in operands
            ],
            out_specs=tuple(row_spec for t in outs),
        ),
        compiler_params=params(),
        cost_estimate=cost(flops, 1 << 22),
        name=name,
    )(me, *[hbm(a) for a in operands])


def weights_kernel(*refs, n_feat):
    shards, grad, out_h, out, sems = refs[: 2 * n_feat], *refs[2 * n_feat :]
    n_dom, chunk = out.shape[0], out.shape[1] - 8
    width = grad.shape[1]
    flipped = grad[...].T
    bias = jnp.sum(grad[...].astype(F32), axis=0, keepdims=True)
    for i, shard in enumerate(shards):
        block = jnp.dot(flipped, shard[...], preferred_element_type=F32).T
        for row in range(0, width, min(chunk, width)):
            q, start = divmod(i * width + row, chunk)
            n = min(chunk, width)
            out[q, start : start + n, :] = block[row : row + n, :]
    for q in range(n_dom):
        out[q, chunk:, :] = jnp.broadcast_to(bias, (8, width))
    wait_copies(start_copies(sems, (out, out_h)))


def weight_parts(shards, grad, n_dom):
    n_feat = len(shards) // 2
    width = grad.shape[1]
    chunk = 2 * n_feat * width // n_dom
    return pl.pallas_call(
        functools.partial(weights_kernel, n_feat=n_feat),
        out_shape=pltpu.HBM((n_dom, chunk + 8, width), F32),
        in_specs=[VMEM] * (2 * n_feat + 1),
        out_specs=HBM,
        scratch_shapes=[
            pltpu.VMEM((n_dom, chunk + 8, width), F32),
            pltpu.SemaphoreType.DMA((1,)),
        ],
        compiler_params=params(),
        cost_estimate=cost(4 * n_feat * width * width * grad.shape[0], 1 << 22),
        name="weight_parts",
    )(*[hbm(a) for a in (*shards, grad)])


def back_kernel(*refs):
    grads, w, out = refs[:-2], refs[-2], refs[-1]
    whole = jnp.concatenate([g[...] for g in grads], axis=1)
    rows = jnp.concatenate([w[k] for k in range(w.shape[0])], axis=1)
    product = lax.dot_general(whole, rows, (((1,), (1,)), ((), ())), preferred_element_type=F32)
    out[...] = product.astype(out.dtype)


def back_dense(grads, w, dtype, name, block=512):
    rows, width = grads[0].shape
    by_rows = pl.BlockSpec((block, width), lambda i: (i, 0))
    return pl.pallas_call(
        back_kernel,
        out_shape=pltpu.HBM((rows, width), dtype),
        grid=(rows // block,),
        in_specs=[by_rows] * len(grads) + [pl.BlockSpec(w.shape, lambda i: (0, 0, 0))],
        out_specs=by_rows,
        compiler_params=params(),
        cost_estimate=cost(2 * rows * width * width * len(grads), 1 << 22),
        name=name,
    )(*[hbm(a) for a in (*grads, w)])


def back_far_kernel(lists, tiles, back_h, out_h, back, acc, out, sems):
    n_dom = out.shape[0]
    own_blocks, tile, _ = back.shape
    hub_dev = out.shape[1] - tile
    hub_blocks = n_dom * hub_dev // tile
    copies = start_copies(sems, (back_h, back))
    acc[...] = jnp.zeros_like(acc)
    wait_copies(copies)
    add_tiles_t(lists, 1, tiles, back, acc, own_blocks)
    for q in range(n_dom):
        out[q, :tile, :] = acc[hub_blocks + q].astype(BF16)
        block, row = divmod(q * hub_dev, tile)
        out[q, tile:, :] = acc[block, row : row + hub_dev, :].astype(BF16)
    wait_copies(start_copies(sems, (out, out_h)))


def back_far(lists, tiles, back, n_dom, hub_dev):
    _, tile, width = back.shape
    far_blocks = n_dom * hub_dev // tile + n_dom
    shape = (n_dom, tile + hub_dev, width)
    return pl.pallas_call(
        back_far_kernel,
        out_shape=pltpu.HBM(shape, BF16),
        in_specs=[SMEM, VMEM, HBM],
        out_specs=HBM,
        scratch_shapes=[
            pltpu.VMEM(back.shape, BF16),
            pltpu.VMEM((far_blocks + 1, tile, width), F32),
            pltpu.VMEM(shape, BF16),
            pltpu.SemaphoreType.DMA((1,)),
        ],
        compiler_params=params(),
        cost_estimate=cost(tiles.shape[0] * 128**3, 1 << 22),
        name="back_far",
    )(lists, tiles, hbm(back))


def back_own_kernel(lists, tiles, back_h, direct_h, out_h, back, acc, sems):
    own_blocks = back.shape[0]
    own = acc.at[pl.ds(0, own_blocks)]
    wait_copies(start_copies(sems, (back_h, back), (direct_h, own)))
    add_tiles_t(lists, 0, tiles, back, acc, own_blocks)
    wait_copies(start_copies(sems, (own, out_h)))


def back_own(lists, tiles, back, direct):
    return pl.pallas_call(
        back_own_kernel,
        out_shape=pltpu.HBM(direct.shape, F32),
        in_specs=[SMEM, VMEM, HBM, HBM],
        out_specs=HBM,
        scratch_shapes=[
            pltpu.VMEM(back.shape, BF16),
            pltpu.VMEM((direct.shape[0] + 1,) + direct.shape[1:], F32),
            pltpu.SemaphoreType.DMA((2,)),
        ],
        compiler_params=params(),
        cost_estimate=cost(2 * tiles.shape[0] * 128**3, 1 << 23),
        name="back_own",
    )(lists, tiles, hbm(back), hbm(direct))


def hot_kernel(count_s, rows, out):
    n_dom, capacity = rows.shape
    block = out.shape[0]
    lane = lax.broadcasted_iota(jnp.int32, (1, capacity), 1)
    vertex = lax.broadcasted_iota(jnp.int32, (block, capacity), 0) + pl.program_id(0) * block
    for q in range(n_dom):
        wanted = jnp.where(lane < count_s[0, q], rows[q : q + 1, :], -1)
        one = (vertex == wanted).astype(F32).astype(BF16)
        out[:, q * capacity : (q + 1) * capacity] = one


def hot_rows(send_rows, send_count, own_count, block=256):
    return pl.pallas_call(
        hot_kernel,
        out_shape=pltpu.HBM((own_count, send_rows.size), BF16),
        grid_spec=pltpu.PrefetchScalarGridSpec(
            num_scalar_prefetch=1,
            grid=(own_count // block,),
            in_specs=[pl.BlockSpec(send_rows.shape, lambda i, c: (0, 0))],
            out_specs=pl.BlockSpec((block, send_rows.size), lambda i, c: (i, 0)),
        ),
        compiler_params=params(),
        cost_estimate=cost(0, 1 << 23),
        name="hot_rows",
    )(hbm(send_count), hbm(send_rows))


def finish_kernel(hub_s, hot, incoming, base, out, sent, hub):
    n_dom, rows, width = incoming.shape
    hub_dev = hub_s.shape[0]
    capacity = rows - hub_dev
    block = base.shape[0]

    @pl.when(pl.program_id(0) == 0)
    def _():
        total = jnp.zeros((hub_dev, width), F32)
        for q in range(n_dom):
            sent[q * capacity : (q + 1) * capacity, :] = incoming[q, :capacity, :]
            total += incoming[q, capacity:, :].astype(F32)
        hub[...] = total

    out[...] = base[...] + jnp.dot(hot[...], sent[...], preferred_element_type=F32)
    start = pl.program_id(0) * block
    for j in range(hub_dev):
        row = hub_s[j] - start

        @pl.when((row >= 0) & (row < block))
        def _():
            out[pl.ds(row, 1), :] += hub[j : j + 1, :]


def finish(hub_ids, hot, incoming, base, block=256):
    own_count, width = base.shape
    n_dom, rows, _ = incoming.shape
    hub_dev = hub_ids.shape[0]
    by_rows = lambda n: pl.BlockSpec((block, n), lambda i, h: (i, 0))
    return pl.pallas_call(
        finish_kernel,
        out_shape=pltpu.HBM(base.shape, F32),
        grid_spec=pltpu.PrefetchScalarGridSpec(
            num_scalar_prefetch=1,
            grid=(own_count // block,),
            in_specs=[
                by_rows(hot.shape[1]),
                pl.BlockSpec(incoming.shape, lambda i, h: (0, 0, 0)),
                by_rows(width),
            ],
            out_specs=by_rows(width),
            scratch_shapes=[
                pltpu.VMEM((n_dom * (rows - hub_dev), width), BF16),
                pltpu.VMEM((hub_dev, width), F32),
            ],
        ),
        compiler_params=params(),
        cost_estimate=cost(2 * hot.size * width, 1 << 23),
        name="finish",
    )(hbm(hub_ids), hbm(hot), hbm(incoming), hbm(base))


def cut_kernel(me_s, w_self, w_neigh, *outs):
    width = w_self.shape[1]
    for k, out in enumerate(outs):
        at = pl.ds(pl.multiple_of((me_s[0] ^ k) * width, width), width)
        out[0] = w_self[at, :]
        out[1] = w_neigh[at, :]


def cut_weights(me, w_self, w_neigh, n_feat):
    width = w_self.shape[1]
    return pl.pallas_call(
        cut_kernel,
        out_shape=(pltpu.HBM((2, width, width), BF16),) * n_feat,
        in_specs=[SMEM, VMEM, VMEM],
        out_specs=(VMEM,) * n_feat,
        compiler_params=params(),
        cost_estimate=cost(0, 1 << 20),
        name="cut_weights",
    )(me, hbm(w_self), hbm(w_neigh))


def place_kernel(me_s, sums, self_out, neigh_out):
    rows, width = self_out.shape
    for i in range(2 * rows // width):
        which, k = divmod(i, rows // width)
        target = (self_out, neigh_out)[which]
        at = pl.ds(pl.multiple_of((me_s[0] ^ k) * width, width), width)
        target[at, :] = sums[i * width : (i + 1) * width, :].astype(F32)


def place_weights(me, sums):
    rows, width = sums.shape[0] // 2, sums.shape[1]
    return pl.pallas_call(
        place_kernel,
        out_shape=(pltpu.HBM((rows, width), F32),) * 2,
        in_specs=[SMEM, VMEM],
        out_specs=(VMEM, VMEM),
        compiler_params=params(),
        cost_estimate=cost(0, 1 << 20),
        name="place_weights",
    )(me, hbm(sums))


def body(
    node_feats,
    edge_tiles,
    tile_dst,
    tile_src,
    hub_ids,
    send_rows,
    send_count,
    w_self,
    w_neigh,
    out_bias,
    grad_out,
    *,
    n_feat,
):
    own_count, width = node_feats.shape
    tile_size = edge_tiles.shape[1]
    listed = send_rows[0]
    n_dom, capacity = listed.shape
    hub_dev = hub_ids.shape[0]
    me = lax.axis_index("feat").astype(jnp.int32)
    me_s = me.reshape(1)
    far_blocks = n_dom * hub_dev // tile_size + n_dom

    def swap(x, k):
        return lax.ppermute(x, "feat", [(j, j ^ k) for j in range(n_feat)])

    def gather_feat(x):
        shards = {0: x}
        bit = n_feat // 2
        while bit:
            for k in list(shards):
                shards[k ^ bit] = swap(shards[k], bit)
            bit //= 2
        return [shards[k] for k in range(n_feat)]

    feats = gather_feat(node_feats)

    outgoing = pick(listed, send_count, hub_ids, node_feats)
    incoming = lax.all_to_all(outgoing, "dom", 0, 0, tiled=True)
    own_feats = node_feats.reshape(-1, tile_size, width)
    base, lists = own_tiles(tile_dst, tile_src, edge_tiles, own_feats, far_blocks)
    aggregated = far_tiles(lists, edge_tiles, incoming, base, far_blocks).reshape(own_count, width)

    aggs = gather_feat(aggregated)
    flops = 2 * own_count * n_feat * width * width
    (own_part,) = row_blocks_call(
        self_kernel, me_s, feats, [*feats, w_self, out_bias[None, :]], [F32], flops, "self_dense"
    )
    output, grad_pre = row_blocks_call(
        forward_kernel,
        me_s,
        aggs,
        [*aggs, w_neigh, own_part, grad_out],
        [BF16, BF16],
        flops,
        "forward_dense",
    )
    grads = gather_feat(grad_pre)

    parts = weight_parts(feats + aggs, grad_pre, n_dom)
    chunk = parts.shape[1] - 8
    summed_w = jnp.sum(lax.all_to_all(parts, "dom", 0, 0, tiled=True), axis=0)
    grad_bias = summed_w[chunk]
    weights_out = jnp.broadcast_to(summed_w[None, :chunk].astype(BF16), (n_dom, chunk, width))

    cut = cut_weights(me_s, w_self, w_neigh, n_feat)
    rows = jnp.stack([cut[0]] + [swap(cut[k], k) for k in range(1, n_feat)], axis=1)
    back_agg = back_dense(grads, rows[1], BF16, "back_agg").reshape(own_feats.shape)
    direct = back_dense(grads, rows[0], F32, "direct").reshape(own_feats.shape)
    back_out = back_far(lists, edge_tiles, back_agg, n_dom, hub_dev)
    back_in = lax.all_to_all(back_out, "dom", 0, 0, tiled=True)
    own = back_own(lists, edge_tiles, back_agg, direct).reshape(own_count, width)
    weights_in = lax.all_to_all(weights_out, "dom", 0, 0, tiled=True)
    hot = hot_rows(listed, send_count, own_count)
    grad_feats = finish(hub_ids, hot, back_in, own)
    grad_self, grad_neigh = place_weights(me_s, weights_in.reshape(-1, width))
    return (output, grad_feats, grad_self, grad_neigh, grad_bias)


def solution(mesh):
    in_specs = (
        P("dom", "feat"),
        P("dom", None, None),
        P("dom"),
        P("dom"),
        P("dom"),
        P("dom", None, None),
        P("dom", None),
        P(None, "feat"),
        P(None, "feat"),
        P("feat"),
        P("dom", "feat"),
    )
    out_specs = (P("dom", "feat"), P("dom", "feat"), P(None, "feat"), P(None, "feat"), P("feat"))
    n_feat = mesh.shape["feat"]

    def run(*args):
        return body(*args, n_feat=n_feat)

    return jax.shard_map(run, mesh=mesh, in_specs=in_specs, out_specs=out_specs, check_vma=False)
```

time: 115 us -> 128 us (1.11)
  Pallas kernels: 37.3 us -> 63.8 us
  local copies, waits for them, and re-layouts: 21.2 us -> 3.96 us
  starting transfers between devices: 23.3 us -> 30.4 us
  waiting for transfers between devices: 28.1 us -> 25.3 us
    pallas_call x8 -> x12, Pallas kernels: 28.4 us -> 53.2 us  [the longest x2 8.99 us: row_blocks_call(): pl.pallas_call(kernel, out_shape=tuple((pltpu.HBM((rows, width), t) for t...]
    unnamed x48 -> x4, local copies, waits for them, and re-layouts: 16.7 us -> 1.99 us
    ppermute x12, waiting for transfers between devices: 17.5 us -> 24.4 us  [swap(): return lax.ppermute(x, 'feat', [(j, j ^ k) for j in range(n_feat)])]
    all_to_all x1, waiting for transfers between devices: 6.92 us -> 0.01 us  [body(): back_in = lax.all_to_all(back_out, 'dom', 0, 0, tiled=True)]
    all_to_all x0 -> x1, starting transfers between devices: none -> 5.72 us  [body(): weights_in = lax.all_to_all(weights_out, 'dom', 0, 0, tiled=True)]
    all_to_all x1, waiting for transfers between devices: 3.7 us -> 0.01 us  [body(): summed_w = jnp.sum(lax.all_to_all(parts, 'dom', 0, 0, tiled=True), axis=0)]
    gather x2 -> x0, local copies, waits for them, and re-layouts: 3.2 us -> none  [body(): both = jnp.stack([w_self, w_neigh]).reshape(2, n_feat, width, -1)[:, order]]
    all_to_all x1, starting transfers between devices: 4.2 us -> 5.72 us  [body(): back_in = lax.all_to_all(back_out, 'dom', 0, 0, tiled=True)]
  transfers between devices with their start and end apart: 15 -> 16, of which waited for: 6 -> 3; matrix products, arithmetic and copies ran while one was open for 6% -> 3% of each run, Pallas kernels for 16% -> 33%
where the time goes in v3:
time: 128 us; the launch traced here: 126 us
  Pallas kernels  63.8 us (50%)
  starting transfers between devices  30.4 us (24%)
  waiting for transfers between devices  25.3 us (20%)
  local copies, waits for them, and re-layouts  3.96 us (3%)
  other arithmetic  2.07 us (2%)
    ppermute x12, waiting for transfers between devices, swap(): return lax.ppermute(x, 'feat', [(j, j ^ k) for j in range(n_feat)])  24.4 us
    pallas_call x2, Pallas kernels, row_blocks_call(): pl.pallas_call(kernel, out_shape=tuple((pltpu.HBM((rows, width), t) for t...  8.99 us
    pallas_call x1, Pallas kernels, finish(): pl.pallas_call(finish_kernel, out_shape=pltpu.HBM(base.shape, F32), grid_...  8.97 us
    pallas_call x2, Pallas kernels, back_dense(): pl.pallas_call(back_kernel, out_shape=pltpu.HBM((rows, width), dtype), gr...  8.58 us
    all_to_all x1, starting transfers between devices, body(): incoming = lax.all_to_all(outgoing, 'dom', 0, 0, tiled=True)  7.26 us
    pallas_call x1, Pallas kernels, own_tiles(): pl.pallas_call(functools.partial(own_kernel, far_blocks=far_blocks), out_...  6.06 us
    ppermute x12, starting transfers between devices, swap(): return lax.ppermute(x, 'feat', [(j, j ^ k) for j in range(n_feat)])  5.99 us
    all_to_all x1, starting transfers between devices, body(): summed_w = jnp.sum(lax.all_to_all(parts, 'dom', 0, 0, tiled=True), axis=0)  5.73 us
  transfers between devices with their start and end apart: 16, of which 3 were waited for; matrix products, arithmetic and copies ran while one was open for 3% of the time, Pallas kernels for 33%

profile of v3, /device:TPU:0, one launch (start us, length us, event | category | flops | bytes accessed | tf_op | source)
XLA Modules:
  0.0 126.3 jit_solution(2499891879620625573)
XLA Ops:
  0.6 4.5 %pick_rows.1 = bf16[8,160,128]{2,1,0:T(8,128)(2,1)} custom-call(s32[8,128]{1,0:T(8,128)} %bitcast.28, s32[1,8]{1,0:T(1,128)} %count_s.1, s32[32]{0:T(128)} %hub_s.1, bf16[2048,128]{1,0:T(8,128)(2,1)} %refs_0_.3), custom_call_target="tpu_custom_call" | custom-call | bytes 2097152 | tf_op jit(solution)/shard_map/pick_rows/pallas_call | solution.py:76
  5.1 7.3 %all-to-all-start = ((bf16[8,160,128]{2,1,0:T(8,128)(2,1)}), bf16[8,160,128]{2,1,0:T(8,128)(2,1)}, u32[]{:S(2)}, u32[]{:S(2)}) async-start(bf16[8,160,128]{2,1,0:T(8,128)(2,1)} %pick_rows.1), calls=%async_computation | async-start | bytes 655360 | tf_op jit(solution)/shard_map/all_to_all | solution.py:557
  12.4 1.5 %collective-permute-start.4 = (bf16[2048,128]{1,0:T(8,128)(2,1)}, bf16[2048,128]{1,0:T(8,128)(2,1)}, u32[]{:S(2)}, u32[]{:S(2)}) collective-permute-start(bf16[2048,128]{1,0:T(8,128)(2,1)} %refs_0_.3), channel_id=1, source_target_pairs={{0,2},{1,3},{2,0},{3,1},{4,6},{5,7},{6,4},{7,5},{8,10},{9,11},{10,... | collective-permute-start | bytes 1572872 | tf_op jit(solution)/shard_map/ppermute | solution.py:543
  13.9 2.0 %copy-done = bf16[106,128,128]{2,1,0:T(8,128)(2,1)S(1)} copy-done((bf16[106,128,128]{2,1,0:T(8,128)(2,1)S(1)}, bf16[106,128,128]{2,1,0:T(8,128)(2,1)}, u32[]{:S(2)}) %copy-start) | copy-done | bytes 3473432
  15.9 6.1 %own_tiles.1 = (f32[16,128,128]{2,1,0:T(8,128)}, s32[2,114]{1,0:T(2,128)S(1)}) custom-call(s32[106]{0:T(128)} %dst_h.1, s32[106]{0:T(128)} %src_h.1, bf16[106,128,128]{2,1,0:T(8,128)(2,1)S(1)} %copy-done, bf16[16,128,128]{2,1,0:T(8,128)(2,1)} %bitcast.1.x_h), custom_call_target="tpu_custom_call" | custom-call | flops 444596224 | bytes 8388608 | tf_op jit(solution)/shard_map/own_tiles/pallas_call | solution.py:169
  21.9 0.9 all-to-all-done.incoming_h
  22.8 4.3 %far_tiles.1 = bf16[16,128,128]{2,1,0:T(8,128)(2,1)} custom-call(s32[2,114]{1,0:T(2,128)S(1)} %get-tuple-element.15.lists, bf16[106,128,128]{2,1,0:T(8,128)(2,1)S(1)} %copy-done.1, bf16[8,160,128]{2,1,0:T(8,128)(2,1)} %all-to-all-done.incoming_h, f32[16,128,128]{2,1,0:T(8,128)} %get-tuple-element.16.base_h), custom_call_target="tpu_custom_call" | custom-call | flops 222298112 | bytes 4194304 | tf_op jit(solution)/shard_map/far_tiles/pallas_call | solution.py:210
  27.1 1.6 %collective-permute-start.1 = (bf16[2048,128]{1,0:T(8,128)(2,1)}, bf16[2048,128]{1,0:T(8,128)(2,1)}, u32[]{:S(2)}, u32[]{:S(2)}) collective-permute-start(bf16[2048,128]{1,0:T(8,128)(2,1)} %bitcast.19), channel_id=1, source_target_pairs={{0,2},{1,3},{2,0},{3,1},{4,6},{5,7},{6,4},{7,5},{8,10},{9,11},{10,... | collective-permute-start | bytes 1572872 | tf_op jit(solution)/shard_map/ppermute | solution.py:543
  28.7 0.5 collective-permute-start.5
  29.2 10.5 %collective-permute-done.1.refs_2_.refs_6_ = bf16[2048,128]{1,0:T(8,128)(2,1)} collective-permute-done((bf16[2048,128]{1,0:T(8,128)(2,1)}, bf16[2048,128]{1,0:T(8,128)(2,1)}, u32[]{:S(2)}, u32[]{:S(2)}) %collective-permute-start.1) | collective-permute-done | bytes 524320 | tf_op jit(solution)/shard_map/ppermute | solution.py:543
  39.7 4.3 %self_dense.1.refs_5_ = f32[2048,128]{1,0:T(8,128)} custom-call(s32[1]{0:T(128)} %bitcast.me_s, bf16[2048,128]{1,0:T(8,128)(2,1)} %refs_0_.3, bf16[2048,128]{1,0:T(8,128)(2,1)} %collective-permute-done.3.refs_1_, bf16[2048,128]{1,0:T(8,128)(2,1)} %collective-permute-done.4.refs_2_, bf16[2048,128]{1,0:T(8,128)(2,1)} %collective-permute-done.5.refs_3_, ...), custom_call_target="tpu_custom_call" | custom-call | flops 268435456 | bytes 4194304 | tf_op jit(solution)/shard_map/self_dense/pallas_call | solution.py:257
  44.1 4.7 %forward_dense.1 = (bf16[2048,128]{1,0:T(8,128)(2,1)}, bf16[2048,128]{1,0:T(8,128)(2,1)}) custom-call(s32[1]{0:T(128)} %bitcast.me_s, bf16[2048,128]{1,0:T(8,128)(2,1)} %bitcast.21, bf16[2048,128]{1,0:T(8,128)(2,1)} %collective-permute-done.refs_1_.refs_5_, bf16[2048,128]{1,0:T(8,128)(2,1)} %collective-permute-done.1.refs_2_.refs_6_, ...), custom_call_target="tpu_custom_call" | custom-call | flops 268435456 | bytes 4194304 | tf_op jit(solution)/shard_map/forward_dense/pallas_call | solution.py:257
  48.7 4.5 %weight_parts.1 = f32[8,136,128]{2,1,0:T(8,128)} custom-call(bf16[2048,128]{1,0:T(8,128)(2,1)} %refs_0_.3, bf16[2048,128]{1,0:T(8,128)(2,1)} %collective-permute-done.3.refs_1_, bf16[2048,128]{1,0:T(8,128)(2,1)} %collective-permute-done.4.refs_2_, bf16[2048,128]{1,0:T(8,128)(2,1)} %collective-permute-done.5.refs_3_, bf16[2048,128]{1,0:T(8,128)(2,1)} %bitcast.22, ...), custom_call_target="tpu_custom_call" | custom-call | flops 536870912 | bytes 4194304 | tf_op jit(solution)/shard_map/weight_parts/pallas_call | solution.py:296
  53.2 5.7 %all-to-all-start.2 = ((f32[8,136,128]{2,1,0:T(8,128)}), f32[8,136,128]{2,1,0:T(8,128)}, u32[]{:S(2)}, u32[]{:S(2)}) async-start(f32[8,136,128]{2,1,0:T(8,128)} %weight_parts.1), calls=%async_computation.2 | async-start | bytes 1114112 | tf_op jit(solution)/shard_map/all_to_all | solution.py:580
  58.9 0.5 collective-permute-start.7
  59.5 13.9 %collective-permute-done.7.refs_2_ = bf16[2048,128]{1,0:T(8,128)(2,1)} collective-permute-done((bf16[2048,128]{1,0:T(8,128)(2,1)}, bf16[2048,128]{1,0:T(8,128)(2,1)}, u32[]{:S(2)}, u32[]{:S(2)}) %collective-permute-start.7) | collective-permute-done | bytes 524320 | tf_op jit(solution)/shard_map/ppermute | solution.py:543
  73.3 1.7 %cut_weights.1 = (bf16[2,128,128]{2,1,0:T(8,128)(2,1)}, bf16[2,128,128]{2,1,0:T(8,128)(2,1)}, bf16[2,128,128]{2,1,0:T(8,128)(2,1)}, bf16[2,128,128]{2,1,0:T(8,128)(2,1)}) custom-call(s32[1]{0:T(128)} %bitcast.me_s, bf16[512,128]{1,0:T(8,128)(2,1)} %w_self.1, bf16[512,128]{1,0:T(8,128)(2,1)} %w_neigh.1), custom_call_target="tpu_custom_call" | custom-call | bytes 1048576 | tf_op jit(solution)/shard_map/cut_weights/pallas_call | solution.py:485
  76.0 0.8 collective-permute-start.11
  76.8 1.1 reduce_sum.9
  78.0 0.7 broadcast_in_dim.10
  78.7 5.7 %all-to-all-start.3 = ((bf16[8,128,128]{2,1,0:T(8,128)(2,1)}), bf16[8,128,128]{2,1,0:T(8,128)(2,1)}, u32[]{:S(2)}, u32[]{:S(2)}) async-start(bf16[8,128,128]{2,1,0:T(8,128)(2,1)} %broadcast_in_dim.10), calls=%async_computation.3 | async-start | bytes 524288 | tf_op jit(solution)/shard_map/all_to_all | solution.py:591
  84.4 1.0 pad_maximum_fusion
  85.4 0.7 slice_bitcast_fusion
  86.1 4.3 %back_agg.1 = bf16[2048,128]{1,0:T(8,128)(2,1)} custom-call(bf16[2048,128]{1,0:T(8,128)(2,1)} %get-tuple-element.18.refs_0_.refs_8_, bf16[2048,128]{1,0:T(8,128)(2,1)} %collective-permute-done.6.refs_1_, bf16[2048,128]{1,0:T(8,128)(2,1)} %collective-permute-done.7.refs_2_, bf16[2048,128]{1,0:T(8,128)(2,1)} %collective-permute-done.8.refs_3_, ...), custom_call_target="tpu_custom_call" | custom-call | flops 268435456 | bytes 4194304 | tf_op jit(solution)/shard_map/back_agg/pallas_call | solution.py:322
  90.4 4.0 %back_far.1 = bf16[8,160,128]{2,1,0:T(8,128)(2,1)} custom-call(s32[2,114]{1,0:T(2,128)S(1)} %get-tuple-element.15.lists, bf16[106,128,128]{2,1,0:T(8,128)(2,1)S(1)} %copy-done.1, bf16[16,128,128]{2,1,0:T(8,128)(2,1)} %bitcast.23), custom_call_target="tpu_custom_call" | custom-call | flops 222298112 | bytes 4194304 | tf_op jit(solution)/shard_map/back_far/pallas_call | solution.py:354
  94.4 5.7 %all-to-all-start.1 = ((bf16[8,160,128]{2,1,0:T(8,128)(2,1)}), bf16[8,160,128]{2,1,0:T(8,128)(2,1)}, u32[]{:S(2)}, u32[]{:S(2)}) async-start(bf16[8,160,128]{2,1,0:T(8,128)(2,1)} %back_far.1), calls=%async_computation.1 | async-start | bytes 655360 | tf_op jit(solution)/shard_map/all_to_all | solution.py:589
  100.1 5.3 %hot_rows.1.hot = bf16[2048,1024]{1,0:T(8,128)(2,1)} custom-call(s32[1,8]{1,0:T(1,128)} %count_s.1, s32[8,128]{1,0:T(8,128)} %bitcast.29), custom_call_target="tpu_custom_call" | custom-call | bytes 8388608 | tf_op jit(solution)/shard_map/hot_rows/pallas_call | solution.py:408
  105.5 0.5 slice_bitcast_fusion.2
  106.0 4.3 %direct.1 = f32[2048,128]{1,0:T(8,128)} custom-call(bf16[2048,128]{1,0:T(8,128)(2,1)} %get-tuple-element.18.refs_0_.refs_8_, bf16[2048,128]{1,0:T(8,128)(2,1)} %collective-permute-done.6.refs_1_, bf16[2048,128]{1,0:T(8,128)(2,1)} %collective-permute-done.7.refs_2_, bf16[2048,128]{1,0:T(8,128)(2,1)} %collective-permute-done.8.refs_3_, ...), custom_call_target="tpu_custom_call" | custom-call | flops 268435456 | bytes 4194304 | tf_op jit(solution)/shard_map/direct/pallas_call | solution.py:322
  110.3 5.2 %back_own.1 = f32[16,128,128]{2,1,0:T(8,128)} custom-call(s32[2,114]{1,0:T(2,128)S(1)} %get-tuple-element.15.lists, bf16[106,128,128]{2,1,0:T(8,128)(2,1)S(1)} %copy-done.1, bf16[16,128,128]{2,1,0:T(8,128)(2,1)} %bitcast.24, f32[16,128,128]{2,1,0:T(8,128)} %bitcast.25), custom_call_target="tpu_custom_call" | custom-call | flops 444596224 | bytes 8388608 | tf_op jit(solution)/shard_map/back_own/pallas_call | solution.py:380
  115.5 1.8 %place_weights.1 = (f32[512,128]{1,0:T(8,128)}, f32[512,128]{1,0:T(8,128)}) custom-call(s32[1]{0:T(128)} %bitcast.me_s, bf16[1024,128]{1,0:T(8,128)(2,1)} %bitcast.14.sums), custom_call_target="tpu_custom_call" | custom-call | bytes 1048576 | tf_op jit(solution)/shard_map/place_weights/pallas_call | solution.py:507
  117.3 9.0 %finish.1 = f32[2048,128]{1,0:T(8,128)} custom-call(s32[32]{0:T(128)} %hub_s.1, bf16[2048,1024]{1,0:T(8,128)(2,1)} %hot_rows.1.hot, bf16[8,160,128]{2,1,0:T(8,128)(2,1)} %all-to-all-done.1.incoming, f32[2048,128]{1,0:T(8,128)} %bitcast.26), custom_call_target="tpu_custom_call" | custom-call | flops 536870912 | bytes 8388608 | tf_op jit(solution)/shard_map/finish/pallas_call | solution.py:452
  (24 shorter events, 1.1 us)
Async XLA Ops:
  5.1 17.7 %all-to-all-start = ((bf16[8,160,128]{2,1,0:T(8,128)(2,1)}), bf16[8,160,128]{2,1,0:T(8,128)(2,1)}, u32[]{:S(2)}, u32[]{:S(2)}) async-start(bf16[8,160,128]{2,1,0:T(8,128)(2,1)} %pick_rows.1), calls=%async_computation | async-start | bytes 655360 | tf_op jit(solution)/shard_map/all_to_all | solution.py:557
  12.4 16.3 %collective-permute-start.4 = (bf16[2048,128]{1,0:T(8,128)(2,1)}, bf16[2048,128]{1,0:T(8,128)(2,1)}, u32[]{:S(2)}, u32[]{:S(2)}) collective-permute-start(bf16[2048,128]{1,0:T(8,128)(2,1)} %refs_0_.3), channel_id=1, source_target_pairs={{0,2},{1,3},{2,0},{3,1},{4,6},{5,7},{6,4},{7,5},{8,10},{9,11},{10,... | collective-permute-start | bytes 1572872 | tf_op jit(solution)/shard_map/ppermute | solution.py:543
  13.9 2.0 %copy-start = (bf16[106,128,128]{2,1,0:T(8,128)(2,1)S(1)}, bf16[106,128,128]{2,1,0:T(8,128)(2,1)}, u32[]{:S(2)}) copy-start(bf16[106,128,128]{2,1,0:T(8,128)(2,1)} %tiles.7) | copy-start | bytes 10420228
  15.9 6.9 %copy-start.1 = (bf16[106,128,128]{2,1,0:T(8,128)(2,1)S(1)}, bf16[106,128,128]{2,1,0:T(8,128)(2,1)}, u32[]{:S(2)}) copy-start(bf16[106,128,128]{2,1,0:T(8,128)(2,1)} %tiles.7) | copy-start | bytes 10420228
  27.1 12.6 %collective-permute-start.1 = (bf16[2048,128]{1,0:T(8,128)(2,1)}, bf16[2048,128]{1,0:T(8,128)(2,1)}, u32[]{:S(2)}, u32[]{:S(2)}) collective-permute-start(bf16[2048,128]{1,0:T(8,128)(2,1)} %bitcast.19), channel_id=1, source_target_pairs={{0,2},{1,3},{2,0},{3,1},{4,6},{5,7},{6,4},{7,5},{8,10},{9,11},{10,... | collective-permute-start | bytes 1572872 | tf_op jit(solution)/shard_map/ppermute | solution.py:543
  28.6 11.1 %collective-permute-start.3 = (bf16[2048,128]{1,0:T(8,128)(2,1)}, bf16[2048,128]{1,0:T(8,128)(2,1)}, u32[]{:S(2)}, u32[]{:S(2)}) collective-permute-start(bf16[2048,128]{1,0:T(8,128)(2,1)} %refs_0_.3), channel_id=1, source_target_pairs={{0,1},{1,0},{2,3},{3,2},{4,5},{5,4},{6,7},{7,6},{8,9},{9,8},{10,11... | collective-permute-start | bytes 1572872 | tf_op jit(solution)/shard_map/ppermute | solution.py:543
  28.7 11.1 %collective-permute-start.5 = (bf16[2048,128]{1,0:T(8,128)(2,1)}, bf16[2048,128]{1,0:T(8,128)(2,1)}, u32[]{:S(2)}, u32[]{:S(2)}) collective-permute-start(bf16[2048,128]{1,0:T(8,128)(2,1)} %collective-permute-done.4.refs_2_), channel_id=1, source_target_pairs={{0,1},{1,0},{2,3},{3,2},{4,5},{5,4},{6,7},{7,6},{8,9},{9,8},{10,11... | collective-permute-start | bytes 1572872 | tf_op jit(solution)/shard_map/ppermute | solution.py:543
  29.2 14.9 %collective-permute-start = (bf16[2048,128]{1,0:T(8,128)(2,1)}, bf16[2048,128]{1,0:T(8,128)(2,1)}, u32[]{:S(2)}, u32[]{:S(2)}) collective-permute-start(bf16[2048,128]{1,0:T(8,128)(2,1)} %bitcast.20), channel_id=1, source_target_pairs={{0,1},{1,0},{2,3},{3,2},{4,5},{5,4},{6,7},{7,6},{8,9},{9,8},{10,11... | collective-permute-start | bytes 1572872 | tf_op jit(solution)/shard_map/ppermute | solution.py:543
  39.7 4.3 %collective-permute-start.2 = (bf16[2048,128]{1,0:T(8,128)(2,1)}, bf16[2048,128]{1,0:T(8,128)(2,1)}, u32[]{:S(2)}, u32[]{:S(2)}) collective-permute-start(bf16[2048,128]{1,0:T(8,128)(2,1)} %collective-permute-done.1.refs_2_.refs_6_), channel_id=1, source_target_pairs={{0,1},{1,0},{2,3},{3,2},{4,5},{5,4},{6,7},{7,6},{8,9},{9,8},{10,11... | collective-permute-start | bytes 1572872 | tf_op jit(solution)/shard_map/ppermute | solution.py:543
  53.2 23.6 %all-to-all-start.2 = ((f32[8,136,128]{2,1,0:T(8,128)}), f32[8,136,128]{2,1,0:T(8,128)}, u32[]{:S(2)}, u32[]{:S(2)}) async-start(f32[8,136,128]{2,1,0:T(8,128)} %weight_parts.1), calls=%async_computation.2 | async-start | bytes 1114112 | tf_op jit(solution)/shard_map/all_to_all | solution.py:580
  58.9 14.4 %collective-permute-start.7 = (bf16[2048,128]{1,0:T(8,128)(2,1)}, bf16[2048,128]{1,0:T(8,128)(2,1)}, u32[]{:S(2)}, u32[]{:S(2)}) collective-permute-start(bf16[2048,128]{1,0:T(8,128)(2,1)} %get-tuple-element.18.refs_0_.refs_8_), channel_id=1, source_target_pairs={{0,2},{1,3},{2,0},{3,1},{4,6},{5,7},{6,4},{7,5},{8,10},{9,11},{10,... | collective-permute-start | bytes 1572872 | tf_op jit(solution)/shard_map/ppermute | solution.py:543
  59.5 26.7 %collective-permute-start.6 = (bf16[2048,128]{1,0:T(8,128)(2,1)}, bf16[2048,128]{1,0:T(8,128)(2,1)}, u32[]{:S(2)}, u32[]{:S(2)}) collective-permute-start(bf16[2048,128]{1,0:T(8,128)(2,1)} %get-tuple-element.18.refs_0_.refs_8_), channel_id=1, source_target_pairs={{0,1},{1,0},{2,3},{3,2},{4,5},{5,4},{6,7},{7,6},{8,9},{9,8},{10,11... | collective-permute-start | bytes 1572872 | tf_op jit(solution)/shard_map/ppermute | solution.py:543
  73.3 12.8 %collective-permute-start.8 = (bf16[2048,128]{1,0:T(8,128)(2,1)}, bf16[2048,128]{1,0:T(8,128)(2,1)}, u32[]{:S(2)}, u32[]{:S(2)}) collective-permute-start(bf16[2048,128]{1,0:T(8,128)(2,1)} %collective-permute-done.7.refs_2_), channel_id=1, source_target_pairs={{0,1},{1,0},{2,3},{3,2},{4,5},{5,4},{6,7},{7,6},{8,9},{9,8},{10,11... | collective-permute-start | bytes 1572872 | tf_op jit(solution)/shard_map/ppermute | solution.py:543
  75.0 9.4 %collective-permute-start.9 = (bf16[2,128,128]{2,1,0:T(8,128)(2,1)}, bf16[2,128,128]{2,1,0:T(8,128)(2,1)}, u32[]{:S(2)}, u32[]{:S(2)}) collective-permute-start(bf16[2,128,128]{2,1,0:T(8,128)(2,1)} %get-tuple-element.20), channel_id=1, source_target_pairs={{0,1},{1,0},{2,3},{3,2},{4,5},{5,4},{6,7},{7,6},{8,9},{9,8},{10,11... | collective-permute-start | bytes 196616 | tf_op jit(solution)/shard_map/ppermute | solution.py:543
  75.5 8.9 %collective-permute-start.10 = (bf16[2,128,128]{2,1,0:T(8,128)(2,1)}, bf16[2,128,128]{2,1,0:T(8,128)(2,1)}, u32[]{:S(2)}, u32[]{:S(2)}) collective-permute-start(bf16[2,128,128]{2,1,0:T(8,128)(2,1)} %get-tuple-element.21), channel_id=1, source_target_pairs={{0,2},{1,3},{2,0},{3,1},{4,6},{5,7},{6,4},{7,5},{8,10},{9,11},{10,... | collective-permute-start | bytes 196616 | tf_op jit(solution)/shard_map/ppermute | solution.py:543
  76.0 8.4 %collective-permute-start.11 = (bf16[2,128,128]{2,1,0:T(8,128)(2,1)}, bf16[2,128,128]{2,1,0:T(8,128)(2,1)}, u32[]{:S(2)}, u32[]{:S(2)}) collective-permute-start(bf16[2,128,128]{2,1,0:T(8,128)(2,1)} %get-tuple-element.22), channel_id=1, source_target_pairs={{0,3},{1,2},{2,1},{3,0},{4,7},{5,6},{6,5},{7,4},{8,11},{9,10},{10,... | collective-permute-start | bytes 196616 | tf_op jit(solution)/shard_map/ppermute | solution.py:543
  78.7 15.7 %all-to-all-start.3 = ((bf16[8,128,128]{2,1,0:T(8,128)(2,1)}), bf16[8,128,128]{2,1,0:T(8,128)(2,1)}, u32[]{:S(2)}, u32[]{:S(2)}) async-start(bf16[8,128,128]{2,1,0:T(8,128)(2,1)} %broadcast_in_dim.10), calls=%async_computation.3 | async-start | bytes 524288 | tf_op jit(solution)/shard_map/all_to_all | solution.py:591
  94.4 22.9 %all-to-all-start.1 = ((bf16[8,160,128]{2,1,0:T(8,128)(2,1)}), bf16[8,160,128]{2,1,0:T(8,128)(2,1)}, u32[]{:S(2)}, u32[]{:S(2)}) async-start(bf16[8,160,128]{2,1,0:T(8,128)(2,1)} %back_far.1), calls=%async_computation.1 | async-start | bytes 655360 | tf_op jit(solution)/shard_map/all_to_all | solution.py:589

commit v4 on v3

--- a/solution.py
+++ b/solution.py
@@ -12,6 +12,7 @@
 VMEM = pl.BlockSpec(memory_space=pltpu.VMEM)
 SMEM = pl.BlockSpec(memory_space=pltpu.SMEM)
 HBM = pl.BlockSpec(memory_space=pltpu.HBM)
+ANY = pl.BlockSpec(memory_space=pl.ANY)
 UNROLL = 8
 T_BITS, S_BITS = 10, 10
 
@@ -236,40 +237,66 @@
     )
 
 
-def self_kernel(me_s, *refs):
-    shards, w, bias, out = refs[:-3], refs[-3], refs[-2], refs[-1]
-    out[...] = by_shards(me_s[0], shards, w) + bias[...]
-
-
-def forward_kernel(me_s, *refs):
-    shards = refs[:-5]
-    w, own_part, grad_out, output, grad_pre = refs[-5:]
-    pre_act = own_part[...] + by_shards(me_s[0], shards, w)
+def stream(step, ins_h, ins, outs_h, outs, sems, block):
+    rows = ins[0].shape[0]
+    n_in = len(ins)
+    pending = []
+    for i in range(rows // block):
+        at = pl.ds(i * block, block)
+        pairs = [(a.at[at], b.at[at]) for a, b in zip(ins_h, ins)]
+        pending.append(start_copies(sems.at[i], *pairs))
+    leaving = []
+    for i in range(rows // block):
+        at = pl.ds(i * block, block)
+        wait_copies(pending[i])
+        step(at, [r.at[at] for r in ins], [r.at[at] for r in outs])
+        pairs = [(a.at[at], b.at[at]) for a, b in zip(outs, outs_h)]
+        leaving.append(start_copies(sems.at[i, pl.ds(n_in, len(outs))], *pairs))
+    for copies in leaving:
+        wait_copies(copies)
+
+
+def stream_call(kernel, me, streamed, whole, outs, flops, name, block=512):
+    rows = streamed[0].shape[0]
+    n_in, n_whole, n_out = len(streamed), len(whole), len(outs)
+
+    def run(me_s, *refs):
+        ins_h, refs = refs[:n_in], refs[n_in:]
+        held, refs = refs[:n_whole], refs[n_whole:]
+        outs_h, refs = refs[:n_out], refs[n_out:]
+        ins, refs = refs[:n_in], refs[n_in:]
+        out, sems = refs[:n_out], refs[n_out]
+        stream(
+            lambda at, i, o: kernel(me_s[0], i, held, o), ins_h, ins, outs_h, out, sems, block
+        )
+
+    return pl.pallas_call(
+        run,
+        out_shape=tuple(pltpu.HBM(shape, t) for shape, t in outs),
+        in_specs=[SMEM] + [ANY] * n_in + [VMEM] * n_whole,
+        out_specs=(HBM,) * n_out,
+        scratch_shapes=[pltpu.VMEM(x.shape, x.dtype) for x in streamed]
+        + [pltpu.VMEM(shape, t) for shape, t in outs]
+        + [pltpu.SemaphoreType.DMA((rows // block, n_in + n_out))],
+        compiler_params=params(),
+        cost_estimate=cost(flops, 1 << 22),
+        name=name,
+    )(me, *streamed, *[hbm(x) for x in whole])
+
+
+def self_step(me, ins, held, outs):
+    w, bias = held
+    outs[0][...] = by_shards(me, ins, w) + bias[...]
+
+
+def forward_step(me, ins, held, outs):
+    *shards, own_part, grad_out = ins
+    output, grad_pre = outs
+    pre_act = own_part[...] + by_shards(me, shards, held[0])
     gate = jax.nn.sigmoid(pre_act)
     output[...] = (pre_act * gate).astype(BF16)
     grad = grad_out[...].astype(F32) * gate * (1.0 + pre_act * (1.0 - gate))
     grad_pre[...] = grad.astype(BF16)
-
-
-def row_blocks_call(kernel, me, by_row, operands, outs, flops, name, block=512):
-    rows, width = by_row[0].shape
-    row_spec = pl.BlockSpec((block, width), lambda i, m: (i, 0))
-    return pl.pallas_call(
-        kernel,
-        out_shape=tuple(pltpu.HBM((rows, width), t) for t in outs),
-        grid_spec=pltpu.PrefetchScalarGridSpec(
-            num_scalar_prefetch=1,
-            grid=(rows // block,),
-            in_specs=[
-                row_spec if a.shape == (rows, width) else pl.BlockSpec(a.shape, lambda i, m: (0, 0))
-                for a in operands
-            ],
-            out_specs=tuple(row_spec for t in outs),
-        ),
-        compiler_params=params(),
-        cost_estimate=cost(flops, 1 << 22),
-        name=name,
-    )(me, *[hbm(a) for a in operands])
 
 
 def weights_kernel(*refs, n_feat):
@@ -305,67 +332,73 @@
         compiler_params=params(),
         cost_estimate=cost(4 * n_feat * width * width * grad.shape[0], 1 << 22),
         name="weight_parts",
-    )(*[hbm(a) for a in (*shards, grad)])
-
-
-def back_kernel(*refs):
-    grads, w, out = refs[:-2], refs[-2], refs[-1]
-    whole = jnp.concatenate([g[...] for g in grads], axis=1)
-    rows = jnp.concatenate([w[k] for k in range(w.shape[0])], axis=1)
-    product = lax.dot_general(whole, rows, (((1,), (1,)), ((), ())), preferred_element_type=F32)
-    out[...] = product.astype(out.dtype)
-
-
-def back_dense(grads, w, dtype, name, block=512):
-    rows, width = grads[0].shape
-    by_rows = pl.BlockSpec((block, width), lambda i: (i, 0))
-    return pl.pallas_call(
-        back_kernel,
-        out_shape=pltpu.HBM((rows, width), dtype),
-        grid=(rows // block,),
-        in_specs=[by_rows] * len(grads) + [pl.BlockSpec(w.shape, lambda i: (0, 0, 0))],
-        out_specs=by_rows,
-        compiler_params=params(),
-        cost_estimate=cost(2 * rows * width * width * len(grads), 1 << 22),
-        name=name,
-    )(*[hbm(a) for a in (*grads, w)])
-
-
-def back_far_kernel(lists, tiles, back_h, out_h, back, acc, out, sems):
+    )(*shards, grad)
+
+
+def split_copies(sems, pairs, block):
+    rows = pairs[0][0].shape[0]
+    return [
+        start_copies(
+            sems.at[i], *[(a.at[pl.ds(i * block, block)], b.at[pl.ds(i * block, block)]) for a, b in pairs]
+        )
+        for i in range(rows // block)
+    ]
+
+
+def back_far_kernel(*refs, n_feat):
+    lists, tiles = refs[:2]
+    grads_h, w = refs[2 : 2 + n_feat], refs[2 + n_feat : 2 + 2 * n_feat]
+    out_h, back_h, direct_h = refs[2 + 2 * n_feat : 5 + 2 * n_feat]
+    grads = refs[5 + 2 * n_feat : 5 + 3 * n_feat]
+    back, direct, acc, out, sems, out_sems = refs[5 + 3 * n_feat :]
     n_dom = out.shape[0]
-    own_blocks, tile, _ = back.shape
+    own_blocks, tile, width = back.shape
     hub_dev = out.shape[1] - tile
     hub_blocks = n_dom * hub_dev // tile
-    copies = start_copies(sems, (back_h, back))
+    block = 4 * tile
+    pending = split_copies(sems, list(zip(grads_h, grads)), block)
     acc[...] = jnp.zeros_like(acc)
-    wait_copies(copies)
+    rows = jnp.concatenate([r[...].reshape(2 * width, -1) for r in w], axis=1)
+    for i, copies in enumerate(pending):
+        wait_copies(copies)
+        whole = jnp.concatenate([g[i * block : (i + 1) * block, :] for g in grads], axis=1)
+        both = lax.dot_general(whole, rows, (((1,), (1,)), ((), ())), preferred_element_type=F32)
+        direct[4 * i : 4 * (i + 1)] = both[:, :width].reshape(4, tile, width)
+        back[4 * i : 4 * (i + 1)] = both[:, width:].astype(BF16).reshape(4, tile, width)
+    leaving = start_copies(out_sems, (direct, direct_h), (back, back_h))
     add_tiles_t(lists, 1, tiles, back, acc, own_blocks)
     for q in range(n_dom):
         out[q, :tile, :] = acc[hub_blocks + q].astype(BF16)
-        block, row = divmod(q * hub_dev, tile)
-        out[q, tile:, :] = acc[block, row : row + hub_dev, :].astype(BF16)
-    wait_copies(start_copies(sems, (out, out_h)))
-
-
-def back_far(lists, tiles, back, n_dom, hub_dev):
-    _, tile, width = back.shape
+        at, row = divmod(q * hub_dev, tile)
+        out[q, tile:, :] = acc[at, row : row + hub_dev, :].astype(BF16)
+    leaving += start_copies(out_sems.at[pl.ds(2, 1)], (out, out_h))
+    wait_copies(leaving)
+
+
+def back_far(lists, tiles, grads, w, n_dom, hub_dev, tile):
+    n_feat = len(grads)
+    rows, width = grads[0].shape
     far_blocks = n_dom * hub_dev // tile + n_dom
     shape = (n_dom, tile + hub_dev, width)
-    return pl.pallas_call(
-        back_far_kernel,
-        out_shape=pltpu.HBM(shape, BF16),
-        in_specs=[SMEM, VMEM, HBM],
-        out_specs=HBM,
-        scratch_shapes=[
-            pltpu.VMEM(back.shape, BF16),
+    back_shape = (rows // tile, tile, width)
+    return pl.pallas_call(
+        functools.partial(back_far_kernel, n_feat=n_feat),
+        out_shape=(pltpu.HBM(shape, BF16), pltpu.HBM(back_shape, BF16), pltpu.HBM(back_shape, F32)),
+        in_specs=[SMEM, VMEM] + [ANY] * n_feat + [VMEM] * n_feat,
+        out_specs=(HBM, HBM, HBM),
+        scratch_shapes=[pltpu.VMEM((rows, width), BF16)] * n_feat
+        + [
+            pltpu.VMEM(back_shape, BF16),
+            pltpu.VMEM(back_shape, F32),
             pltpu.VMEM((far_blocks + 1, tile, width), F32),
             pltpu.VMEM(shape, BF16),
-            pltpu.SemaphoreType.DMA((1,)),
+            pltpu.SemaphoreType.DMA((rows // (4 * tile), n_feat)),
+            pltpu.SemaphoreType.DMA((3,)),
         ],
         compiler_params=params(),
-        cost_estimate=cost(tiles.shape[0] * 128**3, 1 << 22),
+        cost_estimate=cost(4 * rows * width * width * n_feat, 1 << 22),
         name="back_far",
-    )(lists, tiles, hbm(back))
+    )(lists, tiles, *grads, *w)
 
 
 def back_own_kernel(lists, tiles, back_h, direct_h, out_h, back, acc, sems):
@@ -393,83 +426,70 @@
     )(lists, tiles, hbm(back), hbm(direct))
 
 
-def hot_kernel(count_s, rows, out):
-    n_dom, capacity = rows.shape
-    block = out.shape[0]
+def finish_kernel(rows_s, count_h, hub_h, incoming_h, base_h, out_h, count_s, hub_s, sent, hubs, base, sems, out_sems):
+    n_dom, capacity = rows_s.shape
+    hub_dev = hub_s.shape[0]
+    own_count, width = base.shape
+    block, peers = 256, min(8, n_dom)
+    copies = start_copies(
+        sems,
+        (count_h, count_s),
+        (hub_h, hub_s),
+        (incoming_h.at[:, pl.ds(0, capacity), :], sent),
+        (incoming_h.at[:, pl.ds(capacity, hub_dev), :], hubs),
+        (base_h, base),
+    )
+    wait_copies(copies)
+    hub = hubs[0].astype(F32)
+    for q in range(1, n_dom):
+        hub += hubs[q].astype(F32)
+    for j in range(hub_dev):
+        base[pl.ds(hub_s[j], 1), :] += hub[j : j + 1, :]
     lane = lax.broadcasted_iota(jnp.int32, (1, capacity), 1)
-    vertex = lax.broadcasted_iota(jnp.int32, (block, capacity), 0) + pl.program_id(0) * block
-    for q in range(n_dom):
-        wanted = jnp.where(lane < count_s[0, q], rows[q : q + 1, :], -1)
-        one = (vertex == wanted).astype(F32).astype(BF16)
-        out[:, q * capacity : (q + 1) * capacity] = one
-
-
-def hot_rows(send_rows, send_count, own_count, block=256):
-    return pl.pallas_call(
-        hot_kernel,
-        out_shape=pltpu.HBM((own_count, send_rows.size), BF16),
-        grid_spec=pltpu.PrefetchScalarGridSpec(
-            num_scalar_prefetch=1,
-            grid=(own_count // block,),
-            in_specs=[pl.BlockSpec(send_rows.shape, lambda i, c: (0, 0))],
-            out_specs=pl.BlockSpec((block, send_rows.size), lambda i, c: (i, 0)),
-        ),
-        compiler_params=params(),
-        cost_estimate=cost(0, 1 << 23),
-        name="hot_rows",
-    )(hbm(send_count), hbm(send_rows))
-
-
-def finish_kernel(hub_s, hot, incoming, base, out, sent, hub):
-    n_dom, rows, width = incoming.shape
-    hub_dev = hub_s.shape[0]
-    capacity = rows - hub_dev
-    block = base.shape[0]
-
-    @pl.when(pl.program_id(0) == 0)
-    def _():
-        total = jnp.zeros((hub_dev, width), F32)
-        for q in range(n_dom):
-            sent[q * capacity : (q + 1) * capacity, :] = incoming[q, :capacity, :]
-            total += incoming[q, capacity:, :].astype(F32)
-        hub[...] = total
-
-    out[...] = base[...] + jnp.dot(hot[...], sent[...], preferred_element_type=F32)
-    start = pl.program_id(0) * block
-    for j in range(hub_dev):
-        row = hub_s[j] - start
-
-        @pl.when((row >= 0) & (row < block))
-        def _():
-            out[pl.ds(row, 1), :] += hub[j : j + 1, :]
-
-
-def finish(hub_ids, hot, incoming, base, block=256):
+    leaving = []
+    for start in range(0, own_count, block):
+        vertex = lax.broadcasted_iota(jnp.int32, (block, capacity), 0) + start
+        total = base[start : start + block, :]
+        for first in range(0, n_dom, peers):
+            hot, rows = [], []
+            for q in range(first, first + peers):
+                wanted = jnp.where(lane < count_s[0, q], rows_s[q : q + 1, :], -1)
+                hot.append((vertex == wanted).astype(F32).astype(BF16))
+                rows.append(sent[q])
+            total += jnp.dot(
+                jnp.concatenate(hot, axis=1),
+                jnp.concatenate(rows, axis=0),
+                preferred_element_type=F32,
+            )
+        base[start : start + block, :] = total
+        at = pl.ds(start, block)
+        leaving.append(start_copies(out_sems.at[pl.ds(start // block, 1)], (base.at[at], out_h.at[at])))
+    for copies in leaving:
+        wait_copies(copies)
+
+
+def finish(send_rows, send_count, hub_ids, incoming, base):
+    n_dom, capacity = send_rows.shape
+    hub_dev = hub_ids.shape[0]
     own_count, width = base.shape
-    n_dom, rows, _ = incoming.shape
-    hub_dev = hub_ids.shape[0]
-    by_rows = lambda n: pl.BlockSpec((block, n), lambda i, h: (i, 0))
     return pl.pallas_call(
         finish_kernel,
         out_shape=pltpu.HBM(base.shape, F32),
-        grid_spec=pltpu.PrefetchScalarGridSpec(
-            num_scalar_prefetch=1,
-            grid=(own_count // block,),
-            in_specs=[
-                by_rows(hot.shape[1]),
-                pl.BlockSpec(incoming.shape, lambda i, h: (0, 0, 0)),
-                by_rows(width),
-            ],
-            out_specs=by_rows(width),
-            scratch_shapes=[
-                pltpu.VMEM((n_dom * (rows - hub_dev), width), BF16),
-                pltpu.VMEM((hub_dev, width), F32),
-            ],
-        ),
-        compiler_params=params(),
-        cost_estimate=cost(2 * hot.size * width, 1 << 23),
+        in_specs=[VMEM, HBM, HBM, ANY, HBM],
+        out_specs=HBM,
+        scratch_shapes=[
+            pltpu.SMEM(send_count.shape, jnp.int32),
+            pltpu.SMEM(hub_ids.shape, jnp.int32),
+            pltpu.VMEM((n_dom, capacity, width), BF16),
+            pltpu.VMEM((n_dom, hub_dev, width), BF16),
+            pltpu.VMEM(base.shape, F32),
+            pltpu.SemaphoreType.DMA((5,)),
+            pltpu.SemaphoreType.DMA((own_count // 256,)),
+        ],
+        compiler_params=params(),
+        cost_estimate=cost(2 * base.size * send_rows.size, 1 << 22),
         name="finish",
-    )(hbm(hub_ids), hbm(hot), hbm(incoming), hbm(base))
+    )(hbm(send_rows), hbm(send_count), hbm(hub_ids), incoming, hbm(base))
 
 
 def cut_kernel(me_s, w_self, w_neigh, *outs):
@@ -491,6 +511,30 @@
         cost_estimate=cost(0, 1 << 20),
         name="cut_weights",
     )(me, hbm(w_self), hbm(w_neigh))
+
+
+def sum_kernel(parts, out, bias):
+    n_dom, chunk, _ = out.shape
+    total = parts[0]
+    for q in range(1, n_dom):
+        total += parts[q]
+    bias[...] = total[chunk : chunk + 1, :]
+    rows = total[:chunk, :].astype(BF16)
+    for q in range(n_dom):
+        out[q] = rows
+
+
+def sum_parts(parts):
+    n_dom, rows, width = parts.shape
+    return pl.pallas_call(
+        sum_kernel,
+        out_shape=(pltpu.HBM((n_dom, rows - 8, width), BF16), pltpu.HBM((1, width), F32)),
+        in_specs=[VMEM],
+        out_specs=(VMEM, VMEM),
+        compiler_params=params(),
+        cost_estimate=cost(0, 1 << 20),
+        name="sum_parts",
+    )(hbm(parts))
 
 
 def place_kernel(me_s, sums, self_out, neigh_out):
@@ -512,7 +556,7 @@
         compiler_params=params(),
         cost_estimate=cost(0, 1 << 20),
         name="place_weights",
-    )(me, hbm(sums))
+    )(me, sums)
 
 
 def body(
@@ -537,21 +581,14 @@
     hub_dev = hub_ids.shape[0]
     me = lax.axis_index("feat").astype(jnp.int32)
     me_s = me.reshape(1)
+    far, near = 2, 1
+    assert n_feat == 4
     far_blocks = n_dom * hub_dev // tile_size + n_dom
 
     def swap(x, k):
         return lax.ppermute(x, "feat", [(j, j ^ k) for j in range(n_feat)])
 
-    def gather_feat(x):
-        shards = {0: x}
-        bit = n_feat // 2
-        while bit:
-            for k in list(shards):
-                shards[k ^ bit] = swap(shards[k], bit)
-            bit //= 2
-        return [shards[k] for k in range(n_feat)]
-
-    feats = gather_feat(node_feats)
+    feat_far = swap(node_feats, far)
 
     outgoing = pick(listed, send_count, hub_ids, node_feats)
     incoming = lax.all_to_all(outgoing, "dom", 0, 0, tiled=True)
@@ -559,40 +596,50 @@
     base, lists = own_tiles(tile_dst, tile_src, edge_tiles, own_feats, far_blocks)
     aggregated = far_tiles(lists, edge_tiles, incoming, base, far_blocks).reshape(own_count, width)
 
-    aggs = gather_feat(aggregated)
+    agg_far = swap(aggregated, far)
+    feat_far, aggregated = lax.optimization_barrier((feat_far, aggregated))
+    feats = [hbm(node_feats), swap(node_feats, near), feat_far, swap(feat_far, near)]
     flops = 2 * own_count * n_feat * width * width
-    (own_part,) = row_blocks_call(
-        self_kernel, me_s, feats, [*feats, w_self, out_bias[None, :]], [F32], flops, "self_dense"
+    rows_out = ((own_count, width), BF16)
+    (own_part,) = stream_call(
+        self_step,
+        me_s,
+        feats,
+        [w_self, out_bias[None, :]],
+        [((own_count, width), F32)],
+        flops,
+        "self_dense",
     )
-    output, grad_pre = row_blocks_call(
-        forward_kernel,
+    cut = cut_weights(me_s, w_self, w_neigh, n_feat)
+    agg_far, own_part, *cut = lax.optimization_barrier((agg_far, own_part, *cut))
+    w_rows = [hbm(cut[0])] + [swap(cut[k], k) for k in range(1, n_feat)]
+    aggs = [hbm(aggregated), swap(aggregated, near), agg_far, swap(agg_far, near)]
+    output, grad_pre = stream_call(
+        forward_step,
         me_s,
-        aggs,
-        [*aggs, w_neigh, own_part, grad_out],
-        [BF16, BF16],
+        [*aggs, hbm(own_part), hbm(grad_out)],
+        [w_neigh],
+        [rows_out, rows_out],
         flops,
         "forward_dense",
     )
-    grads = gather_feat(grad_pre)
-
-    parts = weight_parts(feats + aggs, grad_pre, n_dom)
-    chunk = parts.shape[1] - 8
-    summed_w = jnp.sum(lax.all_to_all(parts, "dom", 0, 0, tiled=True), axis=0)
-    grad_bias = summed_w[chunk]
-    weights_out = jnp.broadcast_to(summed_w[None, :chunk].astype(BF16), (n_dom, chunk, width))
-
-    cut = cut_weights(me_s, w_self, w_neigh, n_feat)
-    rows = jnp.stack([cut[0]] + [swap(cut[k], k) for k in range(1, n_feat)], axis=1)
-    back_agg = back_dense(grads, rows[1], BF16, "back_agg").reshape(own_feats.shape)
-    direct = back_dense(grads, rows[0], F32, "direct").reshape(own_feats.shape)
-    back_out = back_far(lists, edge_tiles, back_agg, n_dom, hub_dev)
+
+    grad_far = swap(grad_pre, far)
+    parts = weight_parts(feats + aggs, hbm(grad_pre), n_dom)
+    part_sums = lax.all_to_all(parts, "dom", 0, 0, tiled=True)
+    grads = [hbm(grad_pre), swap(grad_pre, near), grad_far, swap(grad_far, near)]
+
+    back_out, back_agg, direct = back_far(
+        lists, edge_tiles, grads, w_rows, n_dom, hub_dev, tile_size
+    )
     back_in = lax.all_to_all(back_out, "dom", 0, 0, tiled=True)
     own = back_own(lists, edge_tiles, back_agg, direct).reshape(own_count, width)
+    weights_out, grad_bias = sum_parts(part_sums)
+    weights_out, back_in, own = lax.optimization_barrier((weights_out, back_in, own))
     weights_in = lax.all_to_all(weights_out, "dom", 0, 0, tiled=True)
-    hot = hot_rows(listed, send_count, own_count)
-    grad_feats = finish(hub_ids, hot, back_in, own)
+    grad_feats = finish(listed, send_count, hub_ids, back_in, own)
     grad_self, grad_neigh = place_weights(me_s, weights_in.reshape(-1, width))
-    return (output, grad_feats, grad_self, grad_neigh, grad_bias)
+    return (output, grad_feats, grad_self, grad_neigh, grad_bias[0])
 
 
 def solution(mesh):

time: 128 us -> 106 us (0.83)
  Pallas kernels: 63.8 us -> 48.4 us
  starting transfers between devices: 30.4 us -> 27.7 us
  other arithmetic: 2.07 us -> 0 us
  local copies, waits for them, and re-layouts: 3.96 us -> 1.99 us
    pallas_call x7 -> x5, Pallas kernels: 35.9 us -> 21.5 us  [the longest x2 9.21 us: stream_call(): pl.pallas_call(run, out_shape=tuple((pltpu.HBM(shape, t) for shape, t in...]
    ppermute x12, waiting for transfers between devices: 24.4 us -> 16.8 us  [swap(): return lax.ppermute(x, 'feat', [(j, j ^ k) for j in range(n_feat)])]
    all_to_all x1, waiting for transfers between devices: 0.01 us -> 5.05 us  [body(): weights_in = lax.all_to_all(weights_out, 'dom', 0, 0, tiled=True)]
    all_to_all x1, waiting for transfers between devices: 0.01 us -> 3.64 us  [body(): back_in = lax.all_to_all(back_out, 'dom', 0, 0, tiled=True)]
    all_to_all x1, starting transfers between devices: 5.72 us -> 3.64 us  [body(): weights_in = lax.all_to_all(weights_out, 'dom', 0, 0, tiled=True)]
  transfers between devices with their start and end apart: 16 -> 16, of which waited for: 3 -> 9; matrix products, arithmetic and copies ran while one was open for 3% -> 0% of each run, Pallas kernels for 33% -> 37%
where the time goes in v4:
time: 106 us; the launch traced here: 105 us
  Pallas kernels  48.4 us (46%)
  starting transfers between devices  27.7 us (26%)
  waiting for transfers between devices  26.1 us (25%)
  local copies, waits for them, and re-layouts  1.99 us (2%)
    ppermute x12, waiting for transfers between devices, swap(): return lax.ppermute(x, 'feat', [(j, j ^ k) for j in range(n_feat)])  16.8 us
    pallas_call x2, Pallas kernels, stream_call(): pl.pallas_call(run, out_shape=tuple((pltpu.HBM(shape, t) for shape, t in...  9.21 us
    all_to_all x1, starting transfers between devices, body(): incoming = lax.all_to_all(outgoing, 'dom', 0, 0, tiled=True)  7.26 us
    ppermute x12, starting transfers between devices, swap(): return lax.ppermute(x, 'feat', [(j, j ^ k) for j in range(n_feat)])  6.96 us
    pallas_call x1, Pallas kernels, back_far(): pl.pallas_call(functools.partial(back_far_kernel, n_feat=n_feat), out_sha...  6.42 us
    pallas_call x1, Pallas kernels, own_tiles(): pl.pallas_call(functools.partial(own_kernel, far_blocks=far_blocks), out_...  6.28 us
    pallas_call x1, Pallas kernels, back_own(): pl.pallas_call(back_own_kernel, out_shape=pltpu.HBM(direct.shape, F32), i...  5.45 us
    all_to_all x1, waiting for transfers between devices, body(): weights_in = lax.all_to_all(weights_out, 'dom', 0, 0, tiled=True)  5.05 us
  transfers between devices with their start and end apart: 16, of which 9 were waited for; matrix products, arithmetic and copies ran while one was open for 0% of the time, Pallas kernels for 37%

profile of v4, /device:TPU:0, one launch (start us, length us, event | category | flops | bytes accessed | tf_op | source)
XLA Modules:
  0.0 104.9 jit_solution(10256145544948369879)
XLA Ops:
  0.6 4.5 %pick_rows.1 = bf16[8,160,128]{2,1,0:T(8,128)(2,1)} custom-call(s32[8,128]{1,0:T(8,128)} %bitcast.15, s32[1,8]{1,0:T(1,128)} %count_h.3, s32[32]{0:T(128)} %hub_h.3, bf16[2048,128]{1,0:T(8,128)(2,1)} %refs_0_.3), custom_call_target="tpu_custom_call" | custom-call | bytes 2097152 | tf_op jit(solution)/shard_map/pick_rows/pallas_call | solution.py:77
  5.1 7.3 %all-to-all-start = ((bf16[8,160,128]{2,1,0:T(8,128)(2,1)}), bf16[8,160,128]{2,1,0:T(8,128)(2,1)}, u32[]{:S(2)}, u32[]{:S(2)}) async-start(bf16[8,160,128]{2,1,0:T(8,128)(2,1)} %pick_rows.1), calls=%async_computation | async-start | bytes 655360 | tf_op jit(solution)/shard_map/all_to_all | solution.py:594
  12.4 1.5 %collective-permute-start = (bf16[2048,128]{1,0:T(8,128)(2,1)}, bf16[2048,128]{1,0:T(8,128)(2,1)}, u32[]{:S(2)}, u32[]{:S(2)}) collective-permute-start(bf16[2048,128]{1,0:T(8,128)(2,1)} %refs_0_.3), channel_id=1, source_target_pairs={{0,2},{1,3},{2,0},{3,1},{4,6},{5,7},{6,4},{7,5},{8,10},{9,11},{10,... | collective-permute-start | bytes 1572872 | tf_op jit(solution)/shard_map/ppermute | solution.py:589
  13.9 2.0 %copy-done = bf16[106,128,128]{2,1,0:T(8,128)(2,1)S(1)} copy-done((bf16[106,128,128]{2,1,0:T(8,128)(2,1)S(1)}, bf16[106,128,128]{2,1,0:T(8,128)(2,1)}, u32[]{:S(2)}) %copy-start) | copy-done | bytes 3473432
  15.9 6.3 %own_tiles.1 = (f32[16,128,128]{2,1,0:T(8,128)}, s32[2,114]{1,0:T(2,128)S(1)}) custom-call(s32[106]{0:T(128)} %dst_h.1, s32[106]{0:T(128)} %src_h.1, bf16[106,128,128]{2,1,0:T(8,128)(2,1)S(1)} %copy-done, bf16[16,128,128]{2,1,0:T(8,128)(2,1)} %bitcast.9), custom_call_target="tpu_custom_call" | custom-call | flops 444596224 | bytes 8388608 | tf_op jit(solution)/shard_map/own_tiles/pallas_call | solution.py:170
  22.2 0.6 all-to-all-done.incoming_h
  22.8 4.0 %far_tiles.1 = bf16[16,128,128]{2,1,0:T(8,128)(2,1)} custom-call(s32[2,114]{1,0:T(2,128)S(1)} %get-tuple-element.31.lists.refs_0_, bf16[106,128,128]{2,1,0:T(8,128)(2,1)S(1)} %copy-done.1, bf16[8,160,128]{2,1,0:T(8,128)(2,1)} %all-to-all-done.incoming_h, f32[16,128,128]{2,1,0:T(8,128)} %get-tuple-element.32.base_h), custom_call_target="tpu_custom_call" | custom-call | flops 222298112 | bytes 4194304 | tf_op jit(solution)/shard_map/far_tiles/pallas_call | solution.py:211
  26.9 1.6 %collective-permute-start.2 = (bf16[2048,128]{1,0:T(8,128)(2,1)}, bf16[2048,128]{1,0:T(8,128)(2,1)}, u32[]{:S(2)}, u32[]{:S(2)}) collective-permute-start(bf16[2048,128]{1,0:T(8,128)(2,1)} %bitcast.10), channel_id=1, source_target_pairs={{0,2},{1,3},{2,0},{3,1},{4,6},{5,7},{6,4},{7,5},{8,10},{9,11},{10,... | collective-permute-start | bytes 1572872 | tf_op jit(solution)/shard_map/ppermute | solution.py:589
  28.5 1.7 %cut_weights.1 = (bf16[2,128,128]{2,1,0:T(8,128)(2,1)}, bf16[2,128,128]{2,1,0:T(8,128)(2,1)}, bf16[2,128,128]{2,1,0:T(8,128)(2,1)}, bf16[2,128,128]{2,1,0:T(8,128)(2,1)}) custom-call(s32[1]{0:T(128)} %bitcast.me_s, bf16[512,128]{1,0:T(8,128)(2,1)} %w_self.1, bf16[512,128]{1,0:T(8,128)(2,1)} %refs_6_.1), custom_call_target="tpu_custom_call" | custom-call | bytes 1048576 | tf_op jit(solution)/shard_map/cut_weights/pallas_call | solution.py:505
  30.2 0.2 collective-permute-start.1
  30.3 4.6 %self_dense.1.refs_4_ = f32[2048,128]{1,0:T(8,128)} custom-call(s32[1]{0:T(128)} %bitcast.me_s, bf16[2048,128]{1,0:T(8,128)(2,1)} %refs_0_.3, bf16[2048,128]{1,0:T(8,128)(2,1)} %collective-permute-done.3.refs_1_, bf16[2048,128]{1,0:T(8,128)(2,1)} %collective-permute-done.refs_2_, bf16[2048,128]{1,0:T(8,128)(2,1)} %collective-permute-done.4.refs_3_, ...), custom_call_target="tpu_custom_call" | custom-call | flops 268435456 | bytes 4194304 | tf_op jit(solution)/shard_map/self_dense/pallas_call | solution.py:273
  34.9 6.6 %collective-permute-done.2.refs_2_.refs_6_ = bf16[2048,128]{1,0:T(8,128)(2,1)} collective-permute-done((bf16[2048,128]{1,0:T(8,128)(2,1)}, bf16[2048,128]{1,0:T(8,128)(2,1)}, u32[]{:S(2)}, u32[]{:S(2)}) %collective-permute-start.2) | collective-permute-done | bytes 524320 | tf_op jit(solution)/shard_map/ppermute | solution.py:589
  41.6 2.1 %collective-permute-done.5.refs_3_.refs_7_ = bf16[2048,128]{1,0:T(8,128)(2,1)S(1)} collective-permute-done((bf16[2048,128]{1,0:T(8,128)(2,1)}, bf16[2048,128]{1,0:T(8,128)(2,1)S(1)}, u32[]{:S(2)}, u32[]{:S(2)}) %collective-permute-start.5) | collective-permute-done | bytes 524320 | tf_op jit(solution)/shard_map/ppermute | solution.py:589
  43.7 4.6 %forward_dense.1 = (bf16[2048,128]{1,0:T(8,128)(2,1)}, bf16[2048,128]{1,0:T(8,128)(2,1)}) custom-call(s32[1]{0:T(128)} %bitcast.me_s, bf16[2048,128]{1,0:T(8,128)(2,1)} %bitcast.12, bf16[2048,128]{1,0:T(8,128)(2,1)S(1)} %collective-permute-done.1.refs_1_.refs_5_, bf16[2048,128]{1,0:T(8,128)(2,1)} %collective-permute-done.2.refs_2_.refs_6_, ...), custom_call_target="tpu_custom_call" | custom-call | flops 268435456 | bytes 4194304 | tf_op jit(solution)/shard_map/forward_dense/pallas_call | solution.py:273
  48.3 1.6 %collective-permute-start.7 = (bf16[2048,128]{1,0:T(8,128)(2,1)}, bf16[2048,128]{1,0:T(8,128)(2,1)}, u32[]{:S(2)}, u32[]{:S(2)}) collective-permute-start(bf16[2048,128]{1,0:T(8,128)(2,1)} %get-tuple-element.42.refs_8_.refs_2_), channel_id=1, source_target_pairs={{0,2},{1,3},{2,0},{3,1},{4,6},{5,7},{6,4},{7,5},{8,10},{9,11},{10,... | collective-permute-start | bytes 1572872 | tf_op jit(solution)/shard_map/ppermute | solution.py:589
  49.9 4.2 %weight_parts.1 = f32[8,136,128]{2,1,0:T(8,128)} custom-call(bf16[2048,128]{1,0:T(8,128)(2,1)} %refs_0_.3, bf16[2048,128]{1,0:T(8,128)(2,1)} %collective-permute-done.3.refs_1_, bf16[2048,128]{1,0:T(8,128)(2,1)} %collective-permute-done.refs_2_, bf16[2048,128]{1,0:T(8,128)(2,1)} %collective-permute-done.4.refs_3_, bf16[2048,128]{1,0:T(8,128)(2,1)} %bitcast.13, ...), custom_call_target="tpu_custom_call" | custom-call | flops 536870912 | bytes 4194304 | tf_op jit(solution)/shard_map/weight_parts/pallas_call | solution.py:323
  54.1 4.9 %all-to-all-start.1 = ((f32[8,136,128]{2,1,0:T(8,128)}), f32[8,136,128]{2,1,0:T(8,128)}, u32[]{:S(2)}, u32[]{:S(2)}) async-start(f32[8,136,128]{2,1,0:T(8,128)} %weight_parts.1), calls=%async_computation.1 | async-start | bytes 1114112 | tf_op jit(solution)/shard_map/all_to_all | solution.py:629
  59.0 3.7 %collective-permute-done.7.refs_4_ = bf16[2048,128]{1,0:T(8,128)(2,1)} collective-permute-done((bf16[2048,128]{1,0:T(8,128)(2,1)}, bf16[2048,128]{1,0:T(8,128)(2,1)}, u32[]{:S(2)}, u32[]{:S(2)}) %collective-permute-start.7) | collective-permute-done | bytes 524320 | tf_op jit(solution)/shard_map/ppermute | solution.py:589
  62.7 0.5 collective-permute-start.9
  63.2 1.5 %collective-permute-start.10 = (bf16[2,128,128]{2,1,0:T(8,128)(2,1)}, bf16[2,128,128]{2,1,0:T(8,128)(2,1)S(1)}, u32[]{:S(2)}, u32[]{:S(2)}) collective-permute-start(bf16[2,128,128]{2,1,0:T(8,128)(2,1)} %get-tuple-element.46), channel_id=1, source_target_pairs={{0,2},{1,3},{2,0},{3,1},{4,6},{5,7},{6,4},{7,5},{8,10},{9,11},{10,... | collective-permute-start | bytes 196616 | tf_op jit(solution)/shard_map/ppermute | solution.py:589
  64.7 0.2 collective-permute-done.9.refs_7_
  64.9 2.8 %collective-permute-done.10.refs_8_ = bf16[2,128,128]{2,1,0:T(8,128)(2,1)S(1)} collective-permute-done((bf16[2,128,128]{2,1,0:T(8,128)(2,1)}, bf16[2,128,128]{2,1,0:T(8,128)(2,1)S(1)}, u32[]{:S(2)}, u32[]{:S(2)}) %collective-permute-start.10) | collective-permute-done | bytes 65568 | tf_op jit(solution)/shard_map/ppermute | solution.py:589
  67.7 1.4 %collective-permute-done.11.refs_9_ = bf16[2,128,128]{2,1,0:T(8,128)(2,1)S(1)} collective-permute-done((bf16[2,128,128]{2,1,0:T(8,128)(2,1)S(1)}, bf16[2,128,128]{2,1,0:T(8,128)(2,1)S(1)}, u32[]{:S(2)}, u32[]{:S(2)}) %collective-permute-start.11) | collective-permute-done | bytes 65568 | tf_op jit(solution)/shard_map/ppermute | solution.py:589
  69.1 6.4 %back_far.1 = (bf16[8,160,128]{2,1,0:T(8,128)(2,1)}, bf16[16,128,128]{2,1,0:T(8,128)(2,1)}, f32[16,128,128]{2,1,0:T(8,128)}) custom-call(s32[2,114]{1,0:T(2,128)S(1)} %get-tuple-element.31.lists.refs_0_, bf16[106,128,128]{2,1,0:T(8,128)(2,1)S(1)} %copy-done.1, bf16[2048,128]{1,0:T(8,128)(2,1)} %get-tuple-element.42.refs_8_.refs_2_, ...), custom_call_target="tpu_custom_call" | custom-call | flops 536870912 | bytes 4194304 | tf_op jit(solution)/shard_map/back_far/pallas_call | solution.py:384
  75.5 4.9 %all-to-all-start.2 = ((bf16[8,160,128]{2,1,0:T(8,128)(2,1)}), bf16[8,160,128]{2,1,0:T(8,128)(2,1)}, u32[]{:S(2)}, u32[]{:S(2)}) async-start(bf16[8,160,128]{2,1,0:T(8,128)(2,1)} %get-tuple-element.48), calls=%async_computation.2 | async-start | bytes 655360 | tf_op jit(solution)/shard_map/all_to_all | solution.py:635
  80.4 1.8 %sum_parts.1 = (bf16[8,128,128]{2,1,0:T(8,128)(2,1)}, f32[1,128]{1,0:T(1,128)}) custom-call(f32[8,136,128]{2,1,0:T(8,128)} %all-to-all-done.1.parts), custom_call_target="tpu_custom_call" | custom-call | bytes 1048576 | tf_op jit(solution)/shard_map/sum_parts/pallas_call | solution.py:529
  82.2 5.4 %back_own.1 = f32[16,128,128]{2,1,0:T(8,128)} custom-call(s32[2,114]{1,0:T(2,128)S(1)} %get-tuple-element.31.lists.refs_0_, bf16[106,128,128]{2,1,0:T(8,128)(2,1)S(1)} %copy-done.1, bf16[16,128,128]{2,1,0:T(8,128)(2,1)} %get-tuple-element.49.back_h, f32[16,128,128]{2,1,0:T(8,128)} %get-tuple-element.50.direct_h), custom_call_target="tpu_custom_call" | custom-call | flops 444596224 | bytes 8388608 | tf_op jit(solution)/shard_map/back_own/pallas_call | solution.py:413
  87.7 3.6 %all-to-all-done.2.incoming_h = bf16[8,160,128]{2,1,0:T(8,128)(2,1)} async-done(((bf16[8,160,128]{2,1,0:T(8,128)(2,1)}), bf16[8,160,128]{2,1,0:T(8,128)(2,1)}, u32[]{:S(2)}, u32[]{:S(2)}) %all-to-all-start.2) | async-done | bytes 327712 | tf_op jit(solution)/shard_map/all_to_all | solution.py:635
  91.3 3.6 %all-to-all-start.3 = ((bf16[8,128,128]{2,1,0:T(8,128)(2,1)}), bf16[8,128,128]{2,1,0:T(8,128)(2,1)S(1)}, u32[]{:S(2)}, u32[]{:S(2)}) async-start(bf16[8,128,128]{2,1,0:T(8,128)(2,1)} %get-tuple-element.53), calls=%async_computation.3 | async-start | bytes 524288 | tf_op jit(solution)/shard_map/all_to_all | solution.py:639
  95.0 4.1 %finish.1 = f32[2048,128]{1,0:T(8,128)} custom-call(s32[8,128]{1,0:T(8,128)} %bitcast.16, s32[1,8]{1,0:T(1,128)} %count_h.3, s32[32]{0:T(128)} %hub_h.3, bf16[8,160,128]{2,1,0:T(8,128)(2,1)} %all-to-all-done.2.incoming_h, f32[2048,128]{1,0:T(8,128)} %bitcast.14), custom_call_target="tpu_custom_call" | custom-call | flops 536870912 | bytes 4194304 | tf_op jit(solution)/shard_map/finish/pallas_call | solution.py:475
  99.0 5.0 %all-to-all-done.3 = bf16[8,128,128]{2,1,0:T(8,128)(2,1)S(1)} async-done(((bf16[8,128,128]{2,1,0:T(8,128)(2,1)}), bf16[8,128,128]{2,1,0:T(8,128)(2,1)S(1)}, u32[]{:S(2)}, u32[]{:S(2)}) %all-to-all-start.3) | async-done | bytes 262176 | tf_op jit(solution)/shard_map/all_to_all | solution.py:639
  104.1 0.8 place_weights.1
  (18 shorter events, 0.1 us)
Async XLA Ops:
  5.1 17.7 %all-to-all-start = ((bf16[8,160,128]{2,1,0:T(8,128)(2,1)}), bf16[8,160,128]{2,1,0:T(8,128)(2,1)}, u32[]{:S(2)}, u32[]{:S(2)}) async-start(bf16[8,160,128]{2,1,0:T(8,128)(2,1)} %pick_rows.1), calls=%async_computation | async-start | bytes 655360 | tf_op jit(solution)/shard_map/all_to_all | solution.py:594
  12.4 14.4 %collective-permute-start = (bf16[2048,128]{1,0:T(8,128)(2,1)}, bf16[2048,128]{1,0:T(8,128)(2,1)}, u32[]{:S(2)}, u32[]{:S(2)}) collective-permute-start(bf16[2048,128]{1,0:T(8,128)(2,1)} %refs_0_.3), channel_id=1, source_target_pairs={{0,2},{1,3},{2,0},{3,1},{4,6},{5,7},{6,4},{7,5},{8,10},{9,11},{10,... | collective-permute-start | bytes 1572872 | tf_op jit(solution)/shard_map/ppermute | solution.py:589
  13.9 16.4 %collective-permute-start.3 = (bf16[2048,128]{1,0:T(8,128)(2,1)}, bf16[2048,128]{1,0:T(8,128)(2,1)}, u32[]{:S(2)}, u32[]{:S(2)}) collective-permute-start(bf16[2048,128]{1,0:T(8,128)(2,1)} %refs_0_.3), channel_id=1, source_target_pairs={{0,1},{1,0},{2,3},{3,2},{4,5},{5,4},{6,7},{7,6},{8,9},{9,8},{10,11... | collective-permute-start | bytes 1572872 | tf_op jit(solution)/shard_map/ppermute | solution.py:589
  13.9 2.0 %copy-start = (bf16[106,128,128]{2,1,0:T(8,128)(2,1)S(1)}, bf16[106,128,128]{2,1,0:T(8,128)(2,1)}, u32[]{:S(2)}) copy-start(bf16[106,128,128]{2,1,0:T(8,128)(2,1)} %tiles.5) | copy-start | bytes 10420228
  15.9 6.9 %copy-start.1 = (bf16[106,128,128]{2,1,0:T(8,128)(2,1)S(1)}, bf16[106,128,128]{2,1,0:T(8,128)(2,1)}, u32[]{:S(2)}) copy-start(bf16[106,128,128]{2,1,0:T(8,128)(2,1)} %tiles.5) | copy-start | bytes 10420228
  26.8 3.5 %collective-permute-start.4 = (bf16[2048,128]{1,0:T(8,128)(2,1)}, bf16[2048,128]{1,0:T(8,128)(2,1)}, u32[]{:S(2)}, u32[]{:S(2)}) collective-permute-start(bf16[2048,128]{1,0:T(8,128)(2,1)} %collective-permute-done.refs_2_), channel_id=1, source_target_pairs={{0,1},{1,0},{2,3},{3,2},{4,5},{5,4},{6,7},{7,6},{8,9},{9,8},{10,11... | collective-permute-start | bytes 1572872 | tf_op jit(solution)/shard_map/ppermute | solution.py:589
  26.9 14.7 %collective-permute-start.2 = (bf16[2048,128]{1,0:T(8,128)(2,1)}, bf16[2048,128]{1,0:T(8,128)(2,1)}, u32[]{:S(2)}, u32[]{:S(2)}) collective-permute-start(bf16[2048,128]{1,0:T(8,128)(2,1)} %bitcast.10), channel_id=1, source_target_pairs={{0,2},{1,3},{2,0},{3,1},{4,6},{5,7},{6,4},{7,5},{8,10},{9,11},{10,... | collective-permute-start | bytes 1572872 | tf_op jit(solution)/shard_map/ppermute | solution.py:589
  30.2 11.4 %collective-permute-start.1 = (bf16[2048,128]{1,0:T(8,128)(2,1)}, bf16[2048,128]{1,0:T(8,128)(2,1)S(1)}, u32[]{:S(2)}, u32[]{:S(2)}) collective-permute-start(bf16[2048,128]{1,0:T(8,128)(2,1)} %bitcast.11), channel_id=1, source_target_pairs={{0,1},{1,0},{2,3},{3,2},{4,5},{5,4},{6,7},{7,6},{8,9},{9,8},{10,11... | collective-permute-start | bytes 1572872 | tf_op jit(solution)/shard_map/ppermute | solution.py:589
  41.6 2.1 %collective-permute-start.5 = (bf16[2048,128]{1,0:T(8,128)(2,1)}, bf16[2048,128]{1,0:T(8,128)(2,1)S(1)}, u32[]{:S(2)}, u32[]{:S(2)}) collective-permute-start(bf16[2048,128]{1,0:T(8,128)(2,1)} %collective-permute-done.2.refs_2_.refs_6_), channel_id=1, source_target_pairs={{0,1},{1,0},{2,3},{3,2},{4,5},{5,4},{6,7},{7,6},{8,9},{9,8},{10,11... | collective-permute-start | bytes 1572872 | tf_op jit(solution)/shard_map/ppermute | solution.py:589
  48.3 16.4 %copy-start.2 = (bf16[2,128,128]{2,1,0:T(8,128)(2,1)S(1)}, bf16[2,128,128]{2,1,0:T(8,128)(2,1)}, u32[]{:S(2)}) copy-start(bf16[2,128,128]{2,1,0:T(8,128)(2,1)} %get-tuple-element.47) | copy-start | bytes 196612
  48.3 14.3 %collective-permute-start.7 = (bf16[2048,128]{1,0:T(8,128)(2,1)}, bf16[2048,128]{1,0:T(8,128)(2,1)}, u32[]{:S(2)}, u32[]{:S(2)}) collective-permute-start(bf16[2048,128]{1,0:T(8,128)(2,1)} %get-tuple-element.42.refs_8_.refs_2_), channel_id=1, source_target_pairs={{0,2},{1,3},{2,0},{3,1},{4,6},{5,7},{6,4},{7,5},{8,10},{9,11},{10,... | collective-permute-start | bytes 1572872 | tf_op jit(solution)/shard_map/ppermute | solution.py:589
  54.1 21.4 %all-to-all-start.1 = ((f32[8,136,128]{2,1,0:T(8,128)}), f32[8,136,128]{2,1,0:T(8,128)}, u32[]{:S(2)}, u32[]{:S(2)}) async-start(f32[8,136,128]{2,1,0:T(8,128)} %weight_parts.1), calls=%async_computation.1 | async-start | bytes 1114112 | tf_op jit(solution)/shard_map/all_to_all | solution.py:629
  59.0 10.1 %collective-permute-start.6 = (bf16[2048,128]{1,0:T(8,128)(2,1)}, bf16[2048,128]{1,0:T(8,128)(2,1)S(1)}, u32[]{:S(2)}, u32[]{:S(2)}) collective-permute-start(bf16[2048,128]{1,0:T(8,128)(2,1)} %get-tuple-element.42.refs_8_.refs_2_), channel_id=1, source_target_pairs={{0,1},{1,0},{2,3},{3,2},{4,5},{5,4},{6,7},{7,6},{8,9},{9,8},{10,11... | collective-permute-start | bytes 1572872 | tf_op jit(solution)/shard_map/ppermute | solution.py:589
  62.7 6.4 %collective-permute-start.8 = (bf16[2048,128]{1,0:T(8,128)(2,1)}, bf16[2048,128]{1,0:T(8,128)(2,1)S(1)}, u32[]{:S(2)}, u32[]{:S(2)}) collective-permute-start(bf16[2048,128]{1,0:T(8,128)(2,1)} %collective-permute-done.7.refs_4_), channel_id=1, source_target_pairs={{0,1},{1,0},{2,3},{3,2},{4,5},{5,4},{6,7},{7,6},{8,9},{9,8},{10,11... | collective-permute-start | bytes 1572872 | tf_op jit(solution)/shard_map/ppermute | solution.py:589
  62.7 2.2 %collective-permute-start.9 = (bf16[2,128,128]{2,1,0:T(8,128)(2,1)}, bf16[2,128,128]{2,1,0:T(8,128)(2,1)S(1)}, u32[]{:S(2)}, u32[]{:S(2)}) collective-permute-start(bf16[2,128,128]{2,1,0:T(8,128)(2,1)} %get-tuple-element.45), channel_id=1, source_target_pairs={{0,1},{1,0},{2,3},{3,2},{4,5},{5,4},{6,7},{7,6},{8,9},{9,8},{10,11... | collective-permute-start | bytes 196616 | tf_op jit(solution)/shard_map/ppermute | solution.py:589
  63.2 4.5 %collective-permute-start.10 = (bf16[2,128,128]{2,1,0:T(8,128)(2,1)}, bf16[2,128,128]{2,1,0:T(8,128)(2,1)S(1)}, u32[]{:S(2)}, u32[]{:S(2)}) collective-permute-start(bf16[2,128,128]{2,1,0:T(8,128)(2,1)} %get-tuple-element.46), channel_id=1, source_target_pairs={{0,2},{1,3},{2,0},{3,1},{4,6},{5,7},{6,4},{7,5},{8,10},{9,11},{10,... | collective-permute-start | bytes 196616 | tf_op jit(solution)/shard_map/ppermute | solution.py:589
  64.7 4.4 %collective-permute-start.11 = (bf16[2,128,128]{2,1,0:T(8,128)(2,1)S(1)}, bf16[2,128,128]{2,1,0:T(8,128)(2,1)S(1)}, u32[]{:S(2)}, u32[]{:S(2)}) collective-permute-start(bf16[2,128,128]{2,1,0:T(8,128)(2,1)S(1)} %copy-done.2), channel_id=1, source_target_pairs={{0,3},{1,2},{2,1},{3,0},{4,7},{5,6},{6,5},{7,4},{8,11},{9,10},{10,... | collective-permute-start | bytes 196616 | tf_op jit(solution)/shard_map/ppermute | solution.py:589
  75.5 15.8 %all-to-all-start.2 = ((bf16[8,160,128]{2,1,0:T(8,128)(2,1)}), bf16[8,160,128]{2,1,0:T(8,128)(2,1)}, u32[]{:S(2)}, u32[]{:S(2)}) async-start(bf16[8,160,128]{2,1,0:T(8,128)(2,1)} %get-tuple-element.48), calls=%async_computation.2 | async-start | bytes 655360 | tf_op jit(solution)/shard_map/all_to_all | solution.py:635
  91.3 12.7 %all-to-all-start.3 = ((bf16[8,128,128]{2,1,0:T(8,128)(2,1)}), bf16[8,128,128]{2,1,0:T(8,128)(2,1)S(1)}, u32[]{:S(2)}, u32[]{:S(2)}) async-start(bf16[8,128,128]{2,1,0:T(8,128)(2,1)} %get-tuple-element.53), calls=%async_computation.3 | async-start | bytes 524288 | tf_op jit(solution)/shard_map/all_to_all | solution.py:639

commit v5 on v4

--- a/solution.py
+++ b/solution.py
@@ -14,6 +14,7 @@
 HBM = pl.BlockSpec(memory_space=pltpu.HBM)
 ANY = pl.BlockSpec(memory_space=pl.ANY)
 UNROLL = 8
+CHUNKS = 2
 T_BITS, S_BITS = 10, 10
 
 
@@ -41,7 +42,7 @@
         copy.wait()
 
 
-def pick_kernel(rows_h, count_h, hub_h, x_h, out_h, rows_s, count_s, hub_s, x, x32, stage, out, sems):
+def pick_kernel(rows_h, count_h, hub_h, x_h, out_h, rows_s, count_s, hub_s, x, x32, stage, out, sems, out_sems):
     copies = start_copies(sems, (x_h, x), (rows_h, rows_s), (count_h, count_s), (hub_h, hub_s))
     n_dom, capacity = rows_s.shape
     hub_dev = hub_s.shape[0]
@@ -64,10 +65,12 @@
         kept = jnp.where(slot < count_s[0, q], stage[:capacity, :], 0.0)
         out[q, :capacity, :] = kept.astype(BF16)
         out[q, capacity:, :] = hub
+        pltpu.make_async_copy(out.at[q], out_h.at[q], out_sems.at[q]).start()
         return carry
 
     lax.fori_loop(0, n_dom, peer, 0)
-    wait_copies(start_copies(sems, (out, out_h)))
+    for q in range(n_dom):
+        pltpu.make_async_copy(out.at[q], out_h.at[q], out_sems.at[q]).wait()
 
 
 def pick(send_rows, send_count, hub_ids, x):
@@ -88,6 +91,7 @@
             pltpu.VMEM((rows, x.shape[1]), F32),
             pltpu.VMEM(shape, BF16),
             pltpu.SemaphoreType.DMA((4,)),
+            pltpu.SemaphoreType.DMA((n_dom,)),
         ],
         compiler_params=params(),
         cost_estimate=cost(0, 1 << 21),
@@ -188,7 +192,8 @@
     )(hbm(tile_dst), hbm(tile_src), tiles, hbm(x))
 
 
-def far_kernel(lists, tiles, incoming_h, base_h, out_h, source, acc, out, sems):
+def far_kernel(lists, tiles, incoming_h, base_h, *refs):
+    *outs_h, source, acc, out, sems = refs
     n_dom, rows, _ = incoming_h.shape
     own_blocks, tile, _ = base_h.shape
     hub_dev = rows - tile
@@ -203,16 +208,19 @@
     wait_copies(start_copies(sems, *pairs))
     add_tiles(lists, 1, tiles, source, acc, own_blocks)
     out[...] = acc[:own_blocks].astype(BF16)
-    wait_copies(start_copies(sems, (out, out_h)))
+    n = own_blocks // len(outs_h)
+    wait_copies(
+        start_copies(sems, *[(out.at[pl.ds(c * n, n)], o) for c, o in enumerate(outs_h)])
+    )
 
 
 def far_tiles(lists, tiles, incoming, base, far_blocks):
     own_blocks, tile, width = base.shape
     return pl.pallas_call(
         far_kernel,
-        out_shape=pltpu.HBM(base.shape, BF16),
+        out_shape=(pltpu.HBM((own_blocks // CHUNKS, tile, width), BF16),) * CHUNKS,
         in_specs=[SMEM, VMEM, HBM, HBM],
-        out_specs=HBM,
+        out_specs=(HBM,) * CHUNKS,
         scratch_shapes=[
             pltpu.VMEM((far_blocks, tile, width), BF16),
             pltpu.VMEM((own_blocks + 1, tile, width), F32),
@@ -225,114 +233,124 @@
     )(lists, tiles, hbm(incoming), hbm(base))
 
 
-def by_shards(me, shards, w):
-    width = shards[0].shape[1]
-    rows = [
-        w[pl.ds(pl.multiple_of((me ^ k) * width, width), width), :] for k in range(len(shards))
-    ]
-    return jnp.dot(
-        jnp.concatenate([s[...] for s in shards], axis=1),
-        jnp.concatenate(rows, axis=0),
-        preferred_element_type=F32,
-    )
-
-
-def stream(step, ins_h, ins, outs_h, outs, sems, block):
-    rows = ins[0].shape[0]
-    n_in = len(ins)
+def forward_kernel(me_s, *refs, n_feat, chunk, block):
+    n_in = 2 * n_feat + 1
+    ins_h, refs = refs[:n_in], refs[n_in:]
+    w_self, w_neigh, bias = refs[:3]
+    output_h, grad_h, *refs = refs[-(n_in + 5) :]
+    ins, (output, grad_pre, sems) = refs[:n_in], refs[n_in:]
+    rows, width = output.shape
+    first = chunk * rows
     pending = []
     for i in range(rows // block):
         at = pl.ds(i * block, block)
-        pairs = [(a.at[at], b.at[at]) for a, b in zip(ins_h, ins)]
+        there = pl.ds(first + i * block, block)
+        pairs = [
+            (a.at[at if n_feat <= j < 2 * n_feat else there], b.at[at])
+            for j, (a, b) in enumerate(zip(ins_h, ins))
+        ]
         pending.append(start_copies(sems.at[i], *pairs))
+
+    def by_shard(w):
+        return [
+            w[pl.ds(pl.multiple_of((me_s[0] ^ k) * width, width), width), :] for k in range(n_feat)
+        ]
+
+    weights = jnp.concatenate(by_shard(w_self) + by_shard(w_neigh), axis=0)
     leaving = []
     for i in range(rows // block):
-        at = pl.ds(i * block, block)
+        at = slice(i * block, (i + 1) * block)
         wait_copies(pending[i])
-        step(at, [r.at[at] for r in ins], [r.at[at] for r in outs])
-        pairs = [(a.at[at], b.at[at]) for a, b in zip(outs, outs_h)]
-        leaving.append(start_copies(sems.at[i, pl.ds(n_in, len(outs))], *pairs))
-    for copies in leaving:
-        wait_copies(copies)
-
-
-def stream_call(kernel, me, streamed, whole, outs, flops, name, block=512):
-    rows = streamed[0].shape[0]
-    n_in, n_whole, n_out = len(streamed), len(whole), len(outs)
-
-    def run(me_s, *refs):
-        ins_h, refs = refs[:n_in], refs[n_in:]
-        held, refs = refs[:n_whole], refs[n_whole:]
-        outs_h, refs = refs[:n_out], refs[n_out:]
-        ins, refs = refs[:n_in], refs[n_in:]
-        out, sems = refs[:n_out], refs[n_out]
-        stream(
-            lambda at, i, o: kernel(me_s[0], i, held, o), ins_h, ins, outs_h, out, sems, block
+        shards = jnp.concatenate([r[at, :] for r in ins[:-1]], axis=1)
+        pre_act = jnp.dot(shards, weights, preferred_element_type=F32) + bias[...]
+        gate = jax.nn.sigmoid(pre_act)
+        output[at, :] = (pre_act * gate).astype(BF16)
+        grad = ins[-1][at, :].astype(F32) * gate * (1.0 + pre_act * (1.0 - gate))
+        grad_pre[at, :] = grad.astype(BF16)
+        here = pl.ds(i * block, block)
+        leaving += start_copies(
+            sems.at[i, pl.ds(n_in, 2)],
+            (output.at[here], output_h.at[pl.ds(first + i * block, block)]),
+            (grad_pre.at[here], grad_h.at[here]),
         )
-
-    return pl.pallas_call(
-        run,
-        out_shape=tuple(pltpu.HBM(shape, t) for shape, t in outs),
-        in_specs=[SMEM] + [ANY] * n_in + [VMEM] * n_whole,
-        out_specs=(HBM,) * n_out,
-        scratch_shapes=[pltpu.VMEM(x.shape, x.dtype) for x in streamed]
-        + [pltpu.VMEM(shape, t) for shape, t in outs]
-        + [pltpu.SemaphoreType.DMA((rows // block, n_in + n_out))],
-        compiler_params=params(),
-        cost_estimate=cost(flops, 1 << 22),
-        name=name,
-    )(me, *streamed, *[hbm(x) for x in whole])
-
-
-def self_step(me, ins, held, outs):
-    w, bias = held
-    outs[0][...] = by_shards(me, ins, w) + bias[...]
-
-
-def forward_step(me, ins, held, outs):
-    *shards, own_part, grad_out = ins
-    output, grad_pre = outs
-    pre_act = own_part[...] + by_shards(me, shards, held[0])
-    gate = jax.nn.sigmoid(pre_act)
-    output[...] = (pre_act * gate).astype(BF16)
-    grad = grad_out[...].astype(F32) * gate * (1.0 + pre_act * (1.0 - gate))
-    grad_pre[...] = grad.astype(BF16)
+    wait_copies(leaving)
+
+
+def forward(me, chunk, feats, aggs, w_self, w_neigh, bias, grad_out, output, block=256):
+    n_feat = len(feats)
+    rows, width = aggs[0].shape
+    streamed = [*feats, *aggs, hbm(grad_out)]
+    n_in = len(streamed)
+    previous = [] if output is None else [output]
+    return pl.pallas_call(
+        functools.partial(forward_kernel, n_feat=n_feat, chunk=chunk, block=block),
+        out_shape=(pltpu.HBM(grad_out.shape, BF16), pltpu.HBM((rows, width), BF16)),
+        in_specs=[SMEM] + [ANY] * n_in + [VMEM] * 3 + [HBM] * len(previous),
+        out_specs=(HBM, HBM),
+        scratch_shapes=[pltpu.VMEM((rows, width), BF16)] * (n_in + 2)
+        + [pltpu.SemaphoreType.DMA((rows // block, n_in + 2))],
+        input_output_aliases={n_in + 4: 0} if previous else {},
+        compiler_params=params(),
+        cost_estimate=cost(4 * rows * width * n_feat * width, 1 << 22),
+        name="forward_dense",
+    )(me, *streamed, hbm(w_self), hbm(w_neigh), hbm(bias), *[hbm(p) for p in previous])
 
 
 def weights_kernel(*refs, n_feat):
-    shards, grad, out_h, out, sems = refs[: 2 * n_feat], *refs[2 * n_feat :]
+    n_agg = n_feat * CHUNKS
+    feats_h, refs = refs[:n_feat], refs[n_feat:]
+    aggs_h, refs = refs[:n_agg], refs[n_agg:]
+    grads_h, out_h, refs = refs[:CHUNKS], refs[CHUNKS], refs[CHUNKS + 1 :]
+    shards, refs = refs[: 2 * n_feat], refs[2 * n_feat :]
+    grad, out, sems, shard_sems = refs
     n_dom, chunk = out.shape[0], out.shape[1] - 8
-    width = grad.shape[1]
+    rows, width = grad.shape
+    piece = rows // CHUNKS
+    part = lambda c: pl.ds(c * piece, piece)
+    first = start_copies(sems, *[(g, grad.at[part(c)]) for c, g in enumerate(grads_h)])
+    pending = []
+    for k in range(n_feat):
+        pending.append(start_copies(shard_sems.at[k], (feats_h[k], shards[k])))
+    for k in range(n_feat):
+        pairs = [(aggs_h[c * n_feat + k], shards[n_feat + k].at[part(c)]) for c in range(CHUNKS)]
+        pending.append(start_copies(shard_sems.at[n_feat + k], *pairs))
+    wait_copies(first)
     flipped = grad[...].T
     bias = jnp.sum(grad[...].astype(F32), axis=0, keepdims=True)
-    for i, shard in enumerate(shards):
-        block = jnp.dot(flipped, shard[...], preferred_element_type=F32).T
-        for row in range(0, width, min(chunk, width)):
-            q, start = divmod(i * width + row, chunk)
-            n = min(chunk, width)
-            out[q, start : start + n, :] = block[row : row + n, :]
     for q in range(n_dom):
         out[q, chunk:, :] = jnp.broadcast_to(bias, (8, width))
+    n = min(chunk, width)
+    for i in range(0, 2 * n_feat, 2):
+        wait_copies(pending[i])
+        wait_copies(pending[i + 1])
+        pair = jnp.concatenate([shards[i][...], shards[i + 1][...]], axis=1)
+        blocks = jnp.dot(flipped, pair, preferred_element_type=F32).T
+        for row in range(0, 2 * width, n):
+            q, start = divmod(i * width + row, chunk)
+            out[q, start : start + n, :] = blocks[row : row + n, :]
     wait_copies(start_copies(sems, (out, out_h)))
 
 
-def weight_parts(shards, grad, n_dom):
-    n_feat = len(shards) // 2
-    width = grad.shape[1]
+def weight_parts(feats, aggs, grads, n_dom):
+    n_feat = len(feats)
+    rows, width = feats[0].shape
     chunk = 2 * n_feat * width // n_dom
+    flat = [*feats, *[a for chunk_aggs in aggs for a in chunk_aggs], *grads]
     return pl.pallas_call(
         functools.partial(weights_kernel, n_feat=n_feat),
         out_shape=pltpu.HBM((n_dom, chunk + 8, width), F32),
-        in_specs=[VMEM] * (2 * n_feat + 1),
+        in_specs=[ANY] * len(flat),
         out_specs=HBM,
-        scratch_shapes=[
+        scratch_shapes=[pltpu.VMEM((rows, width), BF16)] * (2 * n_feat + 1)
+        + [
             pltpu.VMEM((n_dom, chunk + 8, width), F32),
-            pltpu.SemaphoreType.DMA((1,)),
+            pltpu.SemaphoreType.DMA((CHUNKS,)),
+            pltpu.SemaphoreType.DMA((2 * n_feat, CHUNKS)),
         ],
         compiler_params=params(),
-        cost_estimate=cost(4 * n_feat * width * width * grad.shape[0], 1 << 22),
+        cost_estimate=cost(4 * n_feat * width * width * rows, 1 << 22),
         name="weight_parts",
-    )(*shards, grad)
+    )(*flat)
 
 
 def split_copies(sems, pairs, block):
@@ -346,22 +364,32 @@
 
 
 def back_far_kernel(*refs, n_feat):
-    lists, tiles = refs[:2]
-    grads_h, w = refs[2 : 2 + n_feat], refs[2 + n_feat : 2 + 2 * n_feat]
-    out_h, back_h, direct_h = refs[2 + 2 * n_feat : 5 + 2 * n_feat]
-    grads = refs[5 + 2 * n_feat : 5 + 3 * n_feat]
-    back, direct, acc, out, sems, out_sems = refs[5 + 3 * n_feat :]
+    n_grads = n_feat * CHUNKS
+    lists, tiles, *refs = refs
+    grads_h, w, refs = refs[:n_grads], refs[n_grads : n_grads + n_feat], refs[n_grads + n_feat :]
+    out_h, back_h, direct_h, *refs = refs
+    grads, refs = refs[:n_grads], refs[n_grads:]
+    back, direct, acc, out, sems, out_sems = refs
     n_dom = out.shape[0]
     own_blocks, tile, width = back.shape
     hub_dev = out.shape[1] - tile
     hub_blocks = n_dom * hub_dev // tile
     block = 4 * tile
-    pending = split_copies(sems, list(zip(grads_h, grads)), block)
+    pending = []
+    for c in range(CHUNKS):
+        here = slice(c * n_feat, (c + 1) * n_feat)
+        pairs = list(zip(grads_h[here], grads[here]))
+        per_chunk = pairs[0][0].shape[0] // block
+        pending += split_copies(sems.at[pl.ds(c * per_chunk, per_chunk)], pairs, block)
     acc[...] = jnp.zeros_like(acc)
-    rows = jnp.concatenate([r[...].reshape(2 * width, -1) for r in w], axis=1)
+    own_w, near_w, far_w, both_w = w
+    rows = [r.reshape(2 * width, -1) for r in (own_w[...], near_w[...], far_w[0], both_w[1])]
+    rows = jnp.concatenate(rows, axis=1)
     for i, copies in enumerate(pending):
         wait_copies(copies)
-        whole = jnp.concatenate([g[i * block : (i + 1) * block, :] for g in grads], axis=1)
+        c, at = divmod(i, per_chunk)
+        at = slice(at * block, (at + 1) * block)
+        whole = jnp.concatenate([g[at, :] for g in grads[c * n_feat : (c + 1) * n_feat]], axis=1)
         both = lax.dot_general(whole, rows, (((1,), (1,)), ((), ())), preferred_element_type=F32)
         direct[4 * i : 4 * (i + 1)] = both[:, :width].reshape(4, tile, width)
         back[4 * i : 4 * (i + 1)] = both[:, width:].astype(BF16).reshape(4, tile, width)
@@ -376,17 +404,18 @@
 
 
 def back_far(lists, tiles, grads, w, n_dom, hub_dev, tile):
-    n_feat = len(grads)
-    rows, width = grads[0].shape
+    n_feat = len(w)
+    piece, width = grads[0].shape
+    rows = piece * CHUNKS
     far_blocks = n_dom * hub_dev // tile + n_dom
     shape = (n_dom, tile + hub_dev, width)
     back_shape = (rows // tile, tile, width)
     return pl.pallas_call(
         functools.partial(back_far_kernel, n_feat=n_feat),
         out_shape=(pltpu.HBM(shape, BF16), pltpu.HBM(back_shape, BF16), pltpu.HBM(back_shape, F32)),
-        in_specs=[SMEM, VMEM] + [ANY] * n_feat + [VMEM] * n_feat,
+        in_specs=[SMEM, VMEM] + [ANY] * len(grads) + [VMEM] * n_feat,
         out_specs=(HBM, HBM, HBM),
-        scratch_shapes=[pltpu.VMEM((rows, width), BF16)] * n_feat
+        scratch_shapes=[pltpu.VMEM((piece, width), BF16)] * len(grads)
         + [
             pltpu.VMEM(back_shape, BF16),
             pltpu.VMEM(back_shape, F32),
@@ -396,7 +425,7 @@
             pltpu.SemaphoreType.DMA((3,)),
         ],
         compiler_params=params(),
-        cost_estimate=cost(4 * rows * width * width * n_feat, 1 << 22),
+        cost_estimate=cost(45 * rows * width * width * n_feat, 1 << 12),
         name="back_far",
     )(lists, tiles, *grads, *w)
 
@@ -494,19 +523,21 @@
 
 def cut_kernel(me_s, w_self, w_neigh, *outs):
     width = w_self.shape[1]
-    for k, out in enumerate(outs):
+    own, near, far = outs
+    for k, out in enumerate((own, near, far.at[0], far.at[1])):
         at = pl.ds(pl.multiple_of((me_s[0] ^ k) * width, width), width)
         out[0] = w_self[at, :]
         out[1] = w_neigh[at, :]
 
 
-def cut_weights(me, w_self, w_neigh, n_feat):
+def cut_weights(me, w_self, w_neigh):
     width = w_self.shape[1]
+    one = (2, width, width)
     return pl.pallas_call(
         cut_kernel,
-        out_shape=(pltpu.HBM((2, width, width), BF16),) * n_feat,
+        out_shape=tuple(pltpu.HBM(shape, BF16) for shape in (one, one, (2,) + one)),
         in_specs=[SMEM, VMEM, VMEM],
-        out_specs=(VMEM,) * n_feat,
+        out_specs=(VMEM,) * 3,
         compiler_params=params(),
         cost_estimate=cost(0, 1 << 20),
         name="cut_weights",
@@ -594,43 +625,39 @@
     incoming = lax.all_to_all(outgoing, "dom", 0, 0, tiled=True)
     own_feats = node_feats.reshape(-1, tile_size, width)
     base, lists = own_tiles(tile_dst, tile_src, edge_tiles, own_feats, far_blocks)
-    aggregated = far_tiles(lists, edge_tiles, incoming, base, far_blocks).reshape(own_count, width)
-
-    agg_far = swap(aggregated, far)
-    feat_far, aggregated = lax.optimization_barrier((feat_far, aggregated))
+    pieces = far_tiles(lists, edge_tiles, incoming, base, far_blocks)
+    pieces = [p.reshape(-1, width) for p in pieces]
+    feat_far, *pieces = lax.optimization_barrier((feat_far, *pieces))
     feats = [hbm(node_feats), swap(node_feats, near), feat_far, swap(feat_far, near)]
-    flops = 2 * own_count * n_feat * width * width
-    rows_out = ((own_count, width), BF16)
-    (own_part,) = stream_call(
-        self_step,
-        me_s,
-        feats,
-        [w_self, out_bias[None, :]],
-        [((own_count, width), F32)],
-        flops,
-        "self_dense",
-    )
-    cut = cut_weights(me_s, w_self, w_neigh, n_feat)
-    agg_far, own_part, *cut = lax.optimization_barrier((agg_far, own_part, *cut))
-    w_rows = [hbm(cut[0])] + [swap(cut[k], k) for k in range(1, n_feat)]
-    aggs = [hbm(aggregated), swap(aggregated, near), agg_far, swap(agg_far, near)]
-    output, grad_pre = stream_call(
-        forward_step,
-        me_s,
-        [*aggs, hbm(own_part), hbm(grad_out)],
-        [w_neigh],
-        [rows_out, rows_out],
-        flops,
-        "forward_dense",
-    )
-
-    grad_far = swap(grad_pre, far)
-    parts = weight_parts(feats + aggs, hbm(grad_pre), n_dom)
+
+    agg_far = [swap(p, far) for p in pieces]
+    cut = cut_weights(me_s, w_self, w_neigh)
+    agg_far[0], *cut = lax.optimization_barrier((agg_far[0], *cut))
+    far_w = swap(cut[2], far)
+    w_rows = [hbm(cut[0]), swap(cut[1], near), far_w, swap(far_w, near)]
+    output, aggs, grads, grad_far = None, [], [], []
+    for c in range(CHUNKS):
+        if c:
+            agg_far[c], grads[c - 1] = lax.optimization_barrier((agg_far[c], grads[c - 1]))
+        shards = [hbm(pieces[c]), swap(pieces[c], near), agg_far[c], swap(agg_far[c], near)]
+        output, grad = forward(
+            me_s, c, feats, shards, w_self, w_neigh, out_bias[None, :], grad_out, output
+        )
+        aggs.append(shards)
+        grads.append(grad)
+        grad_far.append(swap(grad, far) if c == 0 else None)
+    grad_far[0], grads[1] = lax.optimization_barrier((grad_far[0], grads[1]))
+    grad_far[1] = swap(grads[1], far)
+    parts = weight_parts(feats, aggs, [hbm(g) for g in grads], n_dom)
     part_sums = lax.all_to_all(parts, "dom", 0, 0, tiled=True)
-    grads = [hbm(grad_pre), swap(grad_pre, near), grad_far, swap(grad_far, near)]
+    whole_grads = []
+    for c in range(CHUNKS):
+        whole_grads += [
+            hbm(grads[c]), swap(grads[c], near), grad_far[c], swap(grad_far[c], near)
+        ]
 
     back_out, back_agg, direct = back_far(
-        lists, edge_tiles, grads, w_rows, n_dom, hub_dev, tile_size
+        lists, edge_tiles, whole_grads, w_rows, n_dom, hub_dev, tile_size
     )
     back_in = lax.all_to_all(back_out, "dom", 0, 0, tiled=True)
     own = back_own(lists, edge_tiles, back_agg, direct).reshape(own_count, width)

time: 106 us -> 108 us (1.019)
  starting transfers between devices: 27.7 us -> 30.7 us
    ppermute x12 -> x18, starting transfers between devices: 6.96 us -> 9.58 us  [swap(): return lax.ppermute(x, 'feat', [(j, j ^ k) for j in range(n_feat)])]
    ppermute x12 -> x18, waiting for transfers between devices: 16.8 us -> 15.4 us  [swap(): return lax.ppermute(x, 'feat', [(j, j ^ k) for j in range(n_feat)])]
  transfers between devices with their start and end apart: 16 -> 22, of which waited for: 9 -> 11; matrix products, arithmetic and copies ran while one was open for 0% -> 0% of each run, Pallas kernels for 37% -> 40%
where the time goes in v5:
time: 108 us; the launch traced here: 107 us
  Pallas kernels  48.5 us (45%)
  starting transfers between devices  30.7 us (28%)
  waiting for transfers between devices  25.3 us (23%)
  local copies, waits for them, and re-layouts  1.99 us (2%)
    ppermute x18, waiting for transfers between devices, swap(): return lax.ppermute(x, 'feat', [(j, j ^ k) for j in range(n_feat)])  15.4 us
    ppermute x18, starting transfers between devices, swap(): return lax.ppermute(x, 'feat', [(j, j ^ k) for j in range(n_feat)])  9.58 us
    pallas_call x2, Pallas kernels, forward(): pl.pallas_call(functools.partial(forward_kernel, n_feat=n_feat, chunk=chu...  8.62 us
    all_to_all x1, starting transfers between devices, body(): incoming = lax.all_to_all(outgoing, 'dom', 0, 0, tiled=True)  7.26 us
    pallas_call x1, Pallas kernels, back_far(): pl.pallas_call(functools.partial(back_far_kernel, n_feat=n_feat), out_sha...  6.42 us
    pallas_call x1, Pallas kernels, own_tiles(): pl.pallas_call(functools.partial(own_kernel, far_blocks=far_blocks), out_...  6.3 us
    pallas_call x1, Pallas kernels, back_own(): pl.pallas_call(back_own_kernel, out_shape=pltpu.HBM(direct.shape, F32), i...  5.43 us
    all_to_all x1, starting transfers between devices, body(): part_sums = lax.all_to_all(parts, 'dom', 0, 0, tiled=True)  5.22 us
  transfers between devices with their start and end apart: 22, of which 11 were waited for; matrix products, arithmetic and copies ran while one was open for 0% of the time, Pallas kernels for 40%

profile of v5, /device:TPU:0, one launch (start us, length us, event | category | flops | bytes accessed | tf_op | source)
XLA Modules:
  0.0 107.3 jit_solution(11238673150928183293)
XLA Ops:
  0.6 4.4 %pick_rows.1 = bf16[8,160,128]{2,1,0:T(8,128)(2,1)} custom-call(s32[8,128]{1,0:T(8,128)} %bitcast.19, s32[1,8]{1,0:T(1,128)} %count_h.3, s32[32]{0:T(128)} %hub_h.3, bf16[2048,128]{1,0:T(8,128)(2,1)} %refs_0_.5), custom_call_target="tpu_custom_call" | custom-call | bytes 2097152 | tf_op jit(solution)/shard_map/pick_rows/pallas_call | solution.py:80
  5.1 7.3 %all-to-all-start = ((bf16[8,160,128]{2,1,0:T(8,128)(2,1)}), bf16[8,160,128]{2,1,0:T(8,128)(2,1)}, u32[]{:S(2)}, u32[]{:S(2)}) async-start(bf16[8,160,128]{2,1,0:T(8,128)(2,1)} %pick_rows.1), calls=%async_computation | async-start | bytes 655360 | tf_op jit(solution)/shard_map/all_to_all | solution.py:625
  12.3 1.5 %collective-permute-start.1 = (bf16[2048,128]{1,0:T(8,128)(2,1)}, bf16[2048,128]{1,0:T(8,128)(2,1)}, u32[]{:S(2)}, u32[]{:S(2)}) collective-permute-start(bf16[2048,128]{1,0:T(8,128)(2,1)} %refs_0_.5), channel_id=1, source_target_pairs={{0,2},{1,3},{2,0},{3,1},{4,6},{5,7},{6,4},{7,5},{8,10},{9,11},{10,... | collective-permute-start | bytes 1572872 | tf_op jit(solution)/shard_map/ppermute | solution.py:620
  13.9 2.0 %copy-done = bf16[106,128,128]{2,1,0:T(8,128)(2,1)S(1)} copy-done((bf16[106,128,128]{2,1,0:T(8,128)(2,1)S(1)}, bf16[106,128,128]{2,1,0:T(8,128)(2,1)}, u32[]{:S(2)}) %copy-start) | copy-done | bytes 3473432
  15.9 6.3 %own_tiles.1 = (f32[16,128,128]{2,1,0:T(8,128)}, s32[2,114]{1,0:T(2,128)S(1)}) custom-call(s32[106]{0:T(128)} %dst_h.1, s32[106]{0:T(128)} %src_h.1, bf16[106,128,128]{2,1,0:T(8,128)(2,1)S(1)} %copy-done, bf16[16,128,128]{2,1,0:T(8,128)(2,1)} %bitcast.1.x_h), custom_call_target="tpu_custom_call" | custom-call | flops 444596224 | bytes 8388608 | tf_op jit(solution)/shard_map/own_tiles/pallas_call | solution.py:174
  22.2 0.6 all-to-all-done.incoming_h
  22.8 4.0 %far_tiles.1 = (bf16[8,128,128]{2,1,0:T(8,128)(2,1)}, bf16[8,128,128]{2,1,0:T(8,128)(2,1)}) custom-call(s32[2,114]{1,0:T(2,128)S(1)} %get-tuple-element.37.lists.refs_0_, bf16[106,128,128]{2,1,0:T(8,128)(2,1)S(1)} %copy-done.1, bf16[8,160,128]{2,1,0:T(8,128)(2,1)} %all-to-all-done.incoming_h, f32[16,128,128]{2,1,0:T(8,128)} %get-tuple-element.38.base_h), custom_call_target="tpu_custom_call" | custom-call | flops 222298112 | bytes 4194304 | tf_op jit(solution)/shard_map/far_tiles/pallas_call | solution.py:219
  26.8 1.6 %collective-permute-start.6 = (bf16[1024,128]{1,0:T(8,128)(2,1)}, bf16[1024,128]{1,0:T(8,128)(2,1)}, u32[]{:S(2)}, u32[]{:S(2)}) collective-permute-start(bf16[1024,128]{1,0:T(8,128)(2,1)} %bitcast.11), channel_id=1, source_target_pairs={{0,2},{1,3},{2,0},{3,1},{4,6},{5,7},{6,4},{7,5},{8,10},{9,11},{10,... | collective-permute-start | bytes 786440 | tf_op jit(solution)/shard_map/ppermute | solution.py:620
  28.9 1.7 %cut_weights.1 = (bf16[2,128,128]{2,1,0:T(8,128)(2,1)}, bf16[2,128,128]{2,1,0:T(8,128)(2,1)}, bf16[2,2,128,128]{3,2,1,0:T(8,128)(2,1)}) custom-call(s32[1]{0:T(128)} %bitcast.me_s, bf16[512,128]{1,0:T(8,128)(2,1)} %refs_9_.3, bf16[512,128]{1,0:T(8,128)(2,1)} %refs_10_.3), custom_call_target="tpu_custom_call" | custom-call | bytes 1048576 | tf_op jit(solution)/shard_map/cut_weights/pallas_call | solution.py:536
  30.6 3.5 %collective-permute-done.6.refs_6_ = bf16[1024,128]{1,0:T(8,128)(2,1)} collective-permute-done((bf16[1024,128]{1,0:T(8,128)(2,1)}, bf16[1024,128]{1,0:T(8,128)(2,1)}, u32[]{:S(2)}, u32[]{:S(2)}) %collective-permute-start.6) | collective-permute-done | bytes 262176 | tf_op jit(solution)/shard_map/ppermute | solution.py:620
  34.0 1.0 collective-permute-start.4
  35.8 4.3 %forward_dense.2 = (bf16[2048,128]{1,0:T(8,128)(2,1)}, bf16[1024,128]{1,0:T(8,128)(2,1)}) custom-call(s32[1]{0:T(128)} %bitcast.me_s, bf16[2048,128]{1,0:T(8,128)(2,1)} %refs_0_.5, bf16[2048,128]{1,0:T(8,128)(2,1)} %collective-permute-done.refs_1_, bf16[2048,128]{1,0:T(8,128)(2,1)} %collective-permute-done.1.refs_2_, ...), custom_call_target="tpu_custom_call" | custom-call | flops 268435456 | bytes 4194304 | tf_op jit(solution)/shard_map/forward_dense/pallas_call | solution.py:285
  40.1 2.9 %collective-permute-done.4.refs_6_.refs_10_ = bf16[1024,128]{1,0:T(8,128)(2,1)S(1)} collective-permute-done((bf16[1024,128]{1,0:T(8,128)(2,1)}, bf16[1024,128]{1,0:T(8,128)(2,1)S(1)}, u32[]{:S(2)}, u32[]{:S(2)}) %collective-permute-start.4) | collective-permute-done | bytes 262176 | tf_op jit(solution)/shard_map/ppermute | solution.py:620
  43.0 1.0 collective-permute-start.9
  44.5 4.3 %forward_dense.3 = (bf16[2048,128]{1,0:T(8,128)(2,1)}, bf16[1024,128]{1,0:T(8,128)(2,1)}) custom-call(s32[1]{0:T(128)} %bitcast.me_s, bf16[2048,128]{1,0:T(8,128)(2,1)} %refs_0_.5, bf16[2048,128]{1,0:T(8,128)(2,1)} %collective-permute-done.refs_1_, bf16[2048,128]{1,0:T(8,128)(2,1)} %collective-permute-done.1.refs_2_, ...), custom_call_target="tpu_custom_call", output_to_operand_aliasing={{0}: (13, {})} | custom-call | flops 268435456 | bytes 4194304 | tf_op jit(solution)/shard_map/forward_dense/pallas_call | solution.py:285
  48.9 3.2 %collective-permute-done.9.refs_4_ = bf16[1024,128]{1,0:T(8,128)(2,1)} collective-permute-done((bf16[1024,128]{1,0:T(8,128)(2,1)}, bf16[1024,128]{1,0:T(8,128)(2,1)}, u32[]{:S(2)}, u32[]{:S(2)}) %collective-permute-start.9) | collective-permute-done | bytes 262176 | tf_op jit(solution)/shard_map/ppermute | solution.py:620
  52.0 1.0 collective-permute-start.13
  53.0 4.9 %weight_parts.1 = f32[8,136,128]{2,1,0:T(8,128)} custom-call(bf16[2048,128]{1,0:T(8,128)(2,1)} %refs_0_.5, bf16[2048,128]{1,0:T(8,128)(2,1)} %collective-permute-done.refs_1_, bf16[2048,128]{1,0:T(8,128)(2,1)} %collective-permute-done.1.refs_2_, bf16[2048,128]{1,0:T(8,128)(2,1)} %collective-permute-done.2.refs_3_, bf16[1024,128]{1,0:T(8,128)(2,1)} %bitcast.14, ...), custom_call_target="tpu_custom_call" | custom-call | flops 536870912 | bytes 4194304 | tf_op jit(solution)/shard_map/weight_parts/pallas_call | solution.py:339
  58.0 5.2 %all-to-all-start.1 = ((f32[8,136,128]{2,1,0:T(8,128)}), f32[8,136,128]{2,1,0:T(8,128)}, u32[]{:S(2)}, u32[]{:S(2)}) async-start(f32[8,136,128]{2,1,0:T(8,128)} %weight_parts.1), calls=%async_computation.1 | async-start | bytes 1114112 | tf_op jit(solution)/shard_map/all_to_all | solution.py:652
  63.3 1.6 %collective-permute-start.16 = (bf16[2,2,128,128]{3,2,1,0:T(8,128)(2,1)}, bf16[2,2,128,128]{3,2,1,0:T(8,128)(2,1)S(1)}, u32[]{:S(2)}, u32[]{:S(2)}) collective-permute-start(bf16[2,2,128,128]{3,2,1,0:T(8,128)(2,1)} %get-tuple-element.59), channel_id=1, source_target_pairs={{0,2},{1,3},{2,0},{3,1},{4,6},{5,7},{6,4},{7,5},{8,10},{9,11},{10,... | collective-permute-start | bytes 393224 | tf_op jit(solution)/shard_map/ppermute | solution.py:620
  65.9 3.5 %collective-permute-done.16.refs_12_ = bf16[2,2,128,128]{3,2,1,0:T(8,128)(2,1)S(1)} collective-permute-done((bf16[2,2,128,128]{3,2,1,0:T(8,128)(2,1)}, bf16[2,2,128,128]{3,2,1,0:T(8,128)(2,1)S(1)}, u32[]{:S(2)}, u32[]{:S(2)}) %collective-permute-start.16) | collective-permute-done | bytes 131104 | tf_op jit(solution)/shard_map/ppermute | solution.py:620
  69.4 1.3 %collective-permute-done.17.refs_13_ = bf16[2,2,128,128]{3,2,1,0:T(8,128)(2,1)S(1)} collective-permute-done((bf16[2,2,128,128]{3,2,1,0:T(8,128)(2,1)S(1)}, bf16[2,2,128,128]{3,2,1,0:T(8,128)(2,1)S(1)}, u32[]{:S(2)}, u32[]{:S(2)}) %collective-permute-start.17) | collective-permute-done | bytes 131104 | tf_op jit(solution)/shard_map/ppermute | solution.py:620
  70.8 6.4 %back_far.1 = (bf16[8,160,128]{2,1,0:T(8,128)(2,1)}, bf16[16,128,128]{2,1,0:T(8,128)(2,1)}, f32[16,128,128]{2,1,0:T(8,128)}) custom-call(s32[2,114]{1,0:T(2,128)S(1)} %get-tuple-element.37.lists.refs_0_, bf16[106,128,128]{2,1,0:T(8,128)(2,1)S(1)} %copy-done.1, bf16[1024,128]{1,0:T(8,128)(2,1)} %get-tuple-element.52.refs_12_.refs_2_, ...), custom_call_target="tpu_custom_call" | custom-call | flops 6039797760 | bytes 4096 | tf_op jit(solution)/shard_map/back_far/pallas_call | solution.py:413
  77.2 0.9 all-to-all-done.1.parts
  78.1 5.0 %all-to-all-start.2 = ((bf16[8,160,128]{2,1,0:T(8,128)(2,1)}), bf16[8,160,128]{2,1,0:T(8,128)(2,1)}, u32[]{:S(2)}, u32[]{:S(2)}) async-start(bf16[8,160,128]{2,1,0:T(8,128)(2,1)} %get-tuple-element.60), calls=%async_computation.2 | async-start | bytes 655360 | tf_op jit(solution)/shard_map/all_to_all | solution.py:662
  83.1 5.4 %back_own.1 = f32[16,128,128]{2,1,0:T(8,128)} custom-call(s32[2,114]{1,0:T(2,128)S(1)} %get-tuple-element.37.lists.refs_0_, bf16[106,128,128]{2,1,0:T(8,128)(2,1)S(1)} %copy-done.1, bf16[16,128,128]{2,1,0:T(8,128)(2,1)} %get-tuple-element.61.back_h, f32[16,128,128]{2,1,0:T(8,128)} %get-tuple-element.62.direct_h), custom_call_target="tpu_custom_call" | custom-call | flops 444596224 | bytes 8388608 | tf_op jit(solution)/shard_map/back_own/pallas_call | solution.py:442
  88.6 1.8 %sum_parts.1 = (bf16[8,128,128]{2,1,0:T(8,128)(2,1)}, f32[1,128]{1,0:T(1,128)}) custom-call(f32[8,136,128]{2,1,0:T(8,128)} %all-to-all-done.1.parts), custom_call_target="tpu_custom_call" | custom-call | bytes 1048576 | tf_op jit(solution)/shard_map/sum_parts/pallas_call | solution.py:560
  90.4 3.5 %all-to-all-done.2.incoming_h = bf16[8,160,128]{2,1,0:T(8,128)(2,1)} async-done(((bf16[8,160,128]{2,1,0:T(8,128)(2,1)}), bf16[8,160,128]{2,1,0:T(8,128)(2,1)}, u32[]{:S(2)}, u32[]{:S(2)}) %all-to-all-start.2) | async-done | bytes 327712 | tf_op jit(solution)/shard_map/all_to_all | solution.py:662
  93.8 3.6 %all-to-all-start.3 = ((bf16[8,128,128]{2,1,0:T(8,128)(2,1)}), bf16[8,128,128]{2,1,0:T(8,128)(2,1)S(1)}, u32[]{:S(2)}, u32[]{:S(2)}) async-start(bf16[8,128,128]{2,1,0:T(8,128)(2,1)} %get-tuple-element.65), calls=%async_computation.3 | async-start | bytes 524288 | tf_op jit(solution)/shard_map/all_to_all | solution.py:666
  97.5 4.1 %finish.1 = f32[2048,128]{1,0:T(8,128)} custom-call(s32[8,128]{1,0:T(8,128)} %bitcast.20, s32[1,8]{1,0:T(1,128)} %count_h.3, s32[32]{0:T(128)} %hub_h.3, bf16[8,160,128]{2,1,0:T(8,128)(2,1)} %all-to-all-done.2.incoming_h, f32[2048,128]{1,0:T(8,128)} %bitcast.10), custom_call_target="tpu_custom_call" | custom-call | flops 536870912 | bytes 4194304 | tf_op jit(solution)/shard_map/finish/pallas_call | solution.py:504
  101.5 4.9 %all-to-all-done.3 = bf16[8,128,128]{2,1,0:T(8,128)(2,1)S(1)} async-done(((bf16[8,128,128]{2,1,0:T(8,128)(2,1)}), bf16[8,128,128]{2,1,0:T(8,128)(2,1)S(1)}, u32[]{:S(2)}, u32[]{:S(2)}) %all-to-all-start.3) | async-done | bytes 262176 | tf_op jit(solution)/shard_map/all_to_all | solution.py:666
  106.4 0.8 place_weights.1
  (30 shorter events, 2.9 us)
Async XLA Ops:
  5.1 17.7 %all-to-all-start = ((bf16[8,160,128]{2,1,0:T(8,128)(2,1)}), bf16[8,160,128]{2,1,0:T(8,128)(2,1)}, u32[]{:S(2)}, u32[]{:S(2)}) async-start(bf16[8,160,128]{2,1,0:T(8,128)(2,1)} %pick_rows.1), calls=%async_computation | async-start | bytes 655360 | tf_op jit(solution)/shard_map/all_to_all | solution.py:625
  12.3 14.4 %collective-permute-start.1 = (bf16[2048,128]{1,0:T(8,128)(2,1)}, bf16[2048,128]{1,0:T(8,128)(2,1)}, u32[]{:S(2)}, u32[]{:S(2)}) collective-permute-start(bf16[2048,128]{1,0:T(8,128)(2,1)} %refs_0_.5), channel_id=1, source_target_pairs={{0,2},{1,3},{2,0},{3,1},{4,6},{5,7},{6,4},{7,5},{8,10},{9,11},{10,... | collective-permute-start | bytes 1572872 | tf_op jit(solution)/shard_map/ppermute | solution.py:620
  13.9 2.0 %copy-start = (bf16[106,128,128]{2,1,0:T(8,128)(2,1)S(1)}, bf16[106,128,128]{2,1,0:T(8,128)(2,1)}, u32[]{:S(2)}) copy-start(bf16[106,128,128]{2,1,0:T(8,128)(2,1)} %tiles.5) | copy-start | bytes 10420228
  15.8 6.9 %copy-start.1 = (bf16[106,128,128]{2,1,0:T(8,128)(2,1)S(1)}, bf16[106,128,128]{2,1,0:T(8,128)(2,1)}, u32[]{:S(2)}) copy-start(bf16[106,128,128]{2,1,0:T(8,128)(2,1)} %tiles.5) | copy-start | bytes 10420228
  26.8 7.3 %collective-permute-start.6 = (bf16[1024,128]{1,0:T(8,128)(2,1)}, bf16[1024,128]{1,0:T(8,128)(2,1)}, u32[]{:S(2)}, u32[]{:S(2)}) collective-permute-start(bf16[1024,128]{1,0:T(8,128)(2,1)} %bitcast.11), channel_id=1, source_target_pairs={{0,2},{1,3},{2,0},{3,1},{4,6},{5,7},{6,4},{7,5},{8,10},{9,11},{10,... | collective-permute-start | bytes 786440 | tf_op jit(solution)/shard_map/ppermute | solution.py:620
  28.4 6.7 %collective-permute-start = (bf16[2048,128]{1,0:T(8,128)(2,1)}, bf16[2048,128]{1,0:T(8,128)(2,1)}, u32[]{:S(2)}, u32[]{:S(2)}) collective-permute-start(bf16[2048,128]{1,0:T(8,128)(2,1)} %refs_0_.5), channel_id=1, source_target_pairs={{0,1},{1,0},{2,3},{3,2},{4,5},{5,4},{6,7},{7,6},{8,9},{9,8},{10,11... | collective-permute-start | bytes 1572872 | tf_op jit(solution)/shard_map/ppermute | solution.py:620
  28.4 6.9 %collective-permute-start.2 = (bf16[2048,128]{1,0:T(8,128)(2,1)}, bf16[2048,128]{1,0:T(8,128)(2,1)}, u32[]{:S(2)}, u32[]{:S(2)}) collective-permute-start(bf16[2048,128]{1,0:T(8,128)(2,1)} %collective-permute-done.1.refs_2_), channel_id=1, source_target_pairs={{0,1},{1,0},{2,3},{3,2},{4,5},{5,4},{6,7},{7,6},{8,9},{9,8},{10,11... | collective-permute-start | bytes 1572872 | tf_op jit(solution)/shard_map/ppermute | solution.py:620
  30.6 4.7 %collective-permute-start.5 = (bf16[1024,128]{1,0:T(8,128)(2,1)}, bf16[1024,128]{1,0:T(8,128)(2,1)S(1)}, u32[]{:S(2)}, u32[]{:S(2)}) collective-permute-start(bf16[1024,128]{1,0:T(8,128)(2,1)} %bitcast.12), channel_id=1, source_target_pairs={{0,1},{1,0},{2,3},{3,2},{4,5},{5,4},{6,7},{7,6},{8,9},{9,8},{10,11... | collective-permute-start | bytes 786440 | tf_op jit(solution)/shard_map/ppermute | solution.py:620
  34.0 1.7 %collective-permute-start.7 = (bf16[1024,128]{1,0:T(8,128)(2,1)}, bf16[1024,128]{1,0:T(8,128)(2,1)S(1)}, u32[]{:S(2)}, u32[]{:S(2)}) collective-permute-start(bf16[1024,128]{1,0:T(8,128)(2,1)} %collective-permute-done.6.refs_6_), channel_id=1, source_target_pairs={{0,1},{1,0},{2,3},{3,2},{4,5},{5,4},{6,7},{7,6},{8,9},{9,8},{10,11... | collective-permute-start | bytes 786440 | tf_op jit(solution)/shard_map/ppermute | solution.py:620
  34.0 8.9 %collective-permute-start.4 = (bf16[1024,128]{1,0:T(8,128)(2,1)}, bf16[1024,128]{1,0:T(8,128)(2,1)S(1)}, u32[]{:S(2)}, u32[]{:S(2)}) collective-permute-start(bf16[1024,128]{1,0:T(8,128)(2,1)} %bitcast.15), channel_id=1, source_target_pairs={{0,2},{1,3},{2,0},{3,1},{4,6},{5,7},{6,4},{7,5},{8,10},{9,11},{10,... | collective-permute-start | bytes 786440 | tf_op jit(solution)/shard_map/ppermute | solution.py:620
  35.1 8.9 %collective-permute-start.3 = (bf16[1024,128]{1,0:T(8,128)(2,1)}, bf16[1024,128]{1,0:T(8,128)(2,1)S(1)}, u32[]{:S(2)}, u32[]{:S(2)}) collective-permute-start(bf16[1024,128]{1,0:T(8,128)(2,1)} %bitcast.16), channel_id=1, source_target_pairs={{0,1},{1,0},{2,3},{3,2},{4,5},{5,4},{6,7},{7,6},{8,9},{9,8},{10,11... | collective-permute-start | bytes 786440 | tf_op jit(solution)/shard_map/ppermute | solution.py:620
  43.0 1.5 %collective-permute-start.8 = (bf16[1024,128]{1,0:T(8,128)(2,1)S(1)}, bf16[1024,128]{1,0:T(8,128)(2,1)S(1)}, u32[]{:S(2)}, u32[]{:S(2)}) collective-permute-start(bf16[1024,128]{1,0:T(8,128)(2,1)S(1)} %collective-permute-done.4.refs_6_.refs_10_), channel_id=1, source_target_pairs={{0,1},{1,0},{2,3},{3,2},{4,5},{5,4},{6,7},{7,6},{8,9},{9,8},{10,11... | collective-permute-start | bytes 786440 | tf_op jit(solution)/shard_map/ppermute | solution.py:620
  43.0 9.0 %collective-permute-start.9 = (bf16[1024,128]{1,0:T(8,128)(2,1)}, bf16[1024,128]{1,0:T(8,128)(2,1)}, u32[]{:S(2)}, u32[]{:S(2)}) collective-permute-start(bf16[1024,128]{1,0:T(8,128)(2,1)} %get-tuple-element.52.refs_12_.refs_2_), channel_id=1, source_target_pairs={{0,2},{1,3},{2,0},{3,1},{4,6},{5,7},{6,4},{7,5},{8,10},{9,11},{10,... | collective-permute-start | bytes 786440 | tf_op jit(solution)/shard_map/ppermute | solution.py:620
  48.8 14.3 %copy-start.2 = (bf16[2,128,128]{2,1,0:T(8,128)(2,1)S(1)}, bf16[2,128,128]{2,1,0:T(8,128)(2,1)}, u32[]{:S(2)}) copy-start(bf16[2,128,128]{2,1,0:T(8,128)(2,1)} %get-tuple-element.58) | copy-start | bytes 196612
  52.0 13.5 %collective-permute-start.13 = (bf16[1024,128]{1,0:T(8,128)(2,1)}, bf16[1024,128]{1,0:T(8,128)(2,1)}, u32[]{:S(2)}, u32[]{:S(2)}) collective-permute-start(bf16[1024,128]{1,0:T(8,128)(2,1)} %get-tuple-element.54.refs_13_.refs_6_), channel_id=1, source_target_pairs={{0,2},{1,3},{2,0},{3,1},{4,6},{5,7},{6,4},{7,5},{8,10},{9,11},{10,... | collective-permute-start | bytes 786440 | tf_op jit(solution)/shard_map/ppermute | solution.py:620
  58.0 20.2 %all-to-all-start.1 = ((f32[8,136,128]{2,1,0:T(8,128)}), f32[8,136,128]{2,1,0:T(8,128)}, u32[]{:S(2)}, u32[]{:S(2)}) async-start(f32[8,136,128]{2,1,0:T(8,128)} %weight_parts.1), calls=%async_computation.1 | async-start | bytes 1114112 | tf_op jit(solution)/shard_map/all_to_all | solution.py:652
  63.2 2.2 %collective-permute-start.15 = (bf16[2,128,128]{2,1,0:T(8,128)(2,1)S(1)}, bf16[2,128,128]{2,1,0:T(8,128)(2,1)S(1)}, u32[]{:S(2)}, u32[]{:S(2)}) collective-permute-start(bf16[2,128,128]{2,1,0:T(8,128)(2,1)S(1)} %copy-done.2), channel_id=1, source_target_pairs={{0,1},{1,0},{2,3},{3,2},{4,5},{5,4},{6,7},{7,6},{8,9},{9,8},{10,11... | collective-permute-start | bytes 196616 | tf_op jit(solution)/shard_map/ppermute | solution.py:620
  63.3 6.1 %collective-permute-start.16 = (bf16[2,2,128,128]{3,2,1,0:T(8,128)(2,1)}, bf16[2,2,128,128]{3,2,1,0:T(8,128)(2,1)S(1)}, u32[]{:S(2)}, u32[]{:S(2)}) collective-permute-start(bf16[2,2,128,128]{3,2,1,0:T(8,128)(2,1)} %get-tuple-element.59), channel_id=1, source_target_pairs={{0,2},{1,3},{2,0},{3,1},{4,6},{5,7},{6,4},{7,5},{8,10},{9,11},{10,... | collective-permute-start | bytes 393224 | tf_op jit(solution)/shard_map/ppermute | solution.py:620
  64.9 5.9 %collective-permute-start.10 = (bf16[1024,128]{1,0:T(8,128)(2,1)}, bf16[1024,128]{1,0:T(8,128)(2,1)S(1)}, u32[]{:S(2)}, u32[]{:S(2)}) collective-permute-start(bf16[1024,128]{1,0:T(8,128)(2,1)} %get-tuple-element.52.refs_12_.refs_2_), channel_id=1, source_target_pairs={{0,1},{1,0},{2,3},{3,2},{4,5},{5,4},{6,7},{7,6},{8,9},{9,8},{10,11... | collective-permute-start | bytes 786440 | tf_op jit(solution)/shard_map/ppermute | solution.py:620
  65.0 5.7 %collective-permute-start.12 = (bf16[1024,128]{1,0:T(8,128)(2,1)}, bf16[1024,128]{1,0:T(8,128)(2,1)S(1)}, u32[]{:S(2)}, u32[]{:S(2)}) collective-permute-start(bf16[1024,128]{1,0:T(8,128)(2,1)} %get-tuple-element.54.refs_13_.refs_6_), channel_id=1, source_target_pairs={{0,1},{1,0},{2,3},{3,2},{4,5},{5,4},{6,7},{7,6},{8,9},{9,8},{10,11... | collective-permute-start | bytes 786440 | tf_op jit(solution)/shard_map/ppermute | solution.py:620
  65.4 5.4 %collective-permute-start.11 = (bf16[1024,128]{1,0:T(8,128)(2,1)}, bf16[1024,128]{1,0:T(8,128)(2,1)S(1)}, u32[]{:S(2)}, u32[]{:S(2)}) collective-permute-start(bf16[1024,128]{1,0:T(8,128)(2,1)} %collective-permute-done.9.refs_4_), channel_id=1, source_target_pairs={{0,1},{1,0},{2,3},{3,2},{4,5},{5,4},{6,7},{7,6},{8,9},{9,8},{10,11... | collective-permute-start | bytes 786440 | tf_op jit(solution)/shard_map/ppermute | solution.py:620
  65.5 5.2 %collective-permute-start.14 = (bf16[1024,128]{1,0:T(8,128)(2,1)}, bf16[1024,128]{1,0:T(8,128)(2,1)S(1)}, u32[]{:S(2)}, u32[]{:S(2)}) collective-permute-start(bf16[1024,128]{1,0:T(8,128)(2,1)} %collective-permute-done.13.refs_8_), channel_id=1, source_target_pairs={{0,1},{1,0},{2,3},{3,2},{4,5},{5,4},{6,7},{7,6},{8,9},{9,8},{10,11... | collective-permute-start | bytes 786440 | tf_op jit(solution)/shard_map/ppermute | solution.py:620
  69.4 1.3 %collective-permute-start.17 = (bf16[2,2,128,128]{3,2,1,0:T(8,128)(2,1)S(1)}, bf16[2,2,128,128]{3,2,1,0:T(8,128)(2,1)S(1)}, u32[]{:S(2)}, u32[]{:S(2)}) collective-permute-start(bf16[2,2,128,128]{3,2,1,0:T(8,128)(2,1)S(1)} %collective-permute-done.16.refs_12_), channel_id=1, source_target_pairs={{0,1},{1,0},{2,3},{3,2},{4,5},{5,4},{6,7},{7,6},{8,9},{9,8},{10,11... | collective-permute-start | bytes 393224 | tf_op jit(solution)/shard_map/ppermute | solution.py:620
  78.1 15.7 %all-to-all-start.2 = ((bf16[8,160,128]{2,1,0:T(8,128)(2,1)}), bf16[8,160,128]{2,1,0:T(8,128)(2,1)}, u32[]{:S(2)}, u32[]{:S(2)}) async-start(bf16[8,160,128]{2,1,0:T(8,128)(2,1)} %get-tuple-element.60), calls=%async_computation.2 | async-start | bytes 655360 | tf_op jit(solution)/shard_map/all_to_all | solution.py:662
  93.8 12.6 %all-to-all-start.3 = ((bf16[8,128,128]{2,1,0:T(8,128)(2,1)}), bf16[8,128,128]{2,1,0:T(8,128)(2,1)S(1)}, u32[]{:S(2)}, u32[]{:S(2)}) async-start(bf16[8,128,128]{2,1,0:T(8,128)(2,1)} %get-tuple-element.65), calls=%async_computation.3 | async-start | bytes 524288 | tf_op jit(solution)/shard_map/all_to_all | solution.py:666

commit v6 on v4

--- a/solution.py
+++ b/solution.py
@@ -358,7 +358,9 @@
     block = 4 * tile
     pending = split_copies(sems, list(zip(grads_h, grads)), block)
     acc[...] = jnp.zeros_like(acc)
-    rows = jnp.concatenate([r[...].reshape(2 * width, -1) for r in w], axis=1)
+    own_w, near_w, far_w, both_w = w
+    rows = [r.reshape(2 * width, -1) for r in (own_w[...], near_w[...], far_w[0], both_w[1])]
+    rows = jnp.concatenate(rows, axis=1)
     for i, copies in enumerate(pending):
         wait_copies(copies)
         whole = jnp.concatenate([g[i * block : (i + 1) * block, :] for g in grads], axis=1)
@@ -398,7 +400,7 @@
         compiler_params=params(),
         cost_estimate=cost(4 * rows * width * width * n_feat, 1 << 22),
         name="back_far",
-    )(lists, tiles, *grads, *w)
+    )(lists, tiles, *grads, *[hbm(r) for r in w])
 
 
 def back_own_kernel(lists, tiles, back_h, direct_h, out_h, back, acc, sems):
@@ -494,19 +496,21 @@
 
 def cut_kernel(me_s, w_self, w_neigh, *outs):
     width = w_self.shape[1]
-    for k, out in enumerate(outs):
+    own, near, far = outs
+    for k, out in enumerate((own, near, far.at[0], far.at[1])):
         at = pl.ds(pl.multiple_of((me_s[0] ^ k) * width, width), width)
         out[0] = w_self[at, :]
         out[1] = w_neigh[at, :]
 
 
-def cut_weights(me, w_self, w_neigh, n_feat):
+def cut_weights(me, w_self, w_neigh):
     width = w_self.shape[1]
+    one = (2, width, width)
     return pl.pallas_call(
         cut_kernel,
-        out_shape=(pltpu.HBM((2, width, width), BF16),) * n_feat,
+        out_shape=tuple(pltpu.HBM(shape, BF16) for shape in (one, one, (2,) + one)),
         in_specs=[SMEM, VMEM, VMEM],
-        out_specs=(VMEM,) * n_feat,
+        out_specs=(VMEM,) * 3,
         compiler_params=params(),
         cost_estimate=cost(0, 1 << 20),
         name="cut_weights",
@@ -514,21 +518,19 @@
 
 
 def sum_kernel(parts, out, bias):
-    n_dom, chunk, _ = out.shape
+    n_dom, chunk = parts.shape[0], out.shape[0]
     total = parts[0]
     for q in range(1, n_dom):
         total += parts[q]
     bias[...] = total[chunk : chunk + 1, :]
-    rows = total[:chunk, :].astype(BF16)
-    for q in range(n_dom):
-        out[q] = rows
+    out[...] = total[:chunk, :].astype(BF16)
 
 
 def sum_parts(parts):
-    n_dom, rows, width = parts.shape
+    _, rows, width = parts.shape
     return pl.pallas_call(
         sum_kernel,
-        out_shape=(pltpu.HBM((n_dom, rows - 8, width), BF16), pltpu.HBM((1, width), F32)),
+        out_shape=(pltpu.HBM((rows - 8, width), BF16), pltpu.HBM((1, width), F32)),
         in_specs=[VMEM],
         out_specs=(VMEM, VMEM),
         compiler_params=params(),
@@ -537,26 +539,40 @@
     )(hbm(parts))
 
 
-def place_kernel(me_s, sums, self_out, neigh_out):
+def place_kernel(me_s, *refs, order):
+    *sums, self_out, neigh_out = refs
     rows, width = self_out.shape
-    for i in range(2 * rows // width):
-        which, k = divmod(i, rows // width)
-        target = (self_out, neigh_out)[which]
-        at = pl.ds(pl.multiple_of((me_s[0] ^ k) * width, width), width)
-        target[at, :] = sums[i * width : (i + 1) * width, :].astype(F32)
-
-
-def place_weights(me, sums):
-    rows, width = sums.shape[0] // 2, sums.shape[1]
-    return pl.pallas_call(
-        place_kernel,
+    chunk = 2 * rows // len(order)
+    n = min(chunk, width)
+    per_ref = sums[0].shape[0] // chunk
+    for i, k in enumerate(order):
+        ref, first = sums[i // per_ref], i % per_ref * chunk
+        for part in range(0, chunk, n):
+            row = (me_s[1] ^ k) * chunk + part
+            feat = me_s[0] ^ (row // width % (rows // width))
+            at = pl.ds(pl.multiple_of(feat * width + row % width, n), n)
+            piece = ref[first + part : first + part + n, :].astype(F32)
+
+            @pl.when(row < rows)
+            def _():
+                self_out[at, :] = piece
+
+            @pl.when(row >= rows)
+            def _():
+                neigh_out[at, :] = piece
+
+
+def place_weights(both, sums, order, rows):
+    width = sums[0].shape[1]
+    return pl.pallas_call(
+        functools.partial(place_kernel, order=order),
         out_shape=(pltpu.HBM((rows, width), F32),) * 2,
-        in_specs=[SMEM, VMEM],
+        in_specs=[SMEM] + [VMEM] * len(sums),
         out_specs=(VMEM, VMEM),
         compiler_params=params(),
         cost_estimate=cost(0, 1 << 20),
         name="place_weights",
-    )(me, sums)
+    )(both, *sums)
 
 
 def body(
@@ -610,9 +626,10 @@
         flops,
         "self_dense",
     )
-    cut = cut_weights(me_s, w_self, w_neigh, n_feat)
+    cut = cut_weights(me_s, w_self, w_neigh)
     agg_far, own_part, *cut = lax.optimization_barrier((agg_far, own_part, *cut))
-    w_rows = [hbm(cut[0])] + [swap(cut[k], k) for k in range(1, n_feat)]
+    far_w = swap(cut[2], far)
+    w_rows = [cut[0], swap(cut[1], near), far_w, swap(far_w, near)]
     aggs = [hbm(aggregated), swap(aggregated, near), agg_far, swap(agg_far, near)]
     output, grad_pre = stream_call(
         forward_step,
@@ -624,6 +641,7 @@
         "forward_dense",
     )
 
+    grad_pre, *w_rows = lax.optimization_barrier((grad_pre, *w_rows))
     grad_far = swap(grad_pre, far)
     parts = weight_parts(feats + aggs, hbm(grad_pre), n_dom)
     part_sums = lax.all_to_all(parts, "dom", 0, 0, tiled=True)
@@ -632,13 +650,19 @@
     back_out, back_agg, direct = back_far(
         lists, edge_tiles, grads, w_rows, n_dom, hub_dev, tile_size
     )
+    part_sums, back_out = lax.optimization_barrier((part_sums, back_out))
     back_in = lax.all_to_all(back_out, "dom", 0, 0, tiled=True)
     own = back_own(lists, edge_tiles, back_agg, direct).reshape(own_count, width)
-    weights_out, grad_bias = sum_parts(part_sums)
-    weights_out, back_in, own = lax.optimization_barrier((weights_out, back_in, own))
-    weights_in = lax.all_to_all(weights_out, "dom", 0, 0, tiled=True)
+    weights, grad_bias = sum_parts(part_sums)
+    sums, chunk_of, bit = [weights], [0], n_dom // 2
+    while bit:
+        weights = jnp.concatenate(sums, axis=0)
+        sums = [weights, lax.ppermute(weights, "dom", [(j, j ^ bit) for j in range(n_dom)])]
+        chunk_of += [k ^ bit for k in chunk_of]
+        bit //= 2
     grad_feats = finish(listed, send_count, hub_ids, back_in, own)
-    grad_self, grad_neigh = place_weights(me_s, weights_in.reshape(-1, width))
+    both = jnp.stack([me, lax.axis_index("dom").astype(jnp.int32)])
+    grad_self, grad_neigh = place_weights(both, sums, chunk_of, n_feat * width)
     return (output, grad_feats, grad_self, grad_neigh, grad_bias[0])
 
 

time: 106 us -> 113 us (1.066)
  waiting for transfers between devices: 26.1 us -> 31 us
  local copies, waits for them, and re-layouts: 1.99 us -> 3.61 us
    ppermute x0 -> x3, waiting for transfers between devices: none -> 10.3 us  [body(): lax.ppermute(weights, 'dom', [(j, j ^ bit) for j in range(n_dom)])]
    all_to_all x1 -> x0, waiting for transfers between devices: 5.05 us -> none  [body(): weights_in = lax.all_to_all(weights_out, 'dom', 0, 0, tiled=True)]
    ppermute x0 -> x3, starting transfers between devices: none -> 4.3 us  [body(): lax.ppermute(weights, 'dom', [(j, j ^ bit) for j in range(n_dom)])]
    all_to_all x1, waiting for transfers between devices: 3.64 us -> 0.01 us  [body(): back_in = lax.all_to_all(back_out, 'dom', 0, 0, tiled=True)]
    all_to_all x1 -> x0, starting transfers between devices: 3.64 us -> none  [body(): weights_in = lax.all_to_all(weights_out, 'dom', 0, 0, tiled=True)]
    all_to_all x1, waiting for transfers between devices: 0.01 us -> 3.1 us  [body(): part_sums = lax.all_to_all(parts, 'dom', 0, 0, tiled=True)]
    unnamed x6 -> x12, local copies, waits for them, and re-layouts: 1.99 us -> 3.6 us
  transfers between devices with their start and end apart: 16 -> 18, of which waited for: 9 -> 8; matrix products, arithmetic and copies ran while one was open for 0% -> 1% of each run, Pallas kernels for 37% -> 36%
where the time goes in v6:
time: 113 us; the launch traced here: 112 us
  Pallas kernels  48.8 us (43%)
  waiting for transfers between devices  31 us (27%)
  starting transfers between devices  27.4 us (24%)
  local copies, waits for them, and re-layouts  3.61 us (3%)
    ppermute x12, waiting for transfers between devices, swap(): return lax.ppermute(x, 'feat', [(j, j ^ k) for j in range(n_feat)])  16.9 us
    ppermute x3, waiting for transfers between devices, body(): lax.ppermute(weights, 'dom', [(j, j ^ bit) for j in range(n_dom)])  10.3 us
    pallas_call x2, Pallas kernels, stream_call(): pl.pallas_call(run, out_shape=tuple((pltpu.HBM(shape, t) for shape, t in...  9.19 us
    all_to_all x1, starting transfers between devices, body(): incoming = lax.all_to_all(outgoing, 'dom', 0, 0, tiled=True)  7.27 us
    ppermute x12, starting transfers between devices, swap(): return lax.ppermute(x, 'feat', [(j, j ^ k) for j in range(n_feat)])  6.9 us
    pallas_call x1, Pallas kernels, back_far(): pl.pallas_call(functools.partial(back_far_kernel, n_feat=n_feat), out_sha...  6.28 us
    pallas_call x1, Pallas kernels, own_tiles(): pl.pallas_call(functools.partial(own_kernel, far_blocks=far_blocks), out_...  6.28 us
    pallas_call x1, Pallas kernels, back_own(): pl.pallas_call(back_own_kernel, out_shape=pltpu.HBM(direct.shape, F32), i...  5.46 us
  transfers between devices with their start and end apart: 18, of which 8 were waited for; matrix products, arithmetic and copies ran while one was open for 1% of the time, Pallas kernels for 36%

profile of v6, /device:TPU:0, one launch (start us, length us, event | category | flops | bytes accessed | tf_op | source)
XLA Modules:
  0.0 112.5 jit_solution(13222815607298417980)
XLA Ops:
  0.6 4.5 %pick_rows.1 = bf16[8,160,128]{2,1,0:T(8,128)(2,1)} custom-call(s32[8,128]{1,0:T(8,128)} %bitcast.14, s32[1,8]{1,0:T(1,128)} %count_h.3, s32[32]{0:T(128)} %hub_h.3, bf16[2048,128]{1,0:T(8,128)(2,1)} %refs_0_.3), custom_call_target="tpu_custom_call" | custom-call | bytes 2097152 | tf_op jit(solution)/shard_map/pick_rows/pallas_call | solution.py:77
  5.1 7.3 %all-to-all-start = ((bf16[8,160,128]{2,1,0:T(8,128)(2,1)}), bf16[8,160,128]{2,1,0:T(8,128)(2,1)}, u32[]{:S(2)}, u32[]{:S(2)}) async-start(bf16[8,160,128]{2,1,0:T(8,128)(2,1)} %pick_rows.1), calls=%async_computation | async-start | bytes 655360 | tf_op jit(solution)/shard_map/all_to_all | solution.py:610
  12.4 1.5 %collective-permute-start = (bf16[2048,128]{1,0:T(8,128)(2,1)}, bf16[2048,128]{1,0:T(8,128)(2,1)}, u32[]{:S(2)}, u32[]{:S(2)}) collective-permute-start(bf16[2048,128]{1,0:T(8,128)(2,1)} %refs_0_.3), channel_id=1, source_target_pairs={{0,2},{1,3},{2,0},{3,1},{4,6},{5,7},{6,4},{7,5},{8,10},{9,11},{10,... | collective-permute-start | bytes 1572872 | tf_op jit(solution)/shard_map/ppermute | solution.py:605
  13.9 2.0 %copy-done = bf16[106,128,128]{2,1,0:T(8,128)(2,1)S(1)} copy-done((bf16[106,128,128]{2,1,0:T(8,128)(2,1)S(1)}, bf16[106,128,128]{2,1,0:T(8,128)(2,1)}, u32[]{:S(2)}) %copy-start) | copy-done | bytes 3473432
  15.9 6.3 %own_tiles.1 = (f32[16,128,128]{2,1,0:T(8,128)}, s32[2,114]{1,0:T(2,128)S(1)}) custom-call(s32[106]{0:T(128)} %dst_h.1, s32[106]{0:T(128)} %src_h.1, bf16[106,128,128]{2,1,0:T(8,128)(2,1)S(1)} %copy-done, bf16[16,128,128]{2,1,0:T(8,128)(2,1)} %bitcast.8), custom_call_target="tpu_custom_call" | custom-call | flops 444596224 | bytes 8388608 | tf_op jit(solution)/shard_map/own_tiles/pallas_call | solution.py:170
  22.8 4.0 %far_tiles.1 = bf16[16,128,128]{2,1,0:T(8,128)(2,1)} custom-call(s32[2,114]{1,0:T(2,128)S(1)} %get-tuple-element.33.lists.refs_0_, bf16[106,128,128]{2,1,0:T(8,128)(2,1)S(1)} %copy-done.1, bf16[8,160,128]{2,1,0:T(8,128)(2,1)} %all-to-all-done.incoming_h, f32[16,128,128]{2,1,0:T(8,128)} %get-tuple-element.34.base_h), custom_call_target="tpu_custom_call" | custom-call | flops 222298112 | bytes 4194304 | tf_op jit(solution)/shard_map/far_tiles/pallas_call | solution.py:211
  26.9 1.6 %collective-permute-start.2 = (bf16[2048,128]{1,0:T(8,128)(2,1)}, bf16[2048,128]{1,0:T(8,128)(2,1)}, u32[]{:S(2)}, u32[]{:S(2)}) collective-permute-start(bf16[2048,128]{1,0:T(8,128)(2,1)} %bitcast.9), channel_id=1, source_target_pairs={{0,2},{1,3},{2,0},{3,1},{4,6},{5,7},{6,4},{7,5},{8,10},{9,11},{10,... | collective-permute-start | bytes 1572872 | tf_op jit(solution)/shard_map/ppermute | solution.py:605
  28.5 1.7 %cut_weights.1 = (bf16[2,128,128]{2,1,0:T(8,128)(2,1)}, bf16[2,128,128]{2,1,0:T(8,128)(2,1)}, bf16[2,2,128,128]{3,2,1,0:T(8,128)(2,1)}) custom-call(s32[1]{0:T(128)} %bitcast.me_s, bf16[512,128]{1,0:T(8,128)(2,1)} %w_self.1, bf16[512,128]{1,0:T(8,128)(2,1)} %refs_6_.1), custom_call_target="tpu_custom_call" | custom-call | bytes 1048576 | tf_op jit(solution)/shard_map/cut_weights/pallas_call | solution.py:509
  30.4 4.6 %self_dense.1.refs_4_ = f32[2048,128]{1,0:T(8,128)} custom-call(s32[1]{0:T(128)} %bitcast.me_s, bf16[2048,128]{1,0:T(8,128)(2,1)} %refs_0_.3, bf16[2048,128]{1,0:T(8,128)(2,1)} %collective-permute-done.3.refs_1_, bf16[2048,128]{1,0:T(8,128)(2,1)} %collective-permute-done.refs_2_, bf16[2048,128]{1,0:T(8,128)(2,1)} %collective-permute-done.4.refs_3_, ...), custom_call_target="tpu_custom_call" | custom-call | flops 268435456 | bytes 4194304 | tf_op jit(solution)/shard_map/self_dense/pallas_call | solution.py:273
  34.9 6.6 %collective-permute-done.2.refs_2_.refs_6_ = bf16[2048,128]{1,0:T(8,128)(2,1)} collective-permute-done((bf16[2048,128]{1,0:T(8,128)(2,1)}, bf16[2048,128]{1,0:T(8,128)(2,1)}, u32[]{:S(2)}, u32[]{:S(2)}) %collective-permute-start.2) | collective-permute-done | bytes 524320 | tf_op jit(solution)/shard_map/ppermute | solution.py:605
  41.6 1.5 %collective-permute-start.7 = (bf16[2,2,128,128]{3,2,1,0:T(8,128)(2,1)}, bf16[2,2,128,128]{3,2,1,0:T(8,128)(2,1)S(1)}, u32[]{:S(2)}, u32[]{:S(2)}) collective-permute-start(bf16[2,2,128,128]{3,2,1,0:T(8,128)(2,1)} %get-tuple-element.46), channel_id=1, source_target_pairs={{0,2},{1,3},{2,0},{3,1},{4,6},{5,7},{6,4},{7,5},{8,10},{9,11},{10,... | collective-permute-start | bytes 393224 | tf_op jit(solution)/shard_map/ppermute | solution.py:605
  43.1 4.6 %collective-permute-done.7.refs_8_ = bf16[2,2,128,128]{3,2,1,0:T(8,128)(2,1)S(1)} collective-permute-done((bf16[2,2,128,128]{3,2,1,0:T(8,128)(2,1)}, bf16[2,2,128,128]{3,2,1,0:T(8,128)(2,1)S(1)}, u32[]{:S(2)}, u32[]{:S(2)}) %collective-permute-start.7) | collective-permute-done | bytes 131104 | tf_op jit(solution)/shard_map/ppermute | solution.py:605
  48.3 4.6 %forward_dense.1 = (bf16[2048,128]{1,0:T(8,128)(2,1)}, bf16[2048,128]{1,0:T(8,128)(2,1)}) custom-call(s32[1]{0:T(128)} %bitcast.me_s, bf16[2048,128]{1,0:T(8,128)(2,1)} %bitcast.11, bf16[2048,128]{1,0:T(8,128)(2,1)S(1)} %collective-permute-done.1.refs_1_.refs_5_, bf16[2048,128]{1,0:T(8,128)(2,1)} %collective-permute-done.2.refs_2_.refs_6_, ...), custom_call_target="tpu_custom_call" | custom-call | flops 268435456 | bytes 4194304 | tf_op jit(solution)/shard_map/forward_dense/pallas_call | solution.py:273
  53.0 0.7 copy-done.3
  53.7 1.5 %collective-permute-start.10 = (bf16[2048,128]{1,0:T(8,128)(2,1)}, bf16[2048,128]{1,0:T(8,128)(2,1)}, u32[]{:S(2)}, u32[]{:S(2)}) collective-permute-start(bf16[2048,128]{1,0:T(8,128)(2,1)} %get-tuple-element.47.refs_8_.refs_2_), channel_id=1, source_target_pairs={{0,2},{1,3},{2,0},{3,1},{4,6},{5,7},{6,4},{7,5},{8,10},{9,11},{10,... | collective-permute-start | bytes 1572872 | tf_op jit(solution)/shard_map/ppermute | solution.py:605
  55.2 4.2 %weight_parts.1 = f32[8,136,128]{2,1,0:T(8,128)} custom-call(bf16[2048,128]{1,0:T(8,128)(2,1)} %refs_0_.3, bf16[2048,128]{1,0:T(8,128)(2,1)} %collective-permute-done.3.refs_1_, bf16[2048,128]{1,0:T(8,128)(2,1)} %collective-permute-done.refs_2_, bf16[2048,128]{1,0:T(8,128)(2,1)} %collective-permute-done.4.refs_3_, bf16[2048,128]{1,0:T(8,128)(2,1)} %bitcast.12, ...), custom_call_target="tpu_custom_call" | custom-call | flops 536870912 | bytes 4194304 | tf_op jit(solution)/shard_map/weight_parts/pallas_call | solution.py:323
  59.4 4.9 %all-to-all-start.1 = ((f32[8,136,128]{2,1,0:T(8,128)}), f32[8,136,128]{2,1,0:T(8,128)}, u32[]{:S(2)}, u32[]{:S(2)}) async-start(f32[8,136,128]{2,1,0:T(8,128)} %weight_parts.1), calls=%async_computation.1 | async-start | bytes 1114112 | tf_op jit(solution)/shard_map/all_to_all | solution.py:647
  64.3 3.4 %collective-permute-done.10.refs_4_ = bf16[2048,128]{1,0:T(8,128)(2,1)} collective-permute-done((bf16[2048,128]{1,0:T(8,128)(2,1)}, bf16[2048,128]{1,0:T(8,128)(2,1)}, u32[]{:S(2)}, u32[]{:S(2)}) %collective-permute-start.10) | collective-permute-done | bytes 524320 | tf_op jit(solution)/shard_map/ppermute | solution.py:605
  67.7 2.2 %collective-permute-done.11.refs_5_ = bf16[2048,128]{1,0:T(8,128)(2,1)} collective-permute-done((bf16[2048,128]{1,0:T(8,128)(2,1)}, bf16[2048,128]{1,0:T(8,128)(2,1)}, u32[]{:S(2)}, u32[]{:S(2)}) %collective-permute-start.11) | collective-permute-done | bytes 524320 | tf_op jit(solution)/shard_map/ppermute | solution.py:605
  69.9 6.3 %back_far.1 = (bf16[8,160,128]{2,1,0:T(8,128)(2,1)}, bf16[16,128,128]{2,1,0:T(8,128)(2,1)}, f32[16,128,128]{2,1,0:T(8,128)}) custom-call(s32[2,114]{1,0:T(2,128)S(1)} %get-tuple-element.33.lists.refs_0_, bf16[106,128,128]{2,1,0:T(8,128)(2,1)S(1)} %copy-done.1, bf16[2048,128]{1,0:T(8,128)(2,1)} %get-tuple-element.47.refs_8_.refs_2_, ...), custom_call_target="tpu_custom_call" | custom-call | flops 536870912 | bytes 4194304 | tf_op jit(solution)/shard_map/back_far/pallas_call | solution.py:386
  76.2 3.1 %all-to-all-done.1.parts = f32[8,136,128]{2,1,0:T(8,128)} async-done(((f32[8,136,128]{2,1,0:T(8,128)}), f32[8,136,128]{2,1,0:T(8,128)}, u32[]{:S(2)}, u32[]{:S(2)}) %all-to-all-start.1) | async-done | bytes 557088 | tf_op jit(solution)/shard_map/all_to_all | solution.py:647
  79.3 4.1 %all-to-all-start.2 = ((bf16[8,160,128]{2,1,0:T(8,128)(2,1)}), bf16[8,160,128]{2,1,0:T(8,128)(2,1)}, u32[]{:S(2)}, u32[]{:S(2)}) async-start(bf16[8,160,128]{2,1,0:T(8,128)(2,1)} %get-tuple-element.53), calls=%async_computation.2 | async-start | bytes 655360 | tf_op jit(solution)/shard_map/all_to_all | solution.py:654
  83.4 1.7 %sum_parts.1 = (bf16[128,128]{1,0:T(8,128)(2,1)}, f32[1,128]{1,0:T(1,128)}) custom-call(f32[8,136,128]{2,1,0:T(8,128)} %all-to-all-done.1.parts), custom_call_target="tpu_custom_call" | custom-call | bytes 1048576 | tf_op jit(solution)/shard_map/sum_parts/pallas_call | solution.py:531
  85.1 2.8 %collective-permute-start.12 = (bf16[128,128]{1,0:T(8,128)(2,1)}, bf16[128,128]{1,0:T(8,128)(2,1)S(1)}, u32[]{:S(2)}, u32[]{:S(2)}) collective-permute-start(bf16[128,128]{1,0:T(8,128)(2,1)} %get-tuple-element.57), channel_id=1, source_target_pairs={{0,16},{4,20},{8,24},{12,28},{16,0},{20,4},{24,8},{28,12},{1,17},{... | collective-permute-start | bytes 98312 | tf_op jit(solution)/shard_map/ppermute | solution.py:660
  87.9 0.8 constant_dynamic-update-slice_fusion.2
  88.7 6.1 %collective-permute-done.12 = bf16[128,128]{1,0:T(8,128)(2,1)S(1)} collective-permute-done((bf16[128,128]{1,0:T(8,128)(2,1)}, bf16[128,128]{1,0:T(8,128)(2,1)S(1)}, u32[]{:S(2)}, u32[]{:S(2)}) %collective-permute-start.12) | collective-permute-done | bytes 32800 | tf_op jit(solution)/shard_map/ppermute | solution.py:660
  94.8 0.8 pad_maximum_fusion
  95.6 4.3 %collective-permute-done.13 = bf16[256,128]{1,0:T(8,128)(2,1)S(1)} collective-permute-done((bf16[256,128]{1,0:T(8,128)(2,1)S(1)}, bf16[256,128]{1,0:T(8,128)(2,1)S(1)}, u32[]{:S(2)}, u32[]{:S(2)}) %collective-permute-start.13) | collective-permute-done | bytes 65568 | tf_op jit(solution)/shard_map/ppermute | solution.py:660
  99.9 1.5 %collective-permute-start.14 = (bf16[512,128]{1,0:T(8,128)(2,1)S(1)}, bf16[512,128]{1,0:T(8,128)(2,1)S(1)}, u32[]{:S(2)}, u32[]{:S(2)}) collective-permute-start(bf16[512,128]{1,0:T(8,128)(2,1)S(1)} %constant_dynamic-update-slice_fusion.refs_0_), channel_id=1, source_target_pairs={{0,4},{4,0},{8,12},{12,8},{16,20},{20,16},{24,28},{28,24},{1,5},{5... | collective-permute-start | bytes 393224 | tf_op jit(solution)/shard_map/ppermute | solution.py:660
  101.4 5.5 %back_own.1 = f32[16,128,128]{2,1,0:T(8,128)} custom-call(s32[2,114]{1,0:T(2,128)S(1)} %get-tuple-element.33.lists.refs_0_, bf16[106,128,128]{2,1,0:T(8,128)(2,1)S(1)} %copy-done.1, bf16[16,128,128]{2,1,0:T(8,128)(2,1)} %get-tuple-element.54.back_h, f32[16,128,128]{2,1,0:T(8,128)} %get-tuple-element.55.direct_h), custom_call_target="tpu_custom_call" | custom-call | flops 444596224 | bytes 8388608 | tf_op jit(solution)/shard_map/back_own/pallas_call | solution.py:415
  106.9 1.5 %place_weights.1 = (f32[512,128]{1,0:T(8,128)}, f32[512,128]{1,0:T(8,128)}) custom-call(s32[2]{0:T(128)S(1)} %pad_add_fusion.me_s, bf16[512,128]{1,0:T(8,128)(2,1)S(1)} %constant_dynamic-update-slice_fusion.refs_0_, bf16[512,128]{1,0:T(8,128)(2,1)S(1)} %collective-permute-done.14.refs_1_), custom_call_target="tpu_custom_call" | custom-call | bytes 1048576 | tf_op jit(solution)/shard_map/place_weights/pallas_call | solution.py:567
  108.4 4.1 %finish.1 = f32[2048,128]{1,0:T(8,128)} custom-call(s32[8,128]{1,0:T(8,128)} %bitcast.15, s32[1,8]{1,0:T(1,128)} %count_h.3, s32[32]{0:T(128)} %hub_h.3, bf16[8,160,128]{2,1,0:T(8,128)(2,1)} %all-to-all-done.2.incoming_h, f32[2048,128]{1,0:T(8,128)} %bitcast.13), custom_call_target="tpu_custom_call" | custom-call | flops 536870912 | bytes 4194304 | tf_op jit(solution)/shard_map/finish/pallas_call | solution.py:477
  (31 shorter events, 1.7 us)
Async XLA Ops:
  5.1 17.7 %all-to-all-start = ((bf16[8,160,128]{2,1,0:T(8,128)(2,1)}), bf16[8,160,128]{2,1,0:T(8,128)(2,1)}, u32[]{:S(2)}, u32[]{:S(2)}) async-start(bf16[8,160,128]{2,1,0:T(8,128)(2,1)} %pick_rows.1), calls=%async_computation | async-start | bytes 655360 | tf_op jit(solution)/shard_map/all_to_all | solution.py:610
  12.4 14.5 %collective-permute-start = (bf16[2048,128]{1,0:T(8,128)(2,1)}, bf16[2048,128]{1,0:T(8,128)(2,1)}, u32[]{:S(2)}, u32[]{:S(2)}) collective-permute-start(bf16[2048,128]{1,0:T(8,128)(2,1)} %refs_0_.3), channel_id=1, source_target_pairs={{0,2},{1,3},{2,0},{3,1},{4,6},{5,7},{6,4},{7,5},{8,10},{9,11},{10,... | collective-permute-start | bytes 1572872 | tf_op jit(solution)/shard_map/ppermute | solution.py:605
  13.9 16.5 %collective-permute-start.3 = (bf16[2048,128]{1,0:T(8,128)(2,1)}, bf16[2048,128]{1,0:T(8,128)(2,1)}, u32[]{:S(2)}, u32[]{:S(2)}) collective-permute-start(bf16[2048,128]{1,0:T(8,128)(2,1)} %refs_0_.3), channel_id=1, source_target_pairs={{0,1},{1,0},{2,3},{3,2},{4,5},{5,4},{6,7},{7,6},{8,9},{9,8},{10,11... | collective-permute-start | bytes 1572872 | tf_op jit(solution)/shard_map/ppermute | solution.py:605
  13.9 2.0 %copy-start = (bf16[106,128,128]{2,1,0:T(8,128)(2,1)S(1)}, bf16[106,128,128]{2,1,0:T(8,128)(2,1)}, u32[]{:S(2)}) copy-start(bf16[106,128,128]{2,1,0:T(8,128)(2,1)} %tiles.5) | copy-start | bytes 10420228
  15.9 6.9 %copy-start.1 = (bf16[106,128,128]{2,1,0:T(8,128)(2,1)S(1)}, bf16[106,128,128]{2,1,0:T(8,128)(2,1)}, u32[]{:S(2)}) copy-start(bf16[106,128,128]{2,1,0:T(8,128)(2,1)} %tiles.5) | copy-start | bytes 10420228
  26.8 3.5 %collective-permute-start.4 = (bf16[2048,128]{1,0:T(8,128)(2,1)}, bf16[2048,128]{1,0:T(8,128)(2,1)}, u32[]{:S(2)}, u32[]{:S(2)}) collective-permute-start(bf16[2048,128]{1,0:T(8,128)(2,1)} %collective-permute-done.refs_2_), channel_id=1, source_target_pairs={{0,1},{1,0},{2,3},{3,2},{4,5},{5,4},{6,7},{7,6},{8,9},{9,8},{10,11... | collective-permute-start | bytes 1572872 | tf_op jit(solution)/shard_map/ppermute | solution.py:605
  26.9 14.7 %collective-permute-start.2 = (bf16[2048,128]{1,0:T(8,128)(2,1)}, bf16[2048,128]{1,0:T(8,128)(2,1)}, u32[]{:S(2)}, u32[]{:S(2)}) collective-permute-start(bf16[2048,128]{1,0:T(8,128)(2,1)} %bitcast.9), channel_id=1, source_target_pairs={{0,2},{1,3},{2,0},{3,1},{4,6},{5,7},{6,4},{7,5},{8,10},{9,11},{10,... | collective-permute-start | bytes 1572872 | tf_op jit(solution)/shard_map/ppermute | solution.py:605
  30.2 18.0 %collective-permute-start.1 = (bf16[2048,128]{1,0:T(8,128)(2,1)}, bf16[2048,128]{1,0:T(8,128)(2,1)S(1)}, u32[]{:S(2)}, u32[]{:S(2)}) collective-permute-start(bf16[2048,128]{1,0:T(8,128)(2,1)} %bitcast.10), channel_id=1, source_target_pairs={{0,1},{1,0},{2,3},{3,2},{4,5},{5,4},{6,7},{7,6},{8,9},{9,8},{10,11... | collective-permute-start | bytes 1572872 | tf_op jit(solution)/shard_map/ppermute | solution.py:605
  41.6 6.6 %collective-permute-start.5 = (bf16[2048,128]{1,0:T(8,128)(2,1)}, bf16[2048,128]{1,0:T(8,128)(2,1)S(1)}, u32[]{:S(2)}, u32[]{:S(2)}) collective-permute-start(bf16[2048,128]{1,0:T(8,128)(2,1)} %collective-permute-done.2.refs_2_.refs_6_), channel_id=1, source_target_pairs={{0,1},{1,0},{2,3},{3,2},{4,5},{5,4},{6,7},{7,6},{8,9},{9,8},{10,11... | collective-permute-start | bytes 1572872 | tf_op jit(solution)/shard_map/ppermute | solution.py:605
  41.6 6.1 %collective-permute-start.7 = (bf16[2,2,128,128]{3,2,1,0:T(8,128)(2,1)}, bf16[2,2,128,128]{3,2,1,0:T(8,128)(2,1)S(1)}, u32[]{:S(2)}, u32[]{:S(2)}) collective-permute-start(bf16[2,2,128,128]{3,2,1,0:T(8,128)(2,1)} %get-tuple-element.46), channel_id=1, source_target_pairs={{0,2},{1,3},{2,0},{3,1},{4,6},{5,7},{6,4},{7,5},{8,10},{9,11},{10,... | collective-permute-start | bytes 393224 | tf_op jit(solution)/shard_map/ppermute | solution.py:605
  47.7 0.7 copy-start.2
  47.7 5.3 %collective-permute-start.8 = (bf16[2,2,128,128]{3,2,1,0:T(8,128)(2,1)S(1)}, bf16[2,2,128,128]{3,2,1,0:T(8,128)(2,1)S(1)}, u32[]{:S(2)}, u32[]{:S(2)}) collective-permute-start(bf16[2,2,128,128]{3,2,1,0:T(8,128)(2,1)S(1)} %collective-permute-done.7.refs_8_), channel_id=1, source_target_pairs={{0,1},{1,0},{2,3},{3,2},{4,5},{5,4},{6,7},{7,6},{8,9},{9,8},{10,11... | collective-permute-start | bytes 393224 | tf_op jit(solution)/shard_map/ppermute | solution.py:605
  47.7 5.3 %collective-permute-start.6 = (bf16[2,128,128]{2,1,0:T(8,128)(2,1)}, bf16[2,128,128]{2,1,0:T(8,128)(2,1)S(1)}, u32[]{:S(2)}, u32[]{:S(2)}) collective-permute-start(bf16[2,128,128]{2,1,0:T(8,128)(2,1)} %get-tuple-element.45), channel_id=1, source_target_pairs={{0,1},{1,0},{2,3},{3,2},{4,5},{5,4},{6,7},{7,6},{8,9},{9,8},{10,11... | collective-permute-start | bytes 196616 | tf_op jit(solution)/shard_map/ppermute | solution.py:605
  53.0 17.0 %copy-start.4 = (bf16[2,128,128]{2,1,0:T(8,128)(2,1)}, bf16[2,128,128]{2,1,0:T(8,128)(2,1)S(1)}, u32[]{:S(2)}) copy-start(bf16[2,128,128]{2,1,0:T(8,128)(2,1)S(1)} %collective-permute-done.6.refs_7_) | copy-start | bytes 196612
  53.0 0.7 copy-start.3
  53.7 14.0 %collective-permute-start.10 = (bf16[2048,128]{1,0:T(8,128)(2,1)}, bf16[2048,128]{1,0:T(8,128)(2,1)}, u32[]{:S(2)}, u32[]{:S(2)}) collective-permute-start(bf16[2048,128]{1,0:T(8,128)(2,1)} %get-tuple-element.47.refs_8_.refs_2_), channel_id=1, source_target_pairs={{0,2},{1,3},{2,0},{3,1},{4,6},{5,7},{6,4},{7,5},{8,10},{9,11},{10,... | collective-permute-start | bytes 1572872 | tf_op jit(solution)/shard_map/ppermute | solution.py:605
  59.4 20.0 %all-to-all-start.1 = ((f32[8,136,128]{2,1,0:T(8,128)}), f32[8,136,128]{2,1,0:T(8,128)}, u32[]{:S(2)}, u32[]{:S(2)}) async-start(f32[8,136,128]{2,1,0:T(8,128)} %weight_parts.1), calls=%async_computation.1 | async-start | bytes 1114112 | tf_op jit(solution)/shard_map/all_to_all | solution.py:647
  64.3 3.4 %collective-permute-start.9 = (bf16[2048,128]{1,0:T(8,128)(2,1)}, bf16[2048,128]{1,0:T(8,128)(2,1)}, u32[]{:S(2)}, u32[]{:S(2)}) collective-permute-start(bf16[2048,128]{1,0:T(8,128)(2,1)} %get-tuple-element.47.refs_8_.refs_2_), channel_id=1, source_target_pairs={{0,1},{1,0},{2,3},{3,2},{4,5},{5,4},{6,7},{7,6},{8,9},{9,8},{10,11... | collective-permute-start | bytes 1572872 | tf_op jit(solution)/shard_map/ppermute | solution.py:605
  67.7 2.3 %collective-permute-start.11 = (bf16[2048,128]{1,0:T(8,128)(2,1)}, bf16[2048,128]{1,0:T(8,128)(2,1)}, u32[]{:S(2)}, u32[]{:S(2)}) collective-permute-start(bf16[2048,128]{1,0:T(8,128)(2,1)} %collective-permute-done.10.refs_4_), channel_id=1, source_target_pairs={{0,1},{1,0},{2,3},{3,2},{4,5},{5,4},{6,7},{7,6},{8,9},{9,8},{10,11... | collective-permute-start | bytes 1572872 | tf_op jit(solution)/shard_map/ppermute | solution.py:605
  79.3 29.1 %all-to-all-start.2 = ((bf16[8,160,128]{2,1,0:T(8,128)(2,1)}), bf16[8,160,128]{2,1,0:T(8,128)(2,1)}, u32[]{:S(2)}, u32[]{:S(2)}) async-start(bf16[8,160,128]{2,1,0:T(8,128)(2,1)} %get-tuple-element.53), calls=%async_computation.2 | async-start | bytes 655360 | tf_op jit(solution)/shard_map/all_to_all | solution.py:654
  85.1 9.7 %collective-permute-start.12 = (bf16[128,128]{1,0:T(8,128)(2,1)}, bf16[128,128]{1,0:T(8,128)(2,1)S(1)}, u32[]{:S(2)}, u32[]{:S(2)}) collective-permute-start(bf16[128,128]{1,0:T(8,128)(2,1)} %get-tuple-element.57), channel_id=1, source_target_pairs={{0,16},{4,20},{8,24},{12,28},{16,0},{20,4},{24,8},{28,12},{1,17},{... | collective-permute-start | bytes 98312 | tf_op jit(solution)/shard_map/ppermute | solution.py:660
  95.6 4.3 %collective-permute-start.13 = (bf16[256,128]{1,0:T(8,128)(2,1)S(1)}, bf16[256,128]{1,0:T(8,128)(2,1)S(1)}, u32[]{:S(2)}, u32[]{:S(2)}) collective-permute-start(bf16[256,128]{1,0:T(8,128)(2,1)S(1)} %pad_maximum_fusion), channel_id=1, source_target_pairs={{0,8},{4,12},{8,0},{12,4},{16,24},{20,28},{24,16},{28,20},{1,9},{5... | collective-permute-start | bytes 196616 | tf_op jit(solution)/shard_map/ppermute | solution.py:660
  99.9 7.0 %collective-permute-start.14 = (bf16[512,128]{1,0:T(8,128)(2,1)S(1)}, bf16[512,128]{1,0:T(8,128)(2,1)S(1)}, u32[]{:S(2)}, u32[]{:S(2)}) collective-permute-start(bf16[512,128]{1,0:T(8,128)(2,1)S(1)} %constant_dynamic-update-slice_fusion.refs_0_), channel_id=1, source_target_pairs={{0,4},{4,0},{8,12},{12,8},{16,20},{20,16},{24,28},{28,24},{1,5},{5... | collective-permute-start | bytes 393224 | tf_op jit(solution)/shard_map/ppermute | solution.py:660

commit v7 on v4

--- a/solution.py
+++ b/solution.py
@@ -155,12 +155,15 @@
     lax.fori_loop(0, (n + UNROLL - 1) // UNROLL, group, 0)
 
 
-def own_kernel(dst_h, src_h, tiles, x_h, out_h, lists, dst_s, src_s, x, acc, sems, *, far_blocks):
+def own_kernel(
+    dst_h, src_h, tiles_h, x_h, out_h, lists, dst_s, src_s, x, tiles, acc, sems, *, far_blocks
+):
     own_blocks = x.shape[0]
-    copies = start_copies(sems, (x_h, x), (dst_h, dst_s), (src_h, src_s))
+    copies = start_copies(sems, (dst_h, dst_s), (src_h, src_s), (x_h, x), (tiles_h, tiles))
     acc[...] = jnp.zeros_like(acc)
-    wait_copies(copies)
+    wait_copies(copies[:2])
     make_lists(dst_s, src_s, lists, own_blocks, far_blocks)
+    wait_copies(copies[2:])
     add_tiles(lists, 0, tiles, x, acc, own_blocks)
     wait_copies(start_copies(sems, (acc.at[pl.ds(0, own_blocks)], out_h)))
 
@@ -173,19 +176,20 @@
             pltpu.HBM(x.shape, F32),
             jax.ShapeDtypeStruct((2, n + UNROLL), jnp.int32),
         ),
-        in_specs=[HBM, HBM, VMEM, HBM],
+        in_specs=[HBM, HBM, HBM, HBM],
         out_specs=(HBM, SMEM),
         scratch_shapes=[
             pltpu.SMEM((n,), jnp.int32),
             pltpu.SMEM((n,), jnp.int32),
             pltpu.VMEM(x.shape, BF16),
+            pltpu.VMEM(tiles.shape, BF16),
             pltpu.VMEM((x.shape[0] + 1,) + x.shape[1:], F32),
-            pltpu.SemaphoreType.DMA((3,)),
+            pltpu.SemaphoreType.DMA((4,)),
         ],
         compiler_params=params(),
         cost_estimate=cost(2 * n * 128**3, 1 << 23),
         name="own_tiles",
-    )(hbm(tile_dst), hbm(tile_src), tiles, hbm(x))
+    )(hbm(tile_dst), hbm(tile_src), hbm(tiles), hbm(x))
 
 
 def far_kernel(lists, tiles, incoming_h, base_h, out_h, source, acc, out, sems):
@@ -301,7 +305,7 @@
 
 def weights_kernel(*refs, n_feat):
     shards, grad, out_h, out, sems = refs[: 2 * n_feat], *refs[2 * n_feat :]
-    n_dom, chunk = out.shape[0], out.shape[1] - 8
+    n_dom, chunk = out.shape[0], out.shape[1] - 16
     width = grad.shape[1]
     flipped = grad[...].T
     bias = jnp.sum(grad[...].astype(F32), axis=0, keepdims=True)
@@ -310,9 +314,15 @@
         for row in range(0, width, min(chunk, width)):
             q, start = divmod(i * width + row, chunk)
             n = min(chunk, width)
-            out[q, start : start + n, :] = block[row : row + n, :]
+            out[q, start : start + n, :] = block[row : row + n, :].astype(BF16)
+    line = lax.broadcasted_iota(jnp.int32, (16, width), 0)
+    terms, left = jnp.zeros((16, width), F32), jnp.broadcast_to(bias, (16, width))
+    for i in range(3):
+        term = left.astype(BF16).astype(F32)
+        terms = jnp.where(line == i, term, terms)
+        left = left - term
     for q in range(n_dom):
-        out[q, chunk:, :] = jnp.broadcast_to(bias, (8, width))
+        out[q, chunk:, :] = terms.astype(BF16)
     wait_copies(start_copies(sems, (out, out_h)))
 
 
@@ -322,11 +332,11 @@
     chunk = 2 * n_feat * width // n_dom
     return pl.pallas_call(
         functools.partial(weights_kernel, n_feat=n_feat),
-        out_shape=pltpu.HBM((n_dom, chunk + 8, width), F32),
+        out_shape=pltpu.HBM((n_dom, chunk + 16, width), BF16),
         in_specs=[VMEM] * (2 * n_feat + 1),
         out_specs=HBM,
         scratch_shapes=[
-            pltpu.VMEM((n_dom, chunk + 8, width), F32),
+            pltpu.VMEM((n_dom, chunk + 16, width), BF16),
             pltpu.SemaphoreType.DMA((1,)),
         ],
         compiler_params=params(),
@@ -346,19 +356,23 @@
 
 
 def back_far_kernel(*refs, n_feat):
-    lists, tiles = refs[:2]
-    grads_h, w = refs[2 : 2 + n_feat], refs[2 + n_feat : 2 + 2 * n_feat]
-    out_h, back_h, direct_h = refs[2 + 2 * n_feat : 5 + 2 * n_feat]
-    grads = refs[5 + 2 * n_feat : 5 + 3 * n_feat]
-    back, direct, acc, out, sems, out_sems = refs[5 + 3 * n_feat :]
+    lists, tiles, parts_h, *refs = refs
+    grads_h, w, refs = refs[:n_feat], refs[n_feat : 2 * n_feat], refs[2 * n_feat :]
+    out_h, back_h, direct_h, bias, *refs = refs
+    grads, refs = refs[:n_feat], refs[n_feat:]
+    back, direct, acc, out, parts, sems, out_sems, parts_sem = refs
     n_dom = out.shape[0]
     own_blocks, tile, width = back.shape
-    hub_dev = out.shape[1] - tile
+    chunk = parts.shape[1] - 16
+    hub_dev = out.shape[1] - tile - chunk
     hub_blocks = n_dom * hub_dev // tile
     block = 4 * tile
     pending = split_copies(sems, list(zip(grads_h, grads)), block)
+    parts_copy = start_copies(parts_sem, (parts_h, parts))
     acc[...] = jnp.zeros_like(acc)
-    rows = jnp.concatenate([r[...].reshape(2 * width, -1) for r in w], axis=1)
+    own_w, near_w, far_w, both_w = w
+    rows = [r.reshape(2 * width, -1) for r in (own_w[...], near_w[...], far_w[0], both_w[1])]
+    rows = jnp.concatenate(rows, axis=1)
     for i, copies in enumerate(pending):
         wait_copies(copies)
         whole = jnp.concatenate([g[i * block : (i + 1) * block, :] for g in grads], axis=1)
@@ -366,39 +380,54 @@
         direct[4 * i : 4 * (i + 1)] = both[:, :width].reshape(4, tile, width)
         back[4 * i : 4 * (i + 1)] = both[:, width:].astype(BF16).reshape(4, tile, width)
     leaving = start_copies(out_sems, (direct, direct_h), (back, back_h))
+    wait_copies(parts_copy)
+    total = parts[0].astype(F32)
+    for q in range(1, n_dom):
+        total += parts[q].astype(F32)
+    bias[...] = total[chunk : chunk + 1, :] + total[chunk + 1 : chunk + 2, :] + total[chunk + 2 : chunk + 3, :]
+    weights = total[:chunk, :].astype(BF16)
     add_tiles_t(lists, 1, tiles, back, acc, own_blocks)
     for q in range(n_dom):
         out[q, :tile, :] = acc[hub_blocks + q].astype(BF16)
         at, row = divmod(q * hub_dev, tile)
-        out[q, tile:, :] = acc[at, row : row + hub_dev, :].astype(BF16)
+        out[q, tile : tile + hub_dev, :] = acc[at, row : row + hub_dev, :].astype(BF16)
+        out[q, tile + hub_dev :, :] = weights
     leaving += start_copies(out_sems.at[pl.ds(2, 1)], (out, out_h))
     wait_copies(leaving)
 
 
-def back_far(lists, tiles, grads, w, n_dom, hub_dev, tile):
+def back_far(lists, tiles, part_sums, grads, w, hub_dev, tile):
     n_feat = len(grads)
+    n_dom, part_rows, _ = part_sums.shape
     rows, width = grads[0].shape
     far_blocks = n_dom * hub_dev // tile + n_dom
-    shape = (n_dom, tile + hub_dev, width)
+    shape = (n_dom, tile + hub_dev + part_rows - 16, width)
     back_shape = (rows // tile, tile, width)
     return pl.pallas_call(
         functools.partial(back_far_kernel, n_feat=n_feat),
-        out_shape=(pltpu.HBM(shape, BF16), pltpu.HBM(back_shape, BF16), pltpu.HBM(back_shape, F32)),
-        in_specs=[SMEM, VMEM] + [ANY] * n_feat + [VMEM] * n_feat,
-        out_specs=(HBM, HBM, HBM),
+        out_shape=(
+            pltpu.HBM(shape, BF16),
+            pltpu.HBM(back_shape, BF16),
+            pltpu.HBM(back_shape, F32),
+            pltpu.HBM((1, width), F32),
+        ),
+        in_specs=[SMEM, VMEM, ANY] + [ANY] * n_feat + [VMEM] * n_feat,
+        out_specs=(HBM, HBM, HBM, VMEM),
         scratch_shapes=[pltpu.VMEM((rows, width), BF16)] * n_feat
         + [
             pltpu.VMEM(back_shape, BF16),
             pltpu.VMEM(back_shape, F32),
             pltpu.VMEM((far_blocks + 1, tile, width), F32),
             pltpu.VMEM(shape, BF16),
+            pltpu.VMEM(part_sums.shape, BF16),
             pltpu.SemaphoreType.DMA((rows // (4 * tile), n_feat)),
             pltpu.SemaphoreType.DMA((3,)),
+            pltpu.SemaphoreType.DMA((1,)),
         ],
         compiler_params=params(),
         cost_estimate=cost(4 * rows * width * width * n_feat, 1 << 22),
         name="back_far",
-    )(lists, tiles, *grads, *w)
+    )(lists, tiles, part_sums, *grads, *[hbm(r) for r in w])
 
 
 def back_own_kernel(lists, tiles, back_h, direct_h, out_h, back, acc, sems):
@@ -426,7 +455,7 @@
     )(lists, tiles, hbm(back), hbm(direct))
 
 
-def finish_kernel(rows_s, count_h, hub_h, incoming_h, base_h, out_h, count_s, hub_s, sent, hubs, base, sems, out_sems):
+def finish_kernel(me_s, rows_s, count_h, hub_h, incoming_h, base_h, out_h, self_out, neigh_out, count_s, hub_s, sent, hubs, sums, base, sems, out_sems):
     n_dom, capacity = rows_s.shape
     hub_dev = hub_s.shape[0]
     own_count, width = base.shape
@@ -438,6 +467,7 @@
         (incoming_h.at[:, pl.ds(0, capacity), :], sent),
         (incoming_h.at[:, pl.ds(capacity, hub_dev), :], hubs),
         (base_h, base),
+        (incoming_h.at[:, pl.ds(capacity + hub_dev, sums.shape[1]), :], sums),
     )
     wait_copies(copies)
     hub = hubs[0].astype(F32)
@@ -464,99 +494,63 @@
         base[start : start + block, :] = total
         at = pl.ds(start, block)
         leaving.append(start_copies(out_sems.at[pl.ds(start // block, 1)], (base.at[at], out_h.at[at])))
+    chunk, n_feat = sums.shape[1], self_out.shape[0] // width
+    n = min(chunk, width)
+    for row in range(0, 2 * n_feat * width, n):
+        q, first = divmod(row, chunk)
+        which, k = divmod(row // width, n_feat)
+        at = pl.multiple_of((me_s[0] ^ k) * width + row % width, n)
+        (self_out, neigh_out)[which][pl.ds(at, n), :] = sums[q, first : first + n, :].astype(F32)
     for copies in leaving:
         wait_copies(copies)
 
 
-def finish(send_rows, send_count, hub_ids, incoming, base):
+def finish(me, send_rows, send_count, hub_ids, incoming, base, n_feat):
     n_dom, capacity = send_rows.shape
     hub_dev = hub_ids.shape[0]
     own_count, width = base.shape
     return pl.pallas_call(
         finish_kernel,
-        out_shape=pltpu.HBM(base.shape, F32),
-        in_specs=[VMEM, HBM, HBM, ANY, HBM],
-        out_specs=HBM,
+        out_shape=(pltpu.HBM(base.shape, F32),) + (pltpu.HBM((n_feat * width, width), F32),) * 2,
+        in_specs=[SMEM, VMEM, HBM, HBM, ANY, HBM],
+        out_specs=(HBM, VMEM, VMEM),
         scratch_shapes=[
             pltpu.SMEM(send_count.shape, jnp.int32),
             pltpu.SMEM(hub_ids.shape, jnp.int32),
             pltpu.VMEM((n_dom, capacity, width), BF16),
             pltpu.VMEM((n_dom, hub_dev, width), BF16),
+            pltpu.VMEM((n_dom, 2 * n_feat * width // n_dom, width), BF16),
             pltpu.VMEM(base.shape, F32),
-            pltpu.SemaphoreType.DMA((5,)),
+            pltpu.SemaphoreType.DMA((6,)),
             pltpu.SemaphoreType.DMA((own_count // 256,)),
         ],
         compiler_params=params(),
         cost_estimate=cost(2 * base.size * send_rows.size, 1 << 22),
         name="finish",
-    )(hbm(send_rows), hbm(send_count), hbm(hub_ids), incoming, hbm(base))
+    )(me, hbm(send_rows), hbm(send_count), hbm(hub_ids), incoming, hbm(base))
 
 
 def cut_kernel(me_s, w_self, w_neigh, *outs):
     width = w_self.shape[1]
-    for k, out in enumerate(outs):
+    own, near, far = outs
+    for k, out in enumerate((own, near, far.at[0], far.at[1])):
         at = pl.ds(pl.multiple_of((me_s[0] ^ k) * width, width), width)
         out[0] = w_self[at, :]
         out[1] = w_neigh[at, :]
 
 
-def cut_weights(me, w_self, w_neigh, n_feat):
+def cut_weights(me, w_self, w_neigh):
     width = w_self.shape[1]
+    one = (2, width, width)
     return pl.pallas_call(
         cut_kernel,
-        out_shape=(pltpu.HBM((2, width, width), BF16),) * n_feat,
+        out_shape=tuple(pltpu.HBM(shape, BF16) for shape in (one, one, (2,) + one)),
         in_specs=[SMEM, VMEM, VMEM],
-        out_specs=(VMEM,) * n_feat,
+        out_specs=(VMEM,) * 3,
         compiler_params=params(),
         cost_estimate=cost(0, 1 << 20),
         name="cut_weights",
     )(me, hbm(w_self), hbm(w_neigh))
-
-
-def sum_kernel(parts, out, bias):
-    n_dom, chunk, _ = out.shape
-    total = parts[0]
-    for q in range(1, n_dom):
-        total += parts[q]
-    bias[...] = total[chunk : chunk + 1, :]
-    rows = total[:chunk, :].astype(BF16)
-    for q in range(n_dom):
-        out[q] = rows
-
-
-def sum_parts(parts):
-    n_dom, rows, width = parts.shape
-    return pl.pallas_call(
-        sum_kernel,
-        out_shape=(pltpu.HBM((n_dom, rows - 8, width), BF16), pltpu.HBM((1, width), F32)),
-        in_specs=[VMEM],
-        out_specs=(VMEM, VMEM),
-        compiler_params=params(),
-        cost_estimate=cost(0, 1 << 20),
-        name="sum_parts",
-    )(hbm(parts))
-
-
-def place_kernel(me_s, sums, self_out, neigh_out):
-    rows, width = self_out.shape
-    for i in range(2 * rows // width):
-        which, k = divmod(i, rows // width)
-        target = (self_out, neigh_out)[which]
-        at = pl.ds(pl.multiple_of((me_s[0] ^ k) * width, width), width)
-        target[at, :] = sums[i * width : (i + 1) * width, :].astype(F32)
-
-
-def place_weights(me, sums):
-    rows, width = sums.shape[0] // 2, sums.shape[1]
-    return pl.pallas_call(
-        place_kernel,
-        out_shape=(pltpu.HBM((rows, width), F32),) * 2,
-        in_specs=[SMEM, VMEM],
-        out_specs=(VMEM, VMEM),
-        compiler_params=params(),
-        cost_estimate=cost(0, 1 << 20),
-        name="place_weights",
-    )(me, sums)
 
 
 def body(
@@ -592,10 +586,14 @@
 
     outgoing = pick(listed, send_count, hub_ids, node_feats)
     incoming = lax.all_to_all(outgoing, "dom", 0, 0, tiled=True)
-    own_feats = node_feats.reshape(-1, tile_size, width)
+    cut = cut_weights(me_s, w_self, w_neigh)
+    own_feats, *cut = lax.optimization_barrier((node_feats.reshape(-1, tile_size, width), *cut))
+    far_w = swap(cut[2], far)
     base, lists = own_tiles(tile_dst, tile_src, edge_tiles, own_feats, far_blocks)
     aggregated = far_tiles(lists, edge_tiles, incoming, base, far_blocks).reshape(own_count, width)
 
+    aggregated, far_w = lax.optimization_barrier((aggregated, far_w))
+    w_rows = [cut[0], swap(cut[1], near), far_w, swap(far_w, near)]
     agg_far = swap(aggregated, far)
     feat_far, aggregated = lax.optimization_barrier((feat_far, aggregated))
     feats = [hbm(node_feats), swap(node_feats, near), feat_far, swap(feat_far, near)]
@@ -610,9 +608,7 @@
         flops,
         "self_dense",
     )
-    cut = cut_weights(me_s, w_self, w_neigh, n_feat)
-    agg_far, own_part, *cut = lax.optimization_barrier((agg_far, own_part, *cut))
-    w_rows = [hbm(cut[0])] + [swap(cut[k], k) for k in range(1, n_feat)]
+    agg_far, own_part = lax.optimization_barrier((agg_far, own_part))
     aggs = [hbm(aggregated), swap(aggregated, near), agg_far, swap(agg_far, near)]
     output, grad_pre = stream_call(
         forward_step,
@@ -627,18 +623,17 @@
     grad_far = swap(grad_pre, far)
     parts = weight_parts(feats + aggs, hbm(grad_pre), n_dom)
     part_sums = lax.all_to_all(parts, "dom", 0, 0, tiled=True)
+    grad_far, part_sums = lax.optimization_barrier((grad_far, part_sums))
     grads = [hbm(grad_pre), swap(grad_pre, near), grad_far, swap(grad_far, near)]
 
-    back_out, back_agg, direct = back_far(
-        lists, edge_tiles, grads, w_rows, n_dom, hub_dev, tile_size
+    back_out, back_agg, direct, grad_bias = back_far(
+        lists, edge_tiles, part_sums, grads, w_rows, hub_dev, tile_size
     )
     back_in = lax.all_to_all(back_out, "dom", 0, 0, tiled=True)
     own = back_own(lists, edge_tiles, back_agg, direct).reshape(own_count, width)
-    weights_out, grad_bias = sum_parts(part_sums)
-    weights_out, back_in, own = lax.optimization_barrier((weights_out, back_in, own))
-    weights_in = lax.all_to_all(weights_out, "dom", 0, 0, tiled=True)
-    grad_feats = finish(listed, send_count, hub_ids, back_in, own)
-    grad_self, grad_neigh = place_weights(me_s, weights_in.reshape(-1, width))
+    grad_feats, grad_self, grad_neigh = finish(
+        me_s, listed, send_count, hub_ids, back_in, own, n_feat
+    )
     return (output, grad_feats, grad_self, grad_neigh, grad_bias[0])
 
 

time: 106 us -> 108 us (1.019)
  waiting for transfers between devices: 26.1 us -> 36.3 us
  starting transfers between devices: 27.7 us -> 23.1 us
  Pallas kernels: 48.4 us -> 46.9 us
  local copies, waits for them, and re-layouts: 1.99 us -> 0.66 us
    all_to_all x1, waiting for transfers between devices: 0.01 us -> 9.73 us  [body(): part_sums = lax.all_to_all(parts, 'dom', 0, 0, tiled=True)]
    all_to_all x1, waiting for transfers between devices: 3.64 us -> 11.5 us  [body(): back_in = lax.all_to_all(back_out, 'dom', 0, 0, tiled=True)]
    all_to_all x1 -> x0, waiting for transfers between devices: 5.05 us -> none  [body(): weights_in = lax.all_to_all(weights_out, 'dom', 0, 0, tiled=True)]
    all_to_all x1 -> x0, starting transfers between devices: 3.64 us -> none  [body(): weights_in = lax.all_to_all(weights_out, 'dom', 0, 0, tiled=True)]
    ppermute x12, waiting for transfers between devices: 16.8 us -> 13.6 us  [swap(): return lax.ppermute(x, 'feat', [(j, j ^ k) for j in range(n_feat)])]
    pallas_call x4 -> x2, Pallas kernels: 8.34 us -> 6.57 us  [the longest x1 4.89 us: finish(): pl.pallas_call(finish_kernel, out_shape=(pltpu.HBM(base.shape, F32),) + (...]
    unnamed x6 -> x8, local copies, waits for them, and re-layouts: 1.99 us -> 0.66 us
    ppermute x12, starting transfers between devices: 6.96 us -> 5.88 us  [swap(): return lax.ppermute(x, 'feat', [(j, j ^ k) for j in range(n_feat)])]
  transfers between devices with their start and end apart: 16 -> 15, of which waited for: 9 -> 9; matrix products, arithmetic and copies ran while one was open for 0% -> 0% of each run, Pallas kernels for 37% -> 23%
where the time goes in v7:
time: 108 us
  Pallas kernels  46.9 us (43%)
  waiting for transfers between devices  36.3 us (34%)
  starting transfers between devices  23.1 us (21%)
    ppermute x12, waiting for transfers between devices, swap(): return lax.ppermute(x, 'feat', [(j, j ^ k) for j in range(n_feat)])  13.6 us
    all_to_all x1, waiting for transfers between devices, body(): back_in = lax.all_to_all(back_out, 'dom', 0, 0, tiled=True)  11.5 us
    pallas_call x2, Pallas kernels, stream_call(): pl.pallas_call(run, out_shape=tuple((pltpu.HBM(shape, t) for shape, t in...  9.75 us
    all_to_all x1, waiting for transfers between devices, body(): part_sums = lax.all_to_all(parts, 'dom', 0, 0, tiled=True)  9.73 us
    pallas_call x1, Pallas kernels, back_far(): pl.pallas_call(functools.partial(back_far_kernel, n_feat=n_feat), out_sha...  7.48 us
    all_to_all x1, starting transfers between devices, body(): incoming = lax.all_to_all(outgoing, 'dom', 0, 0, tiled=True)  7.26 us
    ppermute x12, starting transfers between devices, swap(): return lax.ppermute(x, 'feat', [(j, j ^ k) for j in range(n_feat)])  5.88 us
    all_to_all x1, starting transfers between devices, body(): part_sums = lax.all_to_all(parts, 'dom', 0, 0, tiled=True)  5.74 us
  transfers between devices with their start and end apart: 15, of which 9 were waited for; matrix products, arithmetic and copies ran while one was open for 0% of the time, Pallas kernels for 23%

profile of v7, /device:TPU:0, one launch (start us, length us, event | category | flops | bytes accessed | tf_op | source)
XLA Modules:
  0.0 107.7 jit_solution(17421394999536937114)
XLA Ops:
  0.6 0.0 copy-start
  0.6 4.6 %pick_rows.1 = bf16[8,160,128]{2,1,0:T(8,128)(2,1)} custom-call(s32[8,128]{1,0:T(8,128)} %bitcast.13, s32[1,8]{1,0:T(1,128)} %count_h.3, s32[32]{0:T(128)} %hub_h.3, bf16[2048,128]{1,0:T(8,128)(2,1)} %refs_0_.3), custom_call_target="tpu_custom_call" | custom-call | bytes 2097152 | tf_op jit(solution)/shard_map/pick_rows/pallas_call | solution.py:77
  5.3 7.3 %all-to-all-start = ((bf16[8,160,128]{2,1,0:T(8,128)(2,1)}), bf16[8,160,128]{2,1,0:T(8,128)(2,1)}, u32[]{:S(2)}, u32[]{:S(2)}) async-start(bf16[8,160,128]{2,1,0:T(8,128)(2,1)} %pick_rows.1), calls=%async_computation | async-start | bytes 655360 | tf_op jit(solution)/shard_map/all_to_all | solution.py:588
  12.5 1.5 %collective-permute-start = (bf16[2048,128]{1,0:T(8,128)(2,1)}, bf16[2048,128]{1,0:T(8,128)(2,1)}, u32[]{:S(2)}, u32[]{:S(2)}) collective-permute-start(bf16[2048,128]{1,0:T(8,128)(2,1)} %refs_0_.3), channel_id=1, source_target_pairs={{0,2},{1,3},{2,0},{3,1},{4,6},{5,7},{6,4},{7,5},{8,10},{9,11},{10,... | collective-permute-start | bytes 1572872 | tf_op jit(solution)/shard_map/ppermute | solution.py:583
  14.1 1.7 %cut_weights.1 = (bf16[2,128,128]{2,1,0:T(8,128)(2,1)}, bf16[2,128,128]{2,1,0:T(8,128)(2,1)}, bf16[2,2,128,128]{3,2,1,0:T(8,128)(2,1)}) custom-call(s32[1]{0:T(128)} %bitcast.me_s, bf16[512,128]{1,0:T(8,128)(2,1)} %refs_4_.1, bf16[512,128]{1,0:T(8,128)(2,1)} %refs_6_.1), custom_call_target="tpu_custom_call" | custom-call | bytes 1048576 | tf_op jit(solution)/shard_map/cut_weights/pallas_call | solution.py:545
  15.7 0.5 collective-permute-start.1
  16.2 5.4 %own_tiles.1 = (f32[16,128,128]{2,1,0:T(8,128)}, s32[2,114]{1,0:T(2,128)S(1)}) custom-call(s32[106]{0:T(128)} %dst_h.1, s32[106]{0:T(128)} %src_h.1, bf16[106,128,128]{2,1,0:T(8,128)(2,1)} %tiles.3, bf16[16,128,128]{2,1,0:T(8,128)(2,1)} %bitcast.7), custom_call_target="tpu_custom_call" | custom-call | flops 444596224 | bytes 8388608 | tf_op jit(solution)/shard_map/own_tiles/pallas_call | solution.py:173
  21.6 1.4 %all-to-all-done.incoming_h = bf16[8,160,128]{2,1,0:T(8,128)(2,1)} async-done(((bf16[8,160,128]{2,1,0:T(8,128)(2,1)}), bf16[8,160,128]{2,1,0:T(8,128)(2,1)}, u32[]{:S(2)}, u32[]{:S(2)}) %all-to-all-start) | async-done | bytes 327712 | tf_op jit(solution)/shard_map/all_to_all | solution.py:588
  23.0 4.5 %far_tiles.1 = bf16[16,128,128]{2,1,0:T(8,128)(2,1)} custom-call(s32[2,114]{1,0:T(2,128)S(1)} %get-tuple-element.35.lists.refs_0_, bf16[106,128,128]{2,1,0:T(8,128)(2,1)S(1)} %copy-done, bf16[8,160,128]{2,1,0:T(8,128)(2,1)} %all-to-all-done.incoming_h, f32[16,128,128]{2,1,0:T(8,128)} %get-tuple-element.36.base_h), custom_call_target="tpu_custom_call" | custom-call | flops 222298112 | bytes 4194304 | tf_op jit(solution)/shard_map/far_tiles/pallas_call | solution.py:215
  27.5 1.6 %collective-permute-done.1.refs_9_ = bf16[2,2,128,128]{3,2,1,0:T(8,128)(2,1)} collective-permute-done((bf16[2,2,128,128]{3,2,1,0:T(8,128)(2,1)}, bf16[2,2,128,128]{3,2,1,0:T(8,128)(2,1)}, u32[]{:S(2)}, u32[]{:S(2)}) %collective-permute-start.1) | collective-permute-done | bytes 131104 | tf_op jit(solution)/shard_map/ppermute | solution.py:583
  29.0 1.5 %collective-permute-start.3 = (bf16[2048,128]{1,0:T(8,128)(2,1)}, bf16[2048,128]{1,0:T(8,128)(2,1)S(1)}, u32[]{:S(2)}, u32[]{:S(2)}) collective-permute-start(bf16[2048,128]{1,0:T(8,128)(2,1)} %bitcast.8), channel_id=1, source_target_pairs={{0,2},{1,3},{2,0},{3,1},{4,6},{5,7},{6,4},{7,5},{8,10},{9,11},{10,... | collective-permute-start | bytes 1572872 | tf_op jit(solution)/shard_map/ppermute | solution.py:583
  30.6 0.2 collective-permute-start.2
  30.8 0.4 collective-permute-done.5.refs_3_
  31.2 4.5 %self_dense.1.refs_4_ = f32[2048,128]{1,0:T(8,128)} custom-call(s32[1]{0:T(128)} %bitcast.me_s, bf16[2048,128]{1,0:T(8,128)(2,1)} %refs_0_.3, bf16[2048,128]{1,0:T(8,128)(2,1)} %collective-permute-done.4.refs_1_, bf16[2048,128]{1,0:T(8,128)(2,1)} %collective-permute-done.refs_2_, bf16[2048,128]{1,0:T(8,128)(2,1)S(1)} %collective-permute-done.5.refs_3_, ...), custom_call_target="tpu_custom_call" | custom-call | flops 268435456 | bytes 4194304 | tf_op jit(solution)/shard_map/self_dense/pallas_call | solution.py:277
  35.7 7.9 %collective-permute-done.3.refs_2_.refs_6_ = bf16[2048,128]{1,0:T(8,128)(2,1)S(1)} collective-permute-done((bf16[2048,128]{1,0:T(8,128)(2,1)}, bf16[2048,128]{1,0:T(8,128)(2,1)S(1)}, u32[]{:S(2)}, u32[]{:S(2)}) %collective-permute-start.3) | collective-permute-done | bytes 524320 | tf_op jit(solution)/shard_map/ppermute | solution.py:583
  43.6 1.9 %collective-permute-done.6.refs_3_.refs_7_ = bf16[2048,128]{1,0:T(8,128)(2,1)S(1)} collective-permute-done((bf16[2048,128]{1,0:T(8,128)(2,1)S(1)}, bf16[2048,128]{1,0:T(8,128)(2,1)S(1)}, u32[]{:S(2)}, u32[]{:S(2)}) %collective-permute-start.6) | collective-permute-done | bytes 524320 | tf_op jit(solution)/shard_map/ppermute | solution.py:583
  45.5 5.2 %forward_dense.1 = (bf16[2048,128]{1,0:T(8,128)(2,1)}, bf16[2048,128]{1,0:T(8,128)(2,1)}) custom-call(s32[1]{0:T(128)} %bitcast.me_s, bf16[2048,128]{1,0:T(8,128)(2,1)} %bitcast.10, bf16[2048,128]{1,0:T(8,128)(2,1)S(1)} %collective-permute-done.2.refs_1_.refs_5_, bf16[2048,128]{1,0:T(8,128)(2,1)S(1)} %collective-permute-done.3.refs_2_.refs_6_, ...), custom_call_target="tpu_custom_call" | custom-call | flops 268435456 | bytes 4194304 | tf_op jit(solution)/shard_map/forward_dense/pallas_call | solution.py:277
  50.7 1.6 %collective-permute-start.7 = (bf16[2048,128]{1,0:T(8,128)(2,1)}, bf16[2048,128]{1,0:T(8,128)(2,1)}, u32[]{:S(2)}, u32[]{:S(2)}) collective-permute-start(bf16[2048,128]{1,0:T(8,128)(2,1)} %get-tuple-element.44.refs_8_.refs_3_), channel_id=1, source_target_pairs={{0,2},{1,3},{2,0},{3,1},{4,6},{5,7},{6,4},{7,5},{8,10},{9,11},{10,... | collective-permute-start | bytes 1572872 | tf_op jit(solution)/shard_map/ppermute | solution.py:583
  52.3 3.8 %weight_parts.1 = bf16[8,144,128]{2,1,0:T(8,128)(2,1)} custom-call(bf16[2048,128]{1,0:T(8,128)(2,1)} %refs_0_.3, bf16[2048,128]{1,0:T(8,128)(2,1)} %collective-permute-done.4.refs_1_, bf16[2048,128]{1,0:T(8,128)(2,1)} %collective-permute-done.refs_2_, bf16[2048,128]{1,0:T(8,128)(2,1)S(1)} %collective-permute-done.5.refs_3_, bf16[2048,128]{1,0:T(8,128)(2,1)} %bitcast.11, ...), custom_call_target="tpu_custom_call" | custom-call | flops 536870912 | bytes 4194304 | tf_op jit(solution)/shard_map/weight_parts/pallas_call | solution.py:333
  56.1 5.7 %all-to-all-start.1 = ((bf16[8,144,128]{2,1,0:T(8,128)(2,1)}), bf16[8,144,128]{2,1,0:T(8,128)(2,1)}, u32[]{:S(2)}, u32[]{:S(2)}) async-start(bf16[8,144,128]{2,1,0:T(8,128)(2,1)} %weight_parts.1), calls=%async_computation.1 | async-start | bytes 589824 | tf_op jit(solution)/shard_map/all_to_all | solution.py:625
  61.8 9.7 %all-to-all-done.1.refs_2_ = bf16[8,144,128]{2,1,0:T(8,128)(2,1)} async-done(((bf16[8,144,128]{2,1,0:T(8,128)(2,1)}), bf16[8,144,128]{2,1,0:T(8,128)(2,1)}, u32[]{:S(2)}, u32[]{:S(2)}) %all-to-all-start.1) | async-done | bytes 294944 | tf_op jit(solution)/shard_map/all_to_all | solution.py:625
  71.6 0.5 collective-permute-start.11
  72.1 0.0 collective-permute-start.10
  72.1 1.6 %collective-permute-done.10.refs_8_ = bf16[2,128,128]{2,1,0:T(8,128)(2,1)S(1)} collective-permute-done((bf16[2,128,128]{2,1,0:T(8,128)(2,1)S(1)}, bf16[2,128,128]{2,1,0:T(8,128)(2,1)S(1)}, u32[]{:S(2)}, u32[]{:S(2)}) %collective-permute-start.10) | collective-permute-done | bytes 65568 | tf_op jit(solution)/shard_map/ppermute | solution.py:583
  73.7 0.3 collective-permute-done.11.refs_10_
  74.0 0.3 copy-done.2
  74.3 0.3 copy-done.1
  74.6 7.5 %back_far.1 = (bf16[8,288,128]{2,1,0:T(8,128)(2,1)}, bf16[16,128,128]{2,1,0:T(8,128)(2,1)}, f32[16,128,128]{2,1,0:T(8,128)}, f32[1,128]{1,0:T(1,128)}) custom-call(s32[2,114]{1,0:T(2,128)S(1)} %get-tuple-element.35.lists.refs_0_, bf16[106,128,128]{2,1,0:T(8,128)(2,1)S(1)} %copy-done, bf16[8,144,128]{2,1,0:T(8,128)(2,1)} %all-to-all-done.1.refs_2_, ...), custom_call_target="tpu_custom_call" | custom-call | flops 536870912 | bytes 4194304 | tf_op jit(solution)/shard_map/back_far/pallas_call | solution.py:406
  82.1 4.2 %all-to-all-start.2 = ((bf16[8,288,128]{2,1,0:T(8,128)(2,1)}), bf16[8,288,128]{2,1,0:T(8,128)(2,1)}, u32[]{:S(2)}, u32[]{:S(2)}) async-start(bf16[8,288,128]{2,1,0:T(8,128)(2,1)} %get-tuple-element.50), calls=%async_computation.2 | async-start | bytes 1179648 | tf_op jit(solution)/shard_map/all_to_all | solution.py:632
  86.3 4.9 %back_own.1 = f32[16,128,128]{2,1,0:T(8,128)} custom-call(s32[2,114]{1,0:T(2,128)S(1)} %get-tuple-element.35.lists.refs_0_, bf16[106,128,128]{2,1,0:T(8,128)(2,1)S(1)} %copy-done, bf16[16,128,128]{2,1,0:T(8,128)(2,1)} %get-tuple-element.51.back_h, f32[16,128,128]{2,1,0:T(8,128)} %get-tuple-element.52.direct_h), custom_call_target="tpu_custom_call" | custom-call | flops 444596224 | bytes 8388608 | tf_op jit(solution)/shard_map/back_own/pallas_call | solution.py:442
  91.3 11.5 %all-to-all-done.2.incoming_h = bf16[8,288,128]{2,1,0:T(8,128)(2,1)} async-done(((bf16[8,288,128]{2,1,0:T(8,128)(2,1)}), bf16[8,288,128]{2,1,0:T(8,128)(2,1)}, u32[]{:S(2)}, u32[]{:S(2)}) %all-to-all-start.2) | async-done | bytes 589856 | tf_op jit(solution)/shard_map/all_to_all | solution.py:632
  102.8 4.9 %finish.1 = (f32[2048,128]{1,0:T(8,128)}, f32[512,128]{1,0:T(8,128)}, f32[512,128]{1,0:T(8,128)}) custom-call(s32[1]{0:T(128)} %bitcast.me_s, s32[8,128]{1,0:T(8,128)} %bitcast.14, s32[1,8]{1,0:T(1,128)} %count_h.3, s32[32]{0:T(128)} %hub_h.3, bf16[8,288,128]{2,1,0:T(8,128)(2,1)} %all-to-all-done.2.incoming_h, f32[2048,128]{1,0:T(8,128)} %bitcast.12), custom_call_target="tpu_custom_call" | custom-call | flops 536870912 | bytes 4194304 | tf_op jit(solution)/shard_map/finish/pallas_call | solution.py:512
  (16 shorter events, 0.0 us)
Async XLA Ops:
  0.6 22.3 %copy-start = (bf16[106,128,128]{2,1,0:T(8,128)(2,1)S(1)}, bf16[106,128,128]{2,1,0:T(8,128)(2,1)}, u32[]{:S(2)}) copy-start(bf16[106,128,128]{2,1,0:T(8,128)(2,1)} %tiles.3) | copy-start | bytes 10420228
  5.3 17.7 %all-to-all-start = ((bf16[8,160,128]{2,1,0:T(8,128)(2,1)}), bf16[8,160,128]{2,1,0:T(8,128)(2,1)}, u32[]{:S(2)}, u32[]{:S(2)}) async-start(bf16[8,160,128]{2,1,0:T(8,128)(2,1)} %pick_rows.1), calls=%async_computation | async-start | bytes 655360 | tf_op jit(solution)/shard_map/all_to_all | solution.py:588
  12.5 16.5 %collective-permute-start = (bf16[2048,128]{1,0:T(8,128)(2,1)}, bf16[2048,128]{1,0:T(8,128)(2,1)}, u32[]{:S(2)}, u32[]{:S(2)}) collective-permute-start(bf16[2048,128]{1,0:T(8,128)(2,1)} %refs_0_.3), channel_id=1, source_target_pairs={{0,2},{1,3},{2,0},{3,1},{4,6},{5,7},{6,4},{7,5},{8,10},{9,11},{10,... | collective-permute-start | bytes 1572872 | tf_op jit(solution)/shard_map/ppermute | solution.py:583
  15.7 13.3 %collective-permute-start.1 = (bf16[2,2,128,128]{3,2,1,0:T(8,128)(2,1)}, bf16[2,2,128,128]{3,2,1,0:T(8,128)(2,1)}, u32[]{:S(2)}, u32[]{:S(2)}) collective-permute-start(bf16[2,2,128,128]{3,2,1,0:T(8,128)(2,1)} %get-tuple-element.37), channel_id=1, source_target_pairs={{0,2},{1,3},{2,0},{3,1},{4,6},{5,7},{6,4},{7,5},{8,10},{9,11},{10,... | collective-permute-start | bytes 393224 | tf_op jit(solution)/shard_map/ppermute | solution.py:583
  16.2 14.6 %collective-permute-start.4 = (bf16[2048,128]{1,0:T(8,128)(2,1)}, bf16[2048,128]{1,0:T(8,128)(2,1)}, u32[]{:S(2)}, u32[]{:S(2)}) collective-permute-start(bf16[2048,128]{1,0:T(8,128)(2,1)} %refs_0_.3), channel_id=1, source_target_pairs={{0,1},{1,0},{2,3},{3,2},{4,5},{5,4},{6,7},{7,6},{8,9},{9,8},{10,11... | collective-permute-start | bytes 1572872 | tf_op jit(solution)/shard_map/ppermute | solution.py:583
  29.0 2.1 %collective-permute-start.5 = (bf16[2048,128]{1,0:T(8,128)(2,1)}, bf16[2048,128]{1,0:T(8,128)(2,1)S(1)}, u32[]{:S(2)}, u32[]{:S(2)}) collective-permute-start(bf16[2048,128]{1,0:T(8,128)(2,1)} %collective-permute-done.refs_2_), channel_id=1, source_target_pairs={{0,1},{1,0},{2,3},{3,2},{4,5},{5,4},{6,7},{7,6},{8,9},{9,8},{10,11... | collective-permute-start | bytes 1572872 | tf_op jit(solution)/shard_map/ppermute | solution.py:583
  29.0 14.5 %collective-permute-start.3 = (bf16[2048,128]{1,0:T(8,128)(2,1)}, bf16[2048,128]{1,0:T(8,128)(2,1)S(1)}, u32[]{:S(2)}, u32[]{:S(2)}) collective-permute-start(bf16[2048,128]{1,0:T(8,128)(2,1)} %bitcast.8), channel_id=1, source_target_pairs={{0,2},{1,3},{2,0},{3,1},{4,6},{5,7},{6,4},{7,5},{8,10},{9,11},{10,... | collective-permute-start | bytes 1572872 | tf_op jit(solution)/shard_map/ppermute | solution.py:583
  30.6 13.0 %collective-permute-start.2 = (bf16[2048,128]{1,0:T(8,128)(2,1)}, bf16[2048,128]{1,0:T(8,128)(2,1)S(1)}, u32[]{:S(2)}, u32[]{:S(2)}) collective-permute-start(bf16[2048,128]{1,0:T(8,128)(2,1)} %bitcast.9), channel_id=1, source_target_pairs={{0,1},{1,0},{2,3},{3,2},{4,5},{5,4},{6,7},{7,6},{8,9},{9,8},{10,11... | collective-permute-start | bytes 1572872 | tf_op jit(solution)/shard_map/ppermute | solution.py:583
  43.6 1.9 %collective-permute-start.6 = (bf16[2048,128]{1,0:T(8,128)(2,1)S(1)}, bf16[2048,128]{1,0:T(8,128)(2,1)S(1)}, u32[]{:S(2)}, u32[]{:S(2)}) collective-permute-start(bf16[2048,128]{1,0:T(8,128)(2,1)S(1)} %collective-permute-done.3.refs_2_.refs_6_), channel_id=1, source_target_pairs={{0,1},{1,0},{2,3},{3,2},{4,5},{5,4},{6,7},{7,6},{8,9},{9,8},{10,11... | collective-permute-start | bytes 1572872 | tf_op jit(solution)/shard_map/ppermute | solution.py:583
  50.7 21.4 %copy-start.3 = (bf16[2,128,128]{2,1,0:T(8,128)(2,1)S(1)}, bf16[2,128,128]{2,1,0:T(8,128)(2,1)}, u32[]{:S(2)}) copy-start(bf16[2,128,128]{2,1,0:T(8,128)(2,1)} %get-tuple-element.48) | copy-start | bytes 196612
  50.7 20.8 %collective-permute-start.7 = (bf16[2048,128]{1,0:T(8,128)(2,1)}, bf16[2048,128]{1,0:T(8,128)(2,1)}, u32[]{:S(2)}, u32[]{:S(2)}) collective-permute-start(bf16[2048,128]{1,0:T(8,128)(2,1)} %get-tuple-element.44.refs_8_.refs_3_), channel_id=1, source_target_pairs={{0,2},{1,3},{2,0},{3,1},{4,6},{5,7},{6,4},{7,5},{8,10},{9,11},{10,... | collective-permute-start | bytes 1572872 | tf_op jit(solution)/shard_map/ppermute | solution.py:583
  56.1 15.5 %all-to-all-start.1 = ((bf16[8,144,128]{2,1,0:T(8,128)(2,1)}), bf16[8,144,128]{2,1,0:T(8,128)(2,1)}, u32[]{:S(2)}, u32[]{:S(2)}) async-start(bf16[8,144,128]{2,1,0:T(8,128)(2,1)} %weight_parts.1), calls=%async_computation.1 | async-start | bytes 589824 | tf_op jit(solution)/shard_map/all_to_all | solution.py:625
  61.8 12.1 %collective-permute-start.8 = (bf16[2048,128]{1,0:T(8,128)(2,1)}, bf16[2048,128]{1,0:T(8,128)(2,1)}, u32[]{:S(2)}, u32[]{:S(2)}) collective-permute-start(bf16[2048,128]{1,0:T(8,128)(2,1)} %get-tuple-element.44.refs_8_.refs_3_), channel_id=1, source_target_pairs={{0,1},{1,0},{2,3},{3,2},{4,5},{5,4},{6,7},{7,6},{8,9},{9,8},{10,11... | collective-permute-start | bytes 1572872 | tf_op jit(solution)/shard_map/ppermute | solution.py:583
  71.6 2.4 %collective-permute-start.9 = (bf16[2048,128]{1,0:T(8,128)(2,1)}, bf16[2048,128]{1,0:T(8,128)(2,1)S(1)}, u32[]{:S(2)}, u32[]{:S(2)}) collective-permute-start(bf16[2048,128]{1,0:T(8,128)(2,1)} %collective-permute-done.7.refs_5_), channel_id=1, source_target_pairs={{0,1},{1,0},{2,3},{3,2},{4,5},{5,4},{6,7},{7,6},{8,9},{9,8},{10,11... | collective-permute-start | bytes 1572872 | tf_op jit(solution)/shard_map/ppermute | solution.py:583
  71.6 2.4 %collective-permute-start.11 = (bf16[2,2,128,128]{3,2,1,0:T(8,128)(2,1)}, bf16[2,2,128,128]{3,2,1,0:T(8,128)(2,1)S(1)}, u32[]{:S(2)}, u32[]{:S(2)}) collective-permute-start(bf16[2,2,128,128]{3,2,1,0:T(8,128)(2,1)} %collective-permute-done.1.refs_9_), channel_id=1, source_target_pairs={{0,1},{1,0},{2,3},{3,2},{4,5},{5,4},{6,7},{7,6},{8,9},{9,8},{10,11... | collective-permute-start | bytes 393224 | tf_op jit(solution)/shard_map/ppermute | solution.py:583
  72.1 1.6 %collective-permute-start.10 = (bf16[2,128,128]{2,1,0:T(8,128)(2,1)S(1)}, bf16[2,128,128]{2,1,0:T(8,128)(2,1)S(1)}, u32[]{:S(2)}, u32[]{:S(2)}) collective-permute-start(bf16[2,128,128]{2,1,0:T(8,128)(2,1)S(1)} %copy-done.3), channel_id=1, source_target_pairs={{0,1},{1,0},{2,3},{3,2},{4,5},{5,4},{6,7},{7,6},{8,9},{9,8},{10,11... | collective-permute-start | bytes 196616 | tf_op jit(solution)/shard_map/ppermute | solution.py:583
  73.7 0.6 copy-start.2
  74.0 0.7 copy-start.1
  82.1 20.7 %all-to-all-start.2 = ((bf16[8,288,128]{2,1,0:T(8,128)(2,1)}), bf16[8,288,128]{2,1,0:T(8,128)(2,1)}, u32[]{:S(2)}, u32[]{:S(2)}) async-start(bf16[8,288,128]{2,1,0:T(8,128)(2,1)} %get-tuple-element.50), calls=%async_computation.2 | async-start | bytes 1179648 | tf_op jit(solution)/shard_map/all_to_all | solution.py:632

commit v8 on v4

--- a/solution.py
+++ b/solution.py
@@ -41,7 +41,7 @@
         copy.wait()
 
 
-def pick_kernel(rows_h, count_h, hub_h, x_h, out_h, rows_s, count_s, hub_s, x, x32, stage, out, sems):
+def pick_kernel(rows_h, count_h, hub_h, x_h, out_h, rows_s, count_s, hub_s, x, x32, stage, out, sems, out_sems):
     copies = start_copies(sems, (x_h, x), (rows_h, rows_s), (count_h, count_s), (hub_h, hub_s))
     n_dom, capacity = rows_s.shape
     hub_dev = hub_s.shape[0]
@@ -64,10 +64,12 @@
         kept = jnp.where(slot < count_s[0, q], stage[:capacity, :], 0.0)
         out[q, :capacity, :] = kept.astype(BF16)
         out[q, capacity:, :] = hub
+        pltpu.make_async_copy(out.at[q], out_h.at[q], out_sems.at[q]).start()
         return carry
 
     lax.fori_loop(0, n_dom, peer, 0)
-    wait_copies(start_copies(sems, (out, out_h)))
+    for q in range(n_dom):
+        pltpu.make_async_copy(out.at[q], out_h.at[q], out_sems.at[q]).wait()
 
 
 def pick(send_rows, send_count, hub_ids, x):
@@ -88,6 +90,7 @@
             pltpu.VMEM((rows, x.shape[1]), F32),
             pltpu.VMEM(shape, BF16),
             pltpu.SemaphoreType.DMA((4,)),
+            pltpu.SemaphoreType.DMA((n_dom,)),
         ],
         compiler_params=params(),
         cost_estimate=cost(0, 1 << 21),
@@ -155,12 +158,15 @@
     lax.fori_loop(0, (n + UNROLL - 1) // UNROLL, group, 0)
 
 
-def own_kernel(dst_h, src_h, tiles, x_h, out_h, lists, dst_s, src_s, x, acc, sems, *, far_blocks):
+def own_kernel(
+    dst_h, src_h, tiles_h, x_h, out_h, lists, dst_s, src_s, x, tiles, acc, sems, *, far_blocks
+):
     own_blocks = x.shape[0]
-    copies = start_copies(sems, (x_h, x), (dst_h, dst_s), (src_h, src_s))
+    copies = start_copies(sems, (dst_h, dst_s), (src_h, src_s), (x_h, x), (tiles_h, tiles))
     acc[...] = jnp.zeros_like(acc)
-    wait_copies(copies)
+    wait_copies(copies[:2])
     make_lists(dst_s, src_s, lists, own_blocks, far_blocks)
+    wait_copies(copies[2:])
     add_tiles(lists, 0, tiles, x, acc, own_blocks)
     wait_copies(start_copies(sems, (acc.at[pl.ds(0, own_blocks)], out_h)))
 
@@ -173,19 +179,20 @@
             pltpu.HBM(x.shape, F32),
             jax.ShapeDtypeStruct((2, n + UNROLL), jnp.int32),
         ),
-        in_specs=[HBM, HBM, VMEM, HBM],
+        in_specs=[HBM, HBM, HBM, HBM],
         out_specs=(HBM, SMEM),
         scratch_shapes=[
             pltpu.SMEM((n,), jnp.int32),
             pltpu.SMEM((n,), jnp.int32),
             pltpu.VMEM(x.shape, BF16),
+            pltpu.VMEM(tiles.shape, BF16),
             pltpu.VMEM((x.shape[0] + 1,) + x.shape[1:], F32),
-            pltpu.SemaphoreType.DMA((3,)),
+            pltpu.SemaphoreType.DMA((4,)),
         ],
         compiler_params=params(),
         cost_estimate=cost(2 * n * 128**3, 1 << 23),
         name="own_tiles",
-    )(hbm(tile_dst), hbm(tile_src), tiles, hbm(x))
+    )(hbm(tile_dst), hbm(tile_src), hbm(tiles), hbm(x))
 
 
 def far_kernel(lists, tiles, incoming_h, base_h, out_h, source, acc, out, sems):
@@ -256,7 +263,7 @@
         wait_copies(copies)
 
 
-def stream_call(kernel, me, streamed, whole, outs, flops, name, block=512):
+def stream_call(kernel, me, streamed, whole, outs, flops, name, block=256):
     rows = streamed[0].shape[0]
     n_in, n_whole, n_out = len(streamed), len(whole), len(outs)
 
@@ -358,7 +365,9 @@
     block = 4 * tile
     pending = split_copies(sems, list(zip(grads_h, grads)), block)
     acc[...] = jnp.zeros_like(acc)
-    rows = jnp.concatenate([r[...].reshape(2 * width, -1) for r in w], axis=1)
+    own_w, near_w, far_w, both_w = w
+    rows = [r.reshape(2 * width, -1) for r in (own_w[...], near_w[...], far_w[0], both_w[1])]
+    rows = jnp.concatenate(rows, axis=1)
     for i, copies in enumerate(pending):
         wait_copies(copies)
         whole = jnp.concatenate([g[i * block : (i + 1) * block, :] for g in grads], axis=1)
@@ -398,7 +407,7 @@
         compiler_params=params(),
         cost_estimate=cost(4 * rows * width * width * n_feat, 1 << 22),
         name="back_far",
-    )(lists, tiles, *grads, *w)
+    )(lists, tiles, *grads, *[hbm(r) for r in w])
 
 
 def back_own_kernel(lists, tiles, back_h, direct_h, out_h, back, acc, sems):
@@ -494,19 +503,21 @@
 
 def cut_kernel(me_s, w_self, w_neigh, *outs):
     width = w_self.shape[1]
-    for k, out in enumerate(outs):
+    own, near, far = outs
+    for k, out in enumerate((own, near, far.at[0], far.at[1])):
         at = pl.ds(pl.multiple_of((me_s[0] ^ k) * width, width), width)
         out[0] = w_self[at, :]
         out[1] = w_neigh[at, :]
 
 
-def cut_weights(me, w_self, w_neigh, n_feat):
+def cut_weights(me, w_self, w_neigh):
     width = w_self.shape[1]
+    one = (2, width, width)
     return pl.pallas_call(
         cut_kernel,
-        out_shape=(pltpu.HBM((2, width, width), BF16),) * n_feat,
+        out_shape=tuple(pltpu.HBM(shape, BF16) for shape in (one, one, (2,) + one)),
         in_specs=[SMEM, VMEM, VMEM],
-        out_specs=(VMEM,) * n_feat,
+        out_specs=(VMEM,) * 3,
         compiler_params=params(),
         cost_estimate=cost(0, 1 << 20),
         name="cut_weights",
@@ -592,10 +603,14 @@
 
     outgoing = pick(listed, send_count, hub_ids, node_feats)
     incoming = lax.all_to_all(outgoing, "dom", 0, 0, tiled=True)
-    own_feats = node_feats.reshape(-1, tile_size, width)
+    cut = cut_weights(me_s, w_self, w_neigh)
+    own_feats, *cut = lax.optimization_barrier((node_feats.reshape(-1, tile_size, width), *cut))
+    far_w = swap(cut[2], far)
     base, lists = own_tiles(tile_dst, tile_src, edge_tiles, own_feats, far_blocks)
     aggregated = far_tiles(lists, edge_tiles, incoming, base, far_blocks).reshape(own_count, width)
 
+    aggregated, far_w = lax.optimization_barrier((aggregated, far_w))
+    w_rows = [cut[0], swap(cut[1], near), far_w, swap(far_w, near)]
     agg_far = swap(aggregated, far)
     feat_far, aggregated = lax.optimization_barrier((feat_far, aggregated))
     feats = [hbm(node_feats), swap(node_feats, near), feat_far, swap(feat_far, near)]
@@ -610,9 +625,7 @@
         flops,
         "self_dense",
     )
-    cut = cut_weights(me_s, w_self, w_neigh, n_feat)
-    agg_far, own_part, *cut = lax.optimization_barrier((agg_far, own_part, *cut))
-    w_rows = [hbm(cut[0])] + [swap(cut[k], k) for k in range(1, n_feat)]
+    agg_far, own_part, *w_rows = lax.optimization_barrier((agg_far, own_part, *w_rows))
     aggs = [hbm(aggregated), swap(aggregated, near), agg_far, swap(agg_far, near)]
     output, grad_pre = stream_call(
         forward_step,

time: 106 us -> 106 us (level)
  waiting for transfers between devices: 26.1 us -> 28.5 us
  local copies, waits for them, and re-layouts: 1.99 us -> 0.02 us
  starting transfers between devices: 27.7 us -> 26.5 us
  Pallas kernels: 48.4 us -> 49.5 us
    all_to_all x1, waiting for transfers between devices: 0.01 us -> 2.84 us  [body(): part_sums = lax.all_to_all(parts, 'dom', 0, 0, tiled=True)]
    unnamed x6 -> x8, local copies, waits for them, and re-layouts: 1.99 us -> 0.02 us
    pallas_call x2, Pallas kernels: 9.21 us -> 10.8 us  [stream_call(): pl.pallas_call(run, out_shape=tuple((pltpu.HBM(shape, t) for shape, t in...]
    ppermute x12, starting transfers between devices: 6.96 us -> 5.88 us  [swap(): return lax.ppermute(x, 'feat', [(j, j ^ k) for j in range(n_feat)])]
  transfers between devices with their start and end apart: 16 -> 16, of which waited for: 9 -> 9; matrix products, arithmetic and copies ran while one was open for 0% -> 0% of each run, Pallas kernels for 37% -> 36%
where the time goes in v8:
time: 106 us; the launch traced here: 105 us
  Pallas kernels  49.5 us (47%)
  waiting for transfers between devices  28.5 us (27%)
  starting transfers between devices  26.5 us (25%)
    ppermute x12, waiting for transfers between devices, swap(): return lax.ppermute(x, 'feat', [(j, j ^ k) for j in range(n_feat)])  16.3 us
    pallas_call x2, Pallas kernels, stream_call(): pl.pallas_call(run, out_shape=tuple((pltpu.HBM(shape, t) for shape, t in...  10.8 us
    all_to_all x1, starting transfers between devices, body(): incoming = lax.all_to_all(outgoing, 'dom', 0, 0, tiled=True)  7.26 us
    pallas_call x1, Pallas kernels, back_far(): pl.pallas_call(functools.partial(back_far_kernel, n_feat=n_feat), out_sha...  7.19 us
    ppermute x12, starting transfers between devices, swap(): return lax.ppermute(x, 'feat', [(j, j ^ k) for j in range(n_feat)])  5.88 us
    all_to_all x1, starting transfers between devices, body(): part_sums = lax.all_to_all(parts, 'dom', 0, 0, tiled=True)  5.73 us
    pallas_call x1, Pallas kernels, own_tiles(): pl.pallas_call(functools.partial(own_kernel, far_blocks=far_blocks), out_...  5.35 us
    pallas_call x1, Pallas kernels, back_own(): pl.pallas_call(back_own_kernel, out_shape=pltpu.HBM(direct.shape, F32), i...  4.86 us
  transfers between devices with their start and end apart: 16, of which 9 were waited for; matrix products, arithmetic and copies ran while one was open for 0% of the time, Pallas kernels for 36%

profile of v8, /device:TPU:0, one launch (start us, length us, event | category | flops | bytes accessed | tf_op | source)
XLA Modules:
  0.0 105.3 jit_solution(9502484213626130450)
XLA Ops:
  0.6 4.6 %pick_rows.1 = bf16[8,160,128]{2,1,0:T(8,128)(2,1)} custom-call(s32[8,128]{1,0:T(8,128)} %bitcast.15, s32[1,8]{1,0:T(1,128)} %count_h.3, s32[32]{0:T(128)} %hub_h.3, bf16[2048,128]{1,0:T(8,128)(2,1)} %refs_0_.3), custom_call_target="tpu_custom_call" | custom-call | bytes 2097152 | tf_op jit(solution)/shard_map/pick_rows/pallas_call | solution.py:79
  5.2 7.3 %all-to-all-start = ((bf16[8,160,128]{2,1,0:T(8,128)(2,1)}), bf16[8,160,128]{2,1,0:T(8,128)(2,1)}, u32[]{:S(2)}, u32[]{:S(2)}) async-start(bf16[8,160,128]{2,1,0:T(8,128)(2,1)} %pick_rows.1), calls=%async_computation | async-start | bytes 655360 | tf_op jit(solution)/shard_map/all_to_all | solution.py:605
  12.5 1.5 %collective-permute-start = (bf16[2048,128]{1,0:T(8,128)(2,1)}, bf16[2048,128]{1,0:T(8,128)(2,1)}, u32[]{:S(2)}, u32[]{:S(2)}) collective-permute-start(bf16[2048,128]{1,0:T(8,128)(2,1)} %refs_0_.3), channel_id=1, source_target_pairs={{0,2},{1,3},{2,0},{3,1},{4,6},{5,7},{6,4},{7,5},{8,10},{9,11},{10,... | collective-permute-start | bytes 1572872 | tf_op jit(solution)/shard_map/ppermute | solution.py:600
  14.0 1.7 %cut_weights.1 = (bf16[2,128,128]{2,1,0:T(8,128)(2,1)}, bf16[2,128,128]{2,1,0:T(8,128)(2,1)}, bf16[2,2,128,128]{3,2,1,0:T(8,128)(2,1)}) custom-call(s32[1]{0:T(128)} %bitcast.me_s, bf16[512,128]{1,0:T(8,128)(2,1)} %refs_4_.1, bf16[512,128]{1,0:T(8,128)(2,1)} %refs_6_.1), custom_call_target="tpu_custom_call" | custom-call | bytes 1048576 | tf_op jit(solution)/shard_map/cut_weights/pallas_call | solution.py:516
  15.7 0.5 collective-permute-start.1
  16.2 5.4 %own_tiles.1 = (f32[16,128,128]{2,1,0:T(8,128)}, s32[2,114]{1,0:T(2,128)S(1)}) custom-call(s32[106]{0:T(128)} %dst_h.1, s32[106]{0:T(128)} %src_h.1, bf16[106,128,128]{2,1,0:T(8,128)(2,1)} %tiles.3, bf16[16,128,128]{2,1,0:T(8,128)(2,1)} %bitcast.9), custom_call_target="tpu_custom_call" | custom-call | flops 444596224 | bytes 8388608 | tf_op jit(solution)/shard_map/own_tiles/pallas_call | solution.py:176
  21.6 1.4 %all-to-all-done.incoming_h = bf16[8,160,128]{2,1,0:T(8,128)(2,1)} async-done(((bf16[8,160,128]{2,1,0:T(8,128)(2,1)}), bf16[8,160,128]{2,1,0:T(8,128)(2,1)}, u32[]{:S(2)}, u32[]{:S(2)}) %all-to-all-start) | async-done | bytes 327712 | tf_op jit(solution)/shard_map/all_to_all | solution.py:605
  22.9 4.5 %far_tiles.1 = bf16[16,128,128]{2,1,0:T(8,128)(2,1)} custom-call(s32[2,114]{1,0:T(2,128)S(1)} %get-tuple-element.40.lists.refs_0_, bf16[106,128,128]{2,1,0:T(8,128)(2,1)S(1)} %copy-done, bf16[8,160,128]{2,1,0:T(8,128)(2,1)} %all-to-all-done.incoming_h, f32[16,128,128]{2,1,0:T(8,128)} %get-tuple-element.41.base_h), custom_call_target="tpu_custom_call" | custom-call | flops 222298112 | bytes 4194304 | tf_op jit(solution)/shard_map/far_tiles/pallas_call | solution.py:218
  27.5 1.6 %collective-permute-done.1.refs_8_ = bf16[2,2,128,128]{3,2,1,0:T(8,128)(2,1)} collective-permute-done((bf16[2,2,128,128]{3,2,1,0:T(8,128)(2,1)}, bf16[2,2,128,128]{3,2,1,0:T(8,128)(2,1)}, u32[]{:S(2)}, u32[]{:S(2)}) %collective-permute-start.1) | collective-permute-done | bytes 131104 | tf_op jit(solution)/shard_map/ppermute | solution.py:600
  29.0 1.5 %collective-permute-start.3 = (bf16[2048,128]{1,0:T(8,128)(2,1)}, bf16[2048,128]{1,0:T(8,128)(2,1)S(1)}, u32[]{:S(2)}, u32[]{:S(2)}) collective-permute-start(bf16[2048,128]{1,0:T(8,128)(2,1)} %bitcast.10), channel_id=1, source_target_pairs={{0,2},{1,3},{2,0},{3,1},{4,6},{5,7},{6,4},{7,5},{8,10},{9,11},{10,... | collective-permute-start | bytes 1572872 | tf_op jit(solution)/shard_map/ppermute | solution.py:600
  30.5 0.2 collective-permute-start.7
  30.8 0.3 collective-permute-start.6
  31.1 0.2 collective-permute-start.2
  31.3 4.6 %self_dense.1.refs_4_ = f32[2048,128]{1,0:T(8,128)} custom-call(s32[1]{0:T(128)} %bitcast.me_s, bf16[2048,128]{1,0:T(8,128)(2,1)} %refs_0_.3, bf16[2048,128]{1,0:T(8,128)(2,1)} %collective-permute-done.4.refs_1_, bf16[2048,128]{1,0:T(8,128)(2,1)} %collective-permute-done.refs_2_, bf16[2048,128]{1,0:T(8,128)(2,1)S(1)} %collective-permute-done.5.refs_3_, ...), custom_call_target="tpu_custom_call" | custom-call | flops 268435456 | bytes 4194304 | tf_op jit(solution)/shard_map/self_dense/pallas_call | solution.py:280
  36.0 7.6 %collective-permute-done.3.refs_2_.refs_6_ = bf16[2048,128]{1,0:T(8,128)(2,1)S(1)} collective-permute-done((bf16[2048,128]{1,0:T(8,128)(2,1)}, bf16[2048,128]{1,0:T(8,128)(2,1)S(1)}, u32[]{:S(2)}, u32[]{:S(2)}) %collective-permute-start.3) | collective-permute-done | bytes 524320 | tf_op jit(solution)/shard_map/ppermute | solution.py:600
  43.6 1.9 %collective-permute-done.8.refs_3_.refs_7_ = bf16[2048,128]{1,0:T(8,128)(2,1)S(1)} collective-permute-done((bf16[2048,128]{1,0:T(8,128)(2,1)S(1)}, bf16[2048,128]{1,0:T(8,128)(2,1)S(1)}, u32[]{:S(2)}, u32[]{:S(2)}) %collective-permute-start.8) | collective-permute-done | bytes 524320 | tf_op jit(solution)/shard_map/ppermute | solution.py:600
  45.5 6.1 %forward_dense.1 = (bf16[2048,128]{1,0:T(8,128)(2,1)}, bf16[2048,128]{1,0:T(8,128)(2,1)}) custom-call(s32[1]{0:T(128)} %bitcast.me_s, bf16[2048,128]{1,0:T(8,128)(2,1)} %bitcast.12, bf16[2048,128]{1,0:T(8,128)(2,1)S(1)} %collective-permute-done.2.refs_1_.refs_5_, bf16[2048,128]{1,0:T(8,128)(2,1)S(1)} %collective-permute-done.3.refs_2_.refs_6_, ...), custom_call_target="tpu_custom_call" | custom-call | flops 268435456 | bytes 4194304 | tf_op jit(solution)/shard_map/forward_dense/pallas_call | solution.py:280
  51.6 1.6 %collective-permute-start.10 = (bf16[2048,128]{1,0:T(8,128)(2,1)}, bf16[2048,128]{1,0:T(8,128)(2,1)}, u32[]{:S(2)}, u32[]{:S(2)}) collective-permute-start(bf16[2048,128]{1,0:T(8,128)(2,1)} %get-tuple-element.52.refs_8_.refs_2_), channel_id=1, source_target_pairs={{0,2},{1,3},{2,0},{3,1},{4,6},{5,7},{6,4},{7,5},{8,10},{9,11},{10,... | collective-permute-start | bytes 1572872 | tf_op jit(solution)/shard_map/ppermute | solution.py:600
  53.2 3.9 %weight_parts.1 = f32[8,136,128]{2,1,0:T(8,128)} custom-call(bf16[2048,128]{1,0:T(8,128)(2,1)} %refs_0_.3, bf16[2048,128]{1,0:T(8,128)(2,1)} %collective-permute-done.4.refs_1_, bf16[2048,128]{1,0:T(8,128)(2,1)} %collective-permute-done.refs_2_, bf16[2048,128]{1,0:T(8,128)(2,1)S(1)} %collective-permute-done.5.refs_3_, bf16[2048,128]{1,0:T(8,128)(2,1)} %bitcast.13, ...), custom_call_target="tpu_custom_call" | custom-call | flops 536870912 | bytes 4194304 | tf_op jit(solution)/shard_map/weight_parts/pallas_call | solution.py:330
  57.1 5.7 %all-to-all-start.1 = ((f32[8,136,128]{2,1,0:T(8,128)}), f32[8,136,128]{2,1,0:T(8,128)}, u32[]{:S(2)}, u32[]{:S(2)}) async-start(f32[8,136,128]{2,1,0:T(8,128)} %weight_parts.1), calls=%async_computation.1 | async-start | bytes 1114112 | tf_op jit(solution)/shard_map/all_to_all | solution.py:642
  62.8 3.1 %collective-permute-done.10.refs_4_ = bf16[2048,128]{1,0:T(8,128)(2,1)} collective-permute-done((bf16[2048,128]{1,0:T(8,128)(2,1)}, bf16[2048,128]{1,0:T(8,128)(2,1)}, u32[]{:S(2)}, u32[]{:S(2)}) %collective-permute-start.10) | collective-permute-done | bytes 524320 | tf_op jit(solution)/shard_map/ppermute | solution.py:600
  66.0 2.1 %collective-permute-done.11.refs_5_ = bf16[2048,128]{1,0:T(8,128)(2,1)S(1)} collective-permute-done((bf16[2048,128]{1,0:T(8,128)(2,1)}, bf16[2048,128]{1,0:T(8,128)(2,1)S(1)}, u32[]{:S(2)}, u32[]{:S(2)}) %collective-permute-start.11) | collective-permute-done | bytes 524320 | tf_op jit(solution)/shard_map/ppermute | solution.py:600
  68.1 7.2 %back_far.1 = (bf16[8,160,128]{2,1,0:T(8,128)(2,1)}, bf16[16,128,128]{2,1,0:T(8,128)(2,1)}, f32[16,128,128]{2,1,0:T(8,128)}) custom-call(s32[2,114]{1,0:T(2,128)S(1)} %get-tuple-element.40.lists.refs_0_, bf16[106,128,128]{2,1,0:T(8,128)(2,1)S(1)} %copy-done, bf16[2048,128]{1,0:T(8,128)(2,1)} %get-tuple-element.52.refs_8_.refs_2_, ...), custom_call_target="tpu_custom_call" | custom-call | flops 536870912 | bytes 4194304 | tf_op jit(solution)/shard_map/back_far/pallas_call | solution.py:393
  75.3 2.8 %all-to-all-done.1.parts = f32[8,136,128]{2,1,0:T(8,128)} async-done(((f32[8,136,128]{2,1,0:T(8,128)}), f32[8,136,128]{2,1,0:T(8,128)}, u32[]{:S(2)}, u32[]{:S(2)}) %all-to-all-start.1) | async-done | bytes 557088 | tf_op jit(solution)/shard_map/all_to_all | solution.py:642
  78.1 4.1 %all-to-all-start.2 = ((bf16[8,160,128]{2,1,0:T(8,128)(2,1)}), bf16[8,160,128]{2,1,0:T(8,128)(2,1)}, u32[]{:S(2)}, u32[]{:S(2)}) async-start(bf16[8,160,128]{2,1,0:T(8,128)(2,1)} %get-tuple-element.58), calls=%async_computation.2 | async-start | bytes 655360 | tf_op jit(solution)/shard_map/all_to_all | solution.py:648
  82.2 1.8 %sum_parts.1 = (bf16[8,128,128]{2,1,0:T(8,128)(2,1)}, f32[1,128]{1,0:T(1,128)}) custom-call(f32[8,136,128]{2,1,0:T(8,128)} %all-to-all-done.1.parts), custom_call_target="tpu_custom_call" | custom-call | bytes 1048576 | tf_op jit(solution)/shard_map/sum_parts/pallas_call | solution.py:540
  84.0 4.9 %back_own.1 = f32[16,128,128]{2,1,0:T(8,128)} custom-call(s32[2,114]{1,0:T(2,128)S(1)} %get-tuple-element.40.lists.refs_0_, bf16[106,128,128]{2,1,0:T(8,128)(2,1)S(1)} %copy-done, bf16[16,128,128]{2,1,0:T(8,128)(2,1)} %get-tuple-element.59.back_h, f32[16,128,128]{2,1,0:T(8,128)} %get-tuple-element.60.direct_h), custom_call_target="tpu_custom_call" | custom-call | flops 444596224 | bytes 8388608 | tf_op jit(solution)/shard_map/back_own/pallas_call | solution.py:422
  88.9 3.5 %all-to-all-done.2.incoming_h = bf16[8,160,128]{2,1,0:T(8,128)(2,1)} async-done(((bf16[8,160,128]{2,1,0:T(8,128)(2,1)}), bf16[8,160,128]{2,1,0:T(8,128)(2,1)}, u32[]{:S(2)}, u32[]{:S(2)}) %all-to-all-start.2) | async-done | bytes 327712 | tf_op jit(solution)/shard_map/all_to_all | solution.py:648
  92.4 3.6 %all-to-all-start.3 = ((bf16[8,128,128]{2,1,0:T(8,128)(2,1)}), bf16[8,128,128]{2,1,0:T(8,128)(2,1)S(1)}, u32[]{:S(2)}, u32[]{:S(2)}) async-start(bf16[8,128,128]{2,1,0:T(8,128)(2,1)} %get-tuple-element.63), calls=%async_computation.3 | async-start | bytes 524288 | tf_op jit(solution)/shard_map/all_to_all | solution.py:652
  95.9 4.1 %finish.1 = f32[2048,128]{1,0:T(8,128)} custom-call(s32[8,128]{1,0:T(8,128)} %bitcast.16, s32[1,8]{1,0:T(1,128)} %count_h.3, s32[32]{0:T(128)} %hub_h.3, bf16[8,160,128]{2,1,0:T(8,128)(2,1)} %all-to-all-done.2.incoming_h, f32[2048,128]{1,0:T(8,128)} %bitcast.14), custom_call_target="tpu_custom_call" | custom-call | flops 536870912 | bytes 4194304 | tf_op jit(solution)/shard_map/finish/pallas_call | solution.py:484
  100.0 4.5 %all-to-all-done.3 = bf16[8,128,128]{2,1,0:T(8,128)(2,1)S(1)} async-done(((bf16[8,128,128]{2,1,0:T(8,128)(2,1)}), bf16[8,128,128]{2,1,0:T(8,128)(2,1)S(1)}, u32[]{:S(2)}, u32[]{:S(2)}) %all-to-all-start.3) | async-done | bytes 262176 | tf_op jit(solution)/shard_map/all_to_all | solution.py:652
  104.5 0.8 place_weights.1
  (20 shorter events, 0.1 us)
Async XLA Ops:
  0.6 22.3 %copy-start = (bf16[106,128,128]{2,1,0:T(8,128)(2,1)S(1)}, bf16[106,128,128]{2,1,0:T(8,128)(2,1)}, u32[]{:S(2)}) copy-start(bf16[106,128,128]{2,1,0:T(8,128)(2,1)} %tiles.3) | copy-start | bytes 10420228
  5.2 17.7 %all-to-all-start = ((bf16[8,160,128]{2,1,0:T(8,128)(2,1)}), bf16[8,160,128]{2,1,0:T(8,128)(2,1)}, u32[]{:S(2)}, u32[]{:S(2)}) async-start(bf16[8,160,128]{2,1,0:T(8,128)(2,1)} %pick_rows.1), calls=%async_computation | async-start | bytes 655360 | tf_op jit(solution)/shard_map/all_to_all | solution.py:605
  12.5 16.5 %collective-permute-start = (bf16[2048,128]{1,0:T(8,128)(2,1)}, bf16[2048,128]{1,0:T(8,128)(2,1)}, u32[]{:S(2)}, u32[]{:S(2)}) collective-permute-start(bf16[2048,128]{1,0:T(8,128)(2,1)} %refs_0_.3), channel_id=1, source_target_pairs={{0,2},{1,3},{2,0},{3,1},{4,6},{5,7},{6,4},{7,5},{8,10},{9,11},{10,... | collective-permute-start | bytes 1572872 | tf_op jit(solution)/shard_map/ppermute | solution.py:600
  15.7 13.3 %collective-permute-start.1 = (bf16[2,2,128,128]{3,2,1,0:T(8,128)(2,1)}, bf16[2,2,128,128]{3,2,1,0:T(8,128)(2,1)}, u32[]{:S(2)}, u32[]{:S(2)}) collective-permute-start(bf16[2,2,128,128]{3,2,1,0:T(8,128)(2,1)} %get-tuple-element.42), channel_id=1, source_target_pairs={{0,2},{1,3},{2,0},{3,1},{4,6},{5,7},{6,4},{7,5},{8,10},{9,11},{10,... | collective-permute-start | bytes 393224 | tf_op jit(solution)/shard_map/ppermute | solution.py:600
  16.2 14.8 %collective-permute-start.4 = (bf16[2048,128]{1,0:T(8,128)(2,1)}, bf16[2048,128]{1,0:T(8,128)(2,1)}, u32[]{:S(2)}, u32[]{:S(2)}) collective-permute-start(bf16[2048,128]{1,0:T(8,128)(2,1)} %refs_0_.3), channel_id=1, source_target_pairs={{0,1},{1,0},{2,3},{3,2},{4,5},{5,4},{6,7},{7,6},{8,9},{9,8},{10,11... | collective-permute-start | bytes 1572872 | tf_op jit(solution)/shard_map/ppermute | solution.py:600
  22.9 7.8 %copy-start.3 = (bf16[2,128,128]{2,1,0:T(8,128)(2,1)S(1)}, bf16[2,128,128]{2,1,0:T(8,128)(2,1)}, u32[]{:S(2)}) copy-start(bf16[2,128,128]{2,1,0:T(8,128)(2,1)} %get-tuple-element.47) | copy-start | bytes 196612
  29.0 2.3 %collective-permute-start.5 = (bf16[2048,128]{1,0:T(8,128)(2,1)}, bf16[2048,128]{1,0:T(8,128)(2,1)S(1)}, u32[]{:S(2)}, u32[]{:S(2)}) collective-permute-start(bf16[2048,128]{1,0:T(8,128)(2,1)} %collective-permute-done.refs_2_), channel_id=1, source_target_pairs={{0,1},{1,0},{2,3},{3,2},{4,5},{5,4},{6,7},{7,6},{8,9},{9,8},{10,11... | collective-permute-start | bytes 1572872 | tf_op jit(solution)/shard_map/ppermute | solution.py:600
  29.0 14.5 %collective-permute-start.3 = (bf16[2048,128]{1,0:T(8,128)(2,1)}, bf16[2048,128]{1,0:T(8,128)(2,1)S(1)}, u32[]{:S(2)}, u32[]{:S(2)}) collective-permute-start(bf16[2048,128]{1,0:T(8,128)(2,1)} %bitcast.10), channel_id=1, source_target_pairs={{0,2},{1,3},{2,0},{3,1},{4,6},{5,7},{6,4},{7,5},{8,10},{9,11},{10,... | collective-permute-start | bytes 1572872 | tf_op jit(solution)/shard_map/ppermute | solution.py:600
  30.5 5.4 %collective-permute-start.7 = (bf16[2,2,128,128]{3,2,1,0:T(8,128)(2,1)}, bf16[2,2,128,128]{3,2,1,0:T(8,128)(2,1)S(1)}, u32[]{:S(2)}, u32[]{:S(2)}) collective-permute-start(bf16[2,2,128,128]{3,2,1,0:T(8,128)(2,1)} %collective-permute-done.1.refs_8_), channel_id=1, source_target_pairs={{0,1},{1,0},{2,3},{3,2},{4,5},{5,4},{6,7},{7,6},{8,9},{9,8},{10,11... | collective-permute-start | bytes 393224 | tf_op jit(solution)/shard_map/ppermute | solution.py:600
  30.8 5.2 %collective-permute-start.6 = (bf16[2,128,128]{2,1,0:T(8,128)(2,1)S(1)}, bf16[2,128,128]{2,1,0:T(8,128)(2,1)S(1)}, u32[]{:S(2)}, u32[]{:S(2)}) collective-permute-start(bf16[2,128,128]{2,1,0:T(8,128)(2,1)S(1)} %copy-done.3), channel_id=1, source_target_pairs={{0,1},{1,0},{2,3},{3,2},{4,5},{5,4},{6,7},{7,6},{8,9},{9,8},{10,11... | collective-permute-start | bytes 196616 | tf_op jit(solution)/shard_map/ppermute | solution.py:600
  31.1 12.5 %collective-permute-start.2 = (bf16[2048,128]{1,0:T(8,128)(2,1)}, bf16[2048,128]{1,0:T(8,128)(2,1)S(1)}, u32[]{:S(2)}, u32[]{:S(2)}) collective-permute-start(bf16[2048,128]{1,0:T(8,128)(2,1)} %bitcast.11), channel_id=1, source_target_pairs={{0,1},{1,0},{2,3},{3,2},{4,5},{5,4},{6,7},{7,6},{8,9},{9,8},{10,11... | collective-permute-start | bytes 1572872 | tf_op jit(solution)/shard_map/ppermute | solution.py:600
  36.0 32.1 %copy-start.2 = (bf16[2,128,128]{2,1,0:T(8,128)(2,1)}, bf16[2,128,128]{2,1,0:T(8,128)(2,1)S(1)}, u32[]{:S(2)}) copy-start(bf16[2,128,128]{2,1,0:T(8,128)(2,1)S(1)} %collective-permute-done.6.refs_7_) | copy-start | bytes 196612
  36.0 9.5 %copy-start.1 = (bf16[2,2,128,128]{3,2,1,0:T(8,128)(2,1)}, bf16[2,2,128,128]{3,2,1,0:T(8,128)(2,1)S(1)}, u32[]{:S(2)}) copy-start(bf16[2,2,128,128]{3,2,1,0:T(8,128)(2,1)S(1)} %collective-permute-done.7.refs_9_) | copy-start | bytes 393220
  43.6 1.9 %collective-permute-start.8 = (bf16[2048,128]{1,0:T(8,128)(2,1)S(1)}, bf16[2048,128]{1,0:T(8,128)(2,1)S(1)}, u32[]{:S(2)}, u32[]{:S(2)}) collective-permute-start(bf16[2048,128]{1,0:T(8,128)(2,1)S(1)} %collective-permute-done.3.refs_2_.refs_6_), channel_id=1, source_target_pairs={{0,1},{1,0},{2,3},{3,2},{4,5},{5,4},{6,7},{7,6},{8,9},{9,8},{10,11... | collective-permute-start | bytes 1572872 | tf_op jit(solution)/shard_map/ppermute | solution.py:600
  51.6 14.3 %collective-permute-start.10 = (bf16[2048,128]{1,0:T(8,128)(2,1)}, bf16[2048,128]{1,0:T(8,128)(2,1)}, u32[]{:S(2)}, u32[]{:S(2)}) collective-permute-start(bf16[2048,128]{1,0:T(8,128)(2,1)} %get-tuple-element.52.refs_8_.refs_2_), channel_id=1, source_target_pairs={{0,2},{1,3},{2,0},{3,1},{4,6},{5,7},{6,4},{7,5},{8,10},{9,11},{10,... | collective-permute-start | bytes 1572872 | tf_op jit(solution)/shard_map/ppermute | solution.py:600
  57.1 21.0 %all-to-all-start.1 = ((f32[8,136,128]{2,1,0:T(8,128)}), f32[8,136,128]{2,1,0:T(8,128)}, u32[]{:S(2)}, u32[]{:S(2)}) async-start(f32[8,136,128]{2,1,0:T(8,128)} %weight_parts.1), calls=%async_computation.1 | async-start | bytes 1114112 | tf_op jit(solution)/shard_map/all_to_all | solution.py:642
  62.8 3.2 %collective-permute-start.9 = (bf16[2048,128]{1,0:T(8,128)(2,1)}, bf16[2048,128]{1,0:T(8,128)(2,1)S(1)}, u32[]{:S(2)}, u32[]{:S(2)}) collective-permute-start(bf16[2048,128]{1,0:T(8,128)(2,1)} %get-tuple-element.52.refs_8_.refs_2_), channel_id=1, source_target_pairs={{0,1},{1,0},{2,3},{3,2},{4,5},{5,4},{6,7},{7,6},{8,9},{9,8},{10,11... | collective-permute-start | bytes 1572872 | tf_op jit(solution)/shard_map/ppermute | solution.py:600
  65.9 2.1 %collective-permute-start.11 = (bf16[2048,128]{1,0:T(8,128)(2,1)}, bf16[2048,128]{1,0:T(8,128)(2,1)S(1)}, u32[]{:S(2)}, u32[]{:S(2)}) collective-permute-start(bf16[2048,128]{1,0:T(8,128)(2,1)} %collective-permute-done.10.refs_4_), channel_id=1, source_target_pairs={{0,1},{1,0},{2,3},{3,2},{4,5},{5,4},{6,7},{7,6},{8,9},{9,8},{10,11... | collective-permute-start | bytes 1572872 | tf_op jit(solution)/shard_map/ppermute | solution.py:600
  78.1 14.2 %all-to-all-start.2 = ((bf16[8,160,128]{2,1,0:T(8,128)(2,1)}), bf16[8,160,128]{2,1,0:T(8,128)(2,1)}, u32[]{:S(2)}, u32[]{:S(2)}) async-start(bf16[8,160,128]{2,1,0:T(8,128)(2,1)} %get-tuple-element.58), calls=%async_computation.2 | async-start | bytes 655360 | tf_op jit(solution)/shard_map/all_to_all | solution.py:648
  92.4 12.1 %all-to-all-start.3 = ((bf16[8,128,128]{2,1,0:T(8,128)(2,1)}), bf16[8,128,128]{2,1,0:T(8,128)(2,1)S(1)}, u32[]{:S(2)}, u32[]{:S(2)}) async-start(bf16[8,128,128]{2,1,0:T(8,128)(2,1)} %get-tuple-element.63), calls=%async_computation.3 | async-start | bytes 524288 | tf_op jit(solution)/shard_map/all_to_all | solution.py:652

commit v9 on v8

--- a/solution.py
+++ b/solution.py
@@ -263,7 +263,7 @@
         wait_copies(copies)
 
 
-def stream_call(kernel, me, streamed, whole, outs, flops, name, block=256):
+def stream_call(kernel, me, streamed, whole, outs, flops, name, block=512):
     rows = streamed[0].shape[0]
     n_in, n_whole, n_out = len(streamed), len(whole), len(outs)
 

time: 106 us -> 105 us (level)
  no operation moved by 1% of the time
where the time goes in v9:
time: 105 us; the launch traced here: 104 us
  Pallas kernels  48.5 us (46%)
  waiting for transfers between devices  28.6 us (27%)
  starting transfers between devices  26.5 us (25%)
    ppermute x12, waiting for transfers between devices, swap(): return lax.ppermute(x, 'feat', [(j, j ^ k) for j in range(n_feat)])  16.9 us
    pallas_call x2, Pallas kernels, stream_call(): pl.pallas_call(run, out_shape=tuple((pltpu.HBM(shape, t) for shape, t in...  9.78 us
    all_to_all x1, starting transfers between devices, body(): incoming = lax.all_to_all(outgoing, 'dom', 0, 0, tiled=True)  7.26 us
    pallas_call x1, Pallas kernels, back_far(): pl.pallas_call(functools.partial(back_far_kernel, n_feat=n_feat), out_sha...  6.63 us
    ppermute x12, starting transfers between devices, swap(): return lax.ppermute(x, 'feat', [(j, j ^ k) for j in range(n_feat)])  5.88 us
    pallas_call x1, Pallas kernels, own_tiles(): pl.pallas_call(functools.partial(own_kernel, far_blocks=far_blocks), out_...  5.81 us
    all_to_all x1, starting transfers between devices, body(): part_sums = lax.all_to_all(parts, 'dom', 0, 0, tiled=True)  5.73 us
    pallas_call x1, Pallas kernels, back_own(): pl.pallas_call(back_own_kernel, out_shape=pltpu.HBM(direct.shape, F32), i...  5.42 us
  transfers between devices with their start and end apart: 16, of which 9 were waited for; matrix products, arithmetic and copies ran while one was open for 0% of the time, Pallas kernels for 36%

profile of v9, /device:TPU:0, one launch (start us, length us, event | category | flops | bytes accessed | tf_op | source)
XLA Modules:
  0.0 104.4 jit_solution(8037156658061211681)
XLA Ops:
  0.6 4.6 %pick_rows.1 = bf16[8,160,128]{2,1,0:T(8,128)(2,1)} custom-call(s32[8,128]{1,0:T(8,128)} %bitcast.15, s32[1,8]{1,0:T(1,128)} %count_h.3, s32[32]{0:T(128)} %hub_h.3, bf16[2048,128]{1,0:T(8,128)(2,1)} %refs_0_.3), custom_call_target="tpu_custom_call" | custom-call | bytes 2097152 | tf_op jit(solution)/shard_map/pick_rows/pallas_call | solution.py:79
  5.2 7.3 %all-to-all-start = ((bf16[8,160,128]{2,1,0:T(8,128)(2,1)}), bf16[8,160,128]{2,1,0:T(8,128)(2,1)}, u32[]{:S(2)}, u32[]{:S(2)}) async-start(bf16[8,160,128]{2,1,0:T(8,128)(2,1)} %pick_rows.1), calls=%async_computation | async-start | bytes 655360 | tf_op jit(solution)/shard_map/all_to_all | solution.py:605
  12.5 1.5 %collective-permute-start = (bf16[2048,128]{1,0:T(8,128)(2,1)}, bf16[2048,128]{1,0:T(8,128)(2,1)}, u32[]{:S(2)}, u32[]{:S(2)}) collective-permute-start(bf16[2048,128]{1,0:T(8,128)(2,1)} %refs_0_.3), channel_id=1, source_target_pairs={{0,2},{1,3},{2,0},{3,1},{4,6},{5,7},{6,4},{7,5},{8,10},{9,11},{10,... | collective-permute-start | bytes 1572872 | tf_op jit(solution)/shard_map/ppermute | solution.py:600
  14.0 1.7 %cut_weights.1 = (bf16[2,128,128]{2,1,0:T(8,128)(2,1)}, bf16[2,128,128]{2,1,0:T(8,128)(2,1)}, bf16[2,2,128,128]{3,2,1,0:T(8,128)(2,1)}) custom-call(s32[1]{0:T(128)} %bitcast.me_s, bf16[512,128]{1,0:T(8,128)(2,1)} %refs_4_.1, bf16[512,128]{1,0:T(8,128)(2,1)} %refs_6_.1), custom_call_target="tpu_custom_call" | custom-call | bytes 1048576 | tf_op jit(solution)/shard_map/cut_weights/pallas_call | solution.py:516
  15.7 0.5 collective-permute-start.1
  16.2 5.8 %own_tiles.1 = (f32[16,128,128]{2,1,0:T(8,128)}, s32[2,114]{1,0:T(2,128)S(1)}) custom-call(s32[106]{0:T(128)} %dst_h.1, s32[106]{0:T(128)} %src_h.1, bf16[106,128,128]{2,1,0:T(8,128)(2,1)} %tiles.3, bf16[16,128,128]{2,1,0:T(8,128)(2,1)} %bitcast.9), custom_call_target="tpu_custom_call" | custom-call | flops 444596224 | bytes 8388608 | tf_op jit(solution)/shard_map/own_tiles/pallas_call | solution.py:176
  22.0 0.9 all-to-all-done.incoming_h
  22.9 4.0 %far_tiles.1 = bf16[16,128,128]{2,1,0:T(8,128)(2,1)} custom-call(s32[2,114]{1,0:T(2,128)S(1)} %get-tuple-element.40.lists.refs_0_, bf16[106,128,128]{2,1,0:T(8,128)(2,1)S(1)} %copy-done, bf16[8,160,128]{2,1,0:T(8,128)(2,1)} %all-to-all-done.incoming_h, f32[16,128,128]{2,1,0:T(8,128)} %get-tuple-element.41.base_h), custom_call_target="tpu_custom_call" | custom-call | flops 222298112 | bytes 4194304 | tf_op jit(solution)/shard_map/far_tiles/pallas_call | solution.py:218
  27.0 2.0 %collective-permute-done.1.refs_8_ = bf16[2,2,128,128]{3,2,1,0:T(8,128)(2,1)} collective-permute-done((bf16[2,2,128,128]{3,2,1,0:T(8,128)(2,1)}, bf16[2,2,128,128]{3,2,1,0:T(8,128)(2,1)}, u32[]{:S(2)}, u32[]{:S(2)}) %collective-permute-start.1) | collective-permute-done | bytes 131104 | tf_op jit(solution)/shard_map/ppermute | solution.py:600
  29.0 1.5 %collective-permute-start.3 = (bf16[2048,128]{1,0:T(8,128)(2,1)}, bf16[2048,128]{1,0:T(8,128)(2,1)S(1)}, u32[]{:S(2)}, u32[]{:S(2)}) collective-permute-start(bf16[2048,128]{1,0:T(8,128)(2,1)} %bitcast.10), channel_id=1, source_target_pairs={{0,2},{1,3},{2,0},{3,1},{4,6},{5,7},{6,4},{7,5},{8,10},{9,11},{10,... | collective-permute-start | bytes 1572872 | tf_op jit(solution)/shard_map/ppermute | solution.py:600
  30.5 0.2 collective-permute-start.7
  30.8 0.3 collective-permute-start.6
  31.1 0.2 collective-permute-start.2
  31.3 4.5 %self_dense.1.refs_4_ = f32[2048,128]{1,0:T(8,128)} custom-call(s32[1]{0:T(128)} %bitcast.me_s, bf16[2048,128]{1,0:T(8,128)(2,1)} %refs_0_.3, bf16[2048,128]{1,0:T(8,128)(2,1)} %collective-permute-done.4.refs_1_, bf16[2048,128]{1,0:T(8,128)(2,1)} %collective-permute-done.refs_2_, bf16[2048,128]{1,0:T(8,128)(2,1)S(1)} %collective-permute-done.5.refs_3_, ...), custom_call_target="tpu_custom_call" | custom-call | flops 268435456 | bytes 4194304 | tf_op jit(solution)/shard_map/self_dense/pallas_call | solution.py:280
  35.9 7.7 %collective-permute-done.3.refs_2_.refs_6_ = bf16[2048,128]{1,0:T(8,128)(2,1)S(1)} collective-permute-done((bf16[2048,128]{1,0:T(8,128)(2,1)}, bf16[2048,128]{1,0:T(8,128)(2,1)S(1)}, u32[]{:S(2)}, u32[]{:S(2)}) %collective-permute-start.3) | collective-permute-done | bytes 524320 | tf_op jit(solution)/shard_map/ppermute | solution.py:600
  43.6 1.9 %collective-permute-done.8.refs_3_.refs_7_ = bf16[2048,128]{1,0:T(8,128)(2,1)S(1)} collective-permute-done((bf16[2048,128]{1,0:T(8,128)(2,1)S(1)}, bf16[2048,128]{1,0:T(8,128)(2,1)S(1)}, u32[]{:S(2)}, u32[]{:S(2)}) %collective-permute-start.8) | collective-permute-done | bytes 524320 | tf_op jit(solution)/shard_map/ppermute | solution.py:600
  45.5 5.2 %forward_dense.1 = (bf16[2048,128]{1,0:T(8,128)(2,1)}, bf16[2048,128]{1,0:T(8,128)(2,1)}) custom-call(s32[1]{0:T(128)} %bitcast.me_s, bf16[2048,128]{1,0:T(8,128)(2,1)} %bitcast.12, bf16[2048,128]{1,0:T(8,128)(2,1)S(1)} %collective-permute-done.2.refs_1_.refs_5_, bf16[2048,128]{1,0:T(8,128)(2,1)S(1)} %collective-permute-done.3.refs_2_.refs_6_, ...), custom_call_target="tpu_custom_call" | custom-call | flops 268435456 | bytes 4194304 | tf_op jit(solution)/shard_map/forward_dense/pallas_call | solution.py:280
  50.7 1.6 %collective-permute-start.10 = (bf16[2048,128]{1,0:T(8,128)(2,1)}, bf16[2048,128]{1,0:T(8,128)(2,1)}, u32[]{:S(2)}, u32[]{:S(2)}) collective-permute-start(bf16[2048,128]{1,0:T(8,128)(2,1)} %get-tuple-element.52.refs_8_.refs_2_), channel_id=1, source_target_pairs={{0,2},{1,3},{2,0},{3,1},{4,6},{5,7},{6,4},{7,5},{8,10},{9,11},{10,... | collective-permute-start | bytes 1572872 | tf_op jit(solution)/shard_map/ppermute | solution.py:600
  52.3 3.9 %weight_parts.1 = f32[8,136,128]{2,1,0:T(8,128)} custom-call(bf16[2048,128]{1,0:T(8,128)(2,1)} %refs_0_.3, bf16[2048,128]{1,0:T(8,128)(2,1)} %collective-permute-done.4.refs_1_, bf16[2048,128]{1,0:T(8,128)(2,1)} %collective-permute-done.refs_2_, bf16[2048,128]{1,0:T(8,128)(2,1)S(1)} %collective-permute-done.5.refs_3_, bf16[2048,128]{1,0:T(8,128)(2,1)} %bitcast.13, ...), custom_call_target="tpu_custom_call" | custom-call | flops 536870912 | bytes 4194304 | tf_op jit(solution)/shard_map/weight_parts/pallas_call | solution.py:330
  56.2 5.7 %all-to-all-start.1 = ((f32[8,136,128]{2,1,0:T(8,128)}), f32[8,136,128]{2,1,0:T(8,128)}, u32[]{:S(2)}, u32[]{:S(2)}) async-start(f32[8,136,128]{2,1,0:T(8,128)} %weight_parts.1), calls=%async_computation.1 | async-start | bytes 1114112 | tf_op jit(solution)/shard_map/all_to_all | solution.py:642
  61.9 3.1 %collective-permute-done.10.refs_4_ = bf16[2048,128]{1,0:T(8,128)(2,1)} collective-permute-done((bf16[2048,128]{1,0:T(8,128)(2,1)}, bf16[2048,128]{1,0:T(8,128)(2,1)}, u32[]{:S(2)}, u32[]{:S(2)}) %collective-permute-start.10) | collective-permute-done | bytes 524320 | tf_op jit(solution)/shard_map/ppermute | solution.py:600
  65.1 2.1 %collective-permute-done.11.refs_5_ = bf16[2048,128]{1,0:T(8,128)(2,1)S(1)} collective-permute-done((bf16[2048,128]{1,0:T(8,128)(2,1)}, bf16[2048,128]{1,0:T(8,128)(2,1)S(1)}, u32[]{:S(2)}, u32[]{:S(2)}) %collective-permute-start.11) | collective-permute-done | bytes 524320 | tf_op jit(solution)/shard_map/ppermute | solution.py:600
  67.2 6.6 %back_far.1 = (bf16[8,160,128]{2,1,0:T(8,128)(2,1)}, bf16[16,128,128]{2,1,0:T(8,128)(2,1)}, f32[16,128,128]{2,1,0:T(8,128)}) custom-call(s32[2,114]{1,0:T(2,128)S(1)} %get-tuple-element.40.lists.refs_0_, bf16[106,128,128]{2,1,0:T(8,128)(2,1)S(1)} %copy-done, bf16[2048,128]{1,0:T(8,128)(2,1)} %get-tuple-element.52.refs_8_.refs_2_, ...), custom_call_target="tpu_custom_call" | custom-call | flops 536870912 | bytes 4194304 | tf_op jit(solution)/shard_map/back_far/pallas_call | solution.py:393
  73.8 3.4 %all-to-all-done.1.parts = f32[8,136,128]{2,1,0:T(8,128)} async-done(((f32[8,136,128]{2,1,0:T(8,128)}), f32[8,136,128]{2,1,0:T(8,128)}, u32[]{:S(2)}, u32[]{:S(2)}) %all-to-all-start.1) | async-done | bytes 557088 | tf_op jit(solution)/shard_map/all_to_all | solution.py:642
  77.2 4.1 %all-to-all-start.2 = ((bf16[8,160,128]{2,1,0:T(8,128)(2,1)}), bf16[8,160,128]{2,1,0:T(8,128)(2,1)}, u32[]{:S(2)}, u32[]{:S(2)}) async-start(bf16[8,160,128]{2,1,0:T(8,128)(2,1)} %get-tuple-element.58), calls=%async_computation.2 | async-start | bytes 655360 | tf_op jit(solution)/shard_map/all_to_all | solution.py:648
  81.3 1.8 %sum_parts.1 = (bf16[8,128,128]{2,1,0:T(8,128)(2,1)}, f32[1,128]{1,0:T(1,128)}) custom-call(f32[8,136,128]{2,1,0:T(8,128)} %all-to-all-done.1.parts), custom_call_target="tpu_custom_call" | custom-call | bytes 1048576 | tf_op jit(solution)/shard_map/sum_parts/pallas_call | solution.py:540
  83.1 5.4 %back_own.1 = f32[16,128,128]{2,1,0:T(8,128)} custom-call(s32[2,114]{1,0:T(2,128)S(1)} %get-tuple-element.40.lists.refs_0_, bf16[106,128,128]{2,1,0:T(8,128)(2,1)S(1)} %copy-done, bf16[16,128,128]{2,1,0:T(8,128)(2,1)} %get-tuple-element.59.back_h, f32[16,128,128]{2,1,0:T(8,128)} %get-tuple-element.60.direct_h), custom_call_target="tpu_custom_call" | custom-call | flops 444596224 | bytes 8388608 | tf_op jit(solution)/shard_map/back_own/pallas_call | solution.py:422
  88.5 2.9 %all-to-all-done.2.incoming_h = bf16[8,160,128]{2,1,0:T(8,128)(2,1)} async-done(((bf16[8,160,128]{2,1,0:T(8,128)(2,1)}), bf16[8,160,128]{2,1,0:T(8,128)(2,1)}, u32[]{:S(2)}, u32[]{:S(2)}) %all-to-all-start.2) | async-done | bytes 327712 | tf_op jit(solution)/shard_map/all_to_all | solution.py:648
  91.5 3.6 %all-to-all-start.3 = ((bf16[8,128,128]{2,1,0:T(8,128)(2,1)}), bf16[8,128,128]{2,1,0:T(8,128)(2,1)S(1)}, u32[]{:S(2)}, u32[]{:S(2)}) async-start(bf16[8,128,128]{2,1,0:T(8,128)(2,1)} %get-tuple-element.63), calls=%async_computation.3 | async-start | bytes 524288 | tf_op jit(solution)/shard_map/all_to_all | solution.py:652
  95.1 4.1 %finish.1 = f32[2048,128]{1,0:T(8,128)} custom-call(s32[8,128]{1,0:T(8,128)} %bitcast.16, s32[1,8]{1,0:T(1,128)} %count_h.3, s32[32]{0:T(128)} %hub_h.3, bf16[8,160,128]{2,1,0:T(8,128)(2,1)} %all-to-all-done.2.incoming_h, f32[2048,128]{1,0:T(8,128)} %bitcast.14), custom_call_target="tpu_custom_call" | custom-call | flops 536870912 | bytes 4194304 | tf_op jit(solution)/shard_map/finish/pallas_call | solution.py:484
  99.1 4.5 %all-to-all-done.3 = bf16[8,128,128]{2,1,0:T(8,128)(2,1)S(1)} async-done(((bf16[8,128,128]{2,1,0:T(8,128)(2,1)}), bf16[8,128,128]{2,1,0:T(8,128)(2,1)S(1)}, u32[]{:S(2)}, u32[]{:S(2)}) %all-to-all-start.3) | async-done | bytes 262176 | tf_op jit(solution)/shard_map/all_to_all | solution.py:652
  103.6 0.8 place_weights.1
  (20 shorter events, 0.1 us)
Async XLA Ops:
  0.6 22.3 %copy-start = (bf16[106,128,128]{2,1,0:T(8,128)(2,1)S(1)}, bf16[106,128,128]{2,1,0:T(8,128)(2,1)}, u32[]{:S(2)}) copy-start(bf16[106,128,128]{2,1,0:T(8,128)(2,1)} %tiles.3) | copy-start | bytes 10420228
  5.2 17.7 %all-to-all-start = ((bf16[8,160,128]{2,1,0:T(8,128)(2,1)}), bf16[8,160,128]{2,1,0:T(8,128)(2,1)}, u32[]{:S(2)}, u32[]{:S(2)}) async-start(bf16[8,160,128]{2,1,0:T(8,128)(2,1)} %pick_rows.1), calls=%async_computation | async-start | bytes 655360 | tf_op jit(solution)/shard_map/all_to_all | solution.py:605
  12.5 16.5 %collective-permute-start = (bf16[2048,128]{1,0:T(8,128)(2,1)}, bf16[2048,128]{1,0:T(8,128)(2,1)}, u32[]{:S(2)}, u32[]{:S(2)}) collective-permute-start(bf16[2048,128]{1,0:T(8,128)(2,1)} %refs_0_.3), channel_id=1, source_target_pairs={{0,2},{1,3},{2,0},{3,1},{4,6},{5,7},{6,4},{7,5},{8,10},{9,11},{10,... | collective-permute-start | bytes 1572872 | tf_op jit(solution)/shard_map/ppermute | solution.py:600
  15.7 13.3 %collective-permute-start.1 = (bf16[2,2,128,128]{3,2,1,0:T(8,128)(2,1)}, bf16[2,2,128,128]{3,2,1,0:T(8,128)(2,1)}, u32[]{:S(2)}, u32[]{:S(2)}) collective-permute-start(bf16[2,2,128,128]{3,2,1,0:T(8,128)(2,1)} %get-tuple-element.42), channel_id=1, source_target_pairs={{0,2},{1,3},{2,0},{3,1},{4,6},{5,7},{6,4},{7,5},{8,10},{9,11},{10,... | collective-permute-start | bytes 393224 | tf_op jit(solution)/shard_map/ppermute | solution.py:600
  16.2 14.8 %collective-permute-start.4 = (bf16[2048,128]{1,0:T(8,128)(2,1)}, bf16[2048,128]{1,0:T(8,128)(2,1)}, u32[]{:S(2)}, u32[]{:S(2)}) collective-permute-start(bf16[2048,128]{1,0:T(8,128)(2,1)} %refs_0_.3), channel_id=1, source_target_pairs={{0,1},{1,0},{2,3},{3,2},{4,5},{5,4},{6,7},{7,6},{8,9},{9,8},{10,11... | collective-permute-start | bytes 1572872 | tf_op jit(solution)/shard_map/ppermute | solution.py:600
  22.9 7.8 %copy-start.3 = (bf16[2,128,128]{2,1,0:T(8,128)(2,1)S(1)}, bf16[2,128,128]{2,1,0:T(8,128)(2,1)}, u32[]{:S(2)}) copy-start(bf16[2,128,128]{2,1,0:T(8,128)(2,1)} %get-tuple-element.47) | copy-start | bytes 196612
  29.0 2.3 %collective-permute-start.5 = (bf16[2048,128]{1,0:T(8,128)(2,1)}, bf16[2048,128]{1,0:T(8,128)(2,1)S(1)}, u32[]{:S(2)}, u32[]{:S(2)}) collective-permute-start(bf16[2048,128]{1,0:T(8,128)(2,1)} %collective-permute-done.refs_2_), channel_id=1, source_target_pairs={{0,1},{1,0},{2,3},{3,2},{4,5},{5,4},{6,7},{7,6},{8,9},{9,8},{10,11... | collective-permute-start | bytes 1572872 | tf_op jit(solution)/shard_map/ppermute | solution.py:600
  29.0 14.5 %collective-permute-start.3 = (bf16[2048,128]{1,0:T(8,128)(2,1)}, bf16[2048,128]{1,0:T(8,128)(2,1)S(1)}, u32[]{:S(2)}, u32[]{:S(2)}) collective-permute-start(bf16[2048,128]{1,0:T(8,128)(2,1)} %bitcast.10), channel_id=1, source_target_pairs={{0,2},{1,3},{2,0},{3,1},{4,6},{5,7},{6,4},{7,5},{8,10},{9,11},{10,... | collective-permute-start | bytes 1572872 | tf_op jit(solution)/shard_map/ppermute | solution.py:600
  30.5 5.3 %collective-permute-start.7 = (bf16[2,2,128,128]{3,2,1,0:T(8,128)(2,1)}, bf16[2,2,128,128]{3,2,1,0:T(8,128)(2,1)S(1)}, u32[]{:S(2)}, u32[]{:S(2)}) collective-permute-start(bf16[2,2,128,128]{3,2,1,0:T(8,128)(2,1)} %collective-permute-done.1.refs_8_), channel_id=1, source_target_pairs={{0,1},{1,0},{2,3},{3,2},{4,5},{5,4},{6,7},{7,6},{8,9},{9,8},{10,11... | collective-permute-start | bytes 393224 | tf_op jit(solution)/shard_map/ppermute | solution.py:600
  30.8 5.1 %collective-permute-start.6 = (bf16[2,128,128]{2,1,0:T(8,128)(2,1)S(1)}, bf16[2,128,128]{2,1,0:T(8,128)(2,1)S(1)}, u32[]{:S(2)}, u32[]{:S(2)}) collective-permute-start(bf16[2,128,128]{2,1,0:T(8,128)(2,1)S(1)} %copy-done.3), channel_id=1, source_target_pairs={{0,1},{1,0},{2,3},{3,2},{4,5},{5,4},{6,7},{7,6},{8,9},{9,8},{10,11... | collective-permute-start | bytes 196616 | tf_op jit(solution)/shard_map/ppermute | solution.py:600
  31.1 12.5 %collective-permute-start.2 = (bf16[2048,128]{1,0:T(8,128)(2,1)}, bf16[2048,128]{1,0:T(8,128)(2,1)S(1)}, u32[]{:S(2)}, u32[]{:S(2)}) collective-permute-start(bf16[2048,128]{1,0:T(8,128)(2,1)} %bitcast.11), channel_id=1, source_target_pairs={{0,1},{1,0},{2,3},{3,2},{4,5},{5,4},{6,7},{7,6},{8,9},{9,8},{10,11... | collective-permute-start | bytes 1572872 | tf_op jit(solution)/shard_map/ppermute | solution.py:600
  35.8 31.3 %copy-start.2 = (bf16[2,128,128]{2,1,0:T(8,128)(2,1)}, bf16[2,128,128]{2,1,0:T(8,128)(2,1)S(1)}, u32[]{:S(2)}) copy-start(bf16[2,128,128]{2,1,0:T(8,128)(2,1)S(1)} %collective-permute-done.6.refs_7_) | copy-start | bytes 196612
  35.9 9.6 %copy-start.1 = (bf16[2,2,128,128]{3,2,1,0:T(8,128)(2,1)}, bf16[2,2,128,128]{3,2,1,0:T(8,128)(2,1)S(1)}, u32[]{:S(2)}) copy-start(bf16[2,2,128,128]{3,2,1,0:T(8,128)(2,1)S(1)} %collective-permute-done.7.refs_9_) | copy-start | bytes 393220
  43.6 1.9 %collective-permute-start.8 = (bf16[2048,128]{1,0:T(8,128)(2,1)S(1)}, bf16[2048,128]{1,0:T(8,128)(2,1)S(1)}, u32[]{:S(2)}, u32[]{:S(2)}) collective-permute-start(bf16[2048,128]{1,0:T(8,128)(2,1)S(1)} %collective-permute-done.3.refs_2_.refs_6_), channel_id=1, source_target_pairs={{0,1},{1,0},{2,3},{3,2},{4,5},{5,4},{6,7},{7,6},{8,9},{9,8},{10,11... | collective-permute-start | bytes 1572872 | tf_op jit(solution)/shard_map/ppermute | solution.py:600
  50.7 14.3 %collective-permute-start.10 = (bf16[2048,128]{1,0:T(8,128)(2,1)}, bf16[2048,128]{1,0:T(8,128)(2,1)}, u32[]{:S(2)}, u32[]{:S(2)}) collective-permute-start(bf16[2048,128]{1,0:T(8,128)(2,1)} %get-tuple-element.52.refs_8_.refs_2_), channel_id=1, source_target_pairs={{0,2},{1,3},{2,0},{3,1},{4,6},{5,7},{6,4},{7,5},{8,10},{9,11},{10,... | collective-permute-start | bytes 1572872 | tf_op jit(solution)/shard_map/ppermute | solution.py:600
  56.2 21.0 %all-to-all-start.1 = ((f32[8,136,128]{2,1,0:T(8,128)}), f32[8,136,128]{2,1,0:T(8,128)}, u32[]{:S(2)}, u32[]{:S(2)}) async-start(f32[8,136,128]{2,1,0:T(8,128)} %weight_parts.1), calls=%async_computation.1 | async-start | bytes 1114112 | tf_op jit(solution)/shard_map/all_to_all | solution.py:642
  61.9 3.2 %collective-permute-start.9 = (bf16[2048,128]{1,0:T(8,128)(2,1)}, bf16[2048,128]{1,0:T(8,128)(2,1)S(1)}, u32[]{:S(2)}, u32[]{:S(2)}) collective-permute-start(bf16[2048,128]{1,0:T(8,128)(2,1)} %get-tuple-element.52.refs_8_.refs_2_), channel_id=1, source_target_pairs={{0,1},{1,0},{2,3},{3,2},{4,5},{5,4},{6,7},{7,6},{8,9},{9,8},{10,11... | collective-permute-start | bytes 1572872 | tf_op jit(solution)/shard_map/ppermute | solution.py:600
  65.1 2.1 %collective-permute-start.11 = (bf16[2048,128]{1,0:T(8,128)(2,1)}, bf16[2048,128]{1,0:T(8,128)(2,1)S(1)}, u32[]{:S(2)}, u32[]{:S(2)}) collective-permute-start(bf16[2048,128]{1,0:T(8,128)(2,1)} %collective-permute-done.10.refs_4_), channel_id=1, source_target_pairs={{0,1},{1,0},{2,3},{3,2},{4,5},{5,4},{6,7},{7,6},{8,9},{9,8},{10,11... | collective-permute-start | bytes 1572872 | tf_op jit(solution)/shard_map/ppermute | solution.py:600
  77.2 14.2 %all-to-all-start.2 = ((bf16[8,160,128]{2,1,0:T(8,128)(2,1)}), bf16[8,160,128]{2,1,0:T(8,128)(2,1)}, u32[]{:S(2)}, u32[]{:S(2)}) async-start(bf16[8,160,128]{2,1,0:T(8,128)(2,1)} %get-tuple-element.58), calls=%async_computation.2 | async-start | bytes 655360 | tf_op jit(solution)/shard_map/all_to_all | solution.py:648
  91.5 12.1 %all-to-all-start.3 = ((bf16[8,128,128]{2,1,0:T(8,128)(2,1)}), bf16[8,128,128]{2,1,0:T(8,128)(2,1)S(1)}, u32[]{:S(2)}, u32[]{:S(2)}) async-start(bf16[8,128,128]{2,1,0:T(8,128)(2,1)} %get-tuple-element.63), calls=%async_computation.3 | async-start | bytes 524288 | tf_op jit(solution)/shard_map/all_to_all | solution.py:652

commit v10 on v9

--- a/solution.py
+++ b/solution.py
@@ -13,7 +13,7 @@
 SMEM = pl.BlockSpec(memory_space=pltpu.SMEM)
 HBM = pl.BlockSpec(memory_space=pltpu.HBM)
 ANY = pl.BlockSpec(memory_space=pl.ANY)
-UNROLL = 8
+UNROLL = 16
 T_BITS, S_BITS = 10, 10
 
 
@@ -45,7 +45,7 @@
     copies = start_copies(sems, (x_h, x), (rows_h, rows_s), (count_h, count_s), (hub_h, hub_s))
     n_dom, capacity = rows_s.shape
     hub_dev = hub_s.shape[0]
-    step = 16
+    step = 32
     wait_copies(copies)
     x32[...] = x[...].astype(F32)
     for j in range(hub_dev):
@@ -263,7 +263,7 @@
         wait_copies(copies)
 
 
-def stream_call(kernel, me, streamed, whole, outs, flops, name, block=512):
+def stream_call(kernel, me, streamed, whole, outs, flops, name, block=1024):
     rows = streamed[0].shape[0]
     n_in, n_whole, n_out = len(streamed), len(whole), len(outs)
 

time: 105 us -> 104 us (level)
  Pallas kernels: 48.5 us -> 44.3 us
  waiting for transfers between devices: 28.6 us -> 31.4 us
    pallas_call x2, Pallas kernels: 9.78 us -> 8.24 us  [stream_call(): pl.pallas_call(run, out_shape=tuple((pltpu.HBM(shape, t) for shape, t in...]
    all_to_all x1, waiting for transfers between devices: 2.94 us -> 4.05 us  [body(): back_in = lax.all_to_all(back_out, 'dom', 0, 0, tiled=True)]
    pallas_call x1, Pallas kernels: 5.42 us -> 4.3 us  [back_own(): pl.pallas_call(back_own_kernel, out_shape=pltpu.HBM(direct.shape, F32), i...]
  transfers between devices with their start and end apart: 16 -> 16, of which waited for: 9 -> 9; matrix products, arithmetic and copies ran while one was open for 0% -> 0% of each run, Pallas kernels for 36% -> 34%
where the time goes in v10:
time: 104 us; the launch traced here: 103 us
  Pallas kernels  44.3 us (43%)
  waiting for transfers between devices  31.4 us (30%)
  starting transfers between devices  26.5 us (25%)
    ppermute x12, waiting for transfers between devices, swap(): return lax.ppermute(x, 'feat', [(j, j ^ k) for j in range(n_feat)])  17.4 us
    pallas_call x2, Pallas kernels, stream_call(): pl.pallas_call(run, out_shape=tuple((pltpu.HBM(shape, t) for shape, t in...  8.24 us
    all_to_all x1, starting transfers between devices, body(): incoming = lax.all_to_all(outgoing, 'dom', 0, 0, tiled=True)  7.26 us
    pallas_call x1, Pallas kernels, back_far(): pl.pallas_call(functools.partial(back_far_kernel, n_feat=n_feat), out_sha...  6.3 us
    ppermute x12, starting transfers between devices, swap(): return lax.ppermute(x, 'feat', [(j, j ^ k) for j in range(n_feat)])  5.89 us
    all_to_all x1, starting transfers between devices, body(): part_sums = lax.all_to_all(parts, 'dom', 0, 0, tiled=True)  5.73 us
    pallas_call x1, Pallas kernels, own_tiles(): pl.pallas_call(functools.partial(own_kernel, far_blocks=far_blocks), out_...  4.97 us
    all_to_all x1, waiting for transfers between devices, body(): weights_in = lax.all_to_all(weights_out, 'dom', 0, 0, tiled=True)  4.47 us
  transfers between devices with their start and end apart: 16, of which 9 were waited for; matrix products, arithmetic and copies ran while one was open for 0% of the time, Pallas kernels for 34%

profile of v10, /device:TPU:0, one launch (start us, length us, event | category | flops | bytes accessed | tf_op | source)
XLA Modules:
  0.0 103.0 jit_solution(3349421664572108959)
XLA Ops:
  0.6 4.4 %pick_rows.1 = bf16[8,160,128]{2,1,0:T(8,128)(2,1)} custom-call(s32[8,128]{1,0:T(8,128)} %bitcast.15, s32[1,8]{1,0:T(1,128)} %count_h.3, s32[32]{0:T(128)} %hub_h.3, bf16[2048,128]{1,0:T(8,128)(2,1)} %refs_0_.3), custom_call_target="tpu_custom_call" | custom-call | bytes 2097152 | tf_op jit(solution)/shard_map/pick_rows/pallas_call | solution.py:79
  5.1 7.3 %all-to-all-start = ((bf16[8,160,128]{2,1,0:T(8,128)(2,1)}), bf16[8,160,128]{2,1,0:T(8,128)(2,1)}, u32[]{:S(2)}, u32[]{:S(2)}) async-start(bf16[8,160,128]{2,1,0:T(8,128)(2,1)} %pick_rows.1), calls=%async_computation | async-start | bytes 655360 | tf_op jit(solution)/shard_map/all_to_all | solution.py:605
  12.3 1.5 %collective-permute-start = (bf16[2048,128]{1,0:T(8,128)(2,1)}, bf16[2048,128]{1,0:T(8,128)(2,1)}, u32[]{:S(2)}, u32[]{:S(2)}) collective-permute-start(bf16[2048,128]{1,0:T(8,128)(2,1)} %refs_0_.3), channel_id=1, source_target_pairs={{0,2},{1,3},{2,0},{3,1},{4,6},{5,7},{6,4},{7,5},{8,10},{9,11},{10,... | collective-permute-start | bytes 1572872 | tf_op jit(solution)/shard_map/ppermute | solution.py:600
  13.9 1.7 %cut_weights.1 = (bf16[2,128,128]{2,1,0:T(8,128)(2,1)}, bf16[2,128,128]{2,1,0:T(8,128)(2,1)}, bf16[2,2,128,128]{3,2,1,0:T(8,128)(2,1)}) custom-call(s32[1]{0:T(128)} %bitcast.me_s, bf16[512,128]{1,0:T(8,128)(2,1)} %refs_4_.1, bf16[512,128]{1,0:T(8,128)(2,1)} %refs_6_.1), custom_call_target="tpu_custom_call" | custom-call | bytes 1048576 | tf_op jit(solution)/shard_map/cut_weights/pallas_call | solution.py:516
  15.5 0.5 collective-permute-start.1
  16.1 5.0 %own_tiles.1 = (f32[16,128,128]{2,1,0:T(8,128)}, s32[2,122]{1,0:T(2,128)S(1)}) custom-call(s32[106]{0:T(128)} %dst_h.1, s32[106]{0:T(128)} %src_h.1, bf16[106,128,128]{2,1,0:T(8,128)(2,1)} %tiles.3, bf16[16,128,128]{2,1,0:T(8,128)(2,1)} %bitcast.9), custom_call_target="tpu_custom_call" | custom-call | flops 444596224 | bytes 8388608 | tf_op jit(solution)/shard_map/own_tiles/pallas_call | solution.py:176
  21.0 1.7 %all-to-all-done.incoming_h = bf16[8,160,128]{2,1,0:T(8,128)(2,1)} async-done(((bf16[8,160,128]{2,1,0:T(8,128)(2,1)}), bf16[8,160,128]{2,1,0:T(8,128)(2,1)}, u32[]{:S(2)}, u32[]{:S(2)}) %all-to-all-start) | async-done | bytes 327712 | tf_op jit(solution)/shard_map/all_to_all | solution.py:605
  22.8 3.8 %far_tiles.1 = bf16[16,128,128]{2,1,0:T(8,128)(2,1)} custom-call(s32[2,122]{1,0:T(2,128)S(1)} %get-tuple-element.40.lists.refs_0_, bf16[106,128,128]{2,1,0:T(8,128)(2,1)S(1)} %copy-done, bf16[8,160,128]{2,1,0:T(8,128)(2,1)} %all-to-all-done.incoming_h, f32[16,128,128]{2,1,0:T(8,128)} %get-tuple-element.41.base_h), custom_call_target="tpu_custom_call" | custom-call | flops 222298112 | bytes 4194304 | tf_op jit(solution)/shard_map/far_tiles/pallas_call | solution.py:218
  26.6 2.3 %collective-permute-done.1.refs_8_ = bf16[2,2,128,128]{3,2,1,0:T(8,128)(2,1)} collective-permute-done((bf16[2,2,128,128]{3,2,1,0:T(8,128)(2,1)}, bf16[2,2,128,128]{3,2,1,0:T(8,128)(2,1)}, u32[]{:S(2)}, u32[]{:S(2)}) %collective-permute-start.1) | collective-permute-done | bytes 131104 | tf_op jit(solution)/shard_map/ppermute | solution.py:600
  28.9 1.5 %collective-permute-start.3 = (bf16[2048,128]{1,0:T(8,128)(2,1)}, bf16[2048,128]{1,0:T(8,128)(2,1)S(1)}, u32[]{:S(2)}, u32[]{:S(2)}) collective-permute-start(bf16[2048,128]{1,0:T(8,128)(2,1)} %bitcast.10), channel_id=1, source_target_pairs={{0,2},{1,3},{2,0},{3,1},{4,6},{5,7},{6,4},{7,5},{8,10},{9,11},{10,... | collective-permute-start | bytes 1572872 | tf_op jit(solution)/shard_map/ppermute | solution.py:600
  30.4 0.2 collective-permute-start.7
  30.6 0.3 collective-permute-start.6
  30.9 0.2 collective-permute-start.2
  31.1 4.3 %self_dense.1.refs_4_ = f32[2048,128]{1,0:T(8,128)} custom-call(s32[1]{0:T(128)} %bitcast.me_s, bf16[2048,128]{1,0:T(8,128)(2,1)} %refs_0_.3, bf16[2048,128]{1,0:T(8,128)(2,1)} %collective-permute-done.4.refs_1_, bf16[2048,128]{1,0:T(8,128)(2,1)} %collective-permute-done.refs_2_, bf16[2048,128]{1,0:T(8,128)(2,1)S(1)} %collective-permute-done.5.refs_3_, ...), custom_call_target="tpu_custom_call" | custom-call | flops 268435456 | bytes 4194304 | tf_op jit(solution)/shard_map/self_dense/pallas_call | solution.py:280
  35.5 7.9 %collective-permute-done.3.refs_2_.refs_6_ = bf16[2048,128]{1,0:T(8,128)(2,1)S(1)} collective-permute-done((bf16[2048,128]{1,0:T(8,128)(2,1)}, bf16[2048,128]{1,0:T(8,128)(2,1)S(1)}, u32[]{:S(2)}, u32[]{:S(2)}) %collective-permute-start.3) | collective-permute-done | bytes 524320 | tf_op jit(solution)/shard_map/ppermute | solution.py:600
  43.4 1.9 %collective-permute-done.8.refs_3_.refs_7_ = bf16[2048,128]{1,0:T(8,128)(2,1)S(1)} collective-permute-done((bf16[2048,128]{1,0:T(8,128)(2,1)S(1)}, bf16[2048,128]{1,0:T(8,128)(2,1)S(1)}, u32[]{:S(2)}, u32[]{:S(2)}) %collective-permute-start.8) | collective-permute-done | bytes 524320 | tf_op jit(solution)/shard_map/ppermute | solution.py:600
  45.3 4.0 %forward_dense.1 = (bf16[2048,128]{1,0:T(8,128)(2,1)}, bf16[2048,128]{1,0:T(8,128)(2,1)}) custom-call(s32[1]{0:T(128)} %bitcast.me_s, bf16[2048,128]{1,0:T(8,128)(2,1)} %bitcast.12, bf16[2048,128]{1,0:T(8,128)(2,1)S(1)} %collective-permute-done.2.refs_1_.refs_5_, bf16[2048,128]{1,0:T(8,128)(2,1)S(1)} %collective-permute-done.3.refs_2_.refs_6_, ...), custom_call_target="tpu_custom_call" | custom-call | flops 268435456 | bytes 4194304 | tf_op jit(solution)/shard_map/forward_dense/pallas_call | solution.py:280
  49.3 1.6 %collective-permute-start.10 = (bf16[2048,128]{1,0:T(8,128)(2,1)}, bf16[2048,128]{1,0:T(8,128)(2,1)}, u32[]{:S(2)}, u32[]{:S(2)}) collective-permute-start(bf16[2048,128]{1,0:T(8,128)(2,1)} %get-tuple-element.52.refs_8_.refs_2_), channel_id=1, source_target_pairs={{0,2},{1,3},{2,0},{3,1},{4,6},{5,7},{6,4},{7,5},{8,10},{9,11},{10,... | collective-permute-start | bytes 1572872 | tf_op jit(solution)/shard_map/ppermute | solution.py:600
  50.9 3.9 %weight_parts.1 = f32[8,136,128]{2,1,0:T(8,128)} custom-call(bf16[2048,128]{1,0:T(8,128)(2,1)} %refs_0_.3, bf16[2048,128]{1,0:T(8,128)(2,1)} %collective-permute-done.4.refs_1_, bf16[2048,128]{1,0:T(8,128)(2,1)} %collective-permute-done.refs_2_, bf16[2048,128]{1,0:T(8,128)(2,1)S(1)} %collective-permute-done.5.refs_3_, bf16[2048,128]{1,0:T(8,128)(2,1)} %bitcast.13, ...), custom_call_target="tpu_custom_call" | custom-call | flops 536870912 | bytes 4194304 | tf_op jit(solution)/shard_map/weight_parts/pallas_call | solution.py:330
  54.7 5.7 %all-to-all-start.1 = ((f32[8,136,128]{2,1,0:T(8,128)}), f32[8,136,128]{2,1,0:T(8,128)}, u32[]{:S(2)}, u32[]{:S(2)}) async-start(f32[8,136,128]{2,1,0:T(8,128)} %weight_parts.1), calls=%async_computation.1 | async-start | bytes 1114112 | tf_op jit(solution)/shard_map/all_to_all | solution.py:642
  60.5 3.1 %collective-permute-done.10.refs_4_ = bf16[2048,128]{1,0:T(8,128)(2,1)} collective-permute-done((bf16[2048,128]{1,0:T(8,128)(2,1)}, bf16[2048,128]{1,0:T(8,128)(2,1)}, u32[]{:S(2)}, u32[]{:S(2)}) %collective-permute-start.10) | collective-permute-done | bytes 524320 | tf_op jit(solution)/shard_map/ppermute | solution.py:600
  63.6 2.1 %collective-permute-done.11.refs_5_ = bf16[2048,128]{1,0:T(8,128)(2,1)S(1)} collective-permute-done((bf16[2048,128]{1,0:T(8,128)(2,1)}, bf16[2048,128]{1,0:T(8,128)(2,1)S(1)}, u32[]{:S(2)}, u32[]{:S(2)}) %collective-permute-start.11) | collective-permute-done | bytes 524320 | tf_op jit(solution)/shard_map/ppermute | solution.py:600
  65.8 6.3 %back_far.1 = (bf16[8,160,128]{2,1,0:T(8,128)(2,1)}, bf16[16,128,128]{2,1,0:T(8,128)(2,1)}, f32[16,128,128]{2,1,0:T(8,128)}) custom-call(s32[2,122]{1,0:T(2,128)S(1)} %get-tuple-element.40.lists.refs_0_, bf16[106,128,128]{2,1,0:T(8,128)(2,1)S(1)} %copy-done, bf16[2048,128]{1,0:T(8,128)(2,1)} %get-tuple-element.52.refs_8_.refs_2_, ...), custom_call_target="tpu_custom_call" | custom-call | flops 536870912 | bytes 4194304 | tf_op jit(solution)/shard_map/back_far/pallas_call | solution.py:393
  72.1 3.7 %all-to-all-done.1.parts = f32[8,136,128]{2,1,0:T(8,128)} async-done(((f32[8,136,128]{2,1,0:T(8,128)}), f32[8,136,128]{2,1,0:T(8,128)}, u32[]{:S(2)}, u32[]{:S(2)}) %all-to-all-start.1) | async-done | bytes 557088 | tf_op jit(solution)/shard_map/all_to_all | solution.py:642
  75.8 4.1 %all-to-all-start.2 = ((bf16[8,160,128]{2,1,0:T(8,128)(2,1)}), bf16[8,160,128]{2,1,0:T(8,128)(2,1)}, u32[]{:S(2)}, u32[]{:S(2)}) async-start(bf16[8,160,128]{2,1,0:T(8,128)(2,1)} %get-tuple-element.58), calls=%async_computation.2 | async-start | bytes 655360 | tf_op jit(solution)/shard_map/all_to_all | solution.py:648
  79.9 1.8 %sum_parts.1 = (bf16[8,128,128]{2,1,0:T(8,128)(2,1)}, f32[1,128]{1,0:T(1,128)}) custom-call(f32[8,136,128]{2,1,0:T(8,128)} %all-to-all-done.1.parts), custom_call_target="tpu_custom_call" | custom-call | bytes 1048576 | tf_op jit(solution)/shard_map/sum_parts/pallas_call | solution.py:540
  81.7 4.3 %back_own.1 = f32[16,128,128]{2,1,0:T(8,128)} custom-call(s32[2,122]{1,0:T(2,128)S(1)} %get-tuple-element.40.lists.refs_0_, bf16[106,128,128]{2,1,0:T(8,128)(2,1)S(1)} %copy-done, bf16[16,128,128]{2,1,0:T(8,128)(2,1)} %get-tuple-element.59.back_h, f32[16,128,128]{2,1,0:T(8,128)} %get-tuple-element.60.direct_h), custom_call_target="tpu_custom_call" | custom-call | flops 444596224 | bytes 8388608 | tf_op jit(solution)/shard_map/back_own/pallas_call | solution.py:422
  86.0 4.1 %all-to-all-done.2.incoming_h = bf16[8,160,128]{2,1,0:T(8,128)(2,1)} async-done(((bf16[8,160,128]{2,1,0:T(8,128)(2,1)}), bf16[8,160,128]{2,1,0:T(8,128)(2,1)}, u32[]{:S(2)}, u32[]{:S(2)}) %all-to-all-start.2) | async-done | bytes 327712 | tf_op jit(solution)/shard_map/all_to_all | solution.py:648
  90.0 3.6 %all-to-all-start.3 = ((bf16[8,128,128]{2,1,0:T(8,128)(2,1)}), bf16[8,128,128]{2,1,0:T(8,128)(2,1)S(1)}, u32[]{:S(2)}, u32[]{:S(2)}) async-start(bf16[8,128,128]{2,1,0:T(8,128)(2,1)} %get-tuple-element.63), calls=%async_computation.3 | async-start | bytes 524288 | tf_op jit(solution)/shard_map/all_to_all | solution.py:652
  93.6 4.1 %finish.1 = f32[2048,128]{1,0:T(8,128)} custom-call(s32[8,128]{1,0:T(8,128)} %bitcast.16, s32[1,8]{1,0:T(1,128)} %count_h.3, s32[32]{0:T(128)} %hub_h.3, bf16[8,160,128]{2,1,0:T(8,128)(2,1)} %all-to-all-done.2.incoming_h, f32[2048,128]{1,0:T(8,128)} %bitcast.14), custom_call_target="tpu_custom_call" | custom-call | flops 536870912 | bytes 4194304 | tf_op jit(solution)/shard_map/finish/pallas_call | solution.py:484
  97.7 4.5 %all-to-all-done.3 = bf16[8,128,128]{2,1,0:T(8,128)(2,1)S(1)} async-done(((bf16[8,128,128]{2,1,0:T(8,128)(2,1)}), bf16[8,128,128]{2,1,0:T(8,128)(2,1)S(1)}, u32[]{:S(2)}, u32[]{:S(2)}) %all-to-all-start.3) | async-done | bytes 262176 | tf_op jit(solution)/shard_map/all_to_all | solution.py:652
  102.2 0.8 place_weights.1
  (20 shorter events, 0.1 us)
Async XLA Ops:
  0.6 22.1 %copy-start = (bf16[106,128,128]{2,1,0:T(8,128)(2,1)S(1)}, bf16[106,128,128]{2,1,0:T(8,128)(2,1)}, u32[]{:S(2)}) copy-start(bf16[106,128,128]{2,1,0:T(8,128)(2,1)} %tiles.3) | copy-start | bytes 10420228
  5.1 17.7 %all-to-all-start = ((bf16[8,160,128]{2,1,0:T(8,128)(2,1)}), bf16[8,160,128]{2,1,0:T(8,128)(2,1)}, u32[]{:S(2)}, u32[]{:S(2)}) async-start(bf16[8,160,128]{2,1,0:T(8,128)(2,1)} %pick_rows.1), calls=%async_computation | async-start | bytes 655360 | tf_op jit(solution)/shard_map/all_to_all | solution.py:605
  12.3 16.5 %collective-permute-start = (bf16[2048,128]{1,0:T(8,128)(2,1)}, bf16[2048,128]{1,0:T(8,128)(2,1)}, u32[]{:S(2)}, u32[]{:S(2)}) collective-permute-start(bf16[2048,128]{1,0:T(8,128)(2,1)} %refs_0_.3), channel_id=1, source_target_pairs={{0,2},{1,3},{2,0},{3,1},{4,6},{5,7},{6,4},{7,5},{8,10},{9,11},{10,... | collective-permute-start | bytes 1572872 | tf_op jit(solution)/shard_map/ppermute | solution.py:600
  15.5 13.3 %collective-permute-start.1 = (bf16[2,2,128,128]{3,2,1,0:T(8,128)(2,1)}, bf16[2,2,128,128]{3,2,1,0:T(8,128)(2,1)}, u32[]{:S(2)}, u32[]{:S(2)}) collective-permute-start(bf16[2,2,128,128]{3,2,1,0:T(8,128)(2,1)} %get-tuple-element.42), channel_id=1, source_target_pairs={{0,2},{1,3},{2,0},{3,1},{4,6},{5,7},{6,4},{7,5},{8,10},{9,11},{10,... | collective-permute-start | bytes 393224 | tf_op jit(solution)/shard_map/ppermute | solution.py:600
  16.0 14.8 %collective-permute-start.4 = (bf16[2048,128]{1,0:T(8,128)(2,1)}, bf16[2048,128]{1,0:T(8,128)(2,1)}, u32[]{:S(2)}, u32[]{:S(2)}) collective-permute-start(bf16[2048,128]{1,0:T(8,128)(2,1)} %refs_0_.3), channel_id=1, source_target_pairs={{0,1},{1,0},{2,3},{3,2},{4,5},{5,4},{6,7},{7,6},{8,9},{9,8},{10,11... | collective-permute-start | bytes 1572872 | tf_op jit(solution)/shard_map/ppermute | solution.py:600
  22.8 7.8 %copy-start.3 = (bf16[2,128,128]{2,1,0:T(8,128)(2,1)S(1)}, bf16[2,128,128]{2,1,0:T(8,128)(2,1)}, u32[]{:S(2)}) copy-start(bf16[2,128,128]{2,1,0:T(8,128)(2,1)} %get-tuple-element.47) | copy-start | bytes 196612
  28.9 2.3 %collective-permute-start.5 = (bf16[2048,128]{1,0:T(8,128)(2,1)}, bf16[2048,128]{1,0:T(8,128)(2,1)S(1)}, u32[]{:S(2)}, u32[]{:S(2)}) collective-permute-start(bf16[2048,128]{1,0:T(8,128)(2,1)} %collective-permute-done.refs_2_), channel_id=1, source_target_pairs={{0,1},{1,0},{2,3},{3,2},{4,5},{5,4},{6,7},{7,6},{8,9},{9,8},{10,11... | collective-permute-start | bytes 1572872 | tf_op jit(solution)/shard_map/ppermute | solution.py:600
  28.9 14.5 %collective-permute-start.3 = (bf16[2048,128]{1,0:T(8,128)(2,1)}, bf16[2048,128]{1,0:T(8,128)(2,1)S(1)}, u32[]{:S(2)}, u32[]{:S(2)}) collective-permute-start(bf16[2048,128]{1,0:T(8,128)(2,1)} %bitcast.10), channel_id=1, source_target_pairs={{0,2},{1,3},{2,0},{3,1},{4,6},{5,7},{6,4},{7,5},{8,10},{9,11},{10,... | collective-permute-start | bytes 1572872 | tf_op jit(solution)/shard_map/ppermute | solution.py:600
  30.4 5.1 %collective-permute-start.7 = (bf16[2,2,128,128]{3,2,1,0:T(8,128)(2,1)}, bf16[2,2,128,128]{3,2,1,0:T(8,128)(2,1)S(1)}, u32[]{:S(2)}, u32[]{:S(2)}) collective-permute-start(bf16[2,2,128,128]{3,2,1,0:T(8,128)(2,1)} %collective-permute-done.1.refs_8_), channel_id=1, source_target_pairs={{0,1},{1,0},{2,3},{3,2},{4,5},{5,4},{6,7},{7,6},{8,9},{9,8},{10,11... | collective-permute-start | bytes 393224 | tf_op jit(solution)/shard_map/ppermute | solution.py:600
  30.6 4.8 %collective-permute-start.6 = (bf16[2,128,128]{2,1,0:T(8,128)(2,1)S(1)}, bf16[2,128,128]{2,1,0:T(8,128)(2,1)S(1)}, u32[]{:S(2)}, u32[]{:S(2)}) collective-permute-start(bf16[2,128,128]{2,1,0:T(8,128)(2,1)S(1)} %copy-done.3), channel_id=1, source_target_pairs={{0,1},{1,0},{2,3},{3,2},{4,5},{5,4},{6,7},{7,6},{8,9},{9,8},{10,11... | collective-permute-start | bytes 196616 | tf_op jit(solution)/shard_map/ppermute | solution.py:600
  30.9 12.5 %collective-permute-start.2 = (bf16[2048,128]{1,0:T(8,128)(2,1)}, bf16[2048,128]{1,0:T(8,128)(2,1)S(1)}, u32[]{:S(2)}, u32[]{:S(2)}) collective-permute-start(bf16[2048,128]{1,0:T(8,128)(2,1)} %bitcast.11), channel_id=1, source_target_pairs={{0,1},{1,0},{2,3},{3,2},{4,5},{5,4},{6,7},{7,6},{8,9},{9,8},{10,11... | collective-permute-start | bytes 1572872 | tf_op jit(solution)/shard_map/ppermute | solution.py:600
  35.4 30.3 %copy-start.2 = (bf16[2,128,128]{2,1,0:T(8,128)(2,1)}, bf16[2,128,128]{2,1,0:T(8,128)(2,1)S(1)}, u32[]{:S(2)}) copy-start(bf16[2,128,128]{2,1,0:T(8,128)(2,1)S(1)} %collective-permute-done.6.refs_7_) | copy-start | bytes 196612
  35.5 9.9 %copy-start.1 = (bf16[2,2,128,128]{3,2,1,0:T(8,128)(2,1)}, bf16[2,2,128,128]{3,2,1,0:T(8,128)(2,1)S(1)}, u32[]{:S(2)}) copy-start(bf16[2,2,128,128]{3,2,1,0:T(8,128)(2,1)S(1)} %collective-permute-done.7.refs_9_) | copy-start | bytes 393220
  43.4 1.9 %collective-permute-start.8 = (bf16[2048,128]{1,0:T(8,128)(2,1)S(1)}, bf16[2048,128]{1,0:T(8,128)(2,1)S(1)}, u32[]{:S(2)}, u32[]{:S(2)}) collective-permute-start(bf16[2048,128]{1,0:T(8,128)(2,1)S(1)} %collective-permute-done.3.refs_2_.refs_6_), channel_id=1, source_target_pairs={{0,1},{1,0},{2,3},{3,2},{4,5},{5,4},{6,7},{7,6},{8,9},{9,8},{10,11... | collective-permute-start | bytes 1572872 | tf_op jit(solution)/shard_map/ppermute | solution.py:600
  49.3 14.3 %collective-permute-start.10 = (bf16[2048,128]{1,0:T(8,128)(2,1)}, bf16[2048,128]{1,0:T(8,128)(2,1)}, u32[]{:S(2)}, u32[]{:S(2)}) collective-permute-start(bf16[2048,128]{1,0:T(8,128)(2,1)} %get-tuple-element.52.refs_8_.refs_2_), channel_id=1, source_target_pairs={{0,2},{1,3},{2,0},{3,1},{4,6},{5,7},{6,4},{7,5},{8,10},{9,11},{10,... | collective-permute-start | bytes 1572872 | tf_op jit(solution)/shard_map/ppermute | solution.py:600
  54.7 21.1 %all-to-all-start.1 = ((f32[8,136,128]{2,1,0:T(8,128)}), f32[8,136,128]{2,1,0:T(8,128)}, u32[]{:S(2)}, u32[]{:S(2)}) async-start(f32[8,136,128]{2,1,0:T(8,128)} %weight_parts.1), calls=%async_computation.1 | async-start | bytes 1114112 | tf_op jit(solution)/shard_map/all_to_all | solution.py:642
  60.5 3.2 %collective-permute-start.9 = (bf16[2048,128]{1,0:T(8,128)(2,1)}, bf16[2048,128]{1,0:T(8,128)(2,1)S(1)}, u32[]{:S(2)}, u32[]{:S(2)}) collective-permute-start(bf16[2048,128]{1,0:T(8,128)(2,1)} %get-tuple-element.52.refs_8_.refs_2_), channel_id=1, source_target_pairs={{0,1},{1,0},{2,3},{3,2},{4,5},{5,4},{6,7},{7,6},{8,9},{9,8},{10,11... | collective-permute-start | bytes 1572872 | tf_op jit(solution)/shard_map/ppermute | solution.py:600
  63.6 2.1 %collective-permute-start.11 = (bf16[2048,128]{1,0:T(8,128)(2,1)}, bf16[2048,128]{1,0:T(8,128)(2,1)S(1)}, u32[]{:S(2)}, u32[]{:S(2)}) collective-permute-start(bf16[2048,128]{1,0:T(8,128)(2,1)} %collective-permute-done.10.refs_4_), channel_id=1, source_target_pairs={{0,1},{1,0},{2,3},{3,2},{4,5},{5,4},{6,7},{7,6},{8,9},{9,8},{10,11... | collective-permute-start | bytes 1572872 | tf_op jit(solution)/shard_map/ppermute | solution.py:600
  75.8 14.2 %all-to-all-start.2 = ((bf16[8,160,128]{2,1,0:T(8,128)(2,1)}), bf16[8,160,128]{2,1,0:T(8,128)(2,1)}, u32[]{:S(2)}, u32[]{:S(2)}) async-start(bf16[8,160,128]{2,1,0:T(8,128)(2,1)} %get-tuple-element.58), calls=%async_computation.2 | async-start | bytes 655360 | tf_op jit(solution)/shard_map/all_to_all | solution.py:648
  90.0 12.1 %all-to-all-start.3 = ((bf16[8,128,128]{2,1,0:T(8,128)(2,1)}), bf16[8,128,128]{2,1,0:T(8,128)(2,1)S(1)}, u32[]{:S(2)}, u32[]{:S(2)}) async-start(bf16[8,128,128]{2,1,0:T(8,128)(2,1)} %get-tuple-element.63), calls=%async_computation.3 | async-start | bytes 524288 | tf_op jit(solution)/shard_map/all_to_all | solution.py:652

commit v11 on v10

--- a/solution.py
+++ b/solution.py
@@ -307,12 +307,18 @@
 
 
 def weights_kernel(*refs, n_feat):
-    shards, grad, out_h, out, sems = refs[: 2 * n_feat], *refs[2 * n_feat :]
+    n = 2 * n_feat
+    shards_h, grad_h, out_h, refs = refs[:n], refs[n], refs[n + 1], refs[n + 2 :]
+    shards, (grad, out, sems, in_sems) = refs[:n], refs[n:]
+    first = start_copies(sems, (grad_h, grad))
+    pending = start_copies(in_sems, *zip(shards_h, shards))
     n_dom, chunk = out.shape[0], out.shape[1] - 8
     width = grad.shape[1]
+    wait_copies(first)
     flipped = grad[...].T
     bias = jnp.sum(grad[...].astype(F32), axis=0, keepdims=True)
     for i, shard in enumerate(shards):
+        pending[i].wait()
         block = jnp.dot(flipped, shard[...], preferred_element_type=F32).T
         for row in range(0, width, min(chunk, width)):
             q, start = divmod(i * width + row, chunk)
@@ -330,11 +336,13 @@
     return pl.pallas_call(
         functools.partial(weights_kernel, n_feat=n_feat),
         out_shape=pltpu.HBM((n_dom, chunk + 8, width), F32),
-        in_specs=[VMEM] * (2 * n_feat + 1),
+        in_specs=[ANY] * (2 * n_feat + 1),
         out_specs=HBM,
-        scratch_shapes=[
+        scratch_shapes=[pltpu.VMEM(grad.shape, BF16)] * (2 * n_feat + 1)
+        + [
             pltpu.VMEM((n_dom, chunk + 8, width), F32),
             pltpu.SemaphoreType.DMA((1,)),
+            pltpu.SemaphoreType.DMA((2 * n_feat,)),
         ],
         compiler_params=params(),
         cost_estimate=cost(4 * n_feat * width * width * grad.shape[0], 1 << 22),

time: 104 us -> 105 us (level)
  Pallas kernels: 44.3 us -> 46.4 us
    pallas_call x1, Pallas kernels: 3.87 us -> 5.39 us  [weight_parts(): pl.pallas_call(functools.partial(weights_kernel, n_feat=n_feat), out_shap...]
    ppermute x12, waiting for transfers between devices: 17.4 us -> 15.9 us  [swap(): return lax.ppermute(x, 'feat', [(j, j ^ k) for j in range(n_feat)])]
    all_to_all x1, waiting for transfers between devices: 3.73 us -> 5.24 us  [body(): part_sums = lax.all_to_all(parts, 'dom', 0, 0, tiled=True)]
  transfers between devices with their start and end apart: 16 -> 16, of which waited for: 9 -> 10; matrix products, arithmetic and copies ran while one was open for 0% -> 0% of each run, Pallas kernels for 34% -> 36%
where the time goes in v11:
time: 105 us; the launch traced here: 104 us
  Pallas kernels  46.4 us (44%)
  waiting for transfers between devices  30.7 us (29%)
  starting transfers between devices  26.5 us (25%)
    ppermute x12, waiting for transfers between devices, swap(): return lax.ppermute(x, 'feat', [(j, j ^ k) for j in range(n_feat)])  15.9 us
    pallas_call x2, Pallas kernels, stream_call(): pl.pallas_call(run, out_shape=tuple((pltpu.HBM(shape, t) for shape, t in...  8.24 us
    all_to_all x1, starting transfers between devices, body(): incoming = lax.all_to_all(outgoing, 'dom', 0, 0, tiled=True)  7.26 us
    pallas_call x1, Pallas kernels, back_far(): pl.pallas_call(functools.partial(back_far_kernel, n_feat=n_feat), out_sha...  6.3 us
    ppermute x12, starting transfers between devices, swap(): return lax.ppermute(x, 'feat', [(j, j ^ k) for j in range(n_feat)])  5.89 us
    all_to_all x1, starting transfers between devices, body(): part_sums = lax.all_to_all(parts, 'dom', 0, 0, tiled=True)  5.73 us
    pallas_call x1, Pallas kernels, weight_parts(): pl.pallas_call(functools.partial(weights_kernel, n_feat=n_feat), out_shap...  5.39 us
    pallas_call x1, Pallas kernels, own_tiles(): pl.pallas_call(functools.partial(own_kernel, far_blocks=far_blocks), out_...  5.27 us
  transfers between devices with their start and end apart: 16, of which 10 were waited for; matrix products, arithmetic and copies ran while one was open for 0% of the time, Pallas kernels for 36%

profile of v11, /device:TPU:0, one launch (start us, length us, event | category | flops | bytes accessed | tf_op | source)
XLA Modules:
  0.0 104.5 jit_solution(524623490304912476)
XLA Ops:
  0.6 4.4 %pick_rows.1 = bf16[8,160,128]{2,1,0:T(8,128)(2,1)} custom-call(s32[8,128]{1,0:T(8,128)} %bitcast.15, s32[1,8]{1,0:T(1,128)} %count_h.3, s32[32]{0:T(128)} %hub_h.3, bf16[2048,128]{1,0:T(8,128)(2,1)} %refs_0_.3), custom_call_target="tpu_custom_call" | custom-call | bytes 2097152 | tf_op jit(solution)/shard_map/pick_rows/pallas_call | solution.py:79
  5.1 7.3 %all-to-all-start = ((bf16[8,160,128]{2,1,0:T(8,128)(2,1)}), bf16[8,160,128]{2,1,0:T(8,128)(2,1)}, u32[]{:S(2)}, u32[]{:S(2)}) async-start(bf16[8,160,128]{2,1,0:T(8,128)(2,1)} %pick_rows.1), calls=%async_computation | async-start | bytes 655360 | tf_op jit(solution)/shard_map/all_to_all | solution.py:613
  12.3 1.5 %collective-permute-start = (bf16[2048,128]{1,0:T(8,128)(2,1)}, bf16[2048,128]{1,0:T(8,128)(2,1)}, u32[]{:S(2)}, u32[]{:S(2)}) collective-permute-start(bf16[2048,128]{1,0:T(8,128)(2,1)} %refs_0_.3), channel_id=1, source_target_pairs={{0,2},{1,3},{2,0},{3,1},{4,6},{5,7},{6,4},{7,5},{8,10},{9,11},{10,... | collective-permute-start | bytes 1572872 | tf_op jit(solution)/shard_map/ppermute | solution.py:608
  13.9 1.7 %cut_weights.1 = (bf16[2,128,128]{2,1,0:T(8,128)(2,1)}, bf16[2,128,128]{2,1,0:T(8,128)(2,1)}, bf16[2,2,128,128]{3,2,1,0:T(8,128)(2,1)}) custom-call(s32[1]{0:T(128)} %bitcast.me_s, bf16[512,128]{1,0:T(8,128)(2,1)} %refs_4_.1, bf16[512,128]{1,0:T(8,128)(2,1)} %refs_6_.1), custom_call_target="tpu_custom_call" | custom-call | bytes 1048576 | tf_op jit(solution)/shard_map/cut_weights/pallas_call | solution.py:524
  15.5 0.5 collective-permute-start.1
  16.1 5.3 %own_tiles.1 = (f32[16,128,128]{2,1,0:T(8,128)}, s32[2,122]{1,0:T(2,128)S(1)}) custom-call(s32[106]{0:T(128)} %dst_h.1, s32[106]{0:T(128)} %src_h.1, bf16[106,128,128]{2,1,0:T(8,128)(2,1)} %tiles.3, bf16[16,128,128]{2,1,0:T(8,128)(2,1)} %bitcast.9), custom_call_target="tpu_custom_call" | custom-call | flops 444596224 | bytes 8388608 | tf_op jit(solution)/shard_map/own_tiles/pallas_call | solution.py:176
  21.3 1.4 %all-to-all-done.incoming_h = bf16[8,160,128]{2,1,0:T(8,128)(2,1)} async-done(((bf16[8,160,128]{2,1,0:T(8,128)(2,1)}), bf16[8,160,128]{2,1,0:T(8,128)(2,1)}, u32[]{:S(2)}, u32[]{:S(2)}) %all-to-all-start) | async-done | bytes 327712 | tf_op jit(solution)/shard_map/all_to_all | solution.py:613
  22.8 3.8 %far_tiles.1 = bf16[16,128,128]{2,1,0:T(8,128)(2,1)} custom-call(s32[2,122]{1,0:T(2,128)S(1)} %get-tuple-element.40.lists.refs_0_, bf16[106,128,128]{2,1,0:T(8,128)(2,1)S(1)} %copy-done, bf16[8,160,128]{2,1,0:T(8,128)(2,1)} %all-to-all-done.incoming_h, f32[16,128,128]{2,1,0:T(8,128)} %get-tuple-element.41.base_h), custom_call_target="tpu_custom_call" | custom-call | flops 222298112 | bytes 4194304 | tf_op jit(solution)/shard_map/far_tiles/pallas_call | solution.py:218
  26.6 2.3 %collective-permute-done.1.refs_8_ = bf16[2,2,128,128]{3,2,1,0:T(8,128)(2,1)} collective-permute-done((bf16[2,2,128,128]{3,2,1,0:T(8,128)(2,1)}, bf16[2,2,128,128]{3,2,1,0:T(8,128)(2,1)}, u32[]{:S(2)}, u32[]{:S(2)}) %collective-permute-start.1) | collective-permute-done | bytes 131104 | tf_op jit(solution)/shard_map/ppermute | solution.py:608
  28.9 1.5 %collective-permute-start.3 = (bf16[2048,128]{1,0:T(8,128)(2,1)}, bf16[2048,128]{1,0:T(8,128)(2,1)S(1)}, u32[]{:S(2)}, u32[]{:S(2)}) collective-permute-start(bf16[2048,128]{1,0:T(8,128)(2,1)} %bitcast.10), channel_id=1, source_target_pairs={{0,2},{1,3},{2,0},{3,1},{4,6},{5,7},{6,4},{7,5},{8,10},{9,11},{10,... | collective-permute-start | bytes 1572872 | tf_op jit(solution)/shard_map/ppermute | solution.py:608
  30.6 0.3 collective-permute-start.6
  30.9 0.2 collective-permute-start.2
  31.1 4.3 %self_dense.1.refs_4_ = f32[2048,128]{1,0:T(8,128)} custom-call(s32[1]{0:T(128)} %bitcast.me_s, bf16[2048,128]{1,0:T(8,128)(2,1)} %refs_0_.3, bf16[2048,128]{1,0:T(8,128)(2,1)} %collective-permute-done.4.refs_1_, bf16[2048,128]{1,0:T(8,128)(2,1)} %collective-permute-done.refs_2_, bf16[2048,128]{1,0:T(8,128)(2,1)S(1)} %collective-permute-done.5.refs_3_, ...), custom_call_target="tpu_custom_call" | custom-call | flops 268435456 | bytes 4194304 | tf_op jit(solution)/shard_map/self_dense/pallas_call | solution.py:280
  35.5 7.9 %collective-permute-done.3.refs_2_.refs_6_ = bf16[2048,128]{1,0:T(8,128)(2,1)S(1)} collective-permute-done((bf16[2048,128]{1,0:T(8,128)(2,1)}, bf16[2048,128]{1,0:T(8,128)(2,1)S(1)}, u32[]{:S(2)}, u32[]{:S(2)}) %collective-permute-start.3) | collective-permute-done | bytes 524320 | tf_op jit(solution)/shard_map/ppermute | solution.py:608
  43.4 1.9 %collective-permute-done.8.refs_3_.refs_7_ = bf16[2048,128]{1,0:T(8,128)(2,1)S(1)} collective-permute-done((bf16[2048,128]{1,0:T(8,128)(2,1)S(1)}, bf16[2048,128]{1,0:T(8,128)(2,1)S(1)}, u32[]{:S(2)}, u32[]{:S(2)}) %collective-permute-start.8) | collective-permute-done | bytes 524320 | tf_op jit(solution)/shard_map/ppermute | solution.py:608
  45.3 4.0 %forward_dense.1 = (bf16[2048,128]{1,0:T(8,128)(2,1)}, bf16[2048,128]{1,0:T(8,128)(2,1)}) custom-call(s32[1]{0:T(128)} %bitcast.me_s, bf16[2048,128]{1,0:T(8,128)(2,1)} %bitcast.12, bf16[2048,128]{1,0:T(8,128)(2,1)S(1)} %collective-permute-done.2.refs_1_.refs_5_, bf16[2048,128]{1,0:T(8,128)(2,1)S(1)} %collective-permute-done.3.refs_2_.refs_6_, ...), custom_call_target="tpu_custom_call" | custom-call | flops 268435456 | bytes 4194304 | tf_op jit(solution)/shard_map/forward_dense/pallas_call | solution.py:280
  49.3 1.6 %collective-permute-start.10 = (bf16[2048,128]{1,0:T(8,128)(2,1)}, bf16[2048,128]{1,0:T(8,128)(2,1)}, u32[]{:S(2)}, u32[]{:S(2)}) collective-permute-start(bf16[2048,128]{1,0:T(8,128)(2,1)} %get-tuple-element.52.refs_8_.refs_2_), channel_id=1, source_target_pairs={{0,2},{1,3},{2,0},{3,1},{4,6},{5,7},{6,4},{7,5},{8,10},{9,11},{10,... | collective-permute-start | bytes 1572872 | tf_op jit(solution)/shard_map/ppermute | solution.py:608
  50.9 5.4 %weight_parts.1 = f32[8,136,128]{2,1,0:T(8,128)} custom-call(bf16[2048,128]{1,0:T(8,128)(2,1)} %refs_0_.3, bf16[2048,128]{1,0:T(8,128)(2,1)} %collective-permute-done.4.refs_1_, bf16[2048,128]{1,0:T(8,128)(2,1)} %collective-permute-done.refs_2_, bf16[2048,128]{1,0:T(8,128)(2,1)S(1)} %collective-permute-done.5.refs_3_, bf16[2048,128]{1,0:T(8,128)(2,1)} %bitcast.13, ...), custom_call_target="tpu_custom_call" | custom-call | flops 536870912 | bytes 4194304 | tf_op jit(solution)/shard_map/weight_parts/pallas_call | solution.py:336
  56.3 5.7 %all-to-all-start.1 = ((f32[8,136,128]{2,1,0:T(8,128)}), f32[8,136,128]{2,1,0:T(8,128)}, u32[]{:S(2)}, u32[]{:S(2)}) async-start(f32[8,136,128]{2,1,0:T(8,128)} %weight_parts.1), calls=%async_computation.1 | async-start | bytes 1114112 | tf_op jit(solution)/shard_map/all_to_all | solution.py:650
  62.0 1.6 %collective-permute-done.10.refs_4_ = bf16[2048,128]{1,0:T(8,128)(2,1)} collective-permute-done((bf16[2048,128]{1,0:T(8,128)(2,1)}, bf16[2048,128]{1,0:T(8,128)(2,1)}, u32[]{:S(2)}, u32[]{:S(2)}) %collective-permute-start.10) | collective-permute-done | bytes 524320 | tf_op jit(solution)/shard_map/ppermute | solution.py:608
  63.6 0.5 collective-permute-done.9.refs_3_
  64.1 1.6 %collective-permute-done.11.refs_5_ = bf16[2048,128]{1,0:T(8,128)(2,1)S(1)} collective-permute-done((bf16[2048,128]{1,0:T(8,128)(2,1)}, bf16[2048,128]{1,0:T(8,128)(2,1)S(1)}, u32[]{:S(2)}, u32[]{:S(2)}) %collective-permute-start.11) | collective-permute-done | bytes 524320 | tf_op jit(solution)/shard_map/ppermute | solution.py:608
  65.8 6.3 %back_far.1 = (bf16[8,160,128]{2,1,0:T(8,128)(2,1)}, bf16[16,128,128]{2,1,0:T(8,128)(2,1)}, f32[16,128,128]{2,1,0:T(8,128)}) custom-call(s32[2,122]{1,0:T(2,128)S(1)} %get-tuple-element.40.lists.refs_0_, bf16[106,128,128]{2,1,0:T(8,128)(2,1)S(1)} %copy-done, bf16[2048,128]{1,0:T(8,128)(2,1)} %get-tuple-element.52.refs_8_.refs_2_, ...), custom_call_target="tpu_custom_call" | custom-call | flops 536870912 | bytes 4194304 | tf_op jit(solution)/shard_map/back_far/pallas_call | solution.py:401
  72.1 5.2 %all-to-all-done.1.parts = f32[8,136,128]{2,1,0:T(8,128)} async-done(((f32[8,136,128]{2,1,0:T(8,128)}), f32[8,136,128]{2,1,0:T(8,128)}, u32[]{:S(2)}, u32[]{:S(2)}) %all-to-all-start.1) | async-done | bytes 557088 | tf_op jit(solution)/shard_map/all_to_all | solution.py:650
  77.3 4.1 %all-to-all-start.2 = ((bf16[8,160,128]{2,1,0:T(8,128)(2,1)}), bf16[8,160,128]{2,1,0:T(8,128)(2,1)}, u32[]{:S(2)}, u32[]{:S(2)}) async-start(bf16[8,160,128]{2,1,0:T(8,128)(2,1)} %get-tuple-element.58), calls=%async_computation.2 | async-start | bytes 655360 | tf_op jit(solution)/shard_map/all_to_all | solution.py:656
  81.4 1.8 %sum_parts.1 = (bf16[8,128,128]{2,1,0:T(8,128)(2,1)}, f32[1,128]{1,0:T(1,128)}) custom-call(f32[8,136,128]{2,1,0:T(8,128)} %all-to-all-done.1.parts), custom_call_target="tpu_custom_call" | custom-call | bytes 1048576 | tf_op jit(solution)/shard_map/sum_parts/pallas_call | solution.py:548
  83.2 4.7 %back_own.1 = f32[16,128,128]{2,1,0:T(8,128)} custom-call(s32[2,122]{1,0:T(2,128)S(1)} %get-tuple-element.40.lists.refs_0_, bf16[106,128,128]{2,1,0:T(8,128)(2,1)S(1)} %copy-done, bf16[16,128,128]{2,1,0:T(8,128)(2,1)} %get-tuple-element.59.back_h, f32[16,128,128]{2,1,0:T(8,128)} %get-tuple-element.60.direct_h), custom_call_target="tpu_custom_call" | custom-call | flops 444596224 | bytes 8388608 | tf_op jit(solution)/shard_map/back_own/pallas_call | solution.py:430
  87.8 3.7 %all-to-all-done.2.incoming_h = bf16[8,160,128]{2,1,0:T(8,128)(2,1)} async-done(((bf16[8,160,128]{2,1,0:T(8,128)(2,1)}), bf16[8,160,128]{2,1,0:T(8,128)(2,1)}, u32[]{:S(2)}, u32[]{:S(2)}) %all-to-all-start.2) | async-done | bytes 327712 | tf_op jit(solution)/shard_map/all_to_all | solution.py:656
  91.6 3.6 %all-to-all-start.3 = ((bf16[8,128,128]{2,1,0:T(8,128)(2,1)}), bf16[8,128,128]{2,1,0:T(8,128)(2,1)S(1)}, u32[]{:S(2)}, u32[]{:S(2)}) async-start(bf16[8,128,128]{2,1,0:T(8,128)(2,1)} %get-tuple-element.63), calls=%async_computation.3 | async-start | bytes 524288 | tf_op jit(solution)/shard_map/all_to_all | solution.py:660
  95.1 4.1 %finish.1 = f32[2048,128]{1,0:T(8,128)} custom-call(s32[8,128]{1,0:T(8,128)} %bitcast.16, s32[1,8]{1,0:T(1,128)} %count_h.3, s32[32]{0:T(128)} %hub_h.3, bf16[8,160,128]{2,1,0:T(8,128)(2,1)} %all-to-all-done.2.incoming_h, f32[2048,128]{1,0:T(8,128)} %bitcast.14), custom_call_target="tpu_custom_call" | custom-call | flops 536870912 | bytes 4194304 | tf_op jit(solution)/shard_map/finish/pallas_call | solution.py:492
  99.2 4.5 %all-to-all-done.3 = bf16[8,128,128]{2,1,0:T(8,128)(2,1)S(1)} async-done(((bf16[8,128,128]{2,1,0:T(8,128)(2,1)}), bf16[8,128,128]{2,1,0:T(8,128)(2,1)S(1)}, u32[]{:S(2)}, u32[]{:S(2)}) %all-to-all-start.3) | async-done | bytes 262176 | tf_op jit(solution)/shard_map/all_to_all | solution.py:660
  103.7 0.8 place_weights.1
  (20 shorter events, 0.3 us)
Async XLA Ops:
  0.6 22.1 %copy-start = (bf16[106,128,128]{2,1,0:T(8,128)(2,1)S(1)}, bf16[106,128,128]{2,1,0:T(8,128)(2,1)}, u32[]{:S(2)}) copy-start(bf16[106,128,128]{2,1,0:T(8,128)(2,1)} %tiles.3) | copy-start | bytes 10420228
  5.1 17.7 %all-to-all-start = ((bf16[8,160,128]{2,1,0:T(8,128)(2,1)}), bf16[8,160,128]{2,1,0:T(8,128)(2,1)}, u32[]{:S(2)}, u32[]{:S(2)}) async-start(bf16[8,160,128]{2,1,0:T(8,128)(2,1)} %pick_rows.1), calls=%async_computation | async-start | bytes 655360 | tf_op jit(solution)/shard_map/all_to_all | solution.py:613
  12.3 16.5 %collective-permute-start = (bf16[2048,128]{1,0:T(8,128)(2,1)}, bf16[2048,128]{1,0:T(8,128)(2,1)}, u32[]{:S(2)}, u32[]{:S(2)}) collective-permute-start(bf16[2048,128]{1,0:T(8,128)(2,1)} %refs_0_.3), channel_id=1, source_target_pairs={{0,2},{1,3},{2,0},{3,1},{4,6},{5,7},{6,4},{7,5},{8,10},{9,11},{10,... | collective-permute-start | bytes 1572872 | tf_op jit(solution)/shard_map/ppermute | solution.py:608
  15.5 13.3 %collective-permute-start.1 = (bf16[2,2,128,128]{3,2,1,0:T(8,128)(2,1)}, bf16[2,2,128,128]{3,2,1,0:T(8,128)(2,1)}, u32[]{:S(2)}, u32[]{:S(2)}) collective-permute-start(bf16[2,2,128,128]{3,2,1,0:T(8,128)(2,1)} %get-tuple-element.42), channel_id=1, source_target_pairs={{0,2},{1,3},{2,0},{3,1},{4,6},{5,7},{6,4},{7,5},{8,10},{9,11},{10,... | collective-permute-start | bytes 393224 | tf_op jit(solution)/shard_map/ppermute | solution.py:608
  16.0 14.8 %collective-permute-start.4 = (bf16[2048,128]{1,0:T(8,128)(2,1)}, bf16[2048,128]{1,0:T(8,128)(2,1)}, u32[]{:S(2)}, u32[]{:S(2)}) collective-permute-start(bf16[2048,128]{1,0:T(8,128)(2,1)} %refs_0_.3), channel_id=1, source_target_pairs={{0,1},{1,0},{2,3},{3,2},{4,5},{5,4},{6,7},{7,6},{8,9},{9,8},{10,11... | collective-permute-start | bytes 1572872 | tf_op jit(solution)/shard_map/ppermute | solution.py:608
  22.8 7.8 %copy-start.3 = (bf16[2,128,128]{2,1,0:T(8,128)(2,1)S(1)}, bf16[2,128,128]{2,1,0:T(8,128)(2,1)}, u32[]{:S(2)}) copy-start(bf16[2,128,128]{2,1,0:T(8,128)(2,1)} %get-tuple-element.47) | copy-start | bytes 196612
  28.9 2.3 %collective-permute-start.5 = (bf16[2048,128]{1,0:T(8,128)(2,1)}, bf16[2048,128]{1,0:T(8,128)(2,1)S(1)}, u32[]{:S(2)}, u32[]{:S(2)}) collective-permute-start(bf16[2048,128]{1,0:T(8,128)(2,1)} %collective-permute-done.refs_2_), channel_id=1, source_target_pairs={{0,1},{1,0},{2,3},{3,2},{4,5},{5,4},{6,7},{7,6},{8,9},{9,8},{10,11... | collective-permute-start | bytes 1572872 | tf_op jit(solution)/shard_map/ppermute | solution.py:608
  28.9 14.5 %collective-permute-start.3 = (bf16[2048,128]{1,0:T(8,128)(2,1)}, bf16[2048,128]{1,0:T(8,128)(2,1)S(1)}, u32[]{:S(2)}, u32[]{:S(2)}) collective-permute-start(bf16[2048,128]{1,0:T(8,128)(2,1)} %bitcast.10), channel_id=1, source_target_pairs={{0,2},{1,3},{2,0},{3,1},{4,6},{5,7},{6,4},{7,5},{8,10},{9,11},{10,... | collective-permute-start | bytes 1572872 | tf_op jit(solution)/shard_map/ppermute | solution.py:608
  30.4 5.1 %collective-permute-start.7 = (bf16[2,2,128,128]{3,2,1,0:T(8,128)(2,1)}, bf16[2,2,128,128]{3,2,1,0:T(8,128)(2,1)S(1)}, u32[]{:S(2)}, u32[]{:S(2)}) collective-permute-start(bf16[2,2,128,128]{3,2,1,0:T(8,128)(2,1)} %collective-permute-done.1.refs_8_), channel_id=1, source_target_pairs={{0,1},{1,0},{2,3},{3,2},{4,5},{5,4},{6,7},{7,6},{8,9},{9,8},{10,11... | collective-permute-start | bytes 393224 | tf_op jit(solution)/shard_map/ppermute | solution.py:608
  30.6 4.8 %collective-permute-start.6 = (bf16[2,128,128]{2,1,0:T(8,128)(2,1)S(1)}, bf16[2,128,128]{2,1,0:T(8,128)(2,1)S(1)}, u32[]{:S(2)}, u32[]{:S(2)}) collective-permute-start(bf16[2,128,128]{2,1,0:T(8,128)(2,1)S(1)} %copy-done.3), channel_id=1, source_target_pairs={{0,1},{1,0},{2,3},{3,2},{4,5},{5,4},{6,7},{7,6},{8,9},{9,8},{10,11... | collective-permute-start | bytes 196616 | tf_op jit(solution)/shard_map/ppermute | solution.py:608
  30.9 12.5 %collective-permute-start.2 = (bf16[2048,128]{1,0:T(8,128)(2,1)}, bf16[2048,128]{1,0:T(8,128)(2,1)S(1)}, u32[]{:S(2)}, u32[]{:S(2)}) collective-permute-start(bf16[2048,128]{1,0:T(8,128)(2,1)} %bitcast.11), channel_id=1, source_target_pairs={{0,1},{1,0},{2,3},{3,2},{4,5},{5,4},{6,7},{7,6},{8,9},{9,8},{10,11... | collective-permute-start | bytes 1572872 | tf_op jit(solution)/shard_map/ppermute | solution.py:608
  35.4 30.3 %copy-start.2 = (bf16[2,128,128]{2,1,0:T(8,128)(2,1)}, bf16[2,128,128]{2,1,0:T(8,128)(2,1)S(1)}, u32[]{:S(2)}) copy-start(bf16[2,128,128]{2,1,0:T(8,128)(2,1)S(1)} %collective-permute-done.6.refs_7_) | copy-start | bytes 196612
  35.5 9.9 %copy-start.1 = (bf16[2,2,128,128]{3,2,1,0:T(8,128)(2,1)}, bf16[2,2,128,128]{3,2,1,0:T(8,128)(2,1)S(1)}, u32[]{:S(2)}) copy-start(bf16[2,2,128,128]{3,2,1,0:T(8,128)(2,1)S(1)} %collective-permute-done.7.refs_9_) | copy-start | bytes 393220
  43.4 1.9 %collective-permute-start.8 = (bf16[2048,128]{1,0:T(8,128)(2,1)S(1)}, bf16[2048,128]{1,0:T(8,128)(2,1)S(1)}, u32[]{:S(2)}, u32[]{:S(2)}) collective-permute-start(bf16[2048,128]{1,0:T(8,128)(2,1)S(1)} %collective-permute-done.3.refs_2_.refs_6_), channel_id=1, source_target_pairs={{0,1},{1,0},{2,3},{3,2},{4,5},{5,4},{6,7},{7,6},{8,9},{9,8},{10,11... | collective-permute-start | bytes 1572872 | tf_op jit(solution)/shard_map/ppermute | solution.py:608
  49.3 14.3 %collective-permute-start.10 = (bf16[2048,128]{1,0:T(8,128)(2,1)}, bf16[2048,128]{1,0:T(8,128)(2,1)}, u32[]{:S(2)}, u32[]{:S(2)}) collective-permute-start(bf16[2048,128]{1,0:T(8,128)(2,1)} %get-tuple-element.52.refs_8_.refs_2_), channel_id=1, source_target_pairs={{0,2},{1,3},{2,0},{3,1},{4,6},{5,7},{6,4},{7,5},{8,10},{9,11},{10,... | collective-permute-start | bytes 1572872 | tf_op jit(solution)/shard_map/ppermute | solution.py:608
  56.3 21.0 %all-to-all-start.1 = ((f32[8,136,128]{2,1,0:T(8,128)}), f32[8,136,128]{2,1,0:T(8,128)}, u32[]{:S(2)}, u32[]{:S(2)}) async-start(f32[8,136,128]{2,1,0:T(8,128)} %weight_parts.1), calls=%async_computation.1 | async-start | bytes 1114112 | tf_op jit(solution)/shard_map/all_to_all | solution.py:650
  62.0 2.1 %collective-permute-start.9 = (bf16[2048,128]{1,0:T(8,128)(2,1)}, bf16[2048,128]{1,0:T(8,128)(2,1)S(1)}, u32[]{:S(2)}, u32[]{:S(2)}) collective-permute-start(bf16[2048,128]{1,0:T(8,128)(2,1)} %get-tuple-element.52.refs_8_.refs_2_), channel_id=1, source_target_pairs={{0,1},{1,0},{2,3},{3,2},{4,5},{5,4},{6,7},{7,6},{8,9},{9,8},{10,11... | collective-permute-start | bytes 1572872 | tf_op jit(solution)/shard_map/ppermute | solution.py:608
  63.6 2.1 %collective-permute-start.11 = (bf16[2048,128]{1,0:T(8,128)(2,1)}, bf16[2048,128]{1,0:T(8,128)(2,1)S(1)}, u32[]{:S(2)}, u32[]{:S(2)}) collective-permute-start(bf16[2048,128]{1,0:T(8,128)(2,1)} %collective-permute-done.10.refs_4_), channel_id=1, source_target_pairs={{0,1},{1,0},{2,3},{3,2},{4,5},{5,4},{6,7},{7,6},{8,9},{9,8},{10,11... | collective-permute-start | bytes 1572872 | tf_op jit(solution)/shard_map/ppermute | solution.py:608
  77.3 14.2 %all-to-all-start.2 = ((bf16[8,160,128]{2,1,0:T(8,128)(2,1)}), bf16[8,160,128]{2,1,0:T(8,128)(2,1)}, u32[]{:S(2)}, u32[]{:S(2)}) async-start(bf16[8,160,128]{2,1,0:T(8,128)(2,1)} %get-tuple-element.58), calls=%async_computation.2 | async-start | bytes 655360 | tf_op jit(solution)/shard_map/all_to_all | solution.py:656
  91.6 12.1 %all-to-all-start.3 = ((bf16[8,128,128]{2,1,0:T(8,128)(2,1)}), bf16[8,128,128]{2,1,0:T(8,128)(2,1)S(1)}, u32[]{:S(2)}, u32[]{:S(2)}) async-start(bf16[8,128,128]{2,1,0:T(8,128)(2,1)} %get-tuple-element.63), calls=%async_computation.3 | async-start | bytes 524288 | tf_op jit(solution)/shard_map/all_to_all | solution.py:660

commit v12 on v10

--- a/solution.py
+++ b/solution.py
@@ -45,7 +45,7 @@
     copies = start_copies(sems, (x_h, x), (rows_h, rows_s), (count_h, count_s), (hub_h, hub_s))
     n_dom, capacity = rows_s.shape
     hub_dev = hub_s.shape[0]
-    step = 32
+    step = 64
     wait_copies(copies)
     x32[...] = x[...].astype(F32)
     for j in range(hub_dev):
@@ -263,7 +263,7 @@
         wait_copies(copies)
 
 
-def stream_call(kernel, me, streamed, whole, outs, flops, name, block=1024):
+def stream_call(kernel, me, streamed, whole, outs, flops, name, block=2048):
     rows = streamed[0].shape[0]
     n_in, n_whole, n_out = len(streamed), len(whole), len(outs)
 

time: 104 us -> 104 us (level)
  no operation moved by 1% of the time
where the time goes in v12:
time: 104 us; the launch traced here: 103 us
  Pallas kernels  44.1 us (42%)
  waiting for transfers between devices  31.7 us (30%)
  starting transfers between devices  26.5 us (25%)
    ppermute x12, waiting for transfers between devices, swap(): return lax.ppermute(x, 'feat', [(j, j ^ k) for j in range(n_feat)])  17.7 us
    pallas_call x2, Pallas kernels, stream_call(): pl.pallas_call(run, out_shape=tuple((pltpu.HBM(shape, t) for shape, t in...  8.19 us
    all_to_all x1, starting transfers between devices, body(): incoming = lax.all_to_all(outgoing, 'dom', 0, 0, tiled=True)  7.26 us
    pallas_call x1, Pallas kernels, back_far(): pl.pallas_call(functools.partial(back_far_kernel, n_feat=n_feat), out_sha...  6.3 us
    ppermute x12, starting transfers between devices, swap(): return lax.ppermute(x, 'feat', [(j, j ^ k) for j in range(n_feat)])  5.88 us
    all_to_all x1, starting transfers between devices, body(): part_sums = lax.all_to_all(parts, 'dom', 0, 0, tiled=True)  5.72 us
    pallas_call x1, Pallas kernels, own_tiles(): pl.pallas_call(functools.partial(own_kernel, far_blocks=far_blocks), out_...  4.97 us
    all_to_all x1, waiting for transfers between devices, body(): weights_in = lax.all_to_all(weights_out, 'dom', 0, 0, tiled=True)  4.47 us
  transfers between devices with their start and end apart: 16, of which 9 were waited for; matrix products, arithmetic and copies ran while one was open for 0% of the time, Pallas kernels for 34%

profile of v12, /device:TPU:0, one launch (start us, length us, event | category | flops | bytes accessed | tf_op | source)
XLA Modules:
  0.0 103.1 jit_solution(15488286427909004225)
XLA Ops:
  0.6 4.3 %pick_rows.1 = bf16[8,160,128]{2,1,0:T(8,128)(2,1)} custom-call(s32[8,128]{1,0:T(8,128)} %bitcast.15, s32[1,8]{1,0:T(1,128)} %count_h.3, s32[32]{0:T(128)} %hub_h.3, bf16[2048,128]{1,0:T(8,128)(2,1)} %refs_0_.3), custom_call_target="tpu_custom_call" | custom-call | bytes 2097152 | tf_op jit(solution)/shard_map/pick_rows/pallas_call | solution.py:79
  5.0 7.3 %all-to-all-start = ((bf16[8,160,128]{2,1,0:T(8,128)(2,1)}), bf16[8,160,128]{2,1,0:T(8,128)(2,1)}, u32[]{:S(2)}, u32[]{:S(2)}) async-start(bf16[8,160,128]{2,1,0:T(8,128)(2,1)} %pick_rows.1), calls=%async_computation | async-start | bytes 655360 | tf_op jit(solution)/shard_map/all_to_all | solution.py:605
  12.3 1.5 %collective-permute-start = (bf16[2048,128]{1,0:T(8,128)(2,1)}, bf16[2048,128]{1,0:T(8,128)(2,1)}, u32[]{:S(2)}, u32[]{:S(2)}) collective-permute-start(bf16[2048,128]{1,0:T(8,128)(2,1)} %refs_0_.3), channel_id=1, source_target_pairs={{0,2},{1,3},{2,0},{3,1},{4,6},{5,7},{6,4},{7,5},{8,10},{9,11},{10,... | collective-permute-start | bytes 1572872 | tf_op jit(solution)/shard_map/ppermute | solution.py:600
  13.8 1.7 %cut_weights.1 = (bf16[2,128,128]{2,1,0:T(8,128)(2,1)}, bf16[2,128,128]{2,1,0:T(8,128)(2,1)}, bf16[2,2,128,128]{3,2,1,0:T(8,128)(2,1)}) custom-call(s32[1]{0:T(128)} %bitcast.me_s, bf16[512,128]{1,0:T(8,128)(2,1)} %refs_4_.1, bf16[512,128]{1,0:T(8,128)(2,1)} %refs_6_.1), custom_call_target="tpu_custom_call" | custom-call | bytes 1048576 | tf_op jit(solution)/shard_map/cut_weights/pallas_call | solution.py:516
  15.5 0.5 collective-permute-start.1
  16.0 5.0 %own_tiles.1 = (f32[16,128,128]{2,1,0:T(8,128)}, s32[2,122]{1,0:T(2,128)S(1)}) custom-call(s32[106]{0:T(128)} %dst_h.1, s32[106]{0:T(128)} %src_h.1, bf16[106,128,128]{2,1,0:T(8,128)(2,1)} %tiles.3, bf16[16,128,128]{2,1,0:T(8,128)(2,1)} %bitcast.9), custom_call_target="tpu_custom_call" | custom-call | flops 444596224 | bytes 8388608 | tf_op jit(solution)/shard_map/own_tiles/pallas_call | solution.py:176
  20.9 1.7 %all-to-all-done.incoming_h = bf16[8,160,128]{2,1,0:T(8,128)(2,1)} async-done(((bf16[8,160,128]{2,1,0:T(8,128)(2,1)}), bf16[8,160,128]{2,1,0:T(8,128)(2,1)}, u32[]{:S(2)}, u32[]{:S(2)}) %all-to-all-start) | async-done | bytes 327712 | tf_op jit(solution)/shard_map/all_to_all | solution.py:605
  22.7 3.8 %far_tiles.1 = bf16[16,128,128]{2,1,0:T(8,128)(2,1)} custom-call(s32[2,122]{1,0:T(2,128)S(1)} %get-tuple-element.40.lists.refs_0_, bf16[106,128,128]{2,1,0:T(8,128)(2,1)S(1)} %copy-done, bf16[8,160,128]{2,1,0:T(8,128)(2,1)} %all-to-all-done.incoming_h, f32[16,128,128]{2,1,0:T(8,128)} %get-tuple-element.41.base_h), custom_call_target="tpu_custom_call" | custom-call | flops 222298112 | bytes 4194304 | tf_op jit(solution)/shard_map/far_tiles/pallas_call | solution.py:218
  26.5 2.3 %collective-permute-done.1.refs_8_ = bf16[2,2,128,128]{3,2,1,0:T(8,128)(2,1)} collective-permute-done((bf16[2,2,128,128]{3,2,1,0:T(8,128)(2,1)}, bf16[2,2,128,128]{3,2,1,0:T(8,128)(2,1)}, u32[]{:S(2)}, u32[]{:S(2)}) %collective-permute-start.1) | collective-permute-done | bytes 131104 | tf_op jit(solution)/shard_map/ppermute | solution.py:600
  28.8 1.5 %collective-permute-start.3 = (bf16[2048,128]{1,0:T(8,128)(2,1)}, bf16[2048,128]{1,0:T(8,128)(2,1)S(1)}, u32[]{:S(2)}, u32[]{:S(2)}) collective-permute-start(bf16[2048,128]{1,0:T(8,128)(2,1)} %bitcast.10), channel_id=1, source_target_pairs={{0,2},{1,3},{2,0},{3,1},{4,6},{5,7},{6,4},{7,5},{8,10},{9,11},{10,... | collective-permute-start | bytes 1572872 | tf_op jit(solution)/shard_map/ppermute | solution.py:600
  30.3 0.2 collective-permute-start.7
  30.5 0.3 collective-permute-start.6
  30.8 0.2 collective-permute-start.2
  31.0 4.0 %self_dense.1.refs_4_ = f32[2048,128]{1,0:T(8,128)} custom-call(s32[1]{0:T(128)} %bitcast.me_s, bf16[2048,128]{1,0:T(8,128)(2,1)} %refs_0_.3, bf16[2048,128]{1,0:T(8,128)(2,1)} %collective-permute-done.4.refs_1_, bf16[2048,128]{1,0:T(8,128)(2,1)} %collective-permute-done.refs_2_, bf16[2048,128]{1,0:T(8,128)(2,1)S(1)} %collective-permute-done.5.refs_3_, ...), custom_call_target="tpu_custom_call" | custom-call | flops 268435456 | bytes 4194304 | tf_op jit(solution)/shard_map/self_dense/pallas_call | solution.py:280
  35.1 8.2 %collective-permute-done.3.refs_2_.refs_6_ = bf16[2048,128]{1,0:T(8,128)(2,1)S(1)} collective-permute-done((bf16[2048,128]{1,0:T(8,128)(2,1)}, bf16[2048,128]{1,0:T(8,128)(2,1)S(1)}, u32[]{:S(2)}, u32[]{:S(2)}) %collective-permute-start.3) | collective-permute-done | bytes 524320 | tf_op jit(solution)/shard_map/ppermute | solution.py:600
  43.3 1.9 %collective-permute-done.8.refs_3_.refs_7_ = bf16[2048,128]{1,0:T(8,128)(2,1)S(1)} collective-permute-done((bf16[2048,128]{1,0:T(8,128)(2,1)S(1)}, bf16[2048,128]{1,0:T(8,128)(2,1)S(1)}, u32[]{:S(2)}, u32[]{:S(2)}) %collective-permute-start.8) | collective-permute-done | bytes 524320 | tf_op jit(solution)/shard_map/ppermute | solution.py:600
  45.2 4.2 %forward_dense.1 = (bf16[2048,128]{1,0:T(8,128)(2,1)}, bf16[2048,128]{1,0:T(8,128)(2,1)}) custom-call(s32[1]{0:T(128)} %bitcast.me_s, bf16[2048,128]{1,0:T(8,128)(2,1)} %bitcast.12, bf16[2048,128]{1,0:T(8,128)(2,1)S(1)} %collective-permute-done.2.refs_1_.refs_5_, bf16[2048,128]{1,0:T(8,128)(2,1)S(1)} %collective-permute-done.3.refs_2_.refs_6_, ...), custom_call_target="tpu_custom_call" | custom-call | flops 268435456 | bytes 4194304 | tf_op jit(solution)/shard_map/forward_dense/pallas_call | solution.py:280
  49.4 1.6 %collective-permute-start.10 = (bf16[2048,128]{1,0:T(8,128)(2,1)}, bf16[2048,128]{1,0:T(8,128)(2,1)}, u32[]{:S(2)}, u32[]{:S(2)}) collective-permute-start(bf16[2048,128]{1,0:T(8,128)(2,1)} %get-tuple-element.52.refs_8_.refs_2_), channel_id=1, source_target_pairs={{0,2},{1,3},{2,0},{3,1},{4,6},{5,7},{6,4},{7,5},{8,10},{9,11},{10,... | collective-permute-start | bytes 1572872 | tf_op jit(solution)/shard_map/ppermute | solution.py:600
  51.0 3.9 %weight_parts.1 = f32[8,136,128]{2,1,0:T(8,128)} custom-call(bf16[2048,128]{1,0:T(8,128)(2,1)} %refs_0_.3, bf16[2048,128]{1,0:T(8,128)(2,1)} %collective-permute-done.4.refs_1_, bf16[2048,128]{1,0:T(8,128)(2,1)} %collective-permute-done.refs_2_, bf16[2048,128]{1,0:T(8,128)(2,1)S(1)} %collective-permute-done.5.refs_3_, bf16[2048,128]{1,0:T(8,128)(2,1)} %bitcast.13, ...), custom_call_target="tpu_custom_call" | custom-call | flops 536870912 | bytes 4194304 | tf_op jit(solution)/shard_map/weight_parts/pallas_call | solution.py:330
  54.9 5.7 %all-to-all-start.1 = ((f32[8,136,128]{2,1,0:T(8,128)}), f32[8,136,128]{2,1,0:T(8,128)}, u32[]{:S(2)}, u32[]{:S(2)}) async-start(f32[8,136,128]{2,1,0:T(8,128)} %weight_parts.1), calls=%async_computation.1 | async-start | bytes 1114112 | tf_op jit(solution)/shard_map/all_to_all | solution.py:642
  60.6 3.1 %collective-permute-done.10.refs_4_ = bf16[2048,128]{1,0:T(8,128)(2,1)} collective-permute-done((bf16[2048,128]{1,0:T(8,128)(2,1)}, bf16[2048,128]{1,0:T(8,128)(2,1)}, u32[]{:S(2)}, u32[]{:S(2)}) %collective-permute-start.10) | collective-permute-done | bytes 524320 | tf_op jit(solution)/shard_map/ppermute | solution.py:600
  63.8 2.1 %collective-permute-done.11.refs_5_ = bf16[2048,128]{1,0:T(8,128)(2,1)S(1)} collective-permute-done((bf16[2048,128]{1,0:T(8,128)(2,1)}, bf16[2048,128]{1,0:T(8,128)(2,1)S(1)}, u32[]{:S(2)}, u32[]{:S(2)}) %collective-permute-start.11) | collective-permute-done | bytes 524320 | tf_op jit(solution)/shard_map/ppermute | solution.py:600
  65.9 6.3 %back_far.1 = (bf16[8,160,128]{2,1,0:T(8,128)(2,1)}, bf16[16,128,128]{2,1,0:T(8,128)(2,1)}, f32[16,128,128]{2,1,0:T(8,128)}) custom-call(s32[2,122]{1,0:T(2,128)S(1)} %get-tuple-element.40.lists.refs_0_, bf16[106,128,128]{2,1,0:T(8,128)(2,1)S(1)} %copy-done, bf16[2048,128]{1,0:T(8,128)(2,1)} %get-tuple-element.52.refs_8_.refs_2_, ...), custom_call_target="tpu_custom_call" | custom-call | flops 536870912 | bytes 4194304 | tf_op jit(solution)/shard_map/back_far/pallas_call | solution.py:393
  72.2 3.7 %all-to-all-done.1.parts = f32[8,136,128]{2,1,0:T(8,128)} async-done(((f32[8,136,128]{2,1,0:T(8,128)}), f32[8,136,128]{2,1,0:T(8,128)}, u32[]{:S(2)}, u32[]{:S(2)}) %all-to-all-start.1) | async-done | bytes 557088 | tf_op jit(solution)/shard_map/all_to_all | solution.py:642
  76.0 4.1 %all-to-all-start.2 = ((bf16[8,160,128]{2,1,0:T(8,128)(2,1)}), bf16[8,160,128]{2,1,0:T(8,128)(2,1)}, u32[]{:S(2)}, u32[]{:S(2)}) async-start(bf16[8,160,128]{2,1,0:T(8,128)(2,1)} %get-tuple-element.58), calls=%async_computation.2 | async-start | bytes 655360 | tf_op jit(solution)/shard_map/all_to_all | solution.py:648
  80.0 1.8 %sum_parts.1 = (bf16[8,128,128]{2,1,0:T(8,128)(2,1)}, f32[1,128]{1,0:T(1,128)}) custom-call(f32[8,136,128]{2,1,0:T(8,128)} %all-to-all-done.1.parts), custom_call_target="tpu_custom_call" | custom-call | bytes 1048576 | tf_op jit(solution)/shard_map/sum_parts/pallas_call | solution.py:540
  81.8 4.3 %back_own.1 = f32[16,128,128]{2,1,0:T(8,128)} custom-call(s32[2,122]{1,0:T(2,128)S(1)} %get-tuple-element.40.lists.refs_0_, bf16[106,128,128]{2,1,0:T(8,128)(2,1)S(1)} %copy-done, bf16[16,128,128]{2,1,0:T(8,128)(2,1)} %get-tuple-element.59.back_h, f32[16,128,128]{2,1,0:T(8,128)} %get-tuple-element.60.direct_h), custom_call_target="tpu_custom_call" | custom-call | flops 444596224 | bytes 8388608 | tf_op jit(solution)/shard_map/back_own/pallas_call | solution.py:422
  86.2 4.0 %all-to-all-done.2.incoming_h = bf16[8,160,128]{2,1,0:T(8,128)(2,1)} async-done(((bf16[8,160,128]{2,1,0:T(8,128)(2,1)}), bf16[8,160,128]{2,1,0:T(8,128)(2,1)}, u32[]{:S(2)}, u32[]{:S(2)}) %all-to-all-start.2) | async-done | bytes 327712 | tf_op jit(solution)/shard_map/all_to_all | solution.py:648
  90.2 3.6 %all-to-all-start.3 = ((bf16[8,128,128]{2,1,0:T(8,128)(2,1)}), bf16[8,128,128]{2,1,0:T(8,128)(2,1)S(1)}, u32[]{:S(2)}, u32[]{:S(2)}) async-start(bf16[8,128,128]{2,1,0:T(8,128)(2,1)} %get-tuple-element.63), calls=%async_computation.3 | async-start | bytes 524288 | tf_op jit(solution)/shard_map/all_to_all | solution.py:652
  93.8 4.0 %finish.1 = f32[2048,128]{1,0:T(8,128)} custom-call(s32[8,128]{1,0:T(8,128)} %bitcast.16, s32[1,8]{1,0:T(1,128)} %count_h.3, s32[32]{0:T(128)} %hub_h.3, bf16[8,160,128]{2,1,0:T(8,128)(2,1)} %all-to-all-done.2.incoming_h, f32[2048,128]{1,0:T(8,128)} %bitcast.14), custom_call_target="tpu_custom_call" | custom-call | flops 536870912 | bytes 4194304 | tf_op jit(solution)/shard_map/finish/pallas_call | solution.py:484
  97.8 4.5 %all-to-all-done.3 = bf16[8,128,128]{2,1,0:T(8,128)(2,1)S(1)} async-done(((bf16[8,128,128]{2,1,0:T(8,128)(2,1)}), bf16[8,128,128]{2,1,0:T(8,128)(2,1)S(1)}, u32[]{:S(2)}, u32[]{:S(2)}) %all-to-all-start.3) | async-done | bytes 262176 | tf_op jit(solution)/shard_map/all_to_all | solution.py:652
  102.3 0.8 place_weights.1
  (20 shorter events, 0.1 us)
Async XLA Ops:
  0.6 22.1 %copy-start = (bf16[106,128,128]{2,1,0:T(8,128)(2,1)S(1)}, bf16[106,128,128]{2,1,0:T(8,128)(2,1)}, u32[]{:S(2)}) copy-start(bf16[106,128,128]{2,1,0:T(8,128)(2,1)} %tiles.3) | copy-start | bytes 10420228
  5.0 17.7 %all-to-all-start = ((bf16[8,160,128]{2,1,0:T(8,128)(2,1)}), bf16[8,160,128]{2,1,0:T(8,128)(2,1)}, u32[]{:S(2)}, u32[]{:S(2)}) async-start(bf16[8,160,128]{2,1,0:T(8,128)(2,1)} %pick_rows.1), calls=%async_computation | async-start | bytes 655360 | tf_op jit(solution)/shard_map/all_to_all | solution.py:605
  12.3 16.5 %collective-permute-start = (bf16[2048,128]{1,0:T(8,128)(2,1)}, bf16[2048,128]{1,0:T(8,128)(2,1)}, u32[]{:S(2)}, u32[]{:S(2)}) collective-permute-start(bf16[2048,128]{1,0:T(8,128)(2,1)} %refs_0_.3), channel_id=1, source_target_pairs={{0,2},{1,3},{2,0},{3,1},{4,6},{5,7},{6,4},{7,5},{8,10},{9,11},{10,... | collective-permute-start | bytes 1572872 | tf_op jit(solution)/shard_map/ppermute | solution.py:600
  15.5 13.3 %collective-permute-start.1 = (bf16[2,2,128,128]{3,2,1,0:T(8,128)(2,1)}, bf16[2,2,128,128]{3,2,1,0:T(8,128)(2,1)}, u32[]{:S(2)}, u32[]{:S(2)}) collective-permute-start(bf16[2,2,128,128]{3,2,1,0:T(8,128)(2,1)} %get-tuple-element.42), channel_id=1, source_target_pairs={{0,2},{1,3},{2,0},{3,1},{4,6},{5,7},{6,4},{7,5},{8,10},{9,11},{10,... | collective-permute-start | bytes 393224 | tf_op jit(solution)/shard_map/ppermute | solution.py:600
  16.0 14.8 %collective-permute-start.4 = (bf16[2048,128]{1,0:T(8,128)(2,1)}, bf16[2048,128]{1,0:T(8,128)(2,1)}, u32[]{:S(2)}, u32[]{:S(2)}) collective-permute-start(bf16[2048,128]{1,0:T(8,128)(2,1)} %refs_0_.3), channel_id=1, source_target_pairs={{0,1},{1,0},{2,3},{3,2},{4,5},{5,4},{6,7},{7,6},{8,9},{9,8},{10,11... | collective-permute-start | bytes 1572872 | tf_op jit(solution)/shard_map/ppermute | solution.py:600
  22.7 7.8 %copy-start.3 = (bf16[2,128,128]{2,1,0:T(8,128)(2,1)S(1)}, bf16[2,128,128]{2,1,0:T(8,128)(2,1)}, u32[]{:S(2)}) copy-start(bf16[2,128,128]{2,1,0:T(8,128)(2,1)} %get-tuple-element.47) | copy-start | bytes 196612
  28.8 2.3 %collective-permute-start.5 = (bf16[2048,128]{1,0:T(8,128)(2,1)}, bf16[2048,128]{1,0:T(8,128)(2,1)S(1)}, u32[]{:S(2)}, u32[]{:S(2)}) collective-permute-start(bf16[2048,128]{1,0:T(8,128)(2,1)} %collective-permute-done.refs_2_), channel_id=1, source_target_pairs={{0,1},{1,0},{2,3},{3,2},{4,5},{5,4},{6,7},{7,6},{8,9},{9,8},{10,11... | collective-permute-start | bytes 1572872 | tf_op jit(solution)/shard_map/ppermute | solution.py:600
  28.8 14.5 %collective-permute-start.3 = (bf16[2048,128]{1,0:T(8,128)(2,1)}, bf16[2048,128]{1,0:T(8,128)(2,1)S(1)}, u32[]{:S(2)}, u32[]{:S(2)}) collective-permute-start(bf16[2048,128]{1,0:T(8,128)(2,1)} %bitcast.10), channel_id=1, source_target_pairs={{0,2},{1,3},{2,0},{3,1},{4,6},{5,7},{6,4},{7,5},{8,10},{9,11},{10,... | collective-permute-start | bytes 1572872 | tf_op jit(solution)/shard_map/ppermute | solution.py:600
  30.3 4.8 %collective-permute-start.7 = (bf16[2,2,128,128]{3,2,1,0:T(8,128)(2,1)}, bf16[2,2,128,128]{3,2,1,0:T(8,128)(2,1)S(1)}, u32[]{:S(2)}, u32[]{:S(2)}) collective-permute-start(bf16[2,2,128,128]{3,2,1,0:T(8,128)(2,1)} %collective-permute-done.1.refs_8_), channel_id=1, source_target_pairs={{0,1},{1,0},{2,3},{3,2},{4,5},{5,4},{6,7},{7,6},{8,9},{9,8},{10,11... | collective-permute-start | bytes 393224 | tf_op jit(solution)/shard_map/ppermute | solution.py:600
  30.5 4.5 %collective-permute-start.6 = (bf16[2,128,128]{2,1,0:T(8,128)(2,1)S(1)}, bf16[2,128,128]{2,1,0:T(8,128)(2,1)S(1)}, u32[]{:S(2)}, u32[]{:S(2)}) collective-permute-start(bf16[2,128,128]{2,1,0:T(8,128)(2,1)S(1)} %copy-done.3), channel_id=1, source_target_pairs={{0,1},{1,0},{2,3},{3,2},{4,5},{5,4},{6,7},{7,6},{8,9},{9,8},{10,11... | collective-permute-start | bytes 196616 | tf_op jit(solution)/shard_map/ppermute | solution.py:600
  30.8 12.5 %collective-permute-start.2 = (bf16[2048,128]{1,0:T(8,128)(2,1)}, bf16[2048,128]{1,0:T(8,128)(2,1)S(1)}, u32[]{:S(2)}, u32[]{:S(2)}) collective-permute-start(bf16[2048,128]{1,0:T(8,128)(2,1)} %bitcast.11), channel_id=1, source_target_pairs={{0,1},{1,0},{2,3},{3,2},{4,5},{5,4},{6,7},{7,6},{8,9},{9,8},{10,11... | collective-permute-start | bytes 1572872 | tf_op jit(solution)/shard_map/ppermute | solution.py:600
  35.0 30.9 %copy-start.2 = (bf16[2,128,128]{2,1,0:T(8,128)(2,1)}, bf16[2,128,128]{2,1,0:T(8,128)(2,1)S(1)}, u32[]{:S(2)}) copy-start(bf16[2,128,128]{2,1,0:T(8,128)(2,1)S(1)} %collective-permute-done.6.refs_7_) | copy-start | bytes 196612
  35.1 10.2 %copy-start.1 = (bf16[2,2,128,128]{3,2,1,0:T(8,128)(2,1)}, bf16[2,2,128,128]{3,2,1,0:T(8,128)(2,1)S(1)}, u32[]{:S(2)}) copy-start(bf16[2,2,128,128]{3,2,1,0:T(8,128)(2,1)S(1)} %collective-permute-done.7.refs_9_) | copy-start | bytes 393220
  43.3 1.9 %collective-permute-start.8 = (bf16[2048,128]{1,0:T(8,128)(2,1)S(1)}, bf16[2048,128]{1,0:T(8,128)(2,1)S(1)}, u32[]{:S(2)}, u32[]{:S(2)}) collective-permute-start(bf16[2048,128]{1,0:T(8,128)(2,1)S(1)} %collective-permute-done.3.refs_2_.refs_6_), channel_id=1, source_target_pairs={{0,1},{1,0},{2,3},{3,2},{4,5},{5,4},{6,7},{7,6},{8,9},{9,8},{10,11... | collective-permute-start | bytes 1572872 | tf_op jit(solution)/shard_map/ppermute | solution.py:600
  49.4 14.3 %collective-permute-start.10 = (bf16[2048,128]{1,0:T(8,128)(2,1)}, bf16[2048,128]{1,0:T(8,128)(2,1)}, u32[]{:S(2)}, u32[]{:S(2)}) collective-permute-start(bf16[2048,128]{1,0:T(8,128)(2,1)} %get-tuple-element.52.refs_8_.refs_2_), channel_id=1, source_target_pairs={{0,2},{1,3},{2,0},{3,1},{4,6},{5,7},{6,4},{7,5},{8,10},{9,11},{10,... | collective-permute-start | bytes 1572872 | tf_op jit(solution)/shard_map/ppermute | solution.py:600
  54.9 21.0 %all-to-all-start.1 = ((f32[8,136,128]{2,1,0:T(8,128)}), f32[8,136,128]{2,1,0:T(8,128)}, u32[]{:S(2)}, u32[]{:S(2)}) async-start(f32[8,136,128]{2,1,0:T(8,128)} %weight_parts.1), calls=%async_computation.1 | async-start | bytes 1114112 | tf_op jit(solution)/shard_map/all_to_all | solution.py:642
  60.6 3.2 %collective-permute-start.9 = (bf16[2048,128]{1,0:T(8,128)(2,1)}, bf16[2048,128]{1,0:T(8,128)(2,1)S(1)}, u32[]{:S(2)}, u32[]{:S(2)}) collective-permute-start(bf16[2048,128]{1,0:T(8,128)(2,1)} %get-tuple-element.52.refs_8_.refs_2_), channel_id=1, source_target_pairs={{0,1},{1,0},{2,3},{3,2},{4,5},{5,4},{6,7},{7,6},{8,9},{9,8},{10,11... | collective-permute-start | bytes 1572872 | tf_op jit(solution)/shard_map/ppermute | solution.py:600
  63.8 2.1 %collective-permute-start.11 = (bf16[2048,128]{1,0:T(8,128)(2,1)}, bf16[2048,128]{1,0:T(8,128)(2,1)S(1)}, u32[]{:S(2)}, u32[]{:S(2)}) collective-permute-start(bf16[2048,128]{1,0:T(8,128)(2,1)} %collective-permute-done.10.refs_4_), channel_id=1, source_target_pairs={{0,1},{1,0},{2,3},{3,2},{4,5},{5,4},{6,7},{7,6},{8,9},{9,8},{10,11... | collective-permute-start | bytes 1572872 | tf_op jit(solution)/shard_map/ppermute | solution.py:600
  76.0 14.2 %all-to-all-start.2 = ((bf16[8,160,128]{2,1,0:T(8,128)(2,1)}), bf16[8,160,128]{2,1,0:T(8,128)(2,1)}, u32[]{:S(2)}, u32[]{:S(2)}) async-start(bf16[8,160,128]{2,1,0:T(8,128)(2,1)} %get-tuple-element.58), calls=%async_computation.2 | async-start | bytes 655360 | tf_op jit(solution)/shard_map/all_to_all | solution.py:648
  90.2 12.1 %all-to-all-start.3 = ((bf16[8,128,128]{2,1,0:T(8,128)(2,1)}), bf16[8,128,128]{2,1,0:T(8,128)(2,1)S(1)}, u32[]{:S(2)}, u32[]{:S(2)}) async-start(bf16[8,128,128]{2,1,0:T(8,128)(2,1)} %get-tuple-element.63), calls=%async_computation.3 | async-start | bytes 524288 | tf_op jit(solution)/shard_map/all_to_all | solution.py:652

commit v13 on v12

--- a/solution.py
+++ b/solution.py
@@ -525,21 +525,19 @@
 
 
 def sum_kernel(parts, out, bias):
-    n_dom, chunk, _ = out.shape
+    n_dom, chunk = parts.shape[0], out.shape[0]
     total = parts[0]
     for q in range(1, n_dom):
         total += parts[q]
     bias[...] = total[chunk : chunk + 1, :]
-    rows = total[:chunk, :].astype(BF16)
-    for q in range(n_dom):
-        out[q] = rows
+    out[...] = total[:chunk, :].astype(BF16)
 
 
 def sum_parts(parts):
-    n_dom, rows, width = parts.shape
+    _, rows, width = parts.shape
     return pl.pallas_call(
         sum_kernel,
-        out_shape=(pltpu.HBM((n_dom, rows - 8, width), BF16), pltpu.HBM((1, width), F32)),
+        out_shape=(pltpu.HBM((rows - 8, width), BF16), pltpu.HBM((1, width), F32)),
         in_specs=[VMEM],
         out_specs=(VMEM, VMEM),
         compiler_params=params(),
@@ -550,15 +548,28 @@
 
 def place_kernel(me_s, sums, self_out, neigh_out):
     rows, width = self_out.shape
-    for i in range(2 * rows // width):
-        which, k = divmod(i, rows // width)
-        target = (self_out, neigh_out)[which]
-        at = pl.ds(pl.multiple_of((me_s[0] ^ k) * width, width), width)
-        target[at, :] = sums[i * width : (i + 1) * width, :].astype(F32)
-
-
-def place_weights(me, sums):
-    rows, width = sums.shape[0] // 2, sums.shape[1]
+    half, _, chunk, _ = sums.shape
+    n = min(chunk, width)
+    for j in range(half):
+        for t in range(2):
+            index = ((me_s[1] & half) ^ (t * half)) + j
+            for part in range(0, chunk, n):
+                row = index * chunk + part
+                feat = me_s[0] ^ (row // width % (rows // width))
+                at = pl.ds(pl.multiple_of(feat * width + row % width, n), n)
+                piece = sums[j, t, part : part + n, :].astype(F32)
+
+                @pl.when(row < rows)
+                def _():
+                    self_out[at, :] = piece
+
+                @pl.when(row >= rows)
+                def _():
+                    neigh_out[at, :] = piece
+
+
+def place_weights(both, sums, rows):
+    width = sums.shape[-1]
     return pl.pallas_call(
         place_kernel,
         out_shape=(pltpu.HBM((rows, width), F32),) * 2,
@@ -567,7 +578,7 @@
         compiler_params=params(),
         cost_estimate=cost(0, 1 << 20),
         name="place_weights",
-    )(me, sums)
+    )(both, sums)
 
 
 def body(
@@ -647,11 +658,18 @@
     )
     back_in = lax.all_to_all(back_out, "dom", 0, 0, tiled=True)
     own = back_own(lists, edge_tiles, back_agg, direct).reshape(own_count, width)
-    weights_out, grad_bias = sum_parts(part_sums)
+    weights, grad_bias = sum_parts(part_sums)
+    half = n_dom // 2
+    other = lax.ppermute(weights, "dom", [(j, j ^ half) for j in range(n_dom)])
+    other, own = lax.optimization_barrier((other, own))
+    pair = jnp.stack([weights, other])
+    weights_out = jnp.broadcast_to(pair[None], (half,) + pair.shape)
     weights_out, back_in, own = lax.optimization_barrier((weights_out, back_in, own))
-    weights_in = lax.all_to_all(weights_out, "dom", 0, 0, tiled=True)
+    halves = [list(range(half)), list(range(half, n_dom))]
+    weights_in = lax.all_to_all(weights_out, "dom", 0, 0, axis_index_groups=halves, tiled=True)
     grad_feats = finish(listed, send_count, hub_ids, back_in, own)
-    grad_self, grad_neigh = place_weights(me_s, weights_in.reshape(-1, width))
+    both = jnp.stack([me, lax.axis_index("dom").astype(jnp.int32)])
+    grad_self, grad_neigh = place_weights(both, weights_in, n_feat * width)
     return (output, grad_feats, grad_self, grad_neigh, grad_bias[0])
 
 

time: 104 us -> 103 us (level)
  waiting for transfers between devices: 31.7 us -> 27 us
  starting transfers between devices: 26.5 us -> 29.2 us
    all_to_all x1, waiting for transfers between devices: 4.03 us -> 0.01 us  [body(): back_in = lax.all_to_all(back_out, 'dom', 0, 0, tiled=True)]
    all_to_all x1, waiting for transfers between devices: 4.47 us -> 1.2 us  [body(): lax.all_to_all(weights_out, 'dom', 0, 0, axis_index_groups=halves, tiled=...]
    ppermute x0 -> x1, starting transfers between devices: none -> 2.81 us  [body(): other = lax.ppermute(weights, 'dom', [(j, j ^ half) for j in range(n_dom)])]
    ppermute x0 -> x1, waiting for transfers between devices: none -> 2.65 us  [body(): other = lax.ppermute(weights, 'dom', [(j, j ^ half) for j in range(n_dom)])]
  transfers between devices with their start and end apart: 16 -> 17, of which waited for: 9 -> 9; matrix products, arithmetic and copies ran while one was open for 0% -> 0% of each run, Pallas kernels for 34% -> 34%
where the time goes in v13:
time: 103 us
  Pallas kernels  44.7 us (43%)
  starting transfers between devices  29.2 us (28%)
  waiting for transfers between devices  27 us (26%)
    ppermute x12, waiting for transfers between devices, swap(): return lax.ppermute(x, 'feat', [(j, j ^ k) for j in range(n_feat)])  17.7 us
    pallas_call x2, Pallas kernels, stream_call(): pl.pallas_call(run, out_shape=tuple((pltpu.HBM(shape, t) for shape, t in...  8.2 us
    all_to_all x1, starting transfers between devices, body(): incoming = lax.all_to_all(outgoing, 'dom', 0, 0, tiled=True)  7.26 us
    pallas_call x1, Pallas kernels, back_far(): pl.pallas_call(functools.partial(back_far_kernel, n_feat=n_feat), out_sha...  6.29 us
    ppermute x12, starting transfers between devices, swap(): return lax.ppermute(x, 'feat', [(j, j ^ k) for j in range(n_feat)])  5.88 us
    all_to_all x1, starting transfers between devices, body(): part_sums = lax.all_to_all(parts, 'dom', 0, 0, tiled=True)  5.72 us
    pallas_call x1, Pallas kernels, own_tiles(): pl.pallas_call(functools.partial(own_kernel, far_blocks=far_blocks), out_...  4.97 us
    pallas_call x1, Pallas kernels, pick(): pl.pallas_call(pick_kernel, out_shape=pltpu.HBM(shape, BF16), in_specs=[H...  4.34 us
  transfers between devices with their start and end apart: 17, of which 9 were waited for; matrix products, arithmetic and copies ran while one was open for 0% of the time, Pallas kernels for 34%

profile of v13, /device:TPU:0, one launch (start us, length us, event | category | flops | bytes accessed | tf_op | source)
XLA Modules:
  0.0 102.5 jit_solution(7201585459820625244)
XLA Ops:
  0.6 4.3 %pick_rows.1 = bf16[8,160,128]{2,1,0:T(8,128)(2,1)} custom-call(s32[8,128]{1,0:T(8,128)} %bitcast.18, s32[1,8]{1,0:T(1,128)} %count_h.3, s32[32]{0:T(128)} %hub_h.3, bf16[2048,128]{1,0:T(8,128)(2,1)} %refs_0_.3), custom_call_target="tpu_custom_call" | custom-call | bytes 2097152 | tf_op jit(solution)/shard_map/pick_rows/pallas_call | solution.py:79
  5.0 7.3 %all-to-all-start = ((bf16[8,160,128]{2,1,0:T(8,128)(2,1)}), bf16[8,160,128]{2,1,0:T(8,128)(2,1)}, u32[]{:S(2)}, u32[]{:S(2)}) async-start(bf16[8,160,128]{2,1,0:T(8,128)(2,1)} %pick_rows.1), calls=%async_computation | async-start | bytes 655360 | tf_op jit(solution)/shard_map/all_to_all | solution.py:616
  12.3 1.5 %collective-permute-start = (bf16[2048,128]{1,0:T(8,128)(2,1)}, bf16[2048,128]{1,0:T(8,128)(2,1)}, u32[]{:S(2)}, u32[]{:S(2)}) collective-permute-start(bf16[2048,128]{1,0:T(8,128)(2,1)} %refs_0_.3), channel_id=1, source_target_pairs={{0,2},{1,3},{2,0},{3,1},{4,6},{5,7},{6,4},{7,5},{8,10},{9,11},{10,... | collective-permute-start | bytes 1572872 | tf_op jit(solution)/shard_map/ppermute | solution.py:611
  13.8 1.7 %cut_weights.1 = (bf16[2,128,128]{2,1,0:T(8,128)(2,1)}, bf16[2,128,128]{2,1,0:T(8,128)(2,1)}, bf16[2,2,128,128]{3,2,1,0:T(8,128)(2,1)}) custom-call(s32[1]{0:T(128)} %bitcast.me_s, bf16[512,128]{1,0:T(8,128)(2,1)} %refs_4_.1, bf16[512,128]{1,0:T(8,128)(2,1)} %refs_6_.1), custom_call_target="tpu_custom_call" | custom-call | bytes 1048576 | tf_op jit(solution)/shard_map/cut_weights/pallas_call | solution.py:516
  15.5 0.5 collective-permute-start.1
  16.0 5.0 %own_tiles.1 = (f32[16,128,128]{2,1,0:T(8,128)}, s32[2,122]{1,0:T(2,128)S(1)}) custom-call(s32[106]{0:T(128)} %dst_h.1, s32[106]{0:T(128)} %src_h.1, bf16[106,128,128]{2,1,0:T(8,128)(2,1)} %tiles.3, bf16[16,128,128]{2,1,0:T(8,128)(2,1)} %bitcast.10), custom_call_target="tpu_custom_call" | custom-call | flops 444596224 | bytes 8388608 | tf_op jit(solution)/shard_map/own_tiles/pallas_call | solution.py:176
  20.9 1.7 %all-to-all-done.incoming_h = bf16[8,160,128]{2,1,0:T(8,128)(2,1)} async-done(((bf16[8,160,128]{2,1,0:T(8,128)(2,1)}), bf16[8,160,128]{2,1,0:T(8,128)(2,1)}, u32[]{:S(2)}, u32[]{:S(2)}) %all-to-all-start) | async-done | bytes 327712 | tf_op jit(solution)/shard_map/all_to_all | solution.py:616
  22.7 3.8 %far_tiles.1 = bf16[16,128,128]{2,1,0:T(8,128)(2,1)} custom-call(s32[2,122]{1,0:T(2,128)S(1)} %get-tuple-element.42.lists.refs_0_, bf16[106,128,128]{2,1,0:T(8,128)(2,1)S(1)} %copy-done, bf16[8,160,128]{2,1,0:T(8,128)(2,1)} %all-to-all-done.incoming_h, f32[16,128,128]{2,1,0:T(8,128)} %get-tuple-element.43.base_h), custom_call_target="tpu_custom_call" | custom-call | flops 222298112 | bytes 4194304 | tf_op jit(solution)/shard_map/far_tiles/pallas_call | solution.py:218
  26.5 2.3 %collective-permute-done.1.refs_8_ = bf16[2,2,128,128]{3,2,1,0:T(8,128)(2,1)} collective-permute-done((bf16[2,2,128,128]{3,2,1,0:T(8,128)(2,1)}, bf16[2,2,128,128]{3,2,1,0:T(8,128)(2,1)}, u32[]{:S(2)}, u32[]{:S(2)}) %collective-permute-start.1) | collective-permute-done | bytes 131104 | tf_op jit(solution)/shard_map/ppermute | solution.py:611
  28.8 1.5 %collective-permute-start.3 = (bf16[2048,128]{1,0:T(8,128)(2,1)}, bf16[2048,128]{1,0:T(8,128)(2,1)S(1)}, u32[]{:S(2)}, u32[]{:S(2)}) collective-permute-start(bf16[2048,128]{1,0:T(8,128)(2,1)} %bitcast.11), channel_id=1, source_target_pairs={{0,2},{1,3},{2,0},{3,1},{4,6},{5,7},{6,4},{7,5},{8,10},{9,11},{10,... | collective-permute-start | bytes 1572872 | tf_op jit(solution)/shard_map/ppermute | solution.py:611
  30.5 0.3 collective-permute-start.6
  31.0 4.0 %self_dense.1.refs_4_ = f32[2048,128]{1,0:T(8,128)} custom-call(s32[1]{0:T(128)} %bitcast.me_s, bf16[2048,128]{1,0:T(8,128)(2,1)} %refs_0_.3, bf16[2048,128]{1,0:T(8,128)(2,1)} %collective-permute-done.4.refs_1_, bf16[2048,128]{1,0:T(8,128)(2,1)} %collective-permute-done.refs_2_, bf16[2048,128]{1,0:T(8,128)(2,1)S(1)} %collective-permute-done.5.refs_3_, ...), custom_call_target="tpu_custom_call" | custom-call | flops 268435456 | bytes 4194304 | tf_op jit(solution)/shard_map/self_dense/pallas_call | solution.py:280
  35.1 8.2 %collective-permute-done.3.refs_2_.refs_6_ = bf16[2048,128]{1,0:T(8,128)(2,1)S(1)} collective-permute-done((bf16[2048,128]{1,0:T(8,128)(2,1)}, bf16[2048,128]{1,0:T(8,128)(2,1)S(1)}, u32[]{:S(2)}, u32[]{:S(2)}) %collective-permute-start.3) | collective-permute-done | bytes 524320 | tf_op jit(solution)/shard_map/ppermute | solution.py:611
  43.3 1.9 %collective-permute-done.8.refs_3_.refs_7_ = bf16[2048,128]{1,0:T(8,128)(2,1)S(1)} collective-permute-done((bf16[2048,128]{1,0:T(8,128)(2,1)S(1)}, bf16[2048,128]{1,0:T(8,128)(2,1)S(1)}, u32[]{:S(2)}, u32[]{:S(2)}) %collective-permute-start.8) | collective-permute-done | bytes 524320 | tf_op jit(solution)/shard_map/ppermute | solution.py:611
  45.2 4.2 %forward_dense.1 = (bf16[2048,128]{1,0:T(8,128)(2,1)}, bf16[2048,128]{1,0:T(8,128)(2,1)}) custom-call(s32[1]{0:T(128)} %bitcast.me_s, bf16[2048,128]{1,0:T(8,128)(2,1)} %bitcast.13, bf16[2048,128]{1,0:T(8,128)(2,1)S(1)} %collective-permute-done.2.refs_1_.refs_5_, bf16[2048,128]{1,0:T(8,128)(2,1)S(1)} %collective-permute-done.3.refs_2_.refs_6_, ...), custom_call_target="tpu_custom_call" | custom-call | flops 268435456 | bytes 4194304 | tf_op jit(solution)/shard_map/forward_dense/pallas_call | solution.py:280
  49.4 1.6 %collective-permute-start.11 = (bf16[2048,128]{1,0:T(8,128)(2,1)}, bf16[2048,128]{1,0:T(8,128)(2,1)}, u32[]{:S(2)}, u32[]{:S(2)}) collective-permute-start(bf16[2048,128]{1,0:T(8,128)(2,1)} %get-tuple-element.54.refs_8_.refs_2_), channel_id=1, source_target_pairs={{0,2},{1,3},{2,0},{3,1},{4,6},{5,7},{6,4},{7,5},{8,10},{9,11},{10,... | collective-permute-start | bytes 1572872 | tf_op jit(solution)/shard_map/ppermute | solution.py:611
  51.0 3.9 %weight_parts.1 = f32[8,136,128]{2,1,0:T(8,128)} custom-call(bf16[2048,128]{1,0:T(8,128)(2,1)} %refs_0_.3, bf16[2048,128]{1,0:T(8,128)(2,1)} %collective-permute-done.4.refs_1_, bf16[2048,128]{1,0:T(8,128)(2,1)} %collective-permute-done.refs_2_, bf16[2048,128]{1,0:T(8,128)(2,1)S(1)} %collective-permute-done.5.refs_3_, bf16[2048,128]{1,0:T(8,128)(2,1)} %bitcast.14, ...), custom_call_target="tpu_custom_call" | custom-call | flops 536870912 | bytes 4194304 | tf_op jit(solution)/shard_map/weight_parts/pallas_call | solution.py:330
  54.9 5.7 %all-to-all-start.1 = ((f32[8,136,128]{2,1,0:T(8,128)}), f32[8,136,128]{2,1,0:T(8,128)}, u32[]{:S(2)}, u32[]{:S(2)}) async-start(f32[8,136,128]{2,1,0:T(8,128)} %weight_parts.1), calls=%async_computation.1 | async-start | bytes 1114112 | tf_op jit(solution)/shard_map/all_to_all | solution.py:653
  60.7 3.1 %collective-permute-done.11.refs_4_ = bf16[2048,128]{1,0:T(8,128)(2,1)} collective-permute-done((bf16[2048,128]{1,0:T(8,128)(2,1)}, bf16[2048,128]{1,0:T(8,128)(2,1)}, u32[]{:S(2)}, u32[]{:S(2)}) %collective-permute-start.11) | collective-permute-done | bytes 524320 | tf_op jit(solution)/shard_map/ppermute | solution.py:611
  63.8 2.1 %collective-permute-done.12.refs_5_ = bf16[2048,128]{1,0:T(8,128)(2,1)S(1)} collective-permute-done((bf16[2048,128]{1,0:T(8,128)(2,1)}, bf16[2048,128]{1,0:T(8,128)(2,1)S(1)}, u32[]{:S(2)}, u32[]{:S(2)}) %collective-permute-start.12) | collective-permute-done | bytes 524320 | tf_op jit(solution)/shard_map/ppermute | solution.py:611
  65.9 6.3 %back_far.1 = (bf16[8,160,128]{2,1,0:T(8,128)(2,1)}, bf16[16,128,128]{2,1,0:T(8,128)(2,1)}, f32[16,128,128]{2,1,0:T(8,128)}) custom-call(s32[2,122]{1,0:T(2,128)S(1)} %get-tuple-element.42.lists.refs_0_, bf16[106,128,128]{2,1,0:T(8,128)(2,1)S(1)} %copy-done, bf16[2048,128]{1,0:T(8,128)(2,1)} %get-tuple-element.54.refs_8_.refs_2_, ...), custom_call_target="tpu_custom_call" | custom-call | flops 536870912 | bytes 4194304 | tf_op jit(solution)/shard_map/back_far/pallas_call | solution.py:393
  72.2 3.8 %all-to-all-done.1.parts = f32[8,136,128]{2,1,0:T(8,128)} async-done(((f32[8,136,128]{2,1,0:T(8,128)}), f32[8,136,128]{2,1,0:T(8,128)}, u32[]{:S(2)}, u32[]{:S(2)}) %all-to-all-start.1) | async-done | bytes 557088 | tf_op jit(solution)/shard_map/all_to_all | solution.py:653
  76.0 4.1 %all-to-all-start.2 = ((bf16[8,160,128]{2,1,0:T(8,128)(2,1)}), bf16[8,160,128]{2,1,0:T(8,128)(2,1)}, u32[]{:S(2)}, u32[]{:S(2)}) async-start(bf16[8,160,128]{2,1,0:T(8,128)(2,1)} %get-tuple-element.63), calls=%async_computation.2 | async-start | bytes 655360 | tf_op jit(solution)/shard_map/all_to_all | solution.py:659
  80.1 1.7 %sum_parts.1 = (bf16[128,128]{1,0:T(8,128)(2,1)}, f32[1,128]{1,0:T(1,128)}) custom-call(f32[8,136,128]{2,1,0:T(8,128)} %all-to-all-done.1.parts), custom_call_target="tpu_custom_call" | custom-call | bytes 1048576 | tf_op jit(solution)/shard_map/sum_parts/pallas_call | solution.py:538
  81.8 2.8 %collective-permute-start.9 = (bf16[128,128]{1,0:T(8,128)(2,1)}, bf16[128,128]{1,0:T(8,128)(2,1)S(1)}, u32[]{:S(2)}, u32[]{:S(2)}) collective-permute-start(bf16[128,128]{1,0:T(8,128)(2,1)} %get-tuple-element.55), channel_id=1, source_target_pairs={{0,16},{4,20},{8,24},{12,28},{16,0},{20,4},{24,8},{28,12},{1,17},{... | collective-permute-start | bytes 98312 | tf_op jit(solution)/shard_map/ppermute | solution.py:663
  84.6 4.3 %back_own.1 = f32[16,128,128]{2,1,0:T(8,128)} custom-call(s32[2,122]{1,0:T(2,128)S(1)} %get-tuple-element.42.lists.refs_0_, bf16[106,128,128]{2,1,0:T(8,128)(2,1)S(1)} %copy-done, bf16[16,128,128]{2,1,0:T(8,128)(2,1)} %get-tuple-element.60.back_h, f32[16,128,128]{2,1,0:T(8,128)} %get-tuple-element.61.direct_h), custom_call_target="tpu_custom_call" | custom-call | flops 444596224 | bytes 8388608 | tf_op jit(solution)/shard_map/back_own/pallas_call | solution.py:422
  88.9 2.6 %collective-permute-done.9 = bf16[128,128]{1,0:T(8,128)(2,1)S(1)} collective-permute-done((bf16[128,128]{1,0:T(8,128)(2,1)}, bf16[128,128]{1,0:T(8,128)(2,1)S(1)}, u32[]{:S(2)}, u32[]{:S(2)}) %collective-permute-start.9) | collective-permute-done | bytes 32800 | tf_op jit(solution)/shard_map/ppermute | solution.py:663
  91.5 0.7 broadcast_in_dim.10
  92.3 3.4 %all-to-all-start.3 = ((bf16[4,2,128,128]{3,2,1,0:T(8,128)(2,1)}), bf16[4,2,128,128]{3,2,1,0:T(8,128)(2,1)S(1)}, u32[]{:S(2)}, u32[]{:S(2)}) async-start(bf16[4,2,128,128]{3,2,1,0:T(8,128)(2,1)} %broadcast_in_dim.10), calls=%async_computation.3 | async-start | bytes 524288 | tf_op jit(solution)/shard_map/all_to_all | solution.py:669
  95.8 4.1 %finish.1 = f32[2048,128]{1,0:T(8,128)} custom-call(s32[8,128]{1,0:T(8,128)} %bitcast.19, s32[1,8]{1,0:T(1,128)} %count_h.3, s32[32]{0:T(128)} %hub_h.3, bf16[8,160,128]{2,1,0:T(8,128)(2,1)} %all-to-all-done.2.incoming_h, f32[2048,128]{1,0:T(8,128)} %bitcast.15), custom_call_target="tpu_custom_call" | custom-call | flops 536870912 | bytes 4194304 | tf_op jit(solution)/shard_map/finish/pallas_call | solution.py:484
  99.8 1.2 %all-to-all-done.3.sums = bf16[4,2,128,128]{3,2,1,0:T(8,128)(2,1)S(1)} async-done(((bf16[4,2,128,128]{3,2,1,0:T(8,128)(2,1)}), bf16[4,2,128,128]{3,2,1,0:T(8,128)(2,1)S(1)}, u32[]{:S(2)}, u32[]{:S(2)}) %all-to-all-start.3) | async-done | bytes 262176 | tf_op jit(solution)/shard_map/all_to_all | solution.py:669
  101.0 1.5 %place_weights.1 = (f32[512,128]{1,0:T(8,128)}, f32[512,128]{1,0:T(8,128)}) custom-call(s32[2]{0:T(128)S(1)} %pad_add_fusion.me_s, bf16[4,2,128,128]{3,2,1,0:T(8,128)(2,1)S(1)} %all-to-all-done.3.sums), custom_call_target="tpu_custom_call" | custom-call | bytes 1048576 | tf_op jit(solution)/shard_map/place_weights/pallas_call | solution.py:573
  (27 shorter events, 0.6 us)
Async XLA Ops:
  0.6 22.1 %copy-start = (bf16[106,128,128]{2,1,0:T(8,128)(2,1)S(1)}, bf16[106,128,128]{2,1,0:T(8,128)(2,1)}, u32[]{:S(2)}) copy-start(bf16[106,128,128]{2,1,0:T(8,128)(2,1)} %tiles.3) | copy-start | bytes 10420228
  5.0 17.7 %all-to-all-start = ((bf16[8,160,128]{2,1,0:T(8,128)(2,1)}), bf16[8,160,128]{2,1,0:T(8,128)(2,1)}, u32[]{:S(2)}, u32[]{:S(2)}) async-start(bf16[8,160,128]{2,1,0:T(8,128)(2,1)} %pick_rows.1), calls=%async_computation | async-start | bytes 655360 | tf_op jit(solution)/shard_map/all_to_all | solution.py:616
  12.3 16.5 %collective-permute-start = (bf16[2048,128]{1,0:T(8,128)(2,1)}, bf16[2048,128]{1,0:T(8,128)(2,1)}, u32[]{:S(2)}, u32[]{:S(2)}) collective-permute-start(bf16[2048,128]{1,0:T(8,128)(2,1)} %refs_0_.3), channel_id=1, source_target_pairs={{0,2},{1,3},{2,0},{3,1},{4,6},{5,7},{6,4},{7,5},{8,10},{9,11},{10,... | collective-permute-start | bytes 1572872 | tf_op jit(solution)/shard_map/ppermute | solution.py:611
  15.5 13.3 %collective-permute-start.1 = (bf16[2,2,128,128]{3,2,1,0:T(8,128)(2,1)}, bf16[2,2,128,128]{3,2,1,0:T(8,128)(2,1)}, u32[]{:S(2)}, u32[]{:S(2)}) collective-permute-start(bf16[2,2,128,128]{3,2,1,0:T(8,128)(2,1)} %get-tuple-element.44), channel_id=1, source_target_pairs={{0,2},{1,3},{2,0},{3,1},{4,6},{5,7},{6,4},{7,5},{8,10},{9,11},{10,... | collective-permute-start | bytes 393224 | tf_op jit(solution)/shard_map/ppermute | solution.py:611
  16.0 14.8 %collective-permute-start.4 = (bf16[2048,128]{1,0:T(8,128)(2,1)}, bf16[2048,128]{1,0:T(8,128)(2,1)}, u32[]{:S(2)}, u32[]{:S(2)}) collective-permute-start(bf16[2048,128]{1,0:T(8,128)(2,1)} %refs_0_.3), channel_id=1, source_target_pairs={{0,1},{1,0},{2,3},{3,2},{4,5},{5,4},{6,7},{7,6},{8,9},{9,8},{10,11... | collective-permute-start | bytes 1572872 | tf_op jit(solution)/shard_map/ppermute | solution.py:611
  22.7 7.8 %copy-start.4 = (bf16[2,128,128]{2,1,0:T(8,128)(2,1)S(1)}, bf16[2,128,128]{2,1,0:T(8,128)(2,1)}, u32[]{:S(2)}) copy-start(bf16[2,128,128]{2,1,0:T(8,128)(2,1)} %get-tuple-element.49) | copy-start | bytes 196612
  28.8 2.3 %collective-permute-start.5 = (bf16[2048,128]{1,0:T(8,128)(2,1)}, bf16[2048,128]{1,0:T(8,128)(2,1)S(1)}, u32[]{:S(2)}, u32[]{:S(2)}) collective-permute-start(bf16[2048,128]{1,0:T(8,128)(2,1)} %collective-permute-done.refs_2_), channel_id=1, source_target_pairs={{0,1},{1,0},{2,3},{3,2},{4,5},{5,4},{6,7},{7,6},{8,9},{9,8},{10,11... | collective-permute-start | bytes 1572872 | tf_op jit(solution)/shard_map/ppermute | solution.py:611
  28.8 14.5 %collective-permute-start.3 = (bf16[2048,128]{1,0:T(8,128)(2,1)}, bf16[2048,128]{1,0:T(8,128)(2,1)S(1)}, u32[]{:S(2)}, u32[]{:S(2)}) collective-permute-start(bf16[2048,128]{1,0:T(8,128)(2,1)} %bitcast.11), channel_id=1, source_target_pairs={{0,2},{1,3},{2,0},{3,1},{4,6},{5,7},{6,4},{7,5},{8,10},{9,11},{10,... | collective-permute-start | bytes 1572872 | tf_op jit(solution)/shard_map/ppermute | solution.py:611
  30.3 4.8 %collective-permute-start.7 = (bf16[2,2,128,128]{3,2,1,0:T(8,128)(2,1)}, bf16[2,2,128,128]{3,2,1,0:T(8,128)(2,1)S(1)}, u32[]{:S(2)}, u32[]{:S(2)}) collective-permute-start(bf16[2,2,128,128]{3,2,1,0:T(8,128)(2,1)} %collective-permute-done.1.refs_8_), channel_id=1, source_target_pairs={{0,1},{1,0},{2,3},{3,2},{4,5},{5,4},{6,7},{7,6},{8,9},{9,8},{10,11... | collective-permute-start | bytes 393224 | tf_op jit(solution)/shard_map/ppermute | solution.py:611
  30.5 4.5 %collective-permute-start.6 = (bf16[2,128,128]{2,1,0:T(8,128)(2,1)S(1)}, bf16[2,128,128]{2,1,0:T(8,128)(2,1)S(1)}, u32[]{:S(2)}, u32[]{:S(2)}) collective-permute-start(bf16[2,128,128]{2,1,0:T(8,128)(2,1)S(1)} %copy-done.4), channel_id=1, source_target_pairs={{0,1},{1,0},{2,3},{3,2},{4,5},{5,4},{6,7},{7,6},{8,9},{9,8},{10,11... | collective-permute-start | bytes 196616 | tf_op jit(solution)/shard_map/ppermute | solution.py:611
  30.8 12.5 %collective-permute-start.2 = (bf16[2048,128]{1,0:T(8,128)(2,1)}, bf16[2048,128]{1,0:T(8,128)(2,1)S(1)}, u32[]{:S(2)}, u32[]{:S(2)}) collective-permute-start(bf16[2048,128]{1,0:T(8,128)(2,1)} %bitcast.12), channel_id=1, source_target_pairs={{0,1},{1,0},{2,3},{3,2},{4,5},{5,4},{6,7},{7,6},{8,9},{9,8},{10,11... | collective-permute-start | bytes 1572872 | tf_op jit(solution)/shard_map/ppermute | solution.py:611
  35.0 30.9 %copy-start.2 = (bf16[2,128,128]{2,1,0:T(8,128)(2,1)}, bf16[2,128,128]{2,1,0:T(8,128)(2,1)S(1)}, u32[]{:S(2)}) copy-start(bf16[2,128,128]{2,1,0:T(8,128)(2,1)S(1)} %collective-permute-done.6.refs_7_) | copy-start | bytes 196612
  35.1 10.2 %copy-start.1 = (bf16[2,2,128,128]{3,2,1,0:T(8,128)(2,1)}, bf16[2,2,128,128]{3,2,1,0:T(8,128)(2,1)S(1)}, u32[]{:S(2)}) copy-start(bf16[2,2,128,128]{3,2,1,0:T(8,128)(2,1)S(1)} %collective-permute-done.7.refs_9_) | copy-start | bytes 393220
  43.3 1.9 %collective-permute-start.8 = (bf16[2048,128]{1,0:T(8,128)(2,1)S(1)}, bf16[2048,128]{1,0:T(8,128)(2,1)S(1)}, u32[]{:S(2)}, u32[]{:S(2)}) collective-permute-start(bf16[2048,128]{1,0:T(8,128)(2,1)S(1)} %collective-permute-done.3.refs_2_.refs_6_), channel_id=1, source_target_pairs={{0,1},{1,0},{2,3},{3,2},{4,5},{5,4},{6,7},{7,6},{8,9},{9,8},{10,11... | collective-permute-start | bytes 1572872 | tf_op jit(solution)/shard_map/ppermute | solution.py:611
  49.4 14.3 %collective-permute-start.11 = (bf16[2048,128]{1,0:T(8,128)(2,1)}, bf16[2048,128]{1,0:T(8,128)(2,1)}, u32[]{:S(2)}, u32[]{:S(2)}) collective-permute-start(bf16[2048,128]{1,0:T(8,128)(2,1)} %get-tuple-element.54.refs_8_.refs_2_), channel_id=1, source_target_pairs={{0,2},{1,3},{2,0},{3,1},{4,6},{5,7},{6,4},{7,5},{8,10},{9,11},{10,... | collective-permute-start | bytes 1572872 | tf_op jit(solution)/shard_map/ppermute | solution.py:611
  54.9 21.0 %all-to-all-start.1 = ((f32[8,136,128]{2,1,0:T(8,128)}), f32[8,136,128]{2,1,0:T(8,128)}, u32[]{:S(2)}, u32[]{:S(2)}) async-start(f32[8,136,128]{2,1,0:T(8,128)} %weight_parts.1), calls=%async_computation.1 | async-start | bytes 1114112 | tf_op jit(solution)/shard_map/all_to_all | solution.py:653
  60.7 3.1 %collective-permute-start.10 = (bf16[2048,128]{1,0:T(8,128)(2,1)}, bf16[2048,128]{1,0:T(8,128)(2,1)S(1)}, u32[]{:S(2)}, u32[]{:S(2)}) collective-permute-start(bf16[2048,128]{1,0:T(8,128)(2,1)} %get-tuple-element.54.refs_8_.refs_2_), channel_id=1, source_target_pairs={{0,1},{1,0},{2,3},{3,2},{4,5},{5,4},{6,7},{7,6},{8,9},{9,8},{10,11... | collective-permute-start | bytes 1572872 | tf_op jit(solution)/shard_map/ppermute | solution.py:611
  63.8 2.1 %collective-permute-start.12 = (bf16[2048,128]{1,0:T(8,128)(2,1)}, bf16[2048,128]{1,0:T(8,128)(2,1)S(1)}, u32[]{:S(2)}, u32[]{:S(2)}) collective-permute-start(bf16[2048,128]{1,0:T(8,128)(2,1)} %collective-permute-done.11.refs_4_), channel_id=1, source_target_pairs={{0,1},{1,0},{2,3},{3,2},{4,5},{5,4},{6,7},{7,6},{8,9},{9,8},{10,11... | collective-permute-start | bytes 1572872 | tf_op jit(solution)/shard_map/ppermute | solution.py:611
  76.0 15.6 %all-to-all-start.2 = ((bf16[8,160,128]{2,1,0:T(8,128)(2,1)}), bf16[8,160,128]{2,1,0:T(8,128)(2,1)}, u32[]{:S(2)}, u32[]{:S(2)}) async-start(bf16[8,160,128]{2,1,0:T(8,128)(2,1)} %get-tuple-element.63), calls=%async_computation.2 | async-start | bytes 655360 | tf_op jit(solution)/shard_map/all_to_all | solution.py:659
  81.8 9.8 %copy-start.3 = (bf16[128,128]{1,0:T(8,128)(2,1)S(1)}, bf16[128,128]{1,0:T(8,128)(2,1)}, u32[]{:S(2)}) copy-start(bf16[128,128]{1,0:T(8,128)(2,1)} %get-tuple-element.55) | copy-start | bytes 98308
  81.8 9.8 %collective-permute-start.9 = (bf16[128,128]{1,0:T(8,128)(2,1)}, bf16[128,128]{1,0:T(8,128)(2,1)S(1)}, u32[]{:S(2)}, u32[]{:S(2)}) collective-permute-start(bf16[128,128]{1,0:T(8,128)(2,1)} %get-tuple-element.55), channel_id=1, source_target_pairs={{0,16},{4,20},{8,24},{12,28},{16,0},{20,4},{24,8},{28,12},{1,17},{... | collective-permute-start | bytes 98312 | tf_op jit(solution)/shard_map/ppermute | solution.py:663
  92.3 8.8 %all-to-all-start.3 = ((bf16[4,2,128,128]{3,2,1,0:T(8,128)(2,1)}), bf16[4,2,128,128]{3,2,1,0:T(8,128)(2,1)S(1)}, u32[]{:S(2)}, u32[]{:S(2)}) async-start(bf16[4,2,128,128]{3,2,1,0:T(8,128)(2,1)} %broadcast_in_dim.10), calls=%async_computation.3 | async-start | bytes 524288 | tf_op jit(solution)/shard_map/all_to_all | solution.py:669

commit v14 on v12

--- a/solution.py
+++ b/solution.py
@@ -317,6 +317,7 @@
         for row in range(0, width, min(chunk, width)):
             q, start = divmod(i * width + row, chunk)
             n = min(chunk, width)
+            q = q % (n_dom // 2) * 2 + q // (n_dom // 2)
             out[q, start : start + n, :] = block[row : row + n, :]
     for q in range(n_dom):
         out[q, chunk:, :] = jnp.broadcast_to(bias, (8, width))
@@ -524,41 +525,64 @@
     )(me, hbm(w_self), hbm(w_neigh))
 
 
-def sum_kernel(parts, out, bias):
-    n_dom, chunk, _ = out.shape
+def half_kernel(parts, out):
     total = parts[0]
-    for q in range(1, n_dom):
+    for q in range(1, parts.shape[0]):
         total += parts[q]
-    bias[...] = total[chunk : chunk + 1, :]
-    rows = total[:chunk, :].astype(BF16)
-    for q in range(n_dom):
-        out[q] = rows
-
-
-def sum_parts(parts):
-    n_dom, rows, width = parts.shape
+    out[...] = total
+
+
+def half_sum(parts):
+    return pl.pallas_call(
+        half_kernel,
+        out_shape=pltpu.HBM(parts.shape[1:], F32),
+        in_specs=[VMEM],
+        out_specs=VMEM,
+        compiler_params=params(),
+        cost_estimate=cost(0, 1 << 20),
+        name="half_sum",
+    )(hbm(parts))
+
+
+def sum_kernel(mine, other, out, bias):
+    half, _, chunk, _ = out.shape
+    for t in range(2):
+        first = t * (chunk + 8)
+        total = mine[first : first + chunk + 8, :] + other[first : first + chunk + 8, :]
+        if t == 0:
+            bias[...] = total[chunk : chunk + 1, :]
+        rows = total[:chunk, :].astype(BF16)
+        for j in range(half):
+            out[j, t] = rows
+
+
+def sum_parts(mine, other, half):
+    rows, width = mine.shape
     return pl.pallas_call(
         sum_kernel,
-        out_shape=(pltpu.HBM((n_dom, rows - 8, width), BF16), pltpu.HBM((1, width), F32)),
-        in_specs=[VMEM],
+        out_shape=(pltpu.HBM((half, 2, rows // 2 - 8, width), BF16), pltpu.HBM((1, width), F32)),
+        in_specs=[VMEM, VMEM],
         out_specs=(VMEM, VMEM),
         compiler_params=params(),
         cost_estimate=cost(0, 1 << 20),
         name="sum_parts",
-    )(hbm(parts))
+    )(hbm(mine), other)
 
 
 def place_kernel(me_s, sums, self_out, neigh_out):
     rows, width = self_out.shape
-    for i in range(2 * rows // width):
-        which, k = divmod(i, rows // width)
-        target = (self_out, neigh_out)[which]
-        at = pl.ds(pl.multiple_of((me_s[0] ^ k) * width, width), width)
-        target[at, :] = sums[i * width : (i + 1) * width, :].astype(F32)
-
-
-def place_weights(me, sums):
-    rows, width = sums.shape[0] // 2, sums.shape[1]
+    half, _, chunk, _ = sums.shape
+    n = min(chunk, width)
+    for row in range(0, 2 * rows, n):
+        index, part = divmod(row, chunk)
+        t, j = divmod(index, half)
+        which, k = divmod(row // width, rows // width)
+        at = pl.ds(pl.multiple_of((me_s[0] ^ k) * width + row % width, n), n)
+        (self_out, neigh_out)[which][at, :] = sums[j, t, part : part + n, :].astype(F32)
+
+
+def place_weights(me, sums, rows):
+    width = sums.shape[-1]
     return pl.pallas_call(
         place_kernel,
         out_shape=(pltpu.HBM((rows, width), F32),) * 2,
@@ -639,7 +663,10 @@
 
     grad_far = swap(grad_pre, far)
     parts = weight_parts(feats + aggs, hbm(grad_pre), n_dom)
-    part_sums = lax.all_to_all(parts, "dom", 0, 0, tiled=True)
+    half = n_dom // 2
+    halves = [list(range(half)), list(range(half, n_dom))]
+    parts = parts.reshape(half, -1, width)
+    part_sums = lax.all_to_all(parts, "dom", 0, 0, axis_index_groups=halves, tiled=True)
     grads = [hbm(grad_pre), swap(grad_pre, near), grad_far, swap(grad_far, near)]
 
     back_out, back_agg, direct = back_far(
@@ -647,11 +674,14 @@
     )
     back_in = lax.all_to_all(back_out, "dom", 0, 0, tiled=True)
     own = back_own(lists, edge_tiles, back_agg, direct).reshape(own_count, width)
-    weights_out, grad_bias = sum_parts(part_sums)
+    mine = half_sum(part_sums)
+    other = lax.ppermute(mine, "dom", [(j, j ^ half) for j in range(n_dom)])
+    other, own = lax.optimization_barrier((other, own))
+    weights_out, grad_bias = sum_parts(mine, other, half)
     weights_out, back_in, own = lax.optimization_barrier((weights_out, back_in, own))
-    weights_in = lax.all_to_all(weights_out, "dom", 0, 0, tiled=True)
+    weights_in = lax.all_to_all(weights_out, "dom", 0, 0, axis_index_groups=halves, tiled=True)
     grad_feats = finish(listed, send_count, hub_ids, back_in, own)
-    grad_self, grad_neigh = place_weights(me_s, weights_in.reshape(-1, width))
+    grad_self, grad_neigh = place_weights(me_s, weights_in, n_feat * width)
     return (output, grad_feats, grad_self, grad_neigh, grad_bias[0])
 
 

time: 104 us -> 107 us (1.029)
  starting transfers between devices: 26.5 us -> 29.4 us
  waiting for transfers between devices: 31.7 us -> 29.8 us
  Pallas kernels: 44.1 us -> 45.7 us
    ppermute x0 -> x1, waiting for transfers between devices: none -> 7.56 us  [body(): other = lax.ppermute(mine, 'dom', [(j, j ^ half) for j in range(n_dom)])]
    all_to_all x2, waiting for transfers between devices: 8.2 us -> 1.28 us  [the longest x1 1.27 us: body(): lax.all_to_all(weights_out, 'dom', 0, 0, axis_index_groups=halves, tiled=...]
    all_to_all x1, waiting for transfers between devices: 4.03 us -> 0.01 us  [body(): back_in = lax.all_to_all(back_out, 'dom', 0, 0, tiled=True)]
    ppermute x0 -> x1, starting transfers between devices: none -> 2.92 us  [body(): other = lax.ppermute(mine, 'dom', [(j, j ^ half) for j in range(n_dom)])]
    all_to_all x2, starting transfers between devices: 9.32 us -> 7.56 us  [the longest x1 4.15 us: body(): lax.all_to_all(parts, 'dom', 0, 0, axis_index_groups=halves, tiled=True)]
    all_to_all x1, starting transfers between devices: 4.08 us -> 5.74 us  [body(): back_in = lax.all_to_all(back_out, 'dom', 0, 0, tiled=True)]
    pallas_call x1 -> x2, Pallas kernels: 1.79 us -> 3.37 us  [the longest x1 1.74 us: half_sum(): pl.pallas_call(half_kernel, out_shape=pltpu.HBM(parts.shape[1:], F32), in...]
    ppermute x12, waiting for transfers between devices: 17.7 us -> 19.2 us  [swap(): return lax.ppermute(x, 'feat', [(j, j ^ k) for j in range(n_feat)])]
  transfers between devices with their start and end apart: 16 -> 17, of which waited for: 9 -> 8; matrix products, arithmetic and copies ran while one was open for 0% -> 0% of each run, Pallas kernels for 34% -> 34%
where the time goes in v14:
time: 107 us; the launch traced here: 106 us
  Pallas kernels  45.7 us (43%)
  waiting for transfers between devices  29.8 us (28%)
  starting transfers between devices  29.4 us (27%)
    ppermute x12, waiting for transfers between devices, swap(): return lax.ppermute(x, 'feat', [(j, j ^ k) for j in range(n_feat)])  19.2 us
    pallas_call x2, Pallas kernels, stream_call(): pl.pallas_call(run, out_shape=tuple((pltpu.HBM(shape, t) for shape, t in...  8.18 us
    ppermute x1, waiting for transfers between devices, body(): other = lax.ppermute(mine, 'dom', [(j, j ^ half) for j in range(n_dom)])  7.56 us
    all_to_all x1, starting transfers between devices, body(): incoming = lax.all_to_all(outgoing, 'dom', 0, 0, tiled=True)  7.26 us
    pallas_call x1, Pallas kernels, back_far(): pl.pallas_call(functools.partial(back_far_kernel, n_feat=n_feat), out_sha...  6.3 us
    ppermute x12, starting transfers between devices, swap(): return lax.ppermute(x, 'feat', [(j, j ^ k) for j in range(n_feat)])  5.95 us
    all_to_all x1, starting transfers between devices, body(): back_in = lax.all_to_all(back_out, 'dom', 0, 0, tiled=True)  5.74 us
    pallas_call x1, Pallas kernels, own_tiles(): pl.pallas_call(functools.partial(own_kernel, far_blocks=far_blocks), out_...  4.97 us
  transfers between devices with their start and end apart: 17, of which 8 were waited for; matrix products, arithmetic and copies ran while one was open for 0% of the time, Pallas kernels for 34%

profile of v14, /device:TPU:0, one launch (start us, length us, event | category | flops | bytes accessed | tf_op | source)
XLA Modules:
  0.0 105.7 jit_solution(5083210985334590314)
XLA Ops:
  0.6 4.3 %pick_rows.1 = bf16[8,160,128]{2,1,0:T(8,128)(2,1)} custom-call(s32[8,128]{1,0:T(8,128)} %bitcast.15, s32[1,8]{1,0:T(1,128)} %count_h.3, s32[32]{0:T(128)} %hub_h.3, bf16[2048,128]{1,0:T(8,128)(2,1)} %refs_0_.3), custom_call_target="tpu_custom_call" | custom-call | bytes 2097152 | tf_op jit(solution)/shard_map/pick_rows/pallas_call | solution.py:79
  5.0 7.3 %all-to-all-start = ((bf16[8,160,128]{2,1,0:T(8,128)(2,1)}), bf16[8,160,128]{2,1,0:T(8,128)(2,1)}, u32[]{:S(2)}, u32[]{:S(2)}) async-start(bf16[8,160,128]{2,1,0:T(8,128)(2,1)} %pick_rows.1), calls=%async_computation | async-start | bytes 655360 | tf_op jit(solution)/shard_map/all_to_all | solution.py:629
  12.3 1.5 %collective-permute-start = (bf16[2048,128]{1,0:T(8,128)(2,1)}, bf16[2048,128]{1,0:T(8,128)(2,1)}, u32[]{:S(2)}, u32[]{:S(2)}) collective-permute-start(bf16[2048,128]{1,0:T(8,128)(2,1)} %refs_0_.3), channel_id=1, source_target_pairs={{0,2},{1,3},{2,0},{3,1},{4,6},{5,7},{6,4},{7,5},{8,10},{9,11},{10,... | collective-permute-start | bytes 1572872 | tf_op jit(solution)/shard_map/ppermute | solution.py:624
  13.8 1.7 %cut_weights.1 = (bf16[2,128,128]{2,1,0:T(8,128)(2,1)}, bf16[2,128,128]{2,1,0:T(8,128)(2,1)}, bf16[2,2,128,128]{3,2,1,0:T(8,128)(2,1)}) custom-call(s32[1]{0:T(128)} %bitcast.me_s, bf16[512,128]{1,0:T(8,128)(2,1)} %refs_4_.1, bf16[512,128]{1,0:T(8,128)(2,1)} %refs_6_.1), custom_call_target="tpu_custom_call" | custom-call | bytes 1048576 | tf_op jit(solution)/shard_map/cut_weights/pallas_call | solution.py:517
  15.5 0.5 collective-permute-start.1
  16.0 5.0 %own_tiles.1 = (f32[16,128,128]{2,1,0:T(8,128)}, s32[2,122]{1,0:T(2,128)S(1)}) custom-call(s32[106]{0:T(128)} %dst_h.1, s32[106]{0:T(128)} %src_h.1, bf16[106,128,128]{2,1,0:T(8,128)(2,1)} %tiles.3, bf16[16,128,128]{2,1,0:T(8,128)(2,1)} %bitcast.8), custom_call_target="tpu_custom_call" | custom-call | flops 444596224 | bytes 8388608 | tf_op jit(solution)/shard_map/own_tiles/pallas_call | solution.py:176
  20.9 1.7 %all-to-all-done.incoming_h = bf16[8,160,128]{2,1,0:T(8,128)(2,1)} async-done(((bf16[8,160,128]{2,1,0:T(8,128)(2,1)}), bf16[8,160,128]{2,1,0:T(8,128)(2,1)}, u32[]{:S(2)}, u32[]{:S(2)}) %all-to-all-start) | async-done | bytes 327712 | tf_op jit(solution)/shard_map/all_to_all | solution.py:629
  22.7 3.8 %far_tiles.1 = bf16[16,128,128]{2,1,0:T(8,128)(2,1)} custom-call(s32[2,122]{1,0:T(2,128)S(1)} %get-tuple-element.42.lists.refs_0_, bf16[106,128,128]{2,1,0:T(8,128)(2,1)S(1)} %copy-done, bf16[8,160,128]{2,1,0:T(8,128)(2,1)} %all-to-all-done.incoming_h, f32[16,128,128]{2,1,0:T(8,128)} %get-tuple-element.43.base_h), custom_call_target="tpu_custom_call" | custom-call | flops 222298112 | bytes 4194304 | tf_op jit(solution)/shard_map/far_tiles/pallas_call | solution.py:218
  26.5 2.3 %collective-permute-done.1.refs_8_ = bf16[2,2,128,128]{3,2,1,0:T(8,128)(2,1)} collective-permute-done((bf16[2,2,128,128]{3,2,1,0:T(8,128)(2,1)}, bf16[2,2,128,128]{3,2,1,0:T(8,128)(2,1)}, u32[]{:S(2)}, u32[]{:S(2)}) %collective-permute-start.1) | collective-permute-done | bytes 131104 | tf_op jit(solution)/shard_map/ppermute | solution.py:624
  28.8 1.5 %collective-permute-start.3 = (bf16[2048,128]{1,0:T(8,128)(2,1)}, bf16[2048,128]{1,0:T(8,128)(2,1)S(1)}, u32[]{:S(2)}, u32[]{:S(2)}) collective-permute-start(bf16[2048,128]{1,0:T(8,128)(2,1)} %bitcast.9), channel_id=1, source_target_pairs={{0,2},{1,3},{2,0},{3,1},{4,6},{5,7},{6,4},{7,5},{8,10},{9,11},{10,... | collective-permute-start | bytes 1572872 | tf_op jit(solution)/shard_map/ppermute | solution.py:624
  30.5 0.3 collective-permute-start.6
  30.8 0.2 collective-permute-start.2
  31.0 4.0 %self_dense.1.refs_4_ = f32[2048,128]{1,0:T(8,128)} custom-call(s32[1]{0:T(128)} %bitcast.me_s, bf16[2048,128]{1,0:T(8,128)(2,1)} %refs_0_.3, bf16[2048,128]{1,0:T(8,128)(2,1)} %collective-permute-done.4.refs_1_, bf16[2048,128]{1,0:T(8,128)(2,1)} %collective-permute-done.refs_2_, bf16[2048,128]{1,0:T(8,128)(2,1)S(1)} %collective-permute-done.5.refs_3_, ...), custom_call_target="tpu_custom_call" | custom-call | flops 268435456 | bytes 4194304 | tf_op jit(solution)/shard_map/self_dense/pallas_call | solution.py:280
  35.1 8.2 %collective-permute-done.3.refs_2_.refs_6_ = bf16[2048,128]{1,0:T(8,128)(2,1)S(1)} collective-permute-done((bf16[2048,128]{1,0:T(8,128)(2,1)}, bf16[2048,128]{1,0:T(8,128)(2,1)S(1)}, u32[]{:S(2)}, u32[]{:S(2)}) %collective-permute-start.3) | collective-permute-done | bytes 524320 | tf_op jit(solution)/shard_map/ppermute | solution.py:624
  43.3 1.9 %collective-permute-done.8.refs_3_.refs_7_ = bf16[2048,128]{1,0:T(8,128)(2,1)S(1)} collective-permute-done((bf16[2048,128]{1,0:T(8,128)(2,1)S(1)}, bf16[2048,128]{1,0:T(8,128)(2,1)S(1)}, u32[]{:S(2)}, u32[]{:S(2)}) %collective-permute-start.8) | collective-permute-done | bytes 524320 | tf_op jit(solution)/shard_map/ppermute | solution.py:624
  45.2 4.2 %forward_dense.1 = (bf16[2048,128]{1,0:T(8,128)(2,1)}, bf16[2048,128]{1,0:T(8,128)(2,1)}) custom-call(s32[1]{0:T(128)} %bitcast.me_s, bf16[2048,128]{1,0:T(8,128)(2,1)} %bitcast.11, bf16[2048,128]{1,0:T(8,128)(2,1)S(1)} %collective-permute-done.2.refs_1_.refs_5_, bf16[2048,128]{1,0:T(8,128)(2,1)S(1)} %collective-permute-done.3.refs_2_.refs_6_, ...), custom_call_target="tpu_custom_call" | custom-call | flops 268435456 | bytes 4194304 | tf_op jit(solution)/shard_map/forward_dense/pallas_call | solution.py:280
  49.4 1.6 %collective-permute-start.11 = (bf16[2048,128]{1,0:T(8,128)(2,1)}, bf16[2048,128]{1,0:T(8,128)(2,1)}, u32[]{:S(2)}, u32[]{:S(2)}) collective-permute-start(bf16[2048,128]{1,0:T(8,128)(2,1)} %get-tuple-element.54.refs_8_.refs_2_), channel_id=1, source_target_pairs={{0,2},{1,3},{2,0},{3,1},{4,6},{5,7},{6,4},{7,5},{8,10},{9,11},{10,... | collective-permute-start | bytes 1572872 | tf_op jit(solution)/shard_map/ppermute | solution.py:624
  51.0 3.9 %weight_parts.1 = f32[8,136,128]{2,1,0:T(8,128)} custom-call(bf16[2048,128]{1,0:T(8,128)(2,1)} %refs_0_.3, bf16[2048,128]{1,0:T(8,128)(2,1)} %collective-permute-done.4.refs_1_, bf16[2048,128]{1,0:T(8,128)(2,1)} %collective-permute-done.refs_2_, bf16[2048,128]{1,0:T(8,128)(2,1)S(1)} %collective-permute-done.5.refs_3_, bf16[2048,128]{1,0:T(8,128)(2,1)} %bitcast.12, ...), custom_call_target="tpu_custom_call" | custom-call | flops 536870912 | bytes 4194304 | tf_op jit(solution)/shard_map/weight_parts/pallas_call | solution.py:331
  54.9 4.2 %all-to-all-start.1 = ((f32[4,272,128]{2,1,0:T(8,128)}), f32[4,272,128]{2,1,0:T(8,128)}, u32[]{:S(2)}, u32[]{:S(2)}) async-start(f32[4,272,128]{2,1,0:T(8,128)} %bitcast.14), calls=%async_computation.1 | async-start | bytes 1114112 | tf_op jit(solution)/shard_map/all_to_all | solution.py:669
  59.1 4.6 %collective-permute-done.11.refs_4_ = bf16[2048,128]{1,0:T(8,128)(2,1)} collective-permute-done((bf16[2048,128]{1,0:T(8,128)(2,1)}, bf16[2048,128]{1,0:T(8,128)(2,1)}, u32[]{:S(2)}, u32[]{:S(2)}) %collective-permute-start.11) | collective-permute-done | bytes 524320 | tf_op jit(solution)/shard_map/ppermute | solution.py:624
  63.8 2.1 %collective-permute-done.12.refs_5_ = bf16[2048,128]{1,0:T(8,128)(2,1)S(1)} collective-permute-done((bf16[2048,128]{1,0:T(8,128)(2,1)}, bf16[2048,128]{1,0:T(8,128)(2,1)S(1)}, u32[]{:S(2)}, u32[]{:S(2)}) %collective-permute-start.12) | collective-permute-done | bytes 524320 | tf_op jit(solution)/shard_map/ppermute | solution.py:624
  65.9 6.3 %back_far.1 = (bf16[8,160,128]{2,1,0:T(8,128)(2,1)}, bf16[16,128,128]{2,1,0:T(8,128)(2,1)}, f32[16,128,128]{2,1,0:T(8,128)}) custom-call(s32[2,122]{1,0:T(2,128)S(1)} %get-tuple-element.42.lists.refs_0_, bf16[106,128,128]{2,1,0:T(8,128)(2,1)S(1)} %copy-done, bf16[2048,128]{1,0:T(8,128)(2,1)} %get-tuple-element.54.refs_8_.refs_2_, ...), custom_call_target="tpu_custom_call" | custom-call | flops 536870912 | bytes 4194304 | tf_op jit(solution)/shard_map/back_far/pallas_call | solution.py:394
  72.2 5.7 %all-to-all-start.2 = ((bf16[8,160,128]{2,1,0:T(8,128)(2,1)}), bf16[8,160,128]{2,1,0:T(8,128)(2,1)}, u32[]{:S(2)}, u32[]{:S(2)}) async-start(bf16[8,160,128]{2,1,0:T(8,128)(2,1)} %get-tuple-element.63), calls=%async_computation.2 | async-start | bytes 655360 | tf_op jit(solution)/shard_map/all_to_all | solution.py:675
  78.0 1.7 %half_sum.1.mine = f32[272,128]{1,0:T(8,128)} custom-call(f32[4,272,128]{2,1,0:T(8,128)} %all-to-all-done.1.parts), custom_call_target="tpu_custom_call" | custom-call | bytes 1048576 | tf_op jit(solution)/shard_map/half_sum/pallas_call | solution.py:536
  79.7 2.9 %collective-permute-start.9 = (f32[272,128]{1,0:T(8,128)}, f32[272,128]{1,0:T(8,128)S(1)}, u32[]{:S(2)}, u32[]{:S(2)}) collective-permute-start(f32[272,128]{1,0:T(8,128)} %half_sum.1.mine), channel_id=1, source_target_pairs={{0,16},{4,20},{8,24},{12,28},{16,0},{20,4},{24,8},{28,12},{1,17},{... | collective-permute-start | bytes 417800 | tf_op jit(solution)/shard_map/ppermute | solution.py:678
  82.6 4.3 %back_own.1 = f32[16,128,128]{2,1,0:T(8,128)} custom-call(s32[2,122]{1,0:T(2,128)S(1)} %get-tuple-element.42.lists.refs_0_, bf16[106,128,128]{2,1,0:T(8,128)(2,1)S(1)} %copy-done, bf16[16,128,128]{2,1,0:T(8,128)(2,1)} %get-tuple-element.59.back_h, f32[16,128,128]{2,1,0:T(8,128)} %get-tuple-element.60.direct_h), custom_call_target="tpu_custom_call" | custom-call | flops 444596224 | bytes 8388608 | tf_op jit(solution)/shard_map/back_own/pallas_call | solution.py:423
  86.9 7.6 %collective-permute-done.9.other = f32[272,128]{1,0:T(8,128)S(1)} collective-permute-done((f32[272,128]{1,0:T(8,128)}, f32[272,128]{1,0:T(8,128)S(1)}, u32[]{:S(2)}, u32[]{:S(2)}) %collective-permute-start.9) | collective-permute-done | bytes 139296 | tf_op jit(solution)/shard_map/ppermute | solution.py:678
  94.5 1.6 %sum_parts.1 = (bf16[4,2,128,128]{3,2,1,0:T(8,128)(2,1)}, f32[1,128]{1,0:T(1,128)}) custom-call(f32[272,128]{1,0:T(8,128)} %half_sum.1.mine, f32[272,128]{1,0:T(8,128)S(1)} %collective-permute-done.9.other), custom_call_target="tpu_custom_call" | custom-call | bytes 1048576 | tf_op jit(solution)/shard_map/sum_parts/pallas_call | solution.py:561
  96.1 3.4 %all-to-all-start.3 = ((bf16[4,2,128,128]{3,2,1,0:T(8,128)(2,1)}), bf16[4,2,128,128]{3,2,1,0:T(8,128)(2,1)S(1)}, u32[]{:S(2)}, u32[]{:S(2)}) async-start(bf16[4,2,128,128]{3,2,1,0:T(8,128)(2,1)} %get-tuple-element.67), calls=%async_computation.3 | async-start | bytes 524288 | tf_op jit(solution)/shard_map/all_to_all | solution.py:682
  99.6 4.1 %finish.1 = f32[2048,128]{1,0:T(8,128)} custom-call(s32[8,128]{1,0:T(8,128)} %bitcast.16, s32[1,8]{1,0:T(1,128)} %count_h.3, s32[32]{0:T(128)} %hub_h.3, bf16[8,160,128]{2,1,0:T(8,128)(2,1)} %all-to-all-done.2.incoming_h, f32[2048,128]{1,0:T(8,128)} %bitcast.13), custom_call_target="tpu_custom_call" | custom-call | flops 536870912 | bytes 4194304 | tf_op jit(solution)/shard_map/finish/pallas_call | solution.py:485
  103.6 1.3 %all-to-all-done.3.sums = bf16[4,2,128,128]{3,2,1,0:T(8,128)(2,1)S(1)} async-done(((bf16[4,2,128,128]{3,2,1,0:T(8,128)(2,1)}), bf16[4,2,128,128]{3,2,1,0:T(8,128)(2,1)S(1)}, u32[]{:S(2)}, u32[]{:S(2)}) %all-to-all-start.3) | async-done | bytes 262176 | tf_op jit(solution)/shard_map/all_to_all | solution.py:682
  104.9 0.8 place_weights.1
  (23 shorter events, 0.4 us)
Async XLA Ops:
  0.6 22.1 %copy-start = (bf16[106,128,128]{2,1,0:T(8,128)(2,1)S(1)}, bf16[106,128,128]{2,1,0:T(8,128)(2,1)}, u32[]{:S(2)}) copy-start(bf16[106,128,128]{2,1,0:T(8,128)(2,1)} %tiles.3) | copy-start | bytes 10420228
  5.0 17.7 %all-to-all-start = ((bf16[8,160,128]{2,1,0:T(8,128)(2,1)}), bf16[8,160,128]{2,1,0:T(8,128)(2,1)}, u32[]{:S(2)}, u32[]{:S(2)}) async-start(bf16[8,160,128]{2,1,0:T(8,128)(2,1)} %pick_rows.1), calls=%async_computation | async-start | bytes 655360 | tf_op jit(solution)/shard_map/all_to_all | solution.py:629
  12.3 16.5 %collective-permute-start = (bf16[2048,128]{1,0:T(8,128)(2,1)}, bf16[2048,128]{1,0:T(8,128)(2,1)}, u32[]{:S(2)}, u32[]{:S(2)}) collective-permute-start(bf16[2048,128]{1,0:T(8,128)(2,1)} %refs_0_.3), channel_id=1, source_target_pairs={{0,2},{1,3},{2,0},{3,1},{4,6},{5,7},{6,4},{7,5},{8,10},{9,11},{10,... | collective-permute-start | bytes 1572872 | tf_op jit(solution)/shard_map/ppermute | solution.py:624
  15.5 13.3 %collective-permute-start.1 = (bf16[2,2,128,128]{3,2,1,0:T(8,128)(2,1)}, bf16[2,2,128,128]{3,2,1,0:T(8,128)(2,1)}, u32[]{:S(2)}, u32[]{:S(2)}) collective-permute-start(bf16[2,2,128,128]{3,2,1,0:T(8,128)(2,1)} %get-tuple-element.44), channel_id=1, source_target_pairs={{0,2},{1,3},{2,0},{3,1},{4,6},{5,7},{6,4},{7,5},{8,10},{9,11},{10,... | collective-permute-start | bytes 393224 | tf_op jit(solution)/shard_map/ppermute | solution.py:624
  16.0 14.8 %collective-permute-start.4 = (bf16[2048,128]{1,0:T(8,128)(2,1)}, bf16[2048,128]{1,0:T(8,128)(2,1)}, u32[]{:S(2)}, u32[]{:S(2)}) collective-permute-start(bf16[2048,128]{1,0:T(8,128)(2,1)} %refs_0_.3), channel_id=1, source_target_pairs={{0,1},{1,0},{2,3},{3,2},{4,5},{5,4},{6,7},{7,6},{8,9},{9,8},{10,11... | collective-permute-start | bytes 1572872 | tf_op jit(solution)/shard_map/ppermute | solution.py:624
  22.7 7.8 %copy-start.3 = (bf16[2,128,128]{2,1,0:T(8,128)(2,1)S(1)}, bf16[2,128,128]{2,1,0:T(8,128)(2,1)}, u32[]{:S(2)}) copy-start(bf16[2,128,128]{2,1,0:T(8,128)(2,1)} %get-tuple-element.49) | copy-start | bytes 196612
  28.8 2.3 %collective-permute-start.5 = (bf16[2048,128]{1,0:T(8,128)(2,1)}, bf16[2048,128]{1,0:T(8,128)(2,1)S(1)}, u32[]{:S(2)}, u32[]{:S(2)}) collective-permute-start(bf16[2048,128]{1,0:T(8,128)(2,1)} %collective-permute-done.refs_2_), channel_id=1, source_target_pairs={{0,1},{1,0},{2,3},{3,2},{4,5},{5,4},{6,7},{7,6},{8,9},{9,8},{10,11... | collective-permute-start | bytes 1572872 | tf_op jit(solution)/shard_map/ppermute | solution.py:624
  28.8 14.5 %collective-permute-start.3 = (bf16[2048,128]{1,0:T(8,128)(2,1)}, bf16[2048,128]{1,0:T(8,128)(2,1)S(1)}, u32[]{:S(2)}, u32[]{:S(2)}) collective-permute-start(bf16[2048,128]{1,0:T(8,128)(2,1)} %bitcast.9), channel_id=1, source_target_pairs={{0,2},{1,3},{2,0},{3,1},{4,6},{5,7},{6,4},{7,5},{8,10},{9,11},{10,... | collective-permute-start | bytes 1572872 | tf_op jit(solution)/shard_map/ppermute | solution.py:624
  30.3 4.8 %collective-permute-start.7 = (bf16[2,2,128,128]{3,2,1,0:T(8,128)(2,1)}, bf16[2,2,128,128]{3,2,1,0:T(8,128)(2,1)S(1)}, u32[]{:S(2)}, u32[]{:S(2)}) collective-permute-start(bf16[2,2,128,128]{3,2,1,0:T(8,128)(2,1)} %collective-permute-done.1.refs_8_), channel_id=1, source_target_pairs={{0,1},{1,0},{2,3},{3,2},{4,5},{5,4},{6,7},{7,6},{8,9},{9,8},{10,11... | collective-permute-start | bytes 393224 | tf_op jit(solution)/shard_map/ppermute | solution.py:624
  30.5 4.5 %collective-permute-start.6 = (bf16[2,128,128]{2,1,0:T(8,128)(2,1)S(1)}, bf16[2,128,128]{2,1,0:T(8,128)(2,1)S(1)}, u32[]{:S(2)}, u32[]{:S(2)}) collective-permute-start(bf16[2,128,128]{2,1,0:T(8,128)(2,1)S(1)} %copy-done.3), channel_id=1, source_target_pairs={{0,1},{1,0},{2,3},{3,2},{4,5},{5,4},{6,7},{7,6},{8,9},{9,8},{10,11... | collective-permute-start | bytes 196616 | tf_op jit(solution)/shard_map/ppermute | solution.py:624
  30.8 12.5 %collective-permute-start.2 = (bf16[2048,128]{1,0:T(8,128)(2,1)}, bf16[2048,128]{1,0:T(8,128)(2,1)S(1)}, u32[]{:S(2)}, u32[]{:S(2)}) collective-permute-start(bf16[2048,128]{1,0:T(8,128)(2,1)} %bitcast.10), channel_id=1, source_target_pairs={{0,1},{1,0},{2,3},{3,2},{4,5},{5,4},{6,7},{7,6},{8,9},{9,8},{10,11... | collective-permute-start | bytes 1572872 | tf_op jit(solution)/shard_map/ppermute | solution.py:624
  35.0 30.9 %copy-start.2 = (bf16[2,128,128]{2,1,0:T(8,128)(2,1)}, bf16[2,128,128]{2,1,0:T(8,128)(2,1)S(1)}, u32[]{:S(2)}) copy-start(bf16[2,128,128]{2,1,0:T(8,128)(2,1)S(1)} %collective-permute-done.6.refs_7_) | copy-start | bytes 196612
  35.1 10.2 %copy-start.1 = (bf16[2,2,128,128]{3,2,1,0:T(8,128)(2,1)}, bf16[2,2,128,128]{3,2,1,0:T(8,128)(2,1)S(1)}, u32[]{:S(2)}) copy-start(bf16[2,2,128,128]{3,2,1,0:T(8,128)(2,1)S(1)} %collective-permute-done.7.refs_9_) | copy-start | bytes 393220
  43.3 1.9 %collective-permute-start.8 = (bf16[2048,128]{1,0:T(8,128)(2,1)S(1)}, bf16[2048,128]{1,0:T(8,128)(2,1)S(1)}, u32[]{:S(2)}, u32[]{:S(2)}) collective-permute-start(bf16[2048,128]{1,0:T(8,128)(2,1)S(1)} %collective-permute-done.3.refs_2_.refs_6_), channel_id=1, source_target_pairs={{0,1},{1,0},{2,3},{3,2},{4,5},{5,4},{6,7},{7,6},{8,9},{9,8},{10,11... | collective-permute-start | bytes 1572872 | tf_op jit(solution)/shard_map/ppermute | solution.py:624
  49.4 14.3 %collective-permute-start.11 = (bf16[2048,128]{1,0:T(8,128)(2,1)}, bf16[2048,128]{1,0:T(8,128)(2,1)}, u32[]{:S(2)}, u32[]{:S(2)}) collective-permute-start(bf16[2048,128]{1,0:T(8,128)(2,1)} %get-tuple-element.54.refs_8_.refs_2_), channel_id=1, source_target_pairs={{0,2},{1,3},{2,0},{3,1},{4,6},{5,7},{6,4},{7,5},{8,10},{9,11},{10,... | collective-permute-start | bytes 1572872 | tf_op jit(solution)/shard_map/ppermute | solution.py:624
  54.9 17.3 %all-to-all-start.1 = ((f32[4,272,128]{2,1,0:T(8,128)}), f32[4,272,128]{2,1,0:T(8,128)}, u32[]{:S(2)}, u32[]{:S(2)}) async-start(f32[4,272,128]{2,1,0:T(8,128)} %bitcast.14), calls=%async_computation.1 | async-start | bytes 1114112 | tf_op jit(solution)/shard_map/all_to_all | solution.py:669
  59.1 4.7 %collective-permute-start.10 = (bf16[2048,128]{1,0:T(8,128)(2,1)}, bf16[2048,128]{1,0:T(8,128)(2,1)S(1)}, u32[]{:S(2)}, u32[]{:S(2)}) collective-permute-start(bf16[2048,128]{1,0:T(8,128)(2,1)} %get-tuple-element.54.refs_8_.refs_2_), channel_id=1, source_target_pairs={{0,1},{1,0},{2,3},{3,2},{4,5},{5,4},{6,7},{7,6},{8,9},{9,8},{10,11... | collective-permute-start | bytes 1572872 | tf_op jit(solution)/shard_map/ppermute | solution.py:624
  63.8 2.1 %collective-permute-start.12 = (bf16[2048,128]{1,0:T(8,128)(2,1)}, bf16[2048,128]{1,0:T(8,128)(2,1)S(1)}, u32[]{:S(2)}, u32[]{:S(2)}) collective-permute-start(bf16[2048,128]{1,0:T(8,128)(2,1)} %collective-permute-done.11.refs_4_), channel_id=1, source_target_pairs={{0,1},{1,0},{2,3},{3,2},{4,5},{5,4},{6,7},{7,6},{8,9},{9,8},{10,11... | collective-permute-start | bytes 1572872 | tf_op jit(solution)/shard_map/ppermute | solution.py:624
  72.2 23.9 %all-to-all-start.2 = ((bf16[8,160,128]{2,1,0:T(8,128)(2,1)}), bf16[8,160,128]{2,1,0:T(8,128)(2,1)}, u32[]{:S(2)}, u32[]{:S(2)}) async-start(bf16[8,160,128]{2,1,0:T(8,128)(2,1)} %get-tuple-element.63), calls=%async_computation.2 | async-start | bytes 655360 | tf_op jit(solution)/shard_map/all_to_all | solution.py:675
  79.7 14.8 %collective-permute-start.9 = (f32[272,128]{1,0:T(8,128)}, f32[272,128]{1,0:T(8,128)S(1)}, u32[]{:S(2)}, u32[]{:S(2)}) collective-permute-start(f32[272,128]{1,0:T(8,128)} %half_sum.1.mine), channel_id=1, source_target_pairs={{0,16},{4,20},{8,24},{12,28},{16,0},{20,4},{24,8},{28,12},{1,17},{... | collective-permute-start | bytes 417800 | tf_op jit(solution)/shard_map/ppermute | solution.py:678
  96.1 8.8 %all-to-all-start.3 = ((bf16[4,2,128,128]{3,2,1,0:T(8,128)(2,1)}), bf16[4,2,128,128]{3,2,1,0:T(8,128)(2,1)S(1)}, u32[]{:S(2)}, u32[]{:S(2)}) async-start(bf16[4,2,128,128]{3,2,1,0:T(8,128)(2,1)} %get-tuple-element.67), calls=%async_computation.3 | async-start | bytes 524288 | tf_op jit(solution)/shard_map/all_to_all | solution.py:682
